TPU v7x, 128 devices: a whole 4x4x4 slice. The times are simulated.
128 devices in a mesh: slab: 8 (over z, core), sector: 16 (over y, x).
Axes of the slice: x: 4, y: 4, z: 4, core: 2. Of those that a mesh axis runs over, the one named last changes fastest.
Arguments:
- sources: bfloat16 [524288, 128], P(('slab', 'sector')), may hold values from -6 to 6
- bases: bfloat16 [2048, 256, 64], P(('slab', 'sector')), may hold values from -0.375 to 0.375
- leaf_parent: int32 [2048], P(('slab', 'sector')), may hold values from 0 to 1023, as said below
- up_transfer: float32 [2048, 64, 64], P(('slab', 'sector')), may hold values from -0.5 to 0.5
- root_transfer: float32 [1024, 64, 64], P(('slab', 'sector')), may hold values from -0.25 to 0.25
- top_transfer: float32 [256, 64, 64], replicated, may hold values from -0.75 to 0.75
- top_coupling: float32 [256, 64, 64], replicated, may hold values from -0.75 to 0.75
- near_list: int32 [2048, 8], P(('slab', 'sector')), may hold values from 0 to 2047, as said below
- near_blocks: bfloat16 [2048, 8, 256, 256], P(('slab', 'sector')), may hold values from -0.125 to 0.125
- far_list: int32 [2048, 16], P(('slab', 'sector')), may hold values from 0 to 2047, as said below
- far_count: int32 [2048], P(('slab', 'sector')), may hold values from 1 to 16, as said below
- far_coupling: float32 [2048, 16, 64, 64], P(('slab', 'sector')), may hold values from -0.1875 to 0.1875
Outputs:
- field: bfloat16 [524288, 128], P(('slab', 'sector'))
Inputs may be any that keep to these rules, and one draw needn't show every extreme that they name: leaf_parent pairs the leaves of each device d: every cluster d * 8 to (d + 1) * 8 - 1 is the parent of exactly two of device d's leaves. `near_list`: each entry is a leaf on the same device or on a device at most one slab and at most one sector away, sectors counted around the cycle. `far_list`: each entry is a leaf of the same slab. `far_count`: some leaf uses all 16 slots.
All inputs are finite; a program needn't handle non-finite values.
Results may differ from a plain program's by a relative error of at most 0.0085.
Values may be sent and summed in bfloat16 or wider, within the bound.
No kernel may reach another device: no remote copies, remote signals or barrier semaphores. Data moves between devices by JAX's collectives and lax.ppermute only.
A program may use at most 256 MiB of HBM per device.

v0:
```python
import jax
import jax.numpy as jnp
from jax import lax
from jax.sharding import PartitionSpec as P

highest = lax.Precision.HIGHEST


def partner(array, axis, stride):
    return lax.ppermute(array, axis, [(i, i ^ 1 << stride) for i in range(lax.axis_size(axis))])


def with_halo(cells, sides, width, closed):
    for axis, dim in sides:
        count = lax.axis_size(axis)
        ends = count if closed else count - 1
        head = lax.slice_in_dim(cells, 0, width, axis=dim)
        tail = lax.slice_in_dim(cells, cells.shape[dim] - width, cells.shape[dim], axis=dim)
        cells = jnp.concatenate(
            [
                lax.ppermute(tail, axis, [(i, (i + 1) % count) for i in range(ends)]),
                cells,
                lax.ppermute(head, axis, [((i + 1) % count, i) for i in range(ends)]),
            ],
            axis=dim,
        )
    return cells


def pick_matrix(table, position):
    return lax.dynamic_index_in_dim(table, position, axis=0, keepdims=False)


def local(
    sources,
    bases,
    leaf_parent,
    up_transfer,
    root_transfer,
    top_transfer,
    top_coupling,
    near_list,
    near_blocks,
    far_list,
    far_count,
    far_coupling,
):
    leaf_total = bases.shape[0]
    leaf_size = bases.shape[1]
    rank_size = bases.shape[2]
    rhs_count = sources.shape[1]
    near_count = near_list.shape[1]
    cluster_total = leaf_total // 2
    slab_count = lax.axis_size("slab")
    sector_count = lax.axis_size("sector")
    devices = slab_count * sector_count
    depth = devices.bit_length() - 1
    slab_pos = lax.axis_index("slab")
    sector_pos = lax.axis_index("sector")
    device = slab_pos * sector_count + sector_pos
    panels = sources.reshape(leaf_total, leaf_size, rhs_count)
    leaf_coefs = jnp.einsum("lpk,lpr->lkr", bases, panels, preferred_element_type=jnp.float32)
    lifted = jnp.einsum("lkj,lkr->ljr", up_transfer, leaf_coefs, precision=highest)
    local_parent = leaf_parent - device * cluster_total
    member = (local_parent[:, None] == jnp.arange(cluster_total, dtype=jnp.int32)[None, :]).astype(
        jnp.float32
    )
    cluster_coefs = jnp.einsum("lc,ljr->cjr", member, lifted, precision=highest)
    raised = jnp.einsum("ckj,ckr->cjr", root_transfer, cluster_coefs, precision=highest)
    device_root = jnp.sum(raised, axis=0)
    coupled = []
    current = device_root
    for level in range(depth):
        nodes_now = devices >> level
        node = device >> level
        sibling_coef = partner(current, ("slab", "sector"), level)
        own_coupling = pick_matrix(top_coupling, nodes_now + node)
        coupled.append(jnp.dot(own_coupling, sibling_coef, precision=highest))
        own_up = pick_matrix(top_transfer, nodes_now + node)
        sibling_up = pick_matrix(top_transfer, nodes_now + (node ^ 1))
        current = jnp.dot(own_up.T, current, precision=highest) + jnp.dot(
            sibling_up.T, sibling_coef, precision=highest
        )
    downward = jnp.zeros((rank_size, rhs_count), jnp.float32)
    for level in reversed(range(depth)):
        nodes_now = devices >> level
        node = device >> level
        own_down = pick_matrix(top_transfer, nodes_now + node)
        downward = coupled[level] + jnp.dot(own_down, downward, precision=highest)
    on_cluster = jnp.einsum("ckj,jr->ckr", root_transfer, downward, precision=highest)
    parent_terms = jnp.einsum("lc,cjr->ljr", member, on_cluster, precision=highest)
    on_leaf = jnp.einsum("lkj,ljr->lkr", up_transfer, parent_terms, precision=highest)
    far_rows = far_list - slab_pos * (sector_count * leaf_total)
    slab_coefs = lax.all_gather(
        leaf_coefs.astype(jnp.bfloat16), "sector", axis=0, tiled=True
    ).astype(leaf_coefs.dtype)
    far_sources = slab_coefs[far_rows]
    slot_ids = jnp.arange(far_list.shape[1], dtype=jnp.int32)
    live_slots = (slot_ids[None, :] < far_count[:, None]).astype(jnp.float32)
    weights = far_coupling * live_slots[:, :, None, None]
    slot_terms = jnp.einsum("lfij,lfjr->lfir", weights, far_sources, precision=highest)
    far_field = jnp.sum(slot_terms, axis=1)
    expansion = (on_leaf + far_field).astype(jnp.bfloat16)
    own_block = panels[None, None]
    sector_wide = with_halo(own_block, (("sector", 1),), 1, True)
    neighbourhood = with_halo(sector_wide, (("slab", 0),), 1, False)
    neighbourhood = neighbourhood.reshape(9 * leaf_total, leaf_size, rhs_count)
    owner_device = near_list // leaf_total
    slab_offset = owner_device // sector_count - slab_pos + 1
    sector_offset = (owner_device % sector_count - sector_pos + 1) % sector_count
    position = (slab_offset * 3 + sector_offset) * leaf_total + near_list % leaf_total
    near_field = jnp.zeros((leaf_total, leaf_size, rhs_count), jnp.float32)
    for block_slot in range(near_count):
        picked = neighbourhood[position[:, block_slot]]
        near_field = near_field + jnp.einsum(
            "lij,ljr->lir", near_blocks[:, block_slot], picked, preferred_element_type=jnp.float32
        )
    field = (
        jnp.einsum("lpk,lkr->lpr", bases, expansion, preferred_element_type=jnp.float32)
        + near_field
    )
    return field.astype(jnp.bfloat16).reshape(leaf_total * leaf_size, rhs_count)


def solution(mesh):
    placed = (
        P(("slab", "sector"), None),
        P(("slab", "sector"), None, None),
        P(("slab", "sector")),
        P(("slab", "sector"), None, None),
        P(("slab", "sector"), None, None),
        P(),
        P(),
        P(("slab", "sector"), None),
        P(("slab", "sector"), None, None, None),
        P(("slab", "sector"), None),
        P(("slab", "sector")),
        P(("slab", "sector"), None, None, None),
    )
    return jax.shard_map(
        local, mesh=mesh, in_specs=placed, out_specs=P(("slab", "sector"), None), check_vma=False
    )
```

profile of v0, /device:TPU:1, one launch (start us, length us, event | category | flops | bytes accessed | tf_op | source)
XLA Modules:
  0.0 293.7 jit_solution(9292711996396694747)
XLA Ops:
  8.6 3.8 %collective-permute-start.8 = (bf16[1,1,16,256,128]{4,3,2,1,0:T(8,128)(2,1)}, bf16[1,1,16,256,128]{4,3,2,1,0:T(8,128)(2,1)}, u32[]{:S(2)}, u32[]{:S(2)}) collective-permute-start(bf16[1,1,16,256,128]{4,3,2,1,0:T(8,128)(2,1)} %bitcast.216), channel_id=1, source_target_pairs={{1,0},{2,1},{3,2},{4,3},{5,4},{6,5},{7,6},{8,7},{9,8},{10,9},{11,1... | collective-permute-start | bytes 3145736 | tf_op jit(solution)/shard_map/ppermute | solution.py:23
  18.3 20.1 %constant_dynamic-slice_fusion.1 = (f32[1,64,64]{0,2,1:T(8,128)S(1)}, f32[1,64,64]{0,2,1:T(8,128)}, f32[1,64,64]{0,2,1:T(8,128)}, f32[1,64,64]{0,2,1:T(8,128)}, ...) fusion(f32[256,64,64]{0,2,1:T(8,128)} %param.17, ...), kind=kLoop, calls=%fused_computation.125 | loop fusion | bytes 426036 | tf_op jit(solution)/shard_map/jit(dynamic_index_in_dim)/dynamic_slice | solution.py:31
  45.4 14.8 %constant_dynamic-slice_fusion.19 = (f32[1,64,64]{0,2,1:T(8,128)}, f32[1,64,64]{0,2,1:T(8,128)}, f32[1,64,64]{0,2,1:T(8,128)}, f32[1,64,64]{0,2,1:T(8,128)}, f32...) fusion(f32[256,64,64]{0,2,1:T(8,128)} %param.18, s32[]{:T(128)S(6)} %select_n.111, ...), kind=kLoop, calls=%fused_computation.143 | loop fusion | bytes 229404 | tf_op jit(solution)/shard_map/jit(dynamic_index_in_dim)/dynamic_slice | solution.py:31
  62.8 2.9 %copy.119 = f32[1,64,64]{2,1,0:T(8,128)} copy(f32[1,64,64]{0,2,1:T(8,128)} %get-tuple-element.22) | data formatting | bytes 32768
  73.2 2.9 copy.125
  78.4 2.9 copy.128
  91.3 3.0 %copy.133 = f32[1,64,64]{2,1,0:T(8,128)} copy(f32[1,64,64]{0,2,1:T(8,128)} %get-tuple-element.11) | data formatting | bytes 32768
  98.5 3.0 %copy.124 = f32[1,64,64]{2,1,0:T(8,128)} copy(f32[1,64,64]{0,2,1:T(8,128)} %get-tuple-element.8) | data formatting | bytes 32768
  109.6 3.9 %collective-permute-done.1 = f32[64,128]{1,0:T(8,128)S(1)} collective-permute-done((f32[64,128]{1,0:T(8,128)S(1)}, f32[64,128]{1,0:T(8,128)S(1)}, u32[]{:S(2)}, u32[]{:S(2)}) %collective-permute-start.1) | collective-permute-done | bytes 32800 | tf_op jit(solution)/shard_map/ppermute | solution.py:10
  113.7 12.7 %collective-permute-start.2 = (f32[64,128]{1,0:T(8,128)S(1)}, f32[64,128]{1,0:T(8,128)S(1)}, u32[]{:S(2)}, u32[]{:S(2)}) collective-permute-start(f32[64,128]{1,0:T(8,128)S(1)} %convolution_add_fusion.9), channel_id=1, source_target_pairs={{0,4},{1,5},{2,6},{3,7},{4,0},{5,1},{6,2},{7,3},{8,12},{9,13},{10,... | collective-permute-start | bytes 98312 | tf_op jit(solution)/shard_map/ppermute | solution.py:10
  134.0 4.5 %collective-permute-start.4 = (f32[64,128]{1,0:T(8,128)S(1)}, f32[64,128]{1,0:T(8,128)S(1)}, u32[]{:S(2)}, u32[]{:S(2)}) collective-permute-start(f32[64,128]{1,0:T(8,128)S(1)} %convolution_add_fusion.5), channel_id=1, source_target_pairs={{0,16},{1,17},{2,18},{3,19},{4,20},{5,21},{6,22},{7,23},{8,24},{9,... | collective-permute-start | bytes 98312 | tf_op jit(solution)/shard_map/ppermute | solution.py:10
  143.0 3.4 %collective-permute-start.6 = (f32[64,128]{1,0:T(8,128)S(1)}, f32[64,128]{1,0:T(8,128)S(1)}, u32[]{:S(2)}, u32[]{:S(2)}) collective-permute-start(f32[64,128]{1,0:T(8,128)S(1)} %convolution_add_fusion.1), channel_id=1, source_target_pairs={{0,64},{1,65},{2,66},{3,67},{4,68},{5,69},{6,70},{7,71},{8,72},{9,... | collective-permute-start | bytes 98312 | tf_op jit(solution)/shard_map/ppermute | solution.py:10
  148.3 3.7 %collective-permute-start.10 = (bf16[1,3,16,256,128]{4,3,2,1,0:T(8,128)(2,1)S(1)}, bf16[1,3,16,256,128]{4,3,2,1,0:T(8,128)(2,1)S(1)}, u32[]{:S(2)}, u32[]{:S(2)}) collective-permute-start(bf16[1,3,16,256,128]{4,3,2,1,0:T(8,128)(2,1)S(1)} %pad_maximum_fusion.1), channel_id=1, source_target_pairs={{16,0},{32,16},{48,32},{64,48},{80,64},{96,80},{112,96},{17,1},{33... | collective-permute-start | bytes 9437192 | tf_op jit(solution)/shard_map/ppermute | solution.py:23
  159.2 28.3 %collective-permute-done.10 = bf16[1,3,16,256,128]{4,3,2,1,0:T(8,128)(2,1)S(1)} collective-permute-done((bf16[1,3,16,256,128]{4,3,2,1,0:T(8,128)(2,1)S(1)}, bf16[1,3,16,256,128]{4,3,2,1,0:T(8,128)(2,1)S(1)}, u32[]{:S(2)}, u32[]{:S(2)}) %collective-permute-start.10) | collective-permute-done | bytes 3145760 | tf_op jit(solution)/shard_map/ppermute | solution.py:23
  188.7 5.9 %pad_maximum_fusion = bf16[3,3,16,256,128]{4,3,2,1,0:T(8,128)(2,1)} fusion(bf16[1,3,16,256,128]{4,3,2,1,0:T(8,128)(2,1)S(1)} %collective-permute-done.10, bf16[1,1,16,256,128]{4,3,2,1,0:T(8,128)(2,1)} %collective-permute-done.8, bf16[1,1,16,256,128]{4,3,2,1,0:T(8,128)(2,1)S(1)} %bitcast.219, bf16[1,1,16,256,128]{4,3,2,1,0:T(8,128)(2,1)} %collective-permute-done.7, ...), kind=kLoop, calls=%fused_computation.9 | loop fusion | flops 18874368 | bytes 18874368 | tf_op jit(solution)/shard_map/concatenate | solution.py:19
  194.6 5.5 %gather_fusion.4 = bf16[16,256,128]{2,1,0:T(8,128)(2,1)} fusion(bf16[144,256,128]{2,1,0:T(8,128)(2,1)} %bitcast.206, s32[1024]{0:T(1024)} %get-tuple-element.39), kind=kCustom, calls=%fused_computation.4 | custom fusion | bytes 2097216 | tf_op jit(solution)/shard_map/gather | solution.py:114
  200.1 5.5 %gather_fusion.3 = bf16[16,256,128]{2,1,0:T(8,128)(2,1)} fusion(bf16[144,256,128]{2,1,0:T(8,128)(2,1)} %bitcast.207, s32[1024]{0:T(1024)} %get-tuple-element.40), kind=kCustom, calls=%fused_computation.3 | custom fusion | bytes 2097216 | tf_op jit(solution)/shard_map/gather | solution.py:114
  205.6 5.5 %gather_fusion.2 = bf16[16,256,128]{2,1,0:T(8,128)(2,1)} fusion(bf16[144,256,128]{2,1,0:T(8,128)(2,1)} %bitcast.208, s32[1024]{0:T(1024)} %get-tuple-element.41), kind=kCustom, calls=%fused_computation.2 | custom fusion | bytes 2097216 | tf_op jit(solution)/shard_map/gather | solution.py:114
  211.1 5.5 %gather_fusion.1 = bf16[16,256,128]{2,1,0:T(8,128)(2,1)} fusion(bf16[144,256,128]{2,1,0:T(8,128)(2,1)} %bitcast.209, s32[1024]{0:T(1024)} %get-tuple-element.42), kind=kCustom, calls=%fused_computation.1 | custom fusion | bytes 2097216 | tf_op jit(solution)/shard_map/gather | solution.py:114
  216.5 5.5 %gather_fusion.7 = bf16[16,256,128]{2,1,0:T(8,128)(2,1)} fusion(bf16[144,256,128]{2,1,0:T(8,128)(2,1)} %bitcast.210, s32[1024]{0:T(1024)} %get-tuple-element.36), kind=kCustom, calls=%fused_computation.7 | custom fusion | bytes 2097216 | tf_op jit(solution)/shard_map/gather | solution.py:114
  222.0 5.5 %gather_fusion.6 = bf16[16,256,128]{2,1,0:T(8,128)(2,1)} fusion(bf16[144,256,128]{2,1,0:T(8,128)(2,1)} %bitcast.211, s32[1024]{0:T(1024)} %get-tuple-element.37), kind=kCustom, calls=%fused_computation.6 | custom fusion | bytes 2097216 | tf_op jit(solution)/shard_map/gather | solution.py:114
  227.5 5.5 %gather_fusion.5 = bf16[16,256,128]{2,1,0:T(8,128)(2,1)} fusion(bf16[144,256,128]{2,1,0:T(8,128)(2,1)} %bitcast.212, s32[1024]{0:T(1024)} %get-tuple-element.38), kind=kCustom, calls=%fused_computation.5 | custom fusion | bytes 2097216 | tf_op jit(solution)/shard_map/gather | solution.py:114
  233.0 5.3 %gather_fusion.8 = bf16[16,256,128]{2,1,0:T(8,128)(2,1)} fusion(bf16[144,256,128]{2,1,0:T(8,128)(2,1)} %bitcast.213, s32[1024]{0:T(1024)S(1)} %get-tuple-element.35), kind=kCustom, calls=%fused_computation.8 | custom fusion | bytes 2097216 | tf_op jit(solution)/shard_map/gather | solution.py:114
  241.1 3.9 %fusion.13 = f32[16,128,256]{2,1,0:T(8,128)} fusion(bf16[16,256,128]{2,1,0:T(8,128)(2,1)S(1)} %copy-done.11, bf16[16,8,256,256]{3,2,1,0:T(8,128)(2,1)} %param.20), kind=kOutput, calls=%fused_computation.24 | convolution fusion | flops 268435456 | bytes 5242880 | tf_op jit(solution)/shard_map/lij,ljr->lir/dot_general | solution.py:115
  245.1 3.9 %fusion.15 = f32[16,128,256]{2,1,0:T(8,128)} fusion(bf16[16,256,128]{2,1,0:T(8,128)(2,1)S(1)} %copy-done.12, bf16[16,8,256,256]{3,2,1,0:T(8,128)(2,1)} %param.20), kind=kOutput, calls=%fused_computation.26 | convolution fusion | flops 268435456 | bytes 5242880 | tf_op jit(solution)/shard_map/lij,ljr->lir/dot_general | solution.py:115
  249.0 3.8 %fusion.17 = f32[16,128,256]{2,1,0:T(8,128)} fusion(bf16[16,256,128]{2,1,0:T(8,128)(2,1)S(1)} %copy-done.13, bf16[16,8,256,256]{3,2,1,0:T(8,128)(2,1)} %param.20), kind=kOutput, calls=%fused_computation.28 | convolution fusion | flops 268435456 | bytes 5242880 | tf_op jit(solution)/shard_map/lij,ljr->lir/dot_general | solution.py:115
  252.8 3.9 %fusion.5 = f32[16,128,256]{2,1,0:T(8,128)} fusion(bf16[16,256,128]{2,1,0:T(8,128)(2,1)S(1)} %copy-done.14, bf16[16,8,256,256]{3,2,1,0:T(8,128)(2,1)} %param.20), kind=kOutput, calls=%fused_computation.16 | convolution fusion | flops 268435456 | bytes 5242880 | tf_op jit(solution)/shard_map/lij,ljr->lir/dot_general | solution.py:115
  256.7 3.9 %fusion.7 = f32[16,128,256]{2,1,0:T(8,128)} fusion(bf16[16,256,128]{2,1,0:T(8,128)(2,1)S(1)} %copy-done.15, bf16[16,8,256,256]{3,2,1,0:T(8,128)(2,1)} %param.20), kind=kOutput, calls=%fused_computation.18 | convolution fusion | flops 268435456 | bytes 5242880 | tf_op jit(solution)/shard_map/lij,ljr->lir/dot_general | solution.py:115
  260.6 3.8 %fusion.9 = f32[16,128,256]{2,1,0:T(8,128)} fusion(bf16[16,256,128]{2,1,0:T(8,128)(2,1)S(1)} %copy-done.16, bf16[16,8,256,256]{3,2,1,0:T(8,128)(2,1)} %param.20), kind=kOutput, calls=%fused_computation.20 | convolution fusion | flops 268435456 | bytes 5242880 | tf_op jit(solution)/shard_map/lij,ljr->lir/dot_general | solution.py:115
  264.4 5.3 %gather_fusion = bf16[256,64,128]{2,1,0:T(8,128)(2,1)} fusion(bf16[256,64,128]{2,1,0:T(8,128)(2,1)} %all-gather.2.cloned.1.call-done, s32[1024]{0:T(1024)S(1)} %pad_clamp_fusion.8), kind=kCustom, calls=%fused_computation | custom fusion | bytes 8389632 | tf_op jit(solution)/shard_map/gather | solution.py:97
  269.7 8.6 %fusion.32 = f32[16,64,128]{2,1,0:T(8,128)S(1)} fusion(bf16[16,16,64,128]{3,2,1,0:T(8,128)(2,1)} %bitcast.214, f32[16,16,64,64]{3,2,1,0:T(8,128)} %param.23, f32[16,16]{1,0:T(8,128)S(1)} %fusion.86), kind=kOutput, calls=%fused_computation.40 | convolution fusion | flops 1611661312 | bytes 8913920 | tf_op jit(solution)/shard_map/lfij,lfjr->lfir/dot_general | solution.py:101
  280.6 3.8 %fusion.29 = bf16[16,256,128]{1,2,0:T(8,128)(2,1)} fusion(f32[16,128,256]{2,1,0:T(8,128)S(1)} %fusion.114, bf16[16,256,128]{2,1,0:T(8,128)(2,1)S(1)} %copy-done.10, bf16[16,8,256,256]{3,2,1,0:T(8,128)(2,1)} %param.20, f32[16,128,256]{2,1,0:T(8,128)S(1)} %copy-done.7, f32[16,128,256]{2,1,0:T(8,128)S(1)} %copy-done.8, f32[16,128,256]{2,1,0:T(8,128)S(1)} %copy-done.9, ...), kind=kOutput, calls=%fused_computation.39 | convolution fusion | flops 273154048 | bytes 20971520 | tf_op jit(solution)/shard_map/lij,ljr->lir/dot_general | solution.py:115
  (163 shorter events, 79.0 us)
Async XLA Ops:
  6.5 257.9 %all-gather.2.cloned.1.call-start = ((), (), s32[]{:S(2)}) async-start(), calls=%async_computation | async-start | bytes 4456448 | tf_op jit(solution)/shard_map/all_gather | solution.py:94
  6.5 139.9 %collective-permute-start.7 = (bf16[1,1,16,256,128]{4,3,2,1,0:T(8,128)(2,1)}, bf16[1,1,16,256,128]{4,3,2,1,0:T(8,128)(2,1)}, u32[]{:S(2)}, u32[]{:S(2)}) collective-permute-start(bf16[1,1,16,256,128]{4,3,2,1,0:T(8,128)(2,1)} %bitcast.215), channel_id=1, source_target_pairs={{0,1},{1,2},{2,3},{3,4},{4,5},{5,6},{6,7},{7,8},{8,9},{9,10},{10,1... | collective-permute-start | bytes 3145736 | tf_op jit(solution)/shard_map/ppermute | solution.py:21
  8.6 137.8 %collective-permute-start.8 = (bf16[1,1,16,256,128]{4,3,2,1,0:T(8,128)(2,1)}, bf16[1,1,16,256,128]{4,3,2,1,0:T(8,128)(2,1)}, u32[]{:S(2)}, u32[]{:S(2)}) collective-permute-start(bf16[1,1,16,256,128]{4,3,2,1,0:T(8,128)(2,1)} %bitcast.216), channel_id=1, source_target_pairs={{1,0},{2,1},{3,2},{4,3},{5,4},{6,5},{7,6},{8,7},{9,8},{10,9},{11,1... | collective-permute-start | bytes 3145736 | tf_op jit(solution)/shard_map/ppermute | solution.py:23
  18.3 89.8 %collective-permute-start = (f32[64,128]{1,0:T(8,128)}, f32[64,128]{1,0:T(8,128)}, u32[]{:S(2)}, u32[]{:S(2)}) collective-permute-start(f32[64,128]{1,0:T(8,128)} %bitcast.5), channel_id=1, source_target_pairs={{0,1},{1,0},{2,3},{3,2},{4,5},{5,4},{6,7},{7,6},{8,9},{9,8},{10,11... | collective-permute-start | bytes 98312 | tf_op jit(solution)/shard_map/ppermute | solution.py:10
  45.4 14.8 %copy-start.36 = (s32[16,16]{1,0:T(8,128)S(1)}, s32[16,16]{1,0:T(8,128)}, u32[]{:S(2)}) copy-start(s32[16,16]{1,0:T(8,128)} %param.21) | copy-start | bytes 3076
  45.4 14.9 %copy-start.40 = (s32[16]{0:T(128)S(1)}, s32[16]{0:T(128)}, u32[]{:S(2)}) copy-start(s32[16]{0:T(128)} %param.22) | copy-start | bytes 196
  45.4 14.9 %copy-start.37 = (s32[16,8]{0,1:T(8,128)S(1)}, s32[16,8]{0,1:T(8,128)}, u32[]{:S(2)}) copy-start(s32[16,8]{0,1:T(8,128)} %param.19) | copy-start | bytes 1540
  105.7 23.5 %copy-start.31 = (f32[1,64,64]{2,1,0:T(8,128)S(1)}, f32[1,64,64]{2,1,0:T(8,128)}, u32[]{:S(2)}) copy-start(f32[1,64,64]{2,1,0:T(8,128)} %copy.125) | copy-start | bytes 49156
  105.7 28.1 %copy-start.30 = (f32[1,64,64]{2,1,0:T(8,128)S(1)}, f32[1,64,64]{2,1,0:T(8,128)}, u32[]{:S(2)}) copy-start(f32[1,64,64]{2,1,0:T(8,128)} %copy.128) | copy-start | bytes 49156
  105.7 32.8 %copy-start.20 = (f32[1,64,64]{2,1,0:T(8,128)S(1)}, f32[1,64,64]{2,1,0:T(8,128)}, u32[]{:S(2)}) copy-start(f32[1,64,64]{2,1,0:T(8,128)} %copy.129) | copy-start | bytes 49156
  105.7 33.6 %copy-start.29 = (f32[1,64,64]{2,1,0:T(8,128)S(1)}, f32[1,64,64]{2,1,0:T(8,128)}, u32[]{:S(2)}) copy-start(f32[1,64,64]{2,1,0:T(8,128)} %copy.131) | copy-start | bytes 49156
  105.7 35.6 %copy-start.21 = (f32[1,64,64]{2,1,0:T(8,128)S(1)}, f32[1,64,64]{2,1,0:T(8,128)}, u32[]{:S(2)}) copy-start(f32[1,64,64]{2,1,0:T(8,128)} %copy.132) | copy-start | bytes 49156
  105.7 36.9 %copy-start.28 = (f32[1,64,64]{2,1,0:T(8,128)S(1)}, f32[1,64,64]{2,1,0:T(8,128)}, u32[]{:S(2)}) copy-start(f32[1,64,64]{2,1,0:T(8,128)} %copy.134) | copy-start | bytes 49156
  105.7 40.7 %copy-start.1 = (bf16[4096,128]{1,0:T(8,128)(2,1)S(1)}, bf16[4096,128]{1,0:T(8,128)(2,1)}, u32[]{:S(2)}) copy-start(bf16[4096,128]{1,0:T(8,128)(2,1)} %param.12) | copy-start | bytes 3145732
  109.1 4.3 %collective-permute-start.1 = (f32[64,128]{1,0:T(8,128)S(1)}, f32[64,128]{1,0:T(8,128)S(1)}, u32[]{:S(2)}, u32[]{:S(2)}) collective-permute-start(f32[64,128]{1,0:T(8,128)S(1)} %convolution_add_fusion.11), channel_id=1, source_target_pairs={{0,2},{1,3},{2,0},{3,1},{4,6},{5,7},{6,4},{7,5},{8,10},{9,11},{10,... | collective-permute-start | bytes 98312 | tf_op jit(solution)/shard_map/ppermute | solution.py:10
  113.7 15.4 %collective-permute-start.2 = (f32[64,128]{1,0:T(8,128)S(1)}, f32[64,128]{1,0:T(8,128)S(1)}, u32[]{:S(2)}, u32[]{:S(2)}) collective-permute-start(f32[64,128]{1,0:T(8,128)S(1)} %convolution_add_fusion.9), channel_id=1, source_target_pairs={{0,4},{1,5},{2,6},{3,7},{4,0},{5,1},{6,2},{7,3},{8,12},{9,13},{10,... | collective-permute-start | bytes 98312 | tf_op jit(solution)/shard_map/ppermute | solution.py:10
  129.4 4.3 %collective-permute-start.3 = (f32[64,128]{1,0:T(8,128)S(1)}, f32[64,128]{1,0:T(8,128)S(1)}, u32[]{:S(2)}, u32[]{:S(2)}) collective-permute-start(f32[64,128]{1,0:T(8,128)S(1)} %convolution_add_fusion.7), channel_id=1, source_target_pairs={{0,8},{1,9},{2,10},{3,11},{4,12},{5,13},{6,14},{7,15},{8,0},{9,1},... | collective-permute-start | bytes 98312 | tf_op jit(solution)/shard_map/ppermute | solution.py:10
  134.0 5.3 %collective-permute-start.4 = (f32[64,128]{1,0:T(8,128)S(1)}, f32[64,128]{1,0:T(8,128)S(1)}, u32[]{:S(2)}, u32[]{:S(2)}) collective-permute-start(f32[64,128]{1,0:T(8,128)S(1)} %convolution_add_fusion.5), channel_id=1, source_target_pairs={{0,16},{1,17},{2,18},{3,19},{4,20},{5,21},{6,22},{7,23},{8,24},{9,... | collective-permute-start | bytes 98312 | tf_op jit(solution)/shard_map/ppermute | solution.py:10
  139.6 3.1 %collective-permute-start.5 = (f32[64,128]{1,0:T(8,128)S(1)}, f32[64,128]{1,0:T(8,128)S(1)}, u32[]{:S(2)}, u32[]{:S(2)}) collective-permute-start(f32[64,128]{1,0:T(8,128)S(1)} %convolution_add_fusion.3), channel_id=1, source_target_pairs={{0,32},{1,33},{2,34},{3,35},{4,36},{5,37},{6,38},{7,39},{8,40},{9,... | collective-permute-start | bytes 98312 | tf_op jit(solution)/shard_map/ppermute | solution.py:10
  142.9 11.6 %copy-start.27 = (f32[1,64,64]{2,1,0:T(8,128)S(1)}, f32[1,64,64]{2,1,0:T(8,128)}, u32[]{:S(2)}) copy-start(f32[1,64,64]{2,1,0:T(8,128)} %copy.133) | copy-start | bytes 49156
  142.9 11.6 %copy-start.35 = (f32[64,128]{1,0:T(8,128)S(1)}, f32[64,128]{1,0:T(8,128)}, u32[]{:S(2)}) copy-start(f32[64,128]{1,0:T(8,128)} %fusion.45) | copy-start | bytes 98308
  142.9 12.0 %copy-start.26 = (f32[1,64,64]{2,1,0:T(8,128)S(1)}, f32[1,64,64]{2,1,0:T(8,128)}, u32[]{:S(2)}) copy-start(f32[1,64,64]{2,1,0:T(8,128)} %copy.130) | copy-start | bytes 49156
  142.9 12.3 %copy-start.25 = (f32[1,64,64]{2,1,0:T(8,128)S(1)}, f32[1,64,64]{2,1,0:T(8,128)}, u32[]{:S(2)}) copy-start(f32[1,64,64]{2,1,0:T(8,128)} %copy.127) | copy-start | bytes 49156
  143.0 12.7 %copy-start.24 = (f32[1,64,64]{2,1,0:T(8,128)S(1)}, f32[1,64,64]{2,1,0:T(8,128)}, u32[]{:S(2)}) copy-start(f32[1,64,64]{2,1,0:T(8,128)} %copy.124) | copy-start | bytes 49156
  143.0 13.0 %copy-start.23 = (f32[1,64,64]{2,1,0:T(8,128)S(1)}, f32[1,64,64]{2,1,0:T(8,128)}, u32[]{:S(2)}) copy-start(f32[1,64,64]{2,1,0:T(8,128)} %copy.121) | copy-start | bytes 49156
  143.0 13.3 %copy-start.22 = (f32[1,64,64]{2,1,0:T(8,128)S(1)}, f32[1,64,64]{2,1,0:T(8,128)}, u32[]{:S(2)}) copy-start(f32[1,64,64]{2,1,0:T(8,128)} %copy.118) | copy-start | bytes 49156
  143.0 15.0 %copy-start.39 = (s32[16]{0:T(128)S(1)}, s32[16]{0:T(128)}, u32[]{:S(2)}) copy-start(s32[16]{0:T(128)} %copy-done.38) | copy-start | bytes 196
  143.0 11.6 %collective-permute-start.6 = (f32[64,128]{1,0:T(8,128)S(1)}, f32[64,128]{1,0:T(8,128)S(1)}, u32[]{:S(2)}, u32[]{:S(2)}) collective-permute-start(f32[64,128]{1,0:T(8,128)S(1)} %convolution_add_fusion.1), channel_id=1, source_target_pairs={{0,64},{1,65},{2,66},{3,67},{4,68},{5,69},{6,70},{7,71},{8,72},{9,... | collective-permute-start | bytes 98312 | tf_op jit(solution)/shard_map/ppermute | solution.py:10
  148.3 39.3 %collective-permute-start.10 = (bf16[1,3,16,256,128]{4,3,2,1,0:T(8,128)(2,1)S(1)}, bf16[1,3,16,256,128]{4,3,2,1,0:T(8,128)(2,1)S(1)}, u32[]{:S(2)}, u32[]{:S(2)}) collective-permute-start(bf16[1,3,16,256,128]{4,3,2,1,0:T(8,128)(2,1)S(1)} %pad_maximum_fusion.1), channel_id=1, source_target_pairs={{16,0},{32,16},{48,32},{64,48},{80,64},{96,80},{112,96},{17,1},{33... | collective-permute-start | bytes 9437192 | tf_op jit(solution)/shard_map/ppermute | solution.py:23
  152.0 36.7 %collective-permute-start.9 = (bf16[1,3,16,256,128]{4,3,2,1,0:T(8,128)(2,1)S(1)}, bf16[1,3,16,256,128]{4,3,2,1,0:T(8,128)(2,1)S(1)}, u32[]{:S(2)}, u32[]{:S(2)}) collective-permute-start(bf16[1,3,16,256,128]{4,3,2,1,0:T(8,128)(2,1)S(1)} %pad_maximum_fusion.1), channel_id=1, source_target_pairs={{0,16},{16,32},{32,48},{48,64},{64,80},{80,96},{96,112},{1,17},{17... | collective-permute-start | bytes 9437192 | tf_op jit(solution)/shard_map/ppermute | solution.py:21
  269.7 10.0 %copy-start.9 = (f32[16,128,256]{2,1,0:T(8,128)S(1)}, f32[16,128,256]{2,1,0:T(8,128)}, u32[]{:S(2)}) copy-start(f32[16,128,256]{2,1,0:T(8,128)} %fusion.9) | copy-start | bytes 6291460
  269.7 10.0 %copy-start.10 = (bf16[16,256,128]{2,1,0:T(8,128)(2,1)S(1)}, bf16[16,256,128]{2,1,0:T(8,128)(2,1)}, u32[]{:S(2)}) copy-start(bf16[16,256,128]{2,1,0:T(8,128)(2,1)} %gather_fusion.8) | copy-start | bytes 3145732
  (21 other events, 112.6 us)
Sparse Core Ops, SparseCore 0:
  18.4 54.4 all-gather.1
where the time goes:
time: 294 us
  local copies, waits for them, and re-layouts  137 us (47%)
  matrix products  55.2 us (19%)
  waiting for transfers between devices  40.1 us (14%)
  starting transfers between devices  36.3 us (12%)
  between operations  14.3 us (5%)
  other arithmetic  10.9 us (4%)
    unnamed x102, local copies, waits for them, and re-layouts  50.8 us
    gather x8, local copies, waits for them, and re-layouts, local(): picked = neighbourhood[position[:, block_slot]]  43.7 us
    dynamic_slice x2, local copies, waits for them, and re-layouts, pick_matrix(): return lax.dynamic_index_in_dim(table, position, axis=0, keepdims=False)  34.9 us
    dot_general x8, matrix products, local(): jnp.einsum('lij,ljr->lir', near_blocks[:, block_slot], picked, preferred_...  29.8 us
    ppermute x2, waiting for transfers between devices, with_halo(): lax.ppermute(head, axis, [((i + 1) % count, i) for i in range(ends)])  28.3 us
    ppermute x7, starting transfers between devices, partner(): lax.ppermute(array, axis, [(i, i ^ 1 << stride) for i in range(lax.axis_s...  24.2 us
    ppermute x7, waiting for transfers between devices, partner(): lax.ppermute(array, axis, [(i, i ^ 1 << stride) for i in range(lax.axis_s...  10.6 us
    dot_general x1, matrix products, local(): jnp.einsum('lfij,lfjr->lfir', weights, far_sources, precision=highest)  8.64 us
  transfers between devices with their start and end apart: 12, of which 7 were waited for; matrix products, arithmetic and copies ran while one was open for 62% of the time, Pallas kernels for 0%

commit v1 on v0

v1 whole, which is shorter than its diff:
```python
import jax
import jax.numpy as jnp
from jax import lax
from jax.experimental import pallas as pl
from jax.experimental.pallas import tpu as pltpu
from jax.sharding import PartitionSpec as P

highest = lax.Precision.HIGHEST
f32 = jnp.float32
bf16 = jnp.bfloat16


def dot_t(a, b, precision=None):
    return lax.dot_general(a, b, (((0,), (0,)), ((), ())), precision=precision, preferred_element_type=f32)


def dot(a, b, precision=None):
    return lax.dot_general(a, b, (((1,), (0,)), ((), ())), precision=precision, preferred_element_type=f32)


def whole():
    return pl.BlockSpec(memory_space=pltpu.VMEM)


def scalars():
    return pl.BlockSpec(memory_space=pltpu.SMEM)


def params(mib, semantics=None):
    return pltpu.CompilerParams(vmem_limit_bytes=mib << 20, dimension_semantics=semantics)


def cost(flops, nbytes):
    return pl.CostEstimate(flops=flops, bytes_accessed=nbytes, transcendentals=0)


def upward_kernel(parent, sources, bases, up, root, leaf_out, root_out, clusters):
    clusters[...] = jnp.zeros_like(clusters)
    for leaf in range(bases.shape[0]):
        coefs = dot_t(bases[leaf], sources[leaf])
        leaf_out[leaf] = coefs.astype(bf16)
        clusters[parent[leaf]] += dot_t(up[leaf], coefs, highest)
    total = dot_t(root[0], clusters[0], highest)
    for cluster in range(1, root.shape[0]):
        total = total + dot_t(root[cluster], clusters[cluster], highest)
    root_out[...] = total


def upward(local_parent, panels, bases, up_transfer, root_transfer):
    leaves, _, rhs = panels.shape
    rank = bases.shape[2]
    return pl.pallas_call(
        upward_kernel,
        out_shape=(
            jax.ShapeDtypeStruct((leaves, rank, rhs), bf16),
            jax.ShapeDtypeStruct((rank, rhs), f32),
        ),
        in_specs=[scalars(), whole(), whole(), whole(), whole()],
        out_specs=(whole(), whole()),
        scratch_shapes=[pltpu.VMEM((root_transfer.shape[0], rank, rhs), f32)],
        compiler_params=params(16),
        cost_estimate=cost(200_000_000, 4_000_000),
        name="upward",
    )(local_parent, panels, bases, up_transfer, root_transfer)


def tables_kernel(nodes, transfer, coupling, out, sems):
    depth = out.shape[0] // 3
    copies = []
    for level in range(depth):
        for kind in range(3):
            slot = 3 * level + kind
            table = coupling if kind == 2 else transfer
            node = nodes[level] ^ 1 if kind == 1 else nodes[level]
            copies.append(pltpu.make_async_copy(table.at[node], out.at[slot], sems.at[slot]))
    for copy in copies:
        copy.start()
    for copy in copies:
        copy.wait()


def tables(nodes, transfer, coupling):
    count = 3 * nodes.shape[0]
    return pl.pallas_call(
        tables_kernel,
        out_shape=jax.ShapeDtypeStruct((count,) + transfer.shape[1:], f32),
        in_specs=[scalars(), pl.BlockSpec(memory_space=pl.ANY), pl.BlockSpec(memory_space=pl.ANY)],
        out_specs=whole(),
        scratch_shapes=[pltpu.SemaphoreType.DMA((count,))],
        compiler_params=params(4),
        cost_estimate=cost(0, 700_000),
        name="tables",
    )(nodes, transfer, coupling)


def combine_kernel(level, current, sibling, mats, out):
    own = dot_t(mats[3 * level], current[...], highest)
    out[...] = own + dot_t(mats[3 * level + 1], sibling[...], highest)


def combine(level, current, sibling, mats):
    return pl.pallas_call(
        lambda *refs: combine_kernel(level, *refs),
        out_shape=jax.ShapeDtypeStruct(current.shape, f32),
        in_specs=[whole(), whole(), whole()],
        out_specs=whole(),
        compiler_params=params(4),
        cost_estimate=cost(12_000_000, 100_000),
        name="combine",
    )(current, sibling, mats)


def downward_kernel(depth, parent, *refs):
    siblings = refs[:depth]
    mats, root, up, out, clusters = refs[depth:]
    down = dot(mats[3 * depth - 1], siblings[depth - 1][...], highest)
    for level in reversed(range(depth - 1)):
        across = dot(mats[3 * level + 2], siblings[level][...], highest)
        down = across + dot(mats[3 * level], down, highest)
    for cluster in range(root.shape[0]):
        clusters[cluster] = dot(root[cluster], down, highest)
    for leaf in range(up.shape[0]):
        out[leaf] = dot(up[leaf], clusters[parent[leaf]], highest)


def downward(local_parent, siblings, mats, root_transfer, up_transfer):
    depth = len(siblings)
    rank, rhs = siblings[0].shape
    return pl.pallas_call(
        lambda *refs: downward_kernel(depth, *refs),
        out_shape=jax.ShapeDtypeStruct((up_transfer.shape[0], rank, rhs), f32),
        in_specs=[scalars()] + [whole()] * (depth + 3),
        out_specs=whole(),
        scratch_shapes=[pltpu.VMEM((root_transfer.shape[0], rank, rhs), f32)],
        compiler_params=params(16),
        cost_estimate=cost(200_000_000, 2_000_000),
        name="downward",
    )(local_parent, *siblings, mats, root_transfer, up_transfer)


def weights_kernel(count, coupling, out):
    leaf = pl.program_id(0)
    used = count[leaf]
    for pair in range(coupling.shape[1] // 2):
        left = jnp.where(2 * pair < used, coupling[0, 2 * pair], 0.0)
        right = jnp.where(2 * pair + 1 < used, coupling[0, 2 * pair + 1], 0.0)
        width = 2 * coupling.shape[3]
        out[0, :, pair * width : (pair + 1) * width] = jnp.concatenate([left, right], axis=1).astype(bf16)


def weights(far_count, far_coupling):
    leaves, slots, rank, _ = far_coupling.shape
    return pl.pallas_call(
        weights_kernel,
        out_shape=jax.ShapeDtypeStruct((leaves, rank, slots * rank), bf16),
        grid_spec=pltpu.PrefetchScalarGridSpec(
            num_scalar_prefetch=1,
            grid=(leaves,),
            in_specs=[pl.BlockSpec((1, slots, rank, rank), lambda i, n: (i, 0, 0, 0))],
            out_specs=pl.BlockSpec((1, rank, slots * rank), lambda i, n: (i, 0, 0)),
        ),
        compiler_params=params(8, ("arbitrary",)),
        cost_estimate=cost(0, 11_000_000),
        name="weights",
    )(far_count, far_coupling)


def near_kernel(position, blocks, *refs):
    regions = refs[:9]
    out, held, sems = refs[9:]
    leaves = regions[0].shape[0]
    leaf = pl.program_id(0)

    @pl.when(leaf == 0)
    def _():
        copies = [
            pltpu.make_async_copy(region, held.at[pl.ds(place * leaves, leaves)], sems.at[place])
            for place, region in enumerate(regions)
        ]
        for copy in copies:
            copy.start()
        for copy in copies:
            copy.wait()

    slots = blocks.shape[1]
    total = dot(blocks[0, 0], held[position[leaf * slots]])
    for slot in range(1, slots):
        total = total + dot(blocks[0, slot], held[position[leaf * slots + slot]])
    out[0] = total


def near(position, near_blocks, regions):
    leaves, slots, size, _ = near_blocks.shape
    rhs = regions[0].shape[2]
    return pl.pallas_call(
        near_kernel,
        out_shape=jax.ShapeDtypeStruct((leaves, size, rhs), f32),
        grid_spec=pltpu.PrefetchScalarGridSpec(
            num_scalar_prefetch=1,
            grid=(leaves,),
            in_specs=[pl.BlockSpec((1, slots, size, size), lambda i, p: (i, 0, 0, 0))]
            + [pl.BlockSpec(memory_space=pl.ANY)] * 9,
            out_specs=pl.BlockSpec((1, size, rhs), lambda i, p: (i, 0, 0)),
            scratch_shapes=[pltpu.VMEM((9 * leaves, size, rhs), bf16), pltpu.SemaphoreType.DMA((9,))],
        ),
        compiler_params=params(24, ("arbitrary",)),
        cost_estimate=cost(2_200_000_000, 28_000_000),
        name="near",
    )(position, near_blocks, *regions)


def final_kernel(rows, packed, coefs, on_leaf, bases, near_part, out, picked):
    leaf = pl.program_id(0)
    rank = coefs.shape[1]
    slots = packed.shape[2] // rank
    for slot in range(slots):
        picked[slot * rank : (slot + 1) * rank] = coefs[rows[leaf * slots + slot]]
    expansion = (on_leaf[0] + dot(packed[0], picked[...])).astype(bf16)
    out[0] = (dot(bases[0], expansion) + near_part[0]).astype(bf16)


def final(far_rows, packed, slab_coefs, on_leaf, bases, near_part):
    leaves, size, rank = bases.shape
    rhs = near_part.shape[2]
    wide = packed.shape[2]
    return pl.pallas_call(
        final_kernel,
        out_shape=jax.ShapeDtypeStruct((leaves, size, rhs), bf16),
        grid_spec=pltpu.PrefetchScalarGridSpec(
            num_scalar_prefetch=1,
            grid=(leaves,),
            in_specs=[
                pl.BlockSpec((1, rank, wide), lambda i, r: (i, 0, 0)),
                pl.BlockSpec(slab_coefs.shape, lambda i, r: (0, 0, 0), pipeline_mode=pl.Buffered(1)),
                pl.BlockSpec((1, rank, rhs), lambda i, r: (i, 0, 0)),
                pl.BlockSpec((1, size, rank), lambda i, r: (i, 0, 0)),
                pl.BlockSpec((1, size, rhs), lambda i, r: (i, 0, 0)),
            ],
            out_specs=pl.BlockSpec((1, size, rhs), lambda i, r: (i, 0, 0)),
            scratch_shapes=[pltpu.VMEM((wide, rhs), bf16)],
        ),
        compiler_params=params(16, ("arbitrary",)),
        cost_estimate=cost(350_000_000, 12_000_000),
        name="final",
    )(far_rows, packed, slab_coefs, on_leaf, bases, near_part)


def shifted(array, axis, step, closed):
    count = lax.axis_size(axis)
    pairs = [(i, (i + step) % count) for i in range(count) if closed or 0 <= i + step < count]
    return lax.ppermute(array, axis, pairs)


def partner(array, axis, stride):
    return lax.ppermute(array, axis, [(i, i ^ 1 << stride) for i in range(lax.axis_size(axis))])


def local(
    sources,
    bases,
    leaf_parent,
    up_transfer,
    root_transfer,
    top_transfer,
    top_coupling,
    near_list,
    near_blocks,
    far_list,
    far_count,
    far_coupling,
):
    leaf_total, leaf_size, _ = bases.shape
    rhs_count = sources.shape[1]
    cluster_total = leaf_total // 2
    slab_count = lax.axis_size("slab")
    sector_count = lax.axis_size("sector")
    devices = slab_count * sector_count
    depth = devices.bit_length() - 1
    slab_pos = lax.axis_index("slab")
    sector_pos = lax.axis_index("sector")
    device = slab_pos * sector_count + sector_pos
    panels = sources.reshape(leaf_total, leaf_size, rhs_count)

    before, after = shifted(panels, "sector", 1, True), shifted(panels, "sector", -1, True)
    regions = [before, panels, after]
    below = [shifted(region, "slab", 1, False) for region in regions]
    above = [shifted(region, "slab", -1, False) for region in regions]
    regions = below + regions + above

    local_parent = leaf_parent - device * cluster_total
    leaf_coefs, current = upward(local_parent, panels, bases, up_transfer, root_transfer)
    slab_coefs = lax.all_gather(leaf_coefs, "sector", axis=0, tiled=True)
    levels = jnp.arange(depth, dtype=jnp.int32)
    mats = tables((devices + device) >> levels, top_transfer, top_coupling)
    siblings = []
    for level in range(depth):
        siblings.append(partner(current, ("slab", "sector"), level))
        if level < depth - 1:
            current = combine(level, current, siblings[-1], mats)
    on_leaf = downward(local_parent, siblings, mats, root_transfer, up_transfer)

    packed = weights(far_count, far_coupling)

    owner_device = near_list // leaf_total
    slab_offset = owner_device // sector_count - slab_pos + 1
    sector_offset = (owner_device % sector_count - sector_pos + 1) % sector_count
    position = (slab_offset * 3 + sector_offset) * leaf_total + near_list % leaf_total
    near_part = near(position.reshape(-1), near_blocks, regions)

    far_rows = (far_list - slab_pos * (sector_count * leaf_total)).reshape(-1)
    field = final(far_rows, packed, slab_coefs, on_leaf, bases, near_part)
    return field.reshape(leaf_total * leaf_size, rhs_count)


def solution(mesh):
    placed = (
        P(("slab", "sector"), None),
        P(("slab", "sector"), None, None),
        P(("slab", "sector")),
        P(("slab", "sector"), None, None),
        P(("slab", "sector"), None, None),
        P(),
        P(),
        P(("slab", "sector"), None),
        P(("slab", "sector"), None, None, None),
        P(("slab", "sector"), None),
        P(("slab", "sector")),
        P(("slab", "sector"), None, None, None),
    )
    return jax.shard_map(
        local, mesh=mesh, in_specs=placed, out_specs=P(("slab", "sector"), None), check_vma=False
    )
```

time: 294 us -> 156 us (0.53)
  local copies, waits for them, and re-layouts: 137 us -> 47.4 us
  matrix products: 55.2 us -> 0 us
  Pallas kernels: 0 us -> 31.9 us
  waiting for transfers between devices: 40.1 us -> 21.4 us
  other arithmetic: 10.9 us -> 0.7 us
    dot_general x43 -> x0, matrix products: 55.2 us -> none  [the longest x8 29.8 us: local(): jnp.einsum('lij,ljr->lir', near_blocks[:, block_slot], picked, preferred_...]
    gather x9 -> x0, local copies, waits for them, and re-layouts: 49 us -> none  [the longest x8 43.7 us: local(): picked = neighbourhood[position[:, block_slot]]]
    dynamic_slice x2 -> x0, local copies, waits for them, and re-layouts: 34.9 us -> none  [pick_matrix(): return lax.dynamic_index_in_dim(table, position, axis=0, keepdims=False)]
    pallas_call x0 -> x12, Pallas kernels: none -> 31.9 us  [the longest x1 11 us: near(): pl.pallas_call(near_kernel, out_shape=jax.ShapeDtypeStruct((leaves, size,...]
    ppermute x4 -> x8, waiting for transfers between devices: 29.5 us -> 13 us  [shifted(): return lax.ppermute(array, axis, pairs)]
    ppermute x4 -> x8, starting transfers between devices: 12.1 us -> 23.3 us  [shifted(): return lax.ppermute(array, axis, pairs)]
    ppermute x7, starting transfers between devices: 24.2 us -> 15.7 us  [partner(): lax.ppermute(array, axis, [(i, i ^ 1 << stride) for i in range(lax.axis_s...]
    concatenate x2 -> x0, other arithmetic: 7.76 us -> none  [with_halo(): jnp.concatenate([lax.ppermute(tail, axis, [(i, (i + 1) % count) for i in...]
  transfers between devices with their start and end apart: 12 -> 16, of which waited for: 7 -> 8; matrix products, arithmetic and copies ran while one was open for 62% -> 12% of each run, Pallas kernels for 0% -> 13%
where the time goes in v1:
time: 156 us; the launch traced here: 154 us
  local copies, waits for them, and re-layouts  47.4 us (30%)
  starting transfers between devices  39 us (25%)
  Pallas kernels  31.9 us (20%)
  waiting for transfers between devices  21.4 us (14%)
  between operations  13.7 us (9%)
    unnamed x39, local copies, waits for them, and re-layouts  47.2 us
    ppermute x8, starting transfers between devices, shifted(): return lax.ppermute(array, axis, pairs)  23.3 us
    ppermute x7, starting transfers between devices, partner(): lax.ppermute(array, axis, [(i, i ^ 1 << stride) for i in range(lax.axis_s...  15.7 us
    ppermute x8, waiting for transfers between devices, shifted(): return lax.ppermute(array, axis, pairs)  13 us
    pallas_call x1, Pallas kernels, near(): pl.pallas_call(near_kernel, out_shape=jax.ShapeDtypeStruct((leaves, size,...  11 us
    pallas_call x1, Pallas kernels, final(): pl.pallas_call(final_kernel, out_shape=jax.ShapeDtypeStruct((leaves, size...  8.9 us
    ppermute x7, waiting for transfers between devices, partner(): lax.ppermute(array, axis, [(i, i ^ 1 << stride) for i in range(lax.axis_s...  8.46 us
    pallas_call x1, Pallas kernels, upward(): pl.pallas_call(upward_kernel, out_shape=(jax.ShapeDtypeStruct((leaves, ra...  3.53 us
  transfers between devices with their start and end apart: 16, of which 8 were waited for; matrix products, arithmetic and copies ran while one was open for 12% of the time, Pallas kernels for 13%

profile of v1, /device:TPU:1, one launch (start us, length us, event | category | flops | bytes accessed | tf_op | source)
XLA Modules:
  0.0 154.1 jit_solution(17596013487185307661)
XLA Ops:
  12.0 3.5 %upward.1 = (bf16[16,64,128]{2,1,0:T(8,128)(2,1)}, f32[64,128]{1,0:T(8,128)S(1)}) custom-call(s32[16]{0:T(128)S(1)} %broadcast_subtract_fusion.1.parent.refs_0_, bf16[16,256,128]{2,1,0:T(8,128)(2,1)S(1)} %bitcast.2, bf16[16,256,64]{2,1,0:T(8,128)(2,1)S(1)} %copy.23.bases, f32[16,64,64]{2,1,0:T(8,128)S(1)} %copy-done.11, f32[8,64,64]{2,1,0:T(8,128)S(1)} %copy-done.13), custom_call_target="tpu_custom_call" | custom-call | flops 200000000 | bytes 4000000 | tf_op jit(solution)/shard_map/upward/pallas_call | solution.py:52
  15.6 5.8 %collective-permute-start.10 = (bf16[16,256,128]{2,1,0:T(8,128)(2,1)S(1)}, bf16[16,256,128]{2,1,0:T(8,128)(2,1)}, u32[]{:S(2)}, u32[]{:S(2)}) collective-permute-start(bf16[16,256,128]{2,1,0:T(8,128)(2,1)S(1)} %bitcast.3), channel_id=1, source_target_pairs={{0,15},{1,0},{2,1},{3,2},{4,3},{5,4},{6,5},{7,6},{8,7},{9,8},{10,9... | collective-permute-start | bytes 3145736 | tf_op jit(solution)/shard_map/ppermute | solution.py:251
  21.4 2.9 %collective-permute-start.13 = (bf16[16,256,128]{2,1,0:T(8,128)(2,1)S(1)}, bf16[16,256,128]{2,1,0:T(8,128)(2,1)}, u32[]{:S(2)}, u32[]{:S(2)}) collective-permute-start(bf16[16,256,128]{2,1,0:T(8,128)(2,1)S(1)} %bitcast.5), channel_id=1, source_target_pairs={{16,0},{32,16},{48,32},{64,48},{80,64},{96,80},{112,96},{17,1},{33... | collective-permute-start | bytes 3145736 | tf_op jit(solution)/shard_map/ppermute | solution.py:251
  24.4 9.2 %copy.24.transfer = f32[256,64,64]{2,1,0:T(8,128)} copy(f32[256,64,64]{0,2,1:T(8,128)} %param.17) | data formatting | bytes 8388608 | tf_op args[5]
  33.6 9.2 %copy.25.coupling = f32[256,64,64]{2,1,0:T(8,128)} copy(f32[256,64,64]{0,2,1:T(8,128)} %param.18) | data formatting | bytes 8388608 | tf_op args[6]
  42.8 3.4 %copy-done = f32[256,64,64]{2,1,0:T(8,128)S(1)} copy-done((f32[256,64,64]{2,1,0:T(8,128)S(1)}, f32[256,64,64]{2,1,0:T(8,128)}, u32[]{:S(2)}) %copy-start) | copy-done | bytes 4194328
  46.2 3.4 %copy-done.1 = f32[256,64,64]{2,1,0:T(8,128)S(1)} copy-done((f32[256,64,64]{2,1,0:T(8,128)S(1)}, f32[256,64,64]{2,1,0:T(8,128)}, u32[]{:S(2)}) %copy-start.1) | copy-done | bytes 4194328
  49.6 1.7 %tables.1.refs_2_.refs_8_ = f32[21,64,64]{2,1,0:T(8,128)S(1)} custom-call(s32[7]{0:T(128)S(1)} %iota_shift-right-arithmetic_fusion.nodes, f32[256,64,64]{2,1,0:T(8,128)S(1)} %copy-done, f32[256,64,64]{2,1,0:T(8,128)S(1)} %copy-done.1), custom_call_target="tpu_custom_call" | custom-call | bytes 700000 | tf_op jit(solution)/shard_map/tables/pallas_call | solution.py:84
  51.6 2.7 %collective-permute-start.1 = (f32[64,128]{1,0:T(8,128)S(1)}, f32[64,128]{1,0:T(8,128)S(1)}, u32[]{:S(2)}, u32[]{:S(2)}) collective-permute-start(f32[64,128]{1,0:T(8,128)S(1)} %combine.6.refs_0_), channel_id=1, source_target_pairs={{0,2},{1,3},{2,0},{3,1},{4,6},{5,7},{6,4},{7,5},{8,10},{9,11},{10,... | collective-permute-start | bytes 98312 | tf_op jit(solution)/shard_map/ppermute | solution.py:255
  54.2 2.0 %collective-permute-done.1.refs_1_.refs_2_ = f32[64,128]{1,0:T(8,128)S(1)} collective-permute-done((f32[64,128]{1,0:T(8,128)S(1)}, f32[64,128]{1,0:T(8,128)S(1)}, u32[]{:S(2)}, u32[]{:S(2)}) %collective-permute-start.1) | collective-permute-done | bytes 32800 | tf_op jit(solution)/shard_map/ppermute | solution.py:255
  57.5 1.9 %collective-permute-done.2.refs_1_.refs_3_ = f32[64,128]{1,0:T(8,128)S(1)} collective-permute-done((f32[64,128]{1,0:T(8,128)S(1)}, f32[64,128]{1,0:T(8,128)S(1)}, u32[]{:S(2)}, u32[]{:S(2)}) %collective-permute-start.2) | collective-permute-done | bytes 32800 | tf_op jit(solution)/shard_map/ppermute | solution.py:255
  59.6 3.5 %collective-permute-start.3 = (f32[64,128]{1,0:T(8,128)S(1)}, f32[64,128]{1,0:T(8,128)S(1)}, u32[]{:S(2)}, u32[]{:S(2)}) collective-permute-start(f32[64,128]{1,0:T(8,128)S(1)} %combine.8.refs_0_), channel_id=1, source_target_pairs={{0,8},{1,9},{2,10},{3,11},{4,12},{5,13},{6,14},{7,15},{8,0},{9,1},... | collective-permute-start | bytes 98312 | tf_op jit(solution)/shard_map/ppermute | solution.py:255
  63.1 2.0 %collective-permute-done.3.refs_1_.refs_4_ = f32[64,128]{1,0:T(8,128)S(1)} collective-permute-done((f32[64,128]{1,0:T(8,128)S(1)}, f32[64,128]{1,0:T(8,128)S(1)}, u32[]{:S(2)}, u32[]{:S(2)}) %collective-permute-start.3) | collective-permute-done | bytes 32800 | tf_op jit(solution)/shard_map/ppermute | solution.py:255
  65.4 2.3 %collective-permute-start.4 = (f32[64,128]{1,0:T(8,128)S(1)}, f32[64,128]{1,0:T(8,128)S(1)}, u32[]{:S(2)}, u32[]{:S(2)}) collective-permute-start(f32[64,128]{1,0:T(8,128)S(1)} %combine.9.refs_0_), channel_id=1, source_target_pairs={{0,16},{1,17},{2,18},{3,19},{4,20},{5,21},{6,22},{7,23},{8,24},{9,... | collective-permute-start | bytes 98312 | tf_op jit(solution)/shard_map/ppermute | solution.py:255
  68.8 2.7 %collective-permute-start.5 = (f32[64,128]{1,0:T(8,128)S(1)}, f32[64,128]{1,0:T(8,128)S(1)}, u32[]{:S(2)}, u32[]{:S(2)}) collective-permute-start(f32[64,128]{1,0:T(8,128)S(1)} %combine.10.refs_0_), channel_id=1, source_target_pairs={{0,32},{1,33},{2,34},{3,35},{4,36},{5,37},{6,38},{7,39},{8,40},{9,... | collective-permute-start | bytes 98312 | tf_op jit(solution)/shard_map/ppermute | solution.py:255
  71.5 1.7 %collective-permute-done.5.refs_1_.refs_6_ = f32[64,128]{1,0:T(8,128)S(1)} collective-permute-done((f32[64,128]{1,0:T(8,128)S(1)}, f32[64,128]{1,0:T(8,128)S(1)}, u32[]{:S(2)}, u32[]{:S(2)}) %collective-permute-start.5) | collective-permute-done | bytes 32800 | tf_op jit(solution)/shard_map/ppermute | solution.py:255
  73.5 3.4 %collective-permute-start.6 = (f32[64,128]{1,0:T(8,128)S(1)}, f32[64,128]{1,0:T(8,128)S(1)}, u32[]{:S(2)}, u32[]{:S(2)}) collective-permute-start(f32[64,128]{1,0:T(8,128)S(1)} %combine.11), channel_id=1, source_target_pairs={{0,64},{1,65},{2,66},{3,67},{4,68},{5,69},{6,70},{7,71},{8,72},{9,... | collective-permute-start | bytes 98312 | tf_op jit(solution)/shard_map/ppermute | solution.py:255
  76.9 3.7 %collective-permute-start.9 = (bf16[16,256,128]{2,1,0:T(8,128)(2,1)S(1)}, bf16[16,256,128]{2,1,0:T(8,128)(2,1)}, u32[]{:S(2)}, u32[]{:S(2)}) collective-permute-start(bf16[16,256,128]{2,1,0:T(8,128)(2,1)S(1)} %bitcast.6), channel_id=1, source_target_pairs={{0,16},{16,32},{32,48},{48,64},{64,80},{80,96},{96,112},{1,17},{17... | collective-permute-start | bytes 3145736 | tf_op jit(solution)/shard_map/ppermute | solution.py:251
  80.6 1.9 %collective-permute-start.11 = (bf16[16,256,128]{2,1,0:T(8,128)(2,1)}, bf16[16,256,128]{2,1,0:T(8,128)(2,1)}, u32[]{:S(2)}, u32[]{:S(2)}) collective-permute-start(bf16[16,256,128]{2,1,0:T(8,128)(2,1)} %collective-permute-done.10.refs_5_), channel_id=1, source_target_pairs={{0,16},{16,32},{32,48},{48,64},{64,80},{80,96},{96,112},{1,17},{17... | collective-permute-start | bytes 3145736 | tf_op jit(solution)/shard_map/ppermute | solution.py:251
  82.6 3.4 %collective-permute-start.14 = (bf16[16,256,128]{2,1,0:T(8,128)(2,1)}, bf16[16,256,128]{2,1,0:T(8,128)(2,1)}, u32[]{:S(2)}, u32[]{:S(2)}) collective-permute-start(bf16[16,256,128]{2,1,0:T(8,128)(2,1)} %collective-permute-done.10.refs_5_), channel_id=1, source_target_pairs={{16,0},{32,16},{48,32},{64,48},{80,64},{96,80},{112,96},{17,1},{33... | collective-permute-start | bytes 3145736 | tf_op jit(solution)/shard_map/ppermute | solution.py:251
  86.0 1.9 %collective-permute-start.12 = (bf16[16,256,128]{2,1,0:T(8,128)(2,1)}, bf16[16,256,128]{2,1,0:T(8,128)(2,1)}, u32[]{:S(2)}, u32[]{:S(2)}) collective-permute-start(bf16[16,256,128]{2,1,0:T(8,128)(2,1)} %collective-permute-done.7.refs_3_), channel_id=1, source_target_pairs={{16,0},{32,16},{48,32},{64,48},{80,64},{96,80},{112,96},{17,1},{33... | collective-permute-start | bytes 3145736 | tf_op jit(solution)/shard_map/ppermute | solution.py:251
  87.9 3.6 %collective-permute-start.8 = (bf16[16,256,128]{2,1,0:T(8,128)(2,1)}, bf16[16,256,128]{2,1,0:T(8,128)(2,1)}, u32[]{:S(2)}, u32[]{:S(2)}) collective-permute-start(bf16[16,256,128]{2,1,0:T(8,128)(2,1)} %collective-permute-done.7.refs_3_), channel_id=1, source_target_pairs={{0,16},{16,32},{32,48},{48,64},{64,80},{80,96},{96,112},{1,17},{17... | collective-permute-start | bytes 3145736 | tf_op jit(solution)/shard_map/ppermute | solution.py:251
  91.9 3.4 %copy-done.3 = f32[16,16,64,64]{3,2,1,0:T(8,128)S(1)} copy-done((f32[16,16,64,64]{3,2,1,0:T(8,128)S(1)}, f32[16,16,64,64]{3,2,1,0:T(8,128)}, u32[]{:S(2)}) %copy-start.3) | copy-done | bytes 4194328
  95.3 2.4 %weights.1.packed = bf16[16,64,1024]{2,1,0:T(8,128)(2,1)S(1)} custom-call(s32[16]{0:T(128)S(1)} %copy-done.15, f32[16,16,64,64]{3,2,1,0:T(8,128)S(1)} %copy-done.3), custom_call_target="tpu_custom_call" | custom-call | bytes 11000000 | tf_op jit(solution)/shard_map/weights/pallas_call | solution.py:153
  99.0 2.9 %downward.1.on_leaf = f32[16,64,128]{2,1,0:T(8,128)S(1)} custom-call(s32[16]{0:T(128)S(1)} %broadcast_subtract_fusion.1.parent.refs_0_, f32[64,128]{1,0:T(8,128)S(1)} %collective-permute-done.refs_1_, f32[64,128]{1,0:T(8,128)S(1)} %collective-permute-done.1.refs_1_.refs_2_, f32[64,128]{1,0:T(8,128)S(1)} %collective-permute-done.2.refs_1_.refs_3_, ...), custom_call_target="tpu_custom_call" | custom-call | flops 200000000 | bytes 2000000 | tf_op jit(solution)/shard_map/downward/pallas_call | solution.py:129
  102.0 1.7 %collective-permute-done.11.refs_2_ = bf16[16,256,128]{2,1,0:T(8,128)(2,1)} collective-permute-done((bf16[16,256,128]{2,1,0:T(8,128)(2,1)}, bf16[16,256,128]{2,1,0:T(8,128)(2,1)}, u32[]{:S(2)}, u32[]{:S(2)}) %collective-permute-start.11) | collective-permute-done | bytes 1048608 | tf_op jit(solution)/shard_map/ppermute | solution.py:251
  103.7 6.6 %collective-permute-done.12.refs_6_ = bf16[16,256,128]{2,1,0:T(8,128)(2,1)} collective-permute-done((bf16[16,256,128]{2,1,0:T(8,128)(2,1)}, bf16[16,256,128]{2,1,0:T(8,128)(2,1)}, u32[]{:S(2)}, u32[]{:S(2)}) %collective-permute-start.12) | collective-permute-done | bytes 1048608 | tf_op jit(solution)/shard_map/ppermute | solution.py:251
  110.2 4.7 %collective-permute-done.8.refs_0_ = bf16[16,256,128]{2,1,0:T(8,128)(2,1)} collective-permute-done((bf16[16,256,128]{2,1,0:T(8,128)(2,1)}, bf16[16,256,128]{2,1,0:T(8,128)(2,1)}, u32[]{:S(2)}, u32[]{:S(2)}) %collective-permute-start.8) | collective-permute-done | bytes 1048608 | tf_op jit(solution)/shard_map/ppermute | solution.py:251
  114.9 5.8 %copy-done.2 = bf16[16,8,256,256]{3,2,1,0:T(8,128)(2,1)S(1)} copy-done((bf16[16,8,256,256]{3,2,1,0:T(8,128)(2,1)S(1)}, bf16[16,8,256,256]{3,2,1,0:T(8,128)(2,1)}, u32[]{:S(2)}) %copy-start.2) | copy-done | bytes 16777240
  120.7 11.0 %near.1.near_part = f32[16,256,128]{2,1,0:T(8,128)S(1)} custom-call(s32[128]{0:T(128)S(1)} %reshape.14.position, bf16[16,8,256,256]{3,2,1,0:T(8,128)(2,1)S(1)} %copy-done.2, bf16[16,256,128]{2,1,0:T(8,128)(2,1)} %collective-permute-done.8.refs_0_, bf16[16,256,128]{2,1,0:T(8,128)(2,1)} %collective-permute-done.9.refs_1_, ...), custom_call_target="tpu_custom_call" | custom-call | flops 2200000000 | bytes 28000000 | tf_op jit(solution)/shard_map/near/pallas_call | solution.py:195
  136.2 2.2 %copy-done.8 = bf16[256,64,128]{2,1,0:T(8,128)(2,1)S(1)} copy-done((bf16[256,64,128]{2,1,0:T(8,128)(2,1)S(1)}, bf16[256,64,128]{2,1,0:T(8,128)(2,1)}, u32[]{:S(2)}) %copy-start.8) | copy-done | bytes 4194328
  138.4 8.9 %final.1 = bf16[16,256,128]{2,1,0:T(8,128)(2,1)} custom-call(s32[256]{0:T(256)S(1)} %reshape.12.rows, bf16[16,64,1024]{2,1,0:T(8,128)(2,1)S(1)} %copy-done.5, bf16[256,64,128]{2,1,0:T(8,128)(2,1)S(1)} %copy-done.8, f32[16,64,128]{2,1,0:T(8,128)S(1)} %downward.1.on_leaf, bf16[16,256,64]{2,1,0:T(8,128)(2,1)S(1)} %copy.23.bases, f32[16,256,128]{2,1,0:T(8,128)S(1)} %copy-done.7), custom_call_target="tpu_custom_call" | custom-call | flops 350000000 | bytes 12000000 | tf_op jit(solution)/shard_map/final/pallas_call | solution.py:226
  (59 shorter events, 15.1 us)
Async XLA Ops:
  6.5 9.1 %copy-start.10 = (bf16[4096,128]{1,0:T(8,128)(2,1)S(1)}, bf16[4096,128]{1,0:T(8,128)(2,1)}, u32[]{:S(2)}) copy-start(bf16[4096,128]{1,0:T(8,128)(2,1)} %param.12) | copy-start | bytes 3145732
  6.5 126.5 %all-gather.2.cloned.1.call-start = ((), (), s32[]{:S(2)}) async-start(), calls=%async_computation | async-start | bytes 4456448 | tf_op jit(solution)/shard_map/all_gather | solution.py:292
  8.8 1.2 copy-start.9
  15.6 65.0 %collective-permute-start.10 = (bf16[16,256,128]{2,1,0:T(8,128)(2,1)S(1)}, bf16[16,256,128]{2,1,0:T(8,128)(2,1)}, u32[]{:S(2)}, u32[]{:S(2)}) collective-permute-start(bf16[16,256,128]{2,1,0:T(8,128)(2,1)S(1)} %bitcast.3), channel_id=1, source_target_pairs={{0,15},{1,0},{2,1},{3,2},{4,3},{5,4},{6,5},{7,6},{8,7},{9,8},{10,9... | collective-permute-start | bytes 3145736 | tf_op jit(solution)/shard_map/ppermute | solution.py:251
  21.4 64.6 %collective-permute-start.7 = (bf16[16,256,128]{2,1,0:T(8,128)(2,1)S(1)}, bf16[16,256,128]{2,1,0:T(8,128)(2,1)}, u32[]{:S(2)}, u32[]{:S(2)}) collective-permute-start(bf16[16,256,128]{2,1,0:T(8,128)(2,1)S(1)} %bitcast.4), channel_id=1, source_target_pairs={{0,1},{1,2},{2,3},{3,4},{4,5},{5,6},{6,7},{7,8},{8,9},{9,10},{10,1... | collective-permute-start | bytes 3145736 | tf_op jit(solution)/shard_map/ppermute | solution.py:251
  21.4 66.5 %collective-permute-start.13 = (bf16[16,256,128]{2,1,0:T(8,128)(2,1)S(1)}, bf16[16,256,128]{2,1,0:T(8,128)(2,1)}, u32[]{:S(2)}, u32[]{:S(2)}) collective-permute-start(bf16[16,256,128]{2,1,0:T(8,128)(2,1)S(1)} %bitcast.5), channel_id=1, source_target_pairs={{16,0},{32,16},{48,32},{64,48},{80,64},{96,80},{112,96},{17,1},{33... | collective-permute-start | bytes 3145736 | tf_op jit(solution)/shard_map/ppermute | solution.py:251
  24.3 27.0 %collective-permute-start = (f32[64,128]{1,0:T(8,128)S(1)}, f32[64,128]{1,0:T(8,128)S(1)}, u32[]{:S(2)}, u32[]{:S(2)}) collective-permute-start(f32[64,128]{1,0:T(8,128)S(1)} %get-tuple-element.8.refs_0_), channel_id=1, source_target_pairs={{0,1},{1,0},{2,3},{3,2},{4,5},{5,4},{6,7},{7,6},{8,9},{9,8},{10,11... | collective-permute-start | bytes 98312 | tf_op jit(solution)/shard_map/ppermute | solution.py:255
  42.8 3.4 %copy-start = (f32[256,64,64]{2,1,0:T(8,128)S(1)}, f32[256,64,64]{2,1,0:T(8,128)}, u32[]{:S(2)}) copy-start(f32[256,64,64]{2,1,0:T(8,128)} %copy.24.transfer) | copy-start | bytes 12582916
  46.2 3.4 %copy-start.1 = (f32[256,64,64]{2,1,0:T(8,128)S(1)}, f32[256,64,64]{2,1,0:T(8,128)}, u32[]{:S(2)}) copy-start(f32[256,64,64]{2,1,0:T(8,128)} %copy.25.coupling) | copy-start | bytes 12582916
  51.3 40.3 %copy-start.17 = (s32[16,8]{0,1:T(8,128)S(1)}, s32[16,8]{0,1:T(8,128)}, u32[]{:S(2)}) copy-start(s32[16,8]{0,1:T(8,128)} %param.19) | copy-start | bytes 1540
  51.3 40.5 %copy-start.16 = (s32[16,16]{1,0:T(8,128)S(1)}, s32[16,16]{1,0:T(8,128)}, u32[]{:S(2)}) copy-start(s32[16,16]{1,0:T(8,128)} %param.21) | copy-start | bytes 3076
  51.3 40.6 %copy-start.15 = (s32[16]{0:T(128)S(1)}, s32[16]{0:T(128)}, u32[]{:S(2)}) copy-start(s32[16]{0:T(128)} %count.1) | copy-start | bytes 196
  51.6 4.7 %collective-permute-start.1 = (f32[64,128]{1,0:T(8,128)S(1)}, f32[64,128]{1,0:T(8,128)S(1)}, u32[]{:S(2)}, u32[]{:S(2)}) collective-permute-start(f32[64,128]{1,0:T(8,128)S(1)} %combine.6.refs_0_), channel_id=1, source_target_pairs={{0,2},{1,3},{2,0},{3,1},{4,6},{5,7},{6,4},{7,5},{8,10},{9,11},{10,... | collective-permute-start | bytes 98312 | tf_op jit(solution)/shard_map/ppermute | solution.py:255
  56.5 2.8 %collective-permute-start.2 = (f32[64,128]{1,0:T(8,128)S(1)}, f32[64,128]{1,0:T(8,128)S(1)}, u32[]{:S(2)}, u32[]{:S(2)}) collective-permute-start(f32[64,128]{1,0:T(8,128)S(1)} %combine.7.refs_0_), channel_id=1, source_target_pairs={{0,4},{1,5},{2,6},{3,7},{4,0},{5,1},{6,2},{7,3},{8,12},{9,13},{10,... | collective-permute-start | bytes 98312 | tf_op jit(solution)/shard_map/ppermute | solution.py:255
  59.6 5.5 %collective-permute-start.3 = (f32[64,128]{1,0:T(8,128)S(1)}, f32[64,128]{1,0:T(8,128)S(1)}, u32[]{:S(2)}, u32[]{:S(2)}) collective-permute-start(f32[64,128]{1,0:T(8,128)S(1)} %combine.8.refs_0_), channel_id=1, source_target_pairs={{0,8},{1,9},{2,10},{3,11},{4,12},{5,13},{6,14},{7,15},{8,0},{9,1},... | collective-permute-start | bytes 98312 | tf_op jit(solution)/shard_map/ppermute | solution.py:255
  65.4 3.2 %collective-permute-start.4 = (f32[64,128]{1,0:T(8,128)S(1)}, f32[64,128]{1,0:T(8,128)S(1)}, u32[]{:S(2)}, u32[]{:S(2)}) collective-permute-start(f32[64,128]{1,0:T(8,128)S(1)} %combine.9.refs_0_), channel_id=1, source_target_pairs={{0,16},{1,17},{2,18},{3,19},{4,20},{5,21},{6,22},{7,23},{8,24},{9,... | collective-permute-start | bytes 98312 | tf_op jit(solution)/shard_map/ppermute | solution.py:255
  68.8 4.4 %collective-permute-start.5 = (f32[64,128]{1,0:T(8,128)S(1)}, f32[64,128]{1,0:T(8,128)S(1)}, u32[]{:S(2)}, u32[]{:S(2)}) collective-permute-start(f32[64,128]{1,0:T(8,128)S(1)} %combine.10.refs_0_), channel_id=1, source_target_pairs={{0,32},{1,33},{2,34},{3,35},{4,36},{5,37},{6,38},{7,39},{8,40},{9,... | collective-permute-start | bytes 98312 | tf_op jit(solution)/shard_map/ppermute | solution.py:255
  73.5 9.1 %collective-permute-start.6 = (f32[64,128]{1,0:T(8,128)S(1)}, f32[64,128]{1,0:T(8,128)S(1)}, u32[]{:S(2)}, u32[]{:S(2)}) collective-permute-start(f32[64,128]{1,0:T(8,128)S(1)} %combine.11), channel_id=1, source_target_pairs={{0,64},{1,65},{2,66},{3,67},{4,68},{5,69},{6,70},{7,71},{8,72},{9,... | collective-permute-start | bytes 98312 | tf_op jit(solution)/shard_map/ppermute | solution.py:255
  76.9 25.1 %collective-permute-start.9 = (bf16[16,256,128]{2,1,0:T(8,128)(2,1)S(1)}, bf16[16,256,128]{2,1,0:T(8,128)(2,1)}, u32[]{:S(2)}, u32[]{:S(2)}) collective-permute-start(bf16[16,256,128]{2,1,0:T(8,128)(2,1)S(1)} %bitcast.6), channel_id=1, source_target_pairs={{0,16},{16,32},{32,48},{48,64},{64,80},{80,96},{96,112},{1,17},{17... | collective-permute-start | bytes 3145736 | tf_op jit(solution)/shard_map/ppermute | solution.py:251
  80.6 23.1 %collective-permute-start.11 = (bf16[16,256,128]{2,1,0:T(8,128)(2,1)}, bf16[16,256,128]{2,1,0:T(8,128)(2,1)}, u32[]{:S(2)}, u32[]{:S(2)}) collective-permute-start(bf16[16,256,128]{2,1,0:T(8,128)(2,1)} %collective-permute-done.10.refs_5_), channel_id=1, source_target_pairs={{0,16},{16,32},{32,48},{48,64},{64,80},{80,96},{96,112},{1,17},{17... | collective-permute-start | bytes 3145736 | tf_op jit(solution)/shard_map/ppermute | solution.py:251
  82.6 27.7 %collective-permute-start.14 = (bf16[16,256,128]{2,1,0:T(8,128)(2,1)}, bf16[16,256,128]{2,1,0:T(8,128)(2,1)}, u32[]{:S(2)}, u32[]{:S(2)}) collective-permute-start(bf16[16,256,128]{2,1,0:T(8,128)(2,1)} %collective-permute-done.10.refs_5_), channel_id=1, source_target_pairs={{16,0},{32,16},{48,32},{64,48},{80,64},{96,80},{112,96},{17,1},{33... | collective-permute-start | bytes 3145736 | tf_op jit(solution)/shard_map/ppermute | solution.py:251
  86.0 24.2 %collective-permute-start.12 = (bf16[16,256,128]{2,1,0:T(8,128)(2,1)}, bf16[16,256,128]{2,1,0:T(8,128)(2,1)}, u32[]{:S(2)}, u32[]{:S(2)}) collective-permute-start(bf16[16,256,128]{2,1,0:T(8,128)(2,1)} %collective-permute-done.7.refs_3_), channel_id=1, source_target_pairs={{16,0},{32,16},{48,32},{64,48},{80,64},{96,80},{112,96},{17,1},{33... | collective-permute-start | bytes 3145736 | tf_op jit(solution)/shard_map/ppermute | solution.py:251
  87.9 27.0 %collective-permute-start.8 = (bf16[16,256,128]{2,1,0:T(8,128)(2,1)}, bf16[16,256,128]{2,1,0:T(8,128)(2,1)}, u32[]{:S(2)}, u32[]{:S(2)}) collective-permute-start(bf16[16,256,128]{2,1,0:T(8,128)(2,1)} %collective-permute-done.7.refs_3_), channel_id=1, source_target_pairs={{0,16},{16,32},{32,48},{48,64},{64,80},{80,96},{96,112},{1,17},{17... | collective-permute-start | bytes 3145736 | tf_op jit(solution)/shard_map/ppermute | solution.py:251
  91.9 3.4 %copy-start.3 = (f32[16,16,64,64]{3,2,1,0:T(8,128)S(1)}, f32[16,16,64,64]{3,2,1,0:T(8,128)}, u32[]{:S(2)}) copy-start(f32[16,16,64,64]{3,2,1,0:T(8,128)} %coupling.2) | copy-start | bytes 12582916
  95.3 3.7 %copy-start.12 = (f32[16,64,64]{2,1,0:T(8,128)S(1)}, f32[16,64,64]{2,1,0:T(8,128)}, u32[]{:S(2)}) copy-start(f32[16,64,64]{2,1,0:T(8,128)} %refs_10_.1) | copy-start | bytes 786436
  95.3 3.7 %copy-start.14 = (f32[8,64,64]{2,1,0:T(8,128)S(1)}, f32[8,64,64]{2,1,0:T(8,128)}, u32[]{:S(2)}) copy-start(f32[8,64,64]{2,1,0:T(8,128)} %refs_9_.1) | copy-start | bytes 393220
  97.7 1.3 copy-start.4
  114.9 5.8 %copy-start.2 = (bf16[16,8,256,256]{3,2,1,0:T(8,128)(2,1)S(1)}, bf16[16,8,256,256]{3,2,1,0:T(8,128)(2,1)}, u32[]{:S(2)}) copy-start(bf16[16,8,256,256]{3,2,1,0:T(8,128)(2,1)} %blocks.1) | copy-start | bytes 50331652
  131.7 1.3 copy-start.6
  133.0 1.6 %copy-start.5 = (bf16[16,64,1024]{2,1,0:T(8,128)(2,1)S(1)}, bf16[16,64,1024]{2,1,0:T(8,128)(2,1)}, u32[]{:S(2)}) copy-start(bf16[16,64,1024]{2,1,0:T(8,128)(2,1)} %copy-done.4) | copy-start | bytes 6291460
  134.6 1.6 %copy-start.7 = (f32[16,256,128]{2,1,0:T(8,128)S(1)}, f32[16,256,128]{2,1,0:T(8,128)}, u32[]{:S(2)}) copy-start(f32[16,256,128]{2,1,0:T(8,128)} %copy-done.6) | copy-start | bytes 6291460
  136.2 2.2 %copy-start.8 = (bf16[256,64,128]{2,1,0:T(8,128)(2,1)S(1)}, bf16[256,64,128]{2,1,0:T(8,128)(2,1)}, u32[]{:S(2)}) copy-start(bf16[256,64,128]{2,1,0:T(8,128)(2,1)} %all-gather.2.cloned.1.call-done.coefs) | copy-start | bytes 12582916
  (2 other events, 2.0 us)
Sparse Core Ops, SparseCore 0:
  15.7 64.2 all-gather.1

commit v2 on v1

v2 whole, which is shorter than its diff:
```python
import jax
import jax.numpy as jnp
from jax import lax
from jax.experimental import pallas as pl
from jax.experimental.pallas import tpu as pltpu
from jax.sharding import PartitionSpec as P

highest = lax.Precision.HIGHEST
f32 = jnp.float32
bf16 = jnp.bfloat16


def dot_t(a, b, precision=None):
    return lax.dot_general(a, b, (((0,), (0,)), ((), ())), precision=precision, preferred_element_type=f32)


def dot(a, b, precision=None):
    return lax.dot_general(a, b, (((1,), (0,)), ((), ())), precision=precision, preferred_element_type=f32)


def dot_r(a, b):
    return lax.dot_general(a, b, (((1,), (1,)), ((), ())), preferred_element_type=f32)


def in_hbm(array):
    return pltpu.with_memory_space_constraint(array, pltpu.HBM)


def whole():
    return pl.BlockSpec(memory_space=pltpu.VMEM)


def anywhere():
    return pl.BlockSpec(memory_space=pl.ANY)


def scalars():
    return pl.BlockSpec(memory_space=pltpu.SMEM)


def params(mib, semantics=None):
    return pltpu.CompilerParams(vmem_limit_bytes=mib << 20, dimension_semantics=semantics)


def cost(flops, nbytes):
    return pl.CostEstimate(flops=flops, bytes_accessed=nbytes, transcendentals=0)


def coefs_kernel(sources, bases, leaf_out, held, basis, sems):
    group = sems.shape[0]
    step = held.shape[0] // group
    copies = []
    for part in range(group):
        rows = pl.ds(part * step, step)
        copies.append(
            (
                pltpu.make_async_copy(sources.at[rows], held.at[rows], sems.at[part, 0]),
                pltpu.make_async_copy(bases.at[rows], basis.at[rows], sems.at[part, 1]),
            )
        )
    for pair in copies:
        for copy in pair:
            copy.start()
    for part, pair in enumerate(copies):
        for copy in pair:
            copy.wait()
        for leaf in range(part * step, (part + 1) * step):
            leaf_out[leaf] = dot(basis[leaf], held[leaf]).astype(bf16)


def leaf_coefficients(panels, bases):
    leaves, size, rhs = panels.shape
    rank = bases.shape[1]
    return pl.pallas_call(
        coefs_kernel,
        out_shape=jax.ShapeDtypeStruct((leaves, rank, rhs), bf16),
        in_specs=[anywhere(), anywhere()],
        out_specs=whole(),
        scratch_shapes=[
            pltpu.VMEM((leaves, size, rhs), bf16),
            pltpu.VMEM((leaves, rank, size), bf16),
            pltpu.SemaphoreType.DMA((4, 2)),
        ],
        compiler_params=params(8),
        cost_estimate=cost(1000, 1000),
        name="coefs",
    )(in_hbm(panels), in_hbm(bases))


def upward_kernel(parent, coefs, up, root, root_out, clusters):
    clusters[...] = jnp.zeros_like(clusters)
    for leaf in range(coefs.shape[0]):
        clusters[parent[leaf]] += dot_t(up[leaf], coefs[leaf].astype(f32), highest)
    total = dot_t(root[0], clusters[0], highest)
    for cluster in range(1, root.shape[0]):
        total = total + dot_t(root[cluster], clusters[cluster], highest)
    root_out[...] = total


def upward(local_parent, leaf_coefs, up_transfer, root_transfer):
    leaves, rank, rhs = leaf_coefs.shape
    return pl.pallas_call(
        upward_kernel,
        out_shape=jax.ShapeDtypeStruct((rank, rhs), f32),
        in_specs=[scalars(), whole(), whole(), whole()],
        out_specs=whole(),
        scratch_shapes=[pltpu.VMEM((root_transfer.shape[0], rank, rhs), f32)],
        compiler_params=params(8),
        cost_estimate=cost(1000, 1000),
        name="upward",
    )(local_parent, leaf_coefs, up_transfer, root_transfer)


def tables_kernel(nodes, *refs):
    half = len(refs) // 2
    rank, size = refs[0].shape[1:]
    ids = lax.broadcasted_iota(jnp.int32, (nodes.shape[0], size), 1)
    chosen = (ids == nodes[...]).astype(bf16)
    for table, out in zip(refs[:half], refs[half:]):
        values = table[...].reshape(-1, size)
        high = values.astype(bf16)
        low = (values - high.astype(f32)).astype(bf16)
        rows = dot_r(chosen, high) + dot_r(chosen, low)
        for row in range(table.shape[0]):
            out[:, row, :] = rows[:, row * rank : (row + 1) * rank]


def tables(nodes, transfer, coupling):
    count = nodes.shape[0]
    size, rank, _ = transfer.shape
    step = 16
    return pl.pallas_call(
        tables_kernel,
        out_shape=(jax.ShapeDtypeStruct((count, rank, rank), f32),) * 2,
        grid=(rank // step,),
        in_specs=[pl.BlockSpec((count, 1), lambda i: (0, 0))]
        + [pl.BlockSpec((step, rank, size), lambda i: (i, 0, 0))] * 2,
        out_specs=(pl.BlockSpec((count, step, rank), lambda i: (0, i, 0)),) * 2,
        compiler_params=params(16, ("arbitrary",)),
        cost_estimate=cost(1000, 1000),
        name="tables",
    )(nodes, in_hbm(transfer.transpose(1, 2, 0)), in_hbm(coupling.transpose(1, 2, 0)))


def combine_kernel(own, other, current, sibling, mats, out):
    total = dot_t(mats[own], current[...], highest)
    out[...] = total + dot_t(mats[other], sibling[...], highest)


def combine(own, other, current, sibling, mats):
    return pl.pallas_call(
        lambda *refs: combine_kernel(own, other, *refs),
        out_shape=jax.ShapeDtypeStruct(current.shape, f32),
        in_specs=[whole(), whole(), whole()],
        out_specs=whole(),
        compiler_params=params(4),
        cost_estimate=cost(1000, 1000),
        name="combine",
    )(current, sibling, mats)


def downward_kernel(depth, parent, *refs):
    siblings = refs[:depth]
    transfer, coupling, root, up, out, clusters = refs[depth:]
    down = dot(coupling[depth - 1], siblings[depth - 1][...], highest)
    for level in reversed(range(depth - 1)):
        across = dot(coupling[level], siblings[level][...], highest)
        down = across + dot(transfer[level], down, highest)
    for cluster in range(root.shape[0]):
        clusters[cluster] = dot(root[cluster], down, highest)
    for leaf in range(up.shape[0]):
        out[leaf] = dot(up[leaf], clusters[parent[leaf]], highest)


def downward(local_parent, siblings, transfer, coupling, root_transfer, up_transfer):
    depth = len(siblings)
    rank, rhs = siblings[0].shape
    return pl.pallas_call(
        lambda *refs: downward_kernel(depth, *refs),
        out_shape=jax.ShapeDtypeStruct((up_transfer.shape[0], rank, rhs), f32),
        in_specs=[scalars()] + [whole()] * (depth + 4),
        out_specs=whole(),
        scratch_shapes=[pltpu.VMEM((root_transfer.shape[0], rank, rhs), f32)],
        compiler_params=params(16),
        cost_estimate=cost(1000, 1000),
        name="downward",
    )(local_parent, *siblings, transfer, coupling, root_transfer, up_transfer)


def weights_kernel(count, coupling, out):
    group, slots, _, rank = coupling.shape
    for one in range(group):
        used = count[pl.program_id(0) * group + one]
        for pair in range(slots // 2):
            left = jnp.where(2 * pair < used, coupling[one, 2 * pair], 0.0)
            right = jnp.where(2 * pair + 1 < used, coupling[one, 2 * pair + 1], 0.0)
            both = jnp.concatenate([left, right], axis=1).astype(bf16)
            out[one, :, 2 * pair * rank : 2 * (pair + 1) * rank] = both


def weights(far_count, far_coupling):
    leaves, slots, rank, _ = far_coupling.shape
    group = 4
    return pl.pallas_call(
        weights_kernel,
        out_shape=jax.ShapeDtypeStruct((leaves, rank, slots * rank), bf16),
        grid_spec=pltpu.PrefetchScalarGridSpec(
            num_scalar_prefetch=1,
            grid=(leaves // group,),
            in_specs=[pl.BlockSpec((group, slots, rank, rank), lambda i, n: (i, 0, 0, 0))],
            out_specs=pl.BlockSpec((group, rank, slots * rank), lambda i, n: (i, 0, 0)),
        ),
        compiler_params=params(8, ("arbitrary",)),
        cost_estimate=cost(1000, 1000),
        name="weights",
    )(far_count, in_hbm(far_coupling))


def near_kernel(position, blocks, *refs):
    pieces = refs[:-5]
    out, held, matrices, piece_sems, block_sems = refs[-5:]
    leaves, slots = blocks.shape[:2]
    copies = []
    first = 0
    for index, piece in enumerate(pieces):
        rows = pl.ds(first, piece.shape[0])
        copies.append(pltpu.make_async_copy(piece, held.at[rows], piece_sems.at[index]))
        first += piece.shape[0]
    fetches = [
        pltpu.make_async_copy(blocks.at[leaf], matrices.at[leaf], block_sems.at[leaf]) for leaf in range(leaves)
    ]
    for copy in copies:
        copy.start()
    for fetch in fetches:
        fetch.start()
    for copy in copies:
        copy.wait()
    for leaf in range(leaves):
        fetches[leaf].wait()
        wide = jnp.concatenate([matrices[leaf, slot] for slot in range(slots)], axis=1)
        tall = jnp.concatenate([held[position[leaf * slots + slot]] for slot in range(slots)], axis=0)
        out[leaf] = dot(wide, tall)


def near(position, near_blocks, pieces):
    leaves, slots, size, _ = near_blocks.shape
    rhs = pieces[0].shape[2]
    return pl.pallas_call(
        near_kernel,
        out_shape=jax.ShapeDtypeStruct((leaves, size, rhs), f32),
        in_specs=[scalars()] + [anywhere()] * (1 + len(pieces)),
        out_specs=whole(),
        scratch_shapes=[
            pltpu.VMEM((sum(piece.shape[0] for piece in pieces), size, rhs), bf16),
            pltpu.VMEM(near_blocks.shape, bf16),
            pltpu.SemaphoreType.DMA((len(pieces),)),
            pltpu.SemaphoreType.DMA((leaves,)),
        ],
        compiler_params=params(36),
        cost_estimate=cost(1000, 1000),
        name="near",
    )(position, in_hbm(near_blocks), *[in_hbm(piece) for piece in pieces])


def final_kernel(rows, packed, coefs, on_leaf, bases, near_part, out, *scratch):
    held, picked, results, term, basis, close, load_sems, near_sems, out_sems = scratch
    leaves, rank, wide = packed.shape
    slots = wide // rank
    loads = [
        pltpu.make_async_copy(source, target, load_sems.at[index])
        for index, (source, target) in enumerate(((coefs, held), (on_leaf, term), (bases, basis)))
    ]
    nears = [pltpu.make_async_copy(near_part.at[leaf], close.at[leaf], near_sems.at[leaf]) for leaf in range(leaves)]
    for load in loads + nears:
        load.start()
    for load in loads:
        load.wait()
    stores = []
    for leaf in range(leaves):
        for slot in range(slots):
            picked[leaf, slot * rank : (slot + 1) * rank] = held[rows[leaf * slots + slot]]
        expansion = (term[leaf] + dot(packed[leaf], picked[leaf])).astype(bf16)
        nears[leaf].wait()
        results[leaf] = (dot_t(basis[leaf], expansion) + close[leaf]).astype(bf16)
        stores.append(pltpu.make_async_copy(results.at[leaf], out.at[leaf], out_sems.at[leaf]))
        stores[leaf].start()
    for store in stores:
        store.wait()


def final(far_rows, packed, slab_coefs, on_leaf, bases, near_part):
    leaves, rank, size = bases.shape
    rhs = near_part.shape[2]
    wide = packed.shape[2]
    return pl.pallas_call(
        final_kernel,
        out_shape=jax.ShapeDtypeStruct((leaves, size, rhs), bf16),
        in_specs=[scalars(), whole()] + [anywhere()] * 4,
        out_specs=anywhere(),
        scratch_shapes=[
            pltpu.VMEM(slab_coefs.shape, bf16),
            pltpu.VMEM((leaves, wide, rhs), bf16),
            pltpu.VMEM((leaves, size, rhs), bf16),
            pltpu.VMEM(on_leaf.shape, f32),
            pltpu.VMEM(bases.shape, bf16),
            pltpu.VMEM(near_part.shape, f32),
            pltpu.SemaphoreType.DMA((3,)),
            pltpu.SemaphoreType.DMA((leaves,)),
            pltpu.SemaphoreType.DMA((leaves,)),
        ],
        compiler_params=params(24),
        cost_estimate=cost(1000, 1000),
        name="final",
    )(far_rows, packed, *[in_hbm(array) for array in (slab_coefs, on_leaf, bases, near_part)])


def shifted(array, axis, step, closed):
    count = lax.axis_size(axis)
    pairs = [(i, (i + step) % count) for i in range(count) if closed or 0 <= i + step < count]
    return lax.ppermute(array, axis, pairs)


def both(array, axis, closed):
    return shifted(array, axis, 1, closed), shifted(array, axis, -1, closed)


def after(*arrays):
    return lax.optimization_barrier(arrays)


def partner(array, axis, stride):
    return lax.ppermute(array, axis, [(i, i ^ 1 << stride) for i in range(lax.axis_size(axis))])


def local(
    sources,
    bases,
    leaf_parent,
    up_transfer,
    root_transfer,
    top_transfer,
    top_coupling,
    near_list,
    near_blocks,
    far_list,
    far_count,
    far_coupling,
):
    leaf_total, leaf_size, _ = bases.shape
    bases = bases.transpose(0, 2, 1)
    rhs_count = sources.shape[1]
    cluster_total = leaf_total // 2
    slab_count = lax.axis_size("slab")
    sector_count = lax.axis_size("sector")
    devices = slab_count * sector_count
    depth = devices.bit_length() - 1
    slab_pos = lax.axis_index("slab")
    sector_pos = lax.axis_index("sector")
    device = slab_pos * sector_count + sector_pos
    panels = sources.reshape(leaf_total, leaf_size, rhs_count)

    half = leaf_total // 2
    below, above = both(panels, "slab", False)
    first_sides = both(panels[:half], "sector", True)

    local_parent = leaf_parent - device * cluster_total
    leaf_coefs = leaf_coefficients(panels, bases)
    slab_coefs = lax.all_gather(leaf_coefs, "sector", axis=0, tiled=True)
    current = upward(local_parent, leaf_coefs, up_transfer, root_transfer)
    slots = jnp.arange(2 * depth + 2, dtype=jnp.int32)
    nodes = ((devices + device) >> (slots % depth)) ^ (slots // depth)
    transfer, coupling = tables(nodes[:, None], top_transfer, top_coupling)

    siblings = []

    def climb(level, current):
        siblings.append(partner(current, ("slab", "sector"), level))
        return combine(level, depth + level, current, siblings[-1], transfer)

    current = climb(0, current)
    current, below, above, *first_sides = after(current, below, above, *first_sides)
    first_pair = jnp.concatenate(first_sides)
    first_far = both(first_pair, "slab", False)
    current = climb(1, current)
    second, current = after(panels[half:], current)
    second_sides = both(second, "sector", True)
    current = climb(2, current)
    current, *first_far = after(current, *first_far)
    current = climb(3, current)
    current = climb(4, current)
    current, *second_sides = after(current, *second_sides)
    second_pair = jnp.concatenate(second_sides)
    second_far = both(second_pair, "slab", False)
    current = climb(5, current)
    current, *second_far = after(current, *second_far)
    siblings.append(partner(current, ("slab", "sector"), 6))
    on_leaf = downward(local_parent, siblings, transfer, coupling, root_transfer, up_transfer)

    packed = weights(far_count, far_coupling)

    owner_device = near_list // leaf_total
    slab_offset = (owner_device // sector_count - slab_pos) % 3
    sector_offset = (owner_device % sector_count - sector_pos) % sector_count
    leaf = near_list % leaf_total
    place = leaf // half * (3 * leaf_total) + slab_offset * leaf_total + leaf % half
    place = place + jnp.where(sector_offset == 1, half, 0)
    position = jnp.where(sector_offset == 0, slab_offset * leaf_total + leaf, 3 * leaf_total + place)
    pieces = [panels, above, below]
    for pair, far in ((first_pair, first_far), (second_pair, second_far)):
        pieces += [pair, far[1], far[0]]
    near_part = near(position.reshape(-1), near_blocks, pieces)

    far_rows = (far_list - slab_pos * (sector_count * leaf_total)).reshape(-1)
    field = final(far_rows, packed, slab_coefs, on_leaf, bases, near_part)
    return field.reshape(leaf_total * leaf_size, rhs_count)


def solution(mesh):
    placed = (
        P(("slab", "sector"), None),
        P(("slab", "sector"), None, None),
        P(("slab", "sector")),
        P(("slab", "sector"), None, None),
        P(("slab", "sector"), None, None),
        P(),
        P(),
        P(("slab", "sector"), None),
        P(("slab", "sector"), None, None, None),
        P(("slab", "sector"), None),
        P(("slab", "sector")),
        P(("slab", "sector"), None, None, None),
    )
    return jax.shard_map(
        local, mesh=mesh, in_specs=placed, out_specs=P(("slab", "sector"), None), check_vma=False
    )
```

time: 156 us -> 151 us (0.968)
  local copies, waits for them, and re-layouts: 47.4 us -> 10.6 us
  waiting for transfers between devices: 21.4 us -> 39.8 us
  Pallas kernels: 31.9 us -> 45.3 us
    unnamed x39 -> x42, local copies, waits for them, and re-layouts: 47.2 us -> 4.92 us
    ppermute x7, waiting for transfers between devices: 8.46 us -> 26.3 us  [partner(): lax.ppermute(array, axis, [(i, i ^ 1 << stride) for i in range(lax.axis_s...]
    ppermute x8 -> x10, starting transfers between devices: 23.3 us -> 33 us  [shifted(): return lax.ppermute(array, axis, pairs)]
    ppermute x7, starting transfers between devices: 15.7 us -> 6.93 us  [partner(): lax.ppermute(array, axis, [(i, i ^ 1 << stride) for i in range(lax.axis_s...]
    pallas_call x8 -> x9, Pallas kernels: 6.71 us -> 12.8 us  [the longest x1 5.82 us: tables(): pl.pallas_call(tables_kernel, out_shape=(jax.ShapeDtypeStruct((count, ran...]
    pallas_call x1, Pallas kernels: 11 us -> 15.8 us  [near(): pl.pallas_call(near_kernel, out_shape=jax.ShapeDtypeStruct((leaves, size,...]
    pallas_call x1, Pallas kernels: 2.39 us -> 5 us  [weights(): pl.pallas_call(weights_kernel, out_shape=jax.ShapeDtypeStruct((leaves, ra...]
    slice x0 -> x1, local copies, waits for them, and re-layouts: none -> 2.24 us  [local(): second, current = after(panels[half:], current)]
  transfers between devices with their start and end apart: 16 -> 18, of which waited for: 8 -> 10; matrix products, arithmetic and copies ran while one was open for 12% -> 5% of each run, Pallas kernels for 13% -> 23%
where the time goes in v2:
time: 151 us; the launch traced here: 150 us
  Pallas kernels  45.3 us (30%)
  starting transfers between devices  39.9 us (26%)
  waiting for transfers between devices  39.8 us (26%)
  between operations  13.7 us (9%)
  local copies, waits for them, and re-layouts  10.6 us (7%)
    ppermute x10, starting transfers between devices, shifted(): return lax.ppermute(array, axis, pairs)  33 us
    ppermute x7, waiting for transfers between devices, partner(): lax.ppermute(array, axis, [(i, i ^ 1 << stride) for i in range(lax.axis_s...  26.3 us
    pallas_call x1, Pallas kernels, near(): pl.pallas_call(near_kernel, out_shape=jax.ShapeDtypeStruct((leaves, size,...  15.8 us
    ppermute x10, waiting for transfers between devices, shifted(): return lax.ppermute(array, axis, pairs)  13.5 us
    pallas_call x1, Pallas kernels, final(): pl.pallas_call(final_kernel, out_shape=jax.ShapeDtypeStruct((leaves, size...  8.55 us
    ppermute x7, starting transfers between devices, partner(): lax.ppermute(array, axis, [(i, i ^ 1 << stride) for i in range(lax.axis_s...  6.93 us
    pallas_call x1, Pallas kernels, tables(): pl.pallas_call(tables_kernel, out_shape=(jax.ShapeDtypeStruct((count, ran...  5.82 us
    pallas_call x1, Pallas kernels, weights(): pl.pallas_call(weights_kernel, out_shape=jax.ShapeDtypeStruct((leaves, ra...  5 us
  transfers between devices with their start and end apart: 18, of which 10 were waited for; matrix products, arithmetic and copies ran while one was open for 5% of the time, Pallas kernels for 23%

profile of v2, /device:TPU:1, one launch (start us, length us, event | category | flops | bytes accessed | tf_op | source)
XLA Modules:
  0.0 150.0 jit_solution(7705022173294941276)
XLA Ops:
  6.5 2.5 %coefs.1 = bf16[16,64,128]{2,1,0:T(8,128)(2,1)} custom-call(bf16[16,256,128]{2,1,0:T(8,128)(2,1)} %bitcast.7, bf16[16,64,256]{2,1,0:T(8,128)(2,1)} %bitcast.13), custom_call_target="tpu_custom_call" | custom-call | flops 1000 | bytes 1000 | tf_op jit(solution)/shard_map/coefs/pallas_call | solution.py:74
  9.1 4.9 %collective-permute-start.1 = (bf16[16,256,128]{2,1,0:T(8,128)(2,1)}, bf16[16,256,128]{2,1,0:T(8,128)(2,1)S(1)}, u32[]{:S(2)}, u32[]{:S(2)}) collective-permute-start(bf16[16,256,128]{2,1,0:T(8,128)(2,1)} %bitcast.8), channel_id=1, source_target_pairs={{0,16},{16,32},{32,48},{48,64},{64,80},{80,96},{96,112},{1,17},{17... | collective-permute-start | bytes 3145736 | tf_op jit(solution)/shard_map/ppermute | solution.py:320
  14.1 1.9 %collective-permute-start.2 = (bf16[16,256,128]{2,1,0:T(8,128)(2,1)}, bf16[16,256,128]{2,1,0:T(8,128)(2,1)}, u32[]{:S(2)}, u32[]{:S(2)}) collective-permute-start(bf16[16,256,128]{2,1,0:T(8,128)(2,1)} %bitcast.9), channel_id=1, source_target_pairs={{16,0},{32,16},{48,32},{64,48},{80,64},{96,80},{112,96},{17,1},{33... | collective-permute-start | bytes 3145736 | tf_op jit(solution)/shard_map/ppermute | solution.py:320
  16.0 2.2 %fusion.25 = (bf16[2048,128]{1,0:T(8,128)(2,1)}, bf16[2048,128]{1,0:T(8,128)(2,1)}) fusion(bf16[4096,128]{1,0:T(8,128)(2,1)} %param.12), kind=kLoop, calls=%fused_computation.58 | loop fusion | bytes 2097152 | tf_op jit(solution)/shard_map/slice | solution.py:385
  18.2 1.2 collective-permute-start.3
  19.4 3.7 %collective-permute-start.4 = (bf16[8,256,128]{2,1,0:T(8,128)(2,1)}, bf16[8,256,128]{2,1,0:T(8,128)(2,1)}, u32[]{:S(2)}, u32[]{:S(2)}) collective-permute-start(bf16[8,256,128]{2,1,0:T(8,128)(2,1)} %bitcast.4), channel_id=1, source_target_pairs={{0,15},{1,0},{2,1},{3,2},{4,3},{5,4},{6,5},{7,6},{8,7},{9,8},{10,9... | collective-permute-start | bytes 1572872 | tf_op jit(solution)/shard_map/ppermute | solution.py:320
  23.2 2.3 %upward.1.refs_0_ = f32[64,128]{1,0:T(8,128)S(1)} custom-call(s32[16]{0:T(128)S(1)} %broadcast_subtract_fusion.1.parent.refs_0_, bf16[16,64,128]{2,1,0:T(8,128)(2,1)} %coefs.1, f32[16,64,64]{2,1,0:T(8,128)S(1)} %copy-done.1, f32[8,64,64]{2,1,0:T(8,128)S(1)} %copy-done.3), custom_call_target="tpu_custom_call" | custom-call | flops 1000 | bytes 1000 | tf_op jit(solution)/shard_map/upward/pallas_call | solution.py:102
  25.5 5.8 %tables.1 = (f32[16,64,64]{2,1,0:T(8,128)S(1)}, f32[16,64,64]{2,1,0:T(8,128)S(1)}) custom-call(s32[16,1]{1,0:T(8,128)S(1)} %fusion.nodes, f32[64,64,256]{2,1,0:T(8,128)} %bitcast.11, f32[64,64,256]{2,1,0:T(8,128)} %bitcast.12), custom_call_target="tpu_custom_call" | custom-call | flops 1000 | bytes 1000 | tf_op jit(solution)/shard_map/tables/pallas_call | solution.py:132
  31.4 5.0 %collective-permute-done.refs_1_ = f32[64,128]{1,0:T(8,128)S(1)} collective-permute-done((f32[64,128]{1,0:T(8,128)S(1)}, f32[64,128]{1,0:T(8,128)S(1)}, u32[]{:S(2)}, u32[]{:S(2)}) %collective-permute-start) | collective-permute-done | bytes 32800 | tf_op jit(solution)/shard_map/ppermute | solution.py:332
  38.6 1.1 constant_dynamic-update-slice_fusion.1
  39.7 1.1 constant_dynamic-update-slice_fusion.refs_3_
  40.8 6.2 %collective-permute-start.7 = (bf16[16,256,128]{2,1,0:T(8,128)(2,1)S(1)}, bf16[16,256,128]{2,1,0:T(8,128)(2,1)S(1)}, u32[]{:S(2)}, u32[]{:S(2)}) collective-permute-start(bf16[16,256,128]{2,1,0:T(8,128)(2,1)S(1)} %constant_dynamic-update-slice_fusion.refs_3_), channel_id=1, source_target_pairs={{0,16},{16,32},{32,48},{48,64},{64,80},{80,96},{96,112},{1,17},{17... | collective-permute-start | bytes 3145736 | tf_op jit(solution)/shard_map/ppermute | solution.py:320
  47.0 1.9 %collective-permute-start.8 = (bf16[16,256,128]{2,1,0:T(8,128)(2,1)S(1)}, bf16[16,256,128]{2,1,0:T(8,128)(2,1)S(1)}, u32[]{:S(2)}, u32[]{:S(2)}) collective-permute-start(bf16[16,256,128]{2,1,0:T(8,128)(2,1)S(1)} %constant_dynamic-update-slice_fusion.refs_3_), channel_id=1, source_target_pairs={{16,0},{32,16},{48,32},{64,48},{80,64},{96,80},{112,96},{17,1},{33... | collective-permute-start | bytes 3145736 | tf_op jit(solution)/shard_map/ppermute | solution.py:320
  49.0 1.3 collective-permute-start.5
  50.3 3.2 %collective-permute-done.5.refs_1_.refs_2_ = f32[64,128]{1,0:T(8,128)S(1)} collective-permute-done((f32[64,128]{1,0:T(8,128)S(1)}, f32[64,128]{1,0:T(8,128)S(1)}, u32[]{:S(2)}, u32[]{:S(2)}) %collective-permute-start.5) | collective-permute-done | bytes 32800 | tf_op jit(solution)/shard_map/ppermute | solution.py:332
  53.9 4.8 %collective-permute-start.12 = (bf16[8,256,128]{2,1,0:T(8,128)(2,1)S(1)}, bf16[8,256,128]{2,1,0:T(8,128)(2,1)S(1)}, u32[]{:S(2)}, u32[]{:S(2)}) collective-permute-start(bf16[8,256,128]{2,1,0:T(8,128)(2,1)S(1)} %bitcast.16), channel_id=1, source_target_pairs={{0,15},{1,0},{2,1},{3,2},{4,3},{5,4},{6,5},{7,6},{8,7},{9,8},{10,9... | collective-permute-start | bytes 1572872 | tf_op jit(solution)/shard_map/ppermute | solution.py:320
  58.7 3.8 %collective-permute-done.6.refs_1_.refs_3_ = f32[64,128]{1,0:T(8,128)S(1)} collective-permute-done((f32[64,128]{1,0:T(8,128)S(1)}, f32[64,128]{1,0:T(8,128)S(1)}, u32[]{:S(2)}, u32[]{:S(2)}) %collective-permute-start.6) | collective-permute-done | bytes 32800 | tf_op jit(solution)/shard_map/ppermute | solution.py:332
  63.6 1.8 %collective-permute-start.9 = (f32[64,128]{1,0:T(8,128)S(1)}, f32[64,128]{1,0:T(8,128)S(1)}, u32[]{:S(2)}, u32[]{:S(2)}) collective-permute-start(f32[64,128]{1,0:T(8,128)S(1)} %combine.8.refs_0_), channel_id=1, source_target_pairs={{0,8},{1,9},{2,10},{3,11},{4,12},{5,13},{6,14},{7,15},{8,0},{9,1},... | collective-permute-start | bytes 98312 | tf_op jit(solution)/shard_map/ppermute | solution.py:332
  65.3 4.5 %collective-permute-done.9.refs_1_.refs_4_ = f32[64,128]{1,0:T(8,128)S(1)} collective-permute-done((f32[64,128]{1,0:T(8,128)S(1)}, f32[64,128]{1,0:T(8,128)S(1)}, u32[]{:S(2)}, u32[]{:S(2)}) %collective-permute-start.9) | collective-permute-done | bytes 32800 | tf_op jit(solution)/shard_map/ppermute | solution.py:332
  70.2 1.2 collective-permute-done.10.refs_1_.refs_5_
  72.2 8.9 %collective-permute-done.11 = bf16[8,256,128]{2,1,0:T(8,128)(2,1)S(1)} collective-permute-done((bf16[8,256,128]{2,1,0:T(8,128)(2,1)S(1)}, bf16[8,256,128]{2,1,0:T(8,128)(2,1)S(1)}, u32[]{:S(2)}, u32[]{:S(2)}) %collective-permute-start.11) | collective-permute-done | bytes 524320 | tf_op jit(solution)/shard_map/ppermute | solution.py:320
  81.2 6.2 %collective-permute-start.14 = (bf16[16,256,128]{2,1,0:T(8,128)(2,1)S(1)}, bf16[16,256,128]{2,1,0:T(8,128)(2,1)}, u32[]{:S(2)}, u32[]{:S(2)}) collective-permute-start(bf16[16,256,128]{2,1,0:T(8,128)(2,1)S(1)} %constant_dynamic-update-slice_fusion.2.refs_6_), channel_id=1, source_target_pairs={{0,16},{16,32},{32,48},{48,64},{64,80},{80,96},{96,112},{1,17},{17... | collective-permute-start | bytes 3145736 | tf_op jit(solution)/shard_map/ppermute | solution.py:320
  87.4 1.9 %collective-permute-start.15 = (bf16[16,256,128]{2,1,0:T(8,128)(2,1)S(1)}, bf16[16,256,128]{2,1,0:T(8,128)(2,1)}, u32[]{:S(2)}, u32[]{:S(2)}) collective-permute-start(bf16[16,256,128]{2,1,0:T(8,128)(2,1)S(1)} %constant_dynamic-update-slice_fusion.2.refs_6_), channel_id=1, source_target_pairs={{16,0},{32,16},{48,32},{64,48},{80,64},{96,80},{112,96},{17,1},{33... | collective-permute-start | bytes 3145736 | tf_op jit(solution)/shard_map/ppermute | solution.py:320
  89.3 1.3 collective-permute-start.13
  91.2 8.6 %collective-permute-done.13.refs_1_.refs_6_ = f32[64,128]{1,0:T(8,128)S(1)} collective-permute-done((f32[64,128]{1,0:T(8,128)S(1)}, f32[64,128]{1,0:T(8,128)S(1)}, u32[]{:S(2)}, u32[]{:S(2)}) %collective-permute-start.13) | collective-permute-done | bytes 32800 | tf_op jit(solution)/shard_map/ppermute | solution.py:332
  100.7 2.9 %collective-permute-done.15.refs_7_ = bf16[16,256,128]{2,1,0:T(8,128)(2,1)} collective-permute-done((bf16[16,256,128]{2,1,0:T(8,128)(2,1)S(1)}, bf16[16,256,128]{2,1,0:T(8,128)(2,1)}, u32[]{:S(2)}, u32[]{:S(2)}) %collective-permute-start.15) | collective-permute-done | bytes 1048608 | tf_op jit(solution)/shard_map/ppermute | solution.py:320
  103.6 2.4 %collective-permute-start.16 = (f32[64,128]{1,0:T(8,128)}, f32[64,128]{1,0:T(8,128)}, u32[]{:S(2)}, u32[]{:S(2)}) collective-permute-start(f32[64,128]{1,0:T(8,128)} %combine.11), channel_id=1, source_target_pairs={{0,64},{1,65},{2,66},{3,67},{4,68},{5,69},{6,70},{7,71},{8,72},{9,... | collective-permute-start | bytes 98312 | tf_op jit(solution)/shard_map/ppermute | solution.py:332
  106.1 5.0 %weights.1.packed = bf16[16,64,1024]{2,1,0:T(8,128)(2,1)S(1)} custom-call(s32[16]{0:T(128)S(1)} %copy-done.10, f32[16,16,64,64]{3,2,1,0:T(8,128)} %coupling.1), custom_call_target="tpu_custom_call" | custom-call | flops 1000 | bytes 1000 | tf_op jit(solution)/shard_map/weights/pallas_call | solution.py:204
  113.4 15.8 %near.1.near_part = f32[16,256,128]{2,1,0:T(8,128)S(1)} custom-call(s32[128]{0:T(128)S(1)} %reshape.68.position, bf16[16,8,256,256]{3,2,1,0:T(8,128)(2,1)} %blocks.1, bf16[16,256,128]{2,1,0:T(8,128)(2,1)} %bitcast.10, bf16[16,256,128]{2,1,0:T(8,128)(2,1)} %collective-permute-done.2.refs_1_, bf16[16,256,128]{2,1,0:T(8,128)(2,1)} %copy-done.13, ...), custom_call_target="tpu_custom_call" | custom-call | flops 1000 | bytes 1000 | tf_op jit(solution)/shard_map/near/pallas_call | solution.py:248
  129.2 1.4 copy-done
  130.6 3.1 %downward.1.on_leaf = f32[16,64,128]{2,1,0:T(8,128)S(1)} custom-call(s32[16]{0:T(128)S(1)} %broadcast_subtract_fusion.1.parent.refs_0_, f32[64,128]{1,0:T(8,128)S(1)} %collective-permute-done.refs_1_, f32[64,128]{1,0:T(8,128)S(1)} %collective-permute-done.5.refs_1_.refs_2_, f32[64,128]{1,0:T(8,128)S(1)} %collective-permute-done.6.refs_1_.refs_3_, ...), custom_call_target="tpu_custom_call" | custom-call | flops 1000 | bytes 1000 | tf_op jit(solution)/shard_map/downward/pallas_call | solution.py:178
  134.5 8.6 %final.1 = bf16[16,256,128]{2,1,0:T(8,128)(2,1)} custom-call(s32[256]{0:T(256)S(1)} %reshape.66.rows, bf16[16,64,1024]{2,1,0:T(8,128)(2,1)S(1)} %weights.1.packed, bf16[256,64,128]{2,1,0:T(8,128)(2,1)} %all-gather.2.cloned.1.call-done.coefs, f32[16,64,128]{2,1,0:T(8,128)} %copy-done.2, bf16[16,64,256]{2,1,0:T(8,128)(2,1)} %bitcast.14, f32[16,256,128]{2,1,0:T(8,128)} %copy-done), custom_call_target="tpu_custom_call" | custom-call | flops 1000 | bytes 1000 | tf_op jit(solution)/shard_map/final/pallas_call | solution.py:295
  (70 shorter events, 9.6 us)
Async XLA Ops:
  6.5 16.6 %copy-start.1 = (f32[16,64,64]{2,1,0:T(8,128)S(1)}, f32[16,64,64]{2,1,0:T(8,128)}, u32[]{:S(2)}) copy-start(f32[16,64,64]{2,1,0:T(8,128)} %refs_11_.1) | copy-start | bytes 786436
  6.5 16.6 %copy-start.3 = (f32[8,64,64]{2,1,0:T(8,128)S(1)}, f32[8,64,64]{2,1,0:T(8,128)}, u32[]{:S(2)}) copy-start(f32[8,64,64]{2,1,0:T(8,128)} %refs_10_.1) | copy-start | bytes 393220
  6.5 128.0 %all-gather.2.cloned.1.call-start = ((), (), s32[]{:S(2)}) async-start(), calls=%async_computation | async-start | bytes 4456448 | tf_op jit(solution)/shard_map/all_gather | solution.py:368
  9.1 28.5 %collective-permute-start.1 = (bf16[16,256,128]{2,1,0:T(8,128)(2,1)}, bf16[16,256,128]{2,1,0:T(8,128)(2,1)S(1)}, u32[]{:S(2)}, u32[]{:S(2)}) collective-permute-start(bf16[16,256,128]{2,1,0:T(8,128)(2,1)} %bitcast.8), channel_id=1, source_target_pairs={{0,16},{16,32},{32,48},{48,64},{64,80},{80,96},{96,112},{1,17},{17... | collective-permute-start | bytes 3145736 | tf_op jit(solution)/shard_map/ppermute | solution.py:320
  14.1 24.6 %collective-permute-start.2 = (bf16[16,256,128]{2,1,0:T(8,128)(2,1)}, bf16[16,256,128]{2,1,0:T(8,128)(2,1)}, u32[]{:S(2)}, u32[]{:S(2)}) collective-permute-start(bf16[16,256,128]{2,1,0:T(8,128)(2,1)} %bitcast.9), channel_id=1, source_target_pairs={{16,0},{32,16},{48,32},{64,48},{80,64},{96,80},{112,96},{17,1},{33... | collective-permute-start | bytes 3145736 | tf_op jit(solution)/shard_map/ppermute | solution.py:320
  18.2 18.5 %collective-permute-start.3 = (bf16[8,256,128]{2,1,0:T(8,128)(2,1)}, bf16[8,256,128]{2,1,0:T(8,128)(2,1)}, u32[]{:S(2)}, u32[]{:S(2)}) collective-permute-start(bf16[8,256,128]{2,1,0:T(8,128)(2,1)} %bitcast.4), channel_id=1, source_target_pairs={{0,1},{1,2},{2,3},{3,4},{4,5},{5,6},{6,7},{7,8},{8,9},{9,10},{10,1... | collective-permute-start | bytes 1572872 | tf_op jit(solution)/shard_map/ppermute | solution.py:320
  19.4 18.2 %collective-permute-start.4 = (bf16[8,256,128]{2,1,0:T(8,128)(2,1)}, bf16[8,256,128]{2,1,0:T(8,128)(2,1)}, u32[]{:S(2)}, u32[]{:S(2)}) collective-permute-start(bf16[8,256,128]{2,1,0:T(8,128)(2,1)} %bitcast.4), channel_id=1, source_target_pairs={{0,15},{1,0},{2,1},{3,2},{4,3},{5,4},{6,5},{7,6},{8,7},{9,8},{10,9... | collective-permute-start | bytes 1572872 | tf_op jit(solution)/shard_map/ppermute | solution.py:320
  25.5 11.0 %collective-permute-start = (f32[64,128]{1,0:T(8,128)S(1)}, f32[64,128]{1,0:T(8,128)S(1)}, u32[]{:S(2)}, u32[]{:S(2)}) collective-permute-start(f32[64,128]{1,0:T(8,128)S(1)} %upward.1.refs_0_), channel_id=1, source_target_pairs={{0,1},{1,0},{2,3},{3,2},{4,5},{5,4},{6,7},{7,6},{8,9},{9,8},{10,11... | collective-permute-start | bytes 98312 | tf_op jit(solution)/shard_map/ppermute | solution.py:332
  25.5 28.2 %copy-start.16 = (bf16[2048,128]{1,0:T(8,128)(2,1)S(1)}, bf16[2048,128]{1,0:T(8,128)(2,1)}, u32[]{:S(2)}) copy-start(bf16[2048,128]{1,0:T(8,128)(2,1)} %get-tuple-element.41) | copy-start | bytes 1572868
  31.4 74.7 %copy-start.4 = (f32[16,64,64]{2,1,0:T(8,128)}, f32[16,64,64]{2,1,0:T(8,128)S(1)}, u32[]{:S(2)}) copy-start(f32[16,64,64]{2,1,0:T(8,128)S(1)} %get-tuple-element.34.refs_9_) | copy-start | bytes 786436
  31.4 59.3 %copy-start.17 = (s32[16,16]{1,0:T(8,128)S(1)}, s32[16,16]{1,0:T(8,128)}, u32[]{:S(2)}) copy-start(s32[16,16]{1,0:T(8,128)} %param.21) | copy-start | bytes 3076
  31.4 74.7 %copy-start.18 = (s32[16,8]{0,1:T(8,128)S(1)}, s32[16,8]{0,1:T(8,128)}, u32[]{:S(2)}) copy-start(s32[16,8]{0,1:T(8,128)} %param.19) | copy-start | bytes 1540
  31.4 74.7 %copy-start.10 = (s32[16]{0:T(128)S(1)}, s32[16]{0:T(128)}, u32[]{:S(2)}) copy-start(s32[16]{0:T(128)} %count.1) | copy-start | bytes 196
  40.8 29.3 %copy-start.11 = (bf16[16,256,128]{2,1,0:T(8,128)(2,1)}, bf16[16,256,128]{2,1,0:T(8,128)(2,1)S(1)}, u32[]{:S(2)}) copy-start(bf16[16,256,128]{2,1,0:T(8,128)(2,1)S(1)} %constant_dynamic-update-slice_fusion.refs_3_) | copy-start | bytes 3145732
  40.8 22.0 %collective-permute-start.7 = (bf16[16,256,128]{2,1,0:T(8,128)(2,1)S(1)}, bf16[16,256,128]{2,1,0:T(8,128)(2,1)S(1)}, u32[]{:S(2)}, u32[]{:S(2)}) collective-permute-start(bf16[16,256,128]{2,1,0:T(8,128)(2,1)S(1)} %constant_dynamic-update-slice_fusion.refs_3_), channel_id=1, source_target_pairs={{0,16},{16,32},{32,48},{48,64},{64,80},{80,96},{96,112},{1,17},{17... | collective-permute-start | bytes 3145736 | tf_op jit(solution)/shard_map/ppermute | solution.py:320
  47.0 16.5 %collective-permute-start.8 = (bf16[16,256,128]{2,1,0:T(8,128)(2,1)S(1)}, bf16[16,256,128]{2,1,0:T(8,128)(2,1)S(1)}, u32[]{:S(2)}, u32[]{:S(2)}) collective-permute-start(bf16[16,256,128]{2,1,0:T(8,128)(2,1)S(1)} %constant_dynamic-update-slice_fusion.refs_3_), channel_id=1, source_target_pairs={{16,0},{32,16},{48,32},{64,48},{80,64},{96,80},{112,96},{17,1},{33... | collective-permute-start | bytes 3145736 | tf_op jit(solution)/shard_map/ppermute | solution.py:320
  49.0 4.5 %collective-permute-start.5 = (f32[64,128]{1,0:T(8,128)S(1)}, f32[64,128]{1,0:T(8,128)S(1)}, u32[]{:S(2)}, u32[]{:S(2)}) collective-permute-start(f32[64,128]{1,0:T(8,128)S(1)} %combine.6.refs_0_), channel_id=1, source_target_pairs={{0,2},{1,3},{2,0},{3,1},{4,6},{5,7},{6,4},{7,5},{8,10},{9,11},{10,... | collective-permute-start | bytes 98312 | tf_op jit(solution)/shard_map/ppermute | solution.py:332
  53.7 27.4 %collective-permute-start.11 = (bf16[8,256,128]{2,1,0:T(8,128)(2,1)S(1)}, bf16[8,256,128]{2,1,0:T(8,128)(2,1)S(1)}, u32[]{:S(2)}, u32[]{:S(2)}) collective-permute-start(bf16[8,256,128]{2,1,0:T(8,128)(2,1)S(1)} %bitcast.15), channel_id=1, source_target_pairs={{0,1},{1,2},{2,3},{3,4},{4,5},{5,6},{6,7},{7,8},{8,9},{9,10},{10,1... | collective-permute-start | bytes 1572872 | tf_op jit(solution)/shard_map/ppermute | solution.py:320
  53.9 27.2 %collective-permute-start.12 = (bf16[8,256,128]{2,1,0:T(8,128)(2,1)S(1)}, bf16[8,256,128]{2,1,0:T(8,128)(2,1)S(1)}, u32[]{:S(2)}, u32[]{:S(2)}) collective-permute-start(bf16[8,256,128]{2,1,0:T(8,128)(2,1)S(1)} %bitcast.16), channel_id=1, source_target_pairs={{0,15},{1,0},{2,1},{3,2},{4,3},{5,4},{6,5},{7,6},{8,7},{9,8},{10,9... | collective-permute-start | bytes 1572872 | tf_op jit(solution)/shard_map/ppermute | solution.py:320
  58.7 3.8 %collective-permute-start.6 = (f32[64,128]{1,0:T(8,128)S(1)}, f32[64,128]{1,0:T(8,128)S(1)}, u32[]{:S(2)}, u32[]{:S(2)}) collective-permute-start(f32[64,128]{1,0:T(8,128)S(1)} %combine.7.refs_0_), channel_id=1, source_target_pairs={{0,4},{1,5},{2,6},{3,7},{4,0},{5,1},{6,2},{7,3},{8,12},{9,13},{10,... | collective-permute-start | bytes 98312 | tf_op jit(solution)/shard_map/ppermute | solution.py:332
  62.8 18.3 %copy-start.14 = (bf16[16,256,128]{2,1,0:T(8,128)(2,1)}, bf16[16,256,128]{2,1,0:T(8,128)(2,1)S(1)}, u32[]{:S(2)}) copy-start(bf16[16,256,128]{2,1,0:T(8,128)(2,1)S(1)} %collective-permute-done.7.refs_5_) | copy-start | bytes 3145732
  63.6 17.5 %copy-start.15 = (bf16[16,256,128]{2,1,0:T(8,128)(2,1)}, bf16[16,256,128]{2,1,0:T(8,128)(2,1)S(1)}, u32[]{:S(2)}) copy-start(bf16[16,256,128]{2,1,0:T(8,128)(2,1)S(1)} %collective-permute-done.8.refs_4_) | copy-start | bytes 3145732
  63.6 6.3 %collective-permute-start.9 = (f32[64,128]{1,0:T(8,128)S(1)}, f32[64,128]{1,0:T(8,128)S(1)}, u32[]{:S(2)}, u32[]{:S(2)}) collective-permute-start(f32[64,128]{1,0:T(8,128)S(1)} %combine.8.refs_0_), channel_id=1, source_target_pairs={{0,8},{1,9},{2,10},{3,11},{4,12},{5,13},{6,14},{7,15},{8,0},{9,1},... | collective-permute-start | bytes 98312 | tf_op jit(solution)/shard_map/ppermute | solution.py:332
  70.1 1.3 collective-permute-start.10
  81.2 24.9 %copy-start.12 = (bf16[16,256,128]{2,1,0:T(8,128)(2,1)}, bf16[16,256,128]{2,1,0:T(8,128)(2,1)S(1)}, u32[]{:S(2)}) copy-start(bf16[16,256,128]{2,1,0:T(8,128)(2,1)S(1)} %constant_dynamic-update-slice_fusion.2.refs_6_) | copy-start | bytes 3145732
  81.2 19.5 %collective-permute-start.14 = (bf16[16,256,128]{2,1,0:T(8,128)(2,1)S(1)}, bf16[16,256,128]{2,1,0:T(8,128)(2,1)}, u32[]{:S(2)}, u32[]{:S(2)}) collective-permute-start(bf16[16,256,128]{2,1,0:T(8,128)(2,1)S(1)} %constant_dynamic-update-slice_fusion.2.refs_6_), channel_id=1, source_target_pairs={{0,16},{16,32},{32,48},{48,64},{64,80},{80,96},{96,112},{1,17},{17... | collective-permute-start | bytes 3145736 | tf_op jit(solution)/shard_map/ppermute | solution.py:320
  87.4 16.2 %collective-permute-start.15 = (bf16[16,256,128]{2,1,0:T(8,128)(2,1)S(1)}, bf16[16,256,128]{2,1,0:T(8,128)(2,1)}, u32[]{:S(2)}, u32[]{:S(2)}) collective-permute-start(bf16[16,256,128]{2,1,0:T(8,128)(2,1)S(1)} %constant_dynamic-update-slice_fusion.2.refs_6_), channel_id=1, source_target_pairs={{16,0},{32,16},{48,32},{64,48},{80,64},{96,80},{112,96},{17,1},{33... | collective-permute-start | bytes 3145736 | tf_op jit(solution)/shard_map/ppermute | solution.py:320
  89.3 10.5 %collective-permute-start.13 = (f32[64,128]{1,0:T(8,128)S(1)}, f32[64,128]{1,0:T(8,128)S(1)}, u32[]{:S(2)}, u32[]{:S(2)}) collective-permute-start(f32[64,128]{1,0:T(8,128)S(1)} %combine.10.refs_0_), channel_id=1, source_target_pairs={{0,32},{1,33},{2,34},{3,35},{4,36},{5,37},{6,38},{7,39},{8,40},{9,... | collective-permute-start | bytes 98312 | tf_op jit(solution)/shard_map/ppermute | solution.py:332
  103.6 26.9 %collective-permute-start.16 = (f32[64,128]{1,0:T(8,128)}, f32[64,128]{1,0:T(8,128)}, u32[]{:S(2)}, u32[]{:S(2)}) collective-permute-start(f32[64,128]{1,0:T(8,128)} %combine.11), channel_id=1, source_target_pairs={{0,64},{1,65},{2,66},{3,67},{4,68},{5,69},{6,70},{7,71},{8,72},{9,... | collective-permute-start | bytes 98312 | tf_op jit(solution)/shard_map/ppermute | solution.py:332
  113.4 17.2 %copy-start.5 = (f32[16,64,64]{2,1,0:T(8,128)S(1)}, f32[16,64,64]{2,1,0:T(8,128)}, u32[]{:S(2)}) copy-start(f32[16,64,64]{2,1,0:T(8,128)} %copy-done.4) | copy-start | bytes 786436
  113.4 17.2 %copy-start.7 = (f32[64,128]{1,0:T(8,128)S(1)}, f32[64,128]{1,0:T(8,128)}, u32[]{:S(2)}) copy-start(f32[64,128]{1,0:T(8,128)} %copy-done.6) | copy-start | bytes 98308
  113.4 17.2 %copy-start.9 = (f32[64,128]{1,0:T(8,128)S(1)}, f32[64,128]{1,0:T(8,128)}, u32[]{:S(2)}) copy-start(f32[64,128]{1,0:T(8,128)} %copy-done.8) | copy-start | bytes 98308
  (6 other events, 26.6 us)
Sparse Core Ops, SparseCore 0:
  9.5 72.7 all-gather.1

commit v3 on v2

--- a/solution.py
+++ b/solution.py
@@ -46,7 +46,7 @@
     return pl.CostEstimate(flops=flops, bytes_accessed=nbytes, transcendentals=0)
 
 
-def coefs_kernel(sources, bases, leaf_out, held, basis, sems):
+def coefs_kernel(sources, bases, leaf_out, exact_out, held, basis, sems):
     group = sems.shape[0]
     step = held.shape[0] // group
     copies = []
@@ -65,7 +65,9 @@
         for copy in pair:
             copy.wait()
         for leaf in range(part * step, (part + 1) * step):
-            leaf_out[leaf] = dot(basis[leaf], held[leaf]).astype(bf16)
+            coefs = dot(basis[leaf], held[leaf])
+            leaf_out[leaf] = coefs.astype(bf16)
+            exact_out[leaf] = coefs
 
 
 def leaf_coefficients(panels, bases):
@@ -73,9 +75,12 @@
     rank = bases.shape[1]
     return pl.pallas_call(
         coefs_kernel,
-        out_shape=jax.ShapeDtypeStruct((leaves, rank, rhs), bf16),
+        out_shape=(
+            jax.ShapeDtypeStruct((leaves, rank, rhs), bf16),
+            jax.ShapeDtypeStruct((leaves, rank, rhs), f32),
+        ),
         in_specs=[anywhere(), anywhere()],
-        out_specs=whole(),
+        out_specs=(whole(), whole()),
         scratch_shapes=[
             pltpu.VMEM((leaves, size, rhs), bf16),
             pltpu.VMEM((leaves, rank, size), bf16),
@@ -90,7 +95,7 @@
 def upward_kernel(parent, coefs, up, root, root_out, clusters):
     clusters[...] = jnp.zeros_like(clusters)
     for leaf in range(coefs.shape[0]):
-        clusters[parent[leaf]] += dot_t(up[leaf], coefs[leaf].astype(f32), highest)
+        clusters[parent[leaf]] += dot_t(up[leaf], coefs[leaf], highest)
     total = dot_t(root[0], clusters[0], highest)
     for cluster in range(1, root.shape[0]):
         total = total + dot_t(root[cluster], clusters[cluster], highest)
@@ -111,32 +116,41 @@
     )(local_parent, leaf_coefs, up_transfer, root_transfer)
 
 
-def tables_kernel(nodes, *refs):
-    half = len(refs) // 2
-    rank, size = refs[0].shape[1:]
+def tables_kernel(nodes, transfer, coupling, transfer_out, coupling_out, held, sems):
+    parts = sems.shape[1]
+    step = held.shape[1] // parts
+    rank, size = held.shape[2:]
     ids = lax.broadcasted_iota(jnp.int32, (nodes.shape[0], size), 1)
     chosen = (ids == nodes[...]).astype(bf16)
-    for table, out in zip(refs[:half], refs[half:]):
-        values = table[...].reshape(-1, size)
-        high = values.astype(bf16)
-        low = (values - high.astype(f32)).astype(bf16)
-        rows = dot_r(chosen, high) + dot_r(chosen, low)
-        for row in range(table.shape[0]):
-            out[:, row, :] = rows[:, row * rank : (row + 1) * rank]
+    copies = []
+    for kind, table in enumerate((transfer, coupling)):
+        for part in range(parts):
+            rows = pl.ds(part * step, step)
+            copies.append(pltpu.make_async_copy(table.at[rows], held.at[kind, rows], sems.at[kind, part]))
+    for copy in copies:
+        copy.start()
+    for kind, out in enumerate((transfer_out, coupling_out)):
+        for part in range(parts):
+            copies[kind * parts + part].wait()
+            first = part * step
+            values = held[kind, first : first + step].reshape(-1, size)
+            high = values.astype(bf16)
+            low = (values - high.astype(f32)).astype(bf16)
+            rows = dot_r(chosen, high) + dot_r(chosen, low)
+            for row in range(step):
+                out[:, first + row, :] = rows[:, row * rank : (row + 1) * rank]
 
 
 def tables(nodes, transfer, coupling):
     count = nodes.shape[0]
     size, rank, _ = transfer.shape
-    step = 16
     return pl.pallas_call(
         tables_kernel,
         out_shape=(jax.ShapeDtypeStruct((count, rank, rank), f32),) * 2,
-        grid=(rank // step,),
-        in_specs=[pl.BlockSpec((count, 1), lambda i: (0, 0))]
-        + [pl.BlockSpec((step, rank, size), lambda i: (i, 0, 0))] * 2,
-        out_specs=(pl.BlockSpec((count, step, rank), lambda i: (0, i, 0)),) * 2,
-        compiler_params=params(16, ("arbitrary",)),
+        in_specs=[whole(), anywhere(), anywhere()],
+        out_specs=(whole(),) * 2,
+        scratch_shapes=[pltpu.VMEM((2, rank, rank, size), f32), pltpu.SemaphoreType.DMA((2, 8))],
+        compiler_params=params(20),
         cost_estimate=cost(1000, 1000),
         name="tables",
     )(nodes, in_hbm(transfer.transpose(1, 2, 0)), in_hbm(coupling.transpose(1, 2, 0)))
@@ -157,6 +171,26 @@
         cost_estimate=cost(1000, 1000),
         name="combine",
     )(current, sibling, mats)
+
+
+def combine_four_kernel(picks, root, one, two, three, mats, sibling_out, out):
+    own, other, second, third, own_up, other_up = picks
+    sibling = dot_t(mats[second], two[...], highest) + dot_t(mats[third], three[...], highest)
+    sibling_out[...] = sibling
+    lower = dot_t(mats[own], root[...], highest) + dot_t(mats[other], one[...], highest)
+    out[...] = dot_t(mats[own_up], lower, highest) + dot_t(mats[other_up], sibling, highest)
+
+
+def combine_four(picks, roots, mats):
+    return pl.pallas_call(
+        lambda *refs: combine_four_kernel(picks, *refs),
+        out_shape=(jax.ShapeDtypeStruct(roots[0].shape, f32),) * 2,
+        in_specs=[whole()] * 5,
+        out_specs=(whole(),) * 2,
+        compiler_params=params(2),
+        cost_estimate=cost(1000, 1000),
+        name="combine_four",
+    )(*roots, mats)
 
 
 def downward_kernel(depth, parent, *refs):
@@ -187,30 +221,30 @@
     )(local_parent, *siblings, transfer, coupling, root_transfer, up_transfer)
 
 
-def weights_kernel(count, coupling, out):
-    group, slots, _, rank = coupling.shape
-    for one in range(group):
-        used = count[pl.program_id(0) * group + one]
+def weights_kernel(count, coupling, out, held, sems):
+    leaves, slots, _, rank = coupling.shape
+    copies = [pltpu.make_async_copy(coupling.at[leaf], held.at[leaf], sems.at[leaf]) for leaf in range(leaves)]
+    for copy in copies:
+        copy.start()
+    for leaf in range(leaves):
+        used = count[leaf]
+        copies[leaf].wait()
         for pair in range(slots // 2):
-            left = jnp.where(2 * pair < used, coupling[one, 2 * pair], 0.0)
-            right = jnp.where(2 * pair + 1 < used, coupling[one, 2 * pair + 1], 0.0)
-            both = jnp.concatenate([left, right], axis=1).astype(bf16)
-            out[one, :, 2 * pair * rank : 2 * (pair + 1) * rank] = both
+            left = jnp.where(2 * pair < used, held[leaf, 2 * pair], 0.0)
+            right = jnp.where(2 * pair + 1 < used, held[leaf, 2 * pair + 1], 0.0)
+            joined = jnp.concatenate([left, right], axis=1).astype(bf16)
+            out[leaf, :, 2 * pair * rank : 2 * (pair + 1) * rank] = joined
 
 
 def weights(far_count, far_coupling):
     leaves, slots, rank, _ = far_coupling.shape
-    group = 4
     return pl.pallas_call(
         weights_kernel,
         out_shape=jax.ShapeDtypeStruct((leaves, rank, slots * rank), bf16),
-        grid_spec=pltpu.PrefetchScalarGridSpec(
-            num_scalar_prefetch=1,
-            grid=(leaves // group,),
-            in_specs=[pl.BlockSpec((group, slots, rank, rank), lambda i, n: (i, 0, 0, 0))],
-            out_specs=pl.BlockSpec((group, rank, slots * rank), lambda i, n: (i, 0, 0)),
-        ),
-        compiler_params=params(8, ("arbitrary",)),
+        in_specs=[scalars(), anywhere()],
+        out_specs=whole(),
+        scratch_shapes=[pltpu.VMEM(far_coupling.shape, f32), pltpu.SemaphoreType.DMA((leaves,))],
+        compiler_params=params(20),
         cost_estimate=cost(1000, 1000),
         name="weights",
     )(far_count, in_hbm(far_coupling))
@@ -328,8 +362,8 @@
     return lax.optimization_barrier(arrays)
 
 
-def partner(array, axis, stride):
-    return lax.ppermute(array, axis, [(i, i ^ 1 << stride) for i in range(lax.axis_size(axis))])
+def partner(array, axis, flip):
+    return lax.ppermute(array, axis, [(i, i ^ flip) for i in range(lax.axis_size(axis))])
 
 
 def local(
@@ -359,55 +393,53 @@
     device = slab_pos * sector_count + sector_pos
     panels = sources.reshape(leaf_total, leaf_size, rhs_count)
 
-    half = leaf_total // 2
+    sides = both(panels, "sector", True)
     below, above = both(panels, "slab", False)
-    first_sides = both(panels[:half], "sector", True)
-
     local_parent = leaf_parent - device * cluster_total
-    leaf_coefs = leaf_coefficients(panels, bases)
+    leaf_coefs, exact_coefs = leaf_coefficients(panels, bases)
     slab_coefs = lax.all_gather(leaf_coefs, "sector", axis=0, tiled=True)
-    current = upward(local_parent, leaf_coefs, up_transfer, root_transfer)
-    slots = jnp.arange(2 * depth + 2, dtype=jnp.int32)
-    nodes = ((devices + device) >> (slots % depth)) ^ (slots // depth)
+    root = upward(local_parent, exact_coefs, up_transfer, root_transfer)
+    slots = jnp.arange(24, dtype=jnp.int32)
+    starts = [0, 2, 5]
+    level_of = jnp.where(slots < 2 * depth, slots % depth, (slots - 2 * depth) // 2 * 5 // 2)
+    flips = jnp.where(slots < 2 * depth, slots // depth, 2 + slots % 2)
+    nodes = ((devices + device) >> jnp.minimum(level_of, depth - 1)) ^ flips
     transfer, coupling = tables(nodes[:, None], top_transfer, top_coupling)
-
-    siblings = []
-
-    def climb(level, current):
-        siblings.append(partner(current, ("slab", "sector"), level))
-        return combine(level, depth + level, current, siblings[-1], transfer)
-
-    current = climb(0, current)
-    current, below, above, *first_sides = after(current, below, above, *first_sides)
-    first_pair = jnp.concatenate(first_sides)
-    first_far = both(first_pair, "slab", False)
-    current = climb(1, current)
-    second, current = after(panels[half:], current)
-    second_sides = both(second, "sector", True)
-    current = climb(2, current)
-    current, *first_far = after(current, *first_far)
-    current = climb(3, current)
-    current = climb(4, current)
-    current, *second_sides = after(current, *second_sides)
-    second_pair = jnp.concatenate(second_sides)
-    second_far = both(second_pair, "slab", False)
-    current = climb(5, current)
-    current, *second_far = after(current, *second_far)
-    siblings.append(partner(current, ("slab", "sector"), 6))
+    both_axes = ("slab", "sector")
+
+    def exchange(level, root):
+        return [root] + [partner(root, both_axes, flip << level) for flip in (1, 2, 3)]
+
+    def climb(level, quad):
+        extra = 2 * depth + 2 * starts.index(level)
+        picks = (level, depth + level, extra, extra + 1, level + 1, depth + level + 1)
+        return combine_four(picks, quad, transfer)
+
+    packed = weights(far_count, far_coupling)
+    root, below, above, transfer, packed = after(root, below, above, transfer, packed)
+    quad = exchange(0, root)
+    quad[0], *sides = after(quad[0], *sides)
+    pair = jnp.concatenate(sides)
+    far = both(pair, "slab", False)
+    across, current = climb(0, quad)
+    siblings = [quad[1], across]
+    quad = exchange(2, current)
+    across, current = climb(2, quad)
+    siblings += [quad[1], across]
+    siblings.append(partner(current, both_axes, 1 << 4))
+    current = combine(4, depth + 4, current, siblings[-1], transfer)
+    current, *far = after(current, *far)
+    quad = exchange(5, current)
+    across, _ = climb(5, quad)
+    siblings += [quad[1], across]
     on_leaf = downward(local_parent, siblings, transfer, coupling, root_transfer, up_transfer)
-
-    packed = weights(far_count, far_coupling)
 
     owner_device = near_list // leaf_total
     slab_offset = (owner_device // sector_count - slab_pos) % 3
     sector_offset = (owner_device % sector_count - sector_pos) % sector_count
-    leaf = near_list % leaf_total
-    place = leaf // half * (3 * leaf_total) + slab_offset * leaf_total + leaf % half
-    place = place + jnp.where(sector_offset == 1, half, 0)
-    position = jnp.where(sector_offset == 0, slab_offset * leaf_total + leaf, 3 * leaf_total + place)
-    pieces = [panels, above, below]
-    for pair, far in ((first_pair, first_far), (second_pair, second_far)):
-        pieces += [pair, far[1], far[0]]
+    side = (3 + 2 * slab_offset + jnp.where(sector_offset == 1, 1, 0)) * leaf_total
+    position = jnp.where(sector_offset == 0, slab_offset * leaf_total, side) + near_list % leaf_total
+    pieces = [panels, above, below, pair, far[1], far[0]]
     near_part = near(position.reshape(-1), near_blocks, pieces)
 
     far_rows = (far_list - slab_pos * (sector_count * leaf_total)).reshape(-1)

time: 151 us -> 131 us (0.87)
  waiting for transfers between devices: 39.8 us -> 20.9 us
  starting transfers between devices: 39.9 us -> 31.9 us
  local copies, waits for them, and re-layouts: 10.6 us -> 14.7 us
  Pallas kernels: 45.3 us -> 48.9 us
    ppermute x7 -> x10, waiting for transfers between devices: 26.3 us -> 10.4 us  [partner(): lax.ppermute(array, axis, [(i, i ^ flip) for i in range(lax.axis_size(axi...]
    ppermute x10 -> x6, starting transfers between devices: 33 us -> 19.1 us  [shifted(): return lax.ppermute(array, axis, pairs)]
    ppermute x7 -> x10, starting transfers between devices: 6.93 us -> 12.8 us  [partner(): lax.ppermute(array, axis, [(i, i ^ flip) for i in range(lax.axis_size(axi...]
    unnamed x42 -> x35, local copies, waits for them, and re-layouts: 4.92 us -> 10.1 us
    pallas_call x1 -> x4, Pallas kernels: 2.54 us -> 6.23 us  [the longest x3 3.72 us: combine_four(): pl.pallas_call(lambda *refs: combine_four_kernel(picks, *refs), out_shape...]
    ppermute x10 -> x6, waiting for transfers between devices: 13.5 us -> 10.5 us  [shifted(): return lax.ppermute(array, axis, pairs)]
    pallas_call x1, Pallas kernels: 5.82 us -> 8.39 us  [tables(): pl.pallas_call(tables_kernel, out_shape=(jax.ShapeDtypeStruct((count, ran...]
    slice x1 -> x0, local copies, waits for them, and re-layouts: 2.24 us -> none  [local(): second, current = after(panels[half:], current)]
  transfers between devices with their start and end apart: 18 -> 17, of which waited for: 10 -> 7; matrix products, arithmetic and copies ran while one was open for 5% -> 6% of each run, Pallas kernels for 23% -> 29%
where the time goes in v3:
time: 131 us
  Pallas kernels  48.9 us (37%)
  starting transfers between devices  31.9 us (24%)
  waiting for transfers between devices  20.9 us (16%)
  local copies, waits for them, and re-layouts  14.7 us (11%)
  between operations  13.6 us (10%)
    ppermute x6, starting transfers between devices, shifted(): return lax.ppermute(array, axis, pairs)  19.1 us
    pallas_call x1, Pallas kernels, near(): pl.pallas_call(near_kernel, out_shape=jax.ShapeDtypeStruct((leaves, size,...  15.9 us
    ppermute x10, starting transfers between devices, partner(): lax.ppermute(array, axis, [(i, i ^ flip) for i in range(lax.axis_size(axi...  12.8 us
    ppermute x6, waiting for transfers between devices, shifted(): return lax.ppermute(array, axis, pairs)  10.5 us
    ppermute x10, waiting for transfers between devices, partner(): lax.ppermute(array, axis, [(i, i ^ flip) for i in range(lax.axis_size(axi...  10.4 us
    unnamed x35, local copies, waits for them, and re-layouts  10.1 us
    pallas_call x1, Pallas kernels, final(): pl.pallas_call(final_kernel, out_shape=jax.ShapeDtypeStruct((leaves, size...  8.55 us
    pallas_call x1, Pallas kernels, tables(): pl.pallas_call(tables_kernel, out_shape=(jax.ShapeDtypeStruct((count, ran...  8.39 us
  transfers between devices with their start and end apart: 17, of which 7 were waited for; matrix products, arithmetic and copies ran while one was open for 6% of the time, Pallas kernels for 29%

profile of v3, /device:TPU:1, one launch (start us, length us, event | category | flops | bytes accessed | tf_op | source)
XLA Modules:
  0.0 130.7 jit_solution(7592490691686004017)
XLA Ops:
  6.5 2.5 %coefs.1 = (bf16[16,64,128]{2,1,0:T(8,128)(2,1)}, f32[16,64,128]{2,1,0:T(8,128)S(1)}) custom-call(bf16[16,256,128]{2,1,0:T(8,128)(2,1)} %bitcast.7, bf16[16,64,256]{2,1,0:T(8,128)(2,1)} %bitcast.13), custom_call_target="tpu_custom_call" | custom-call | flops 1000 | bytes 1000 | tf_op jit(solution)/shard_map/coefs/pallas_call | solution.py:76
  9.9 4.9 %collective-permute-start = (bf16[16,256,128]{2,1,0:T(8,128)(2,1)}, bf16[16,256,128]{2,1,0:T(8,128)(2,1)}, u32[]{:S(2)}, u32[]{:S(2)}) collective-permute-start(bf16[16,256,128]{2,1,0:T(8,128)(2,1)} %bitcast.8), channel_id=1, source_target_pairs={{0,16},{16,32},{32,48},{48,64},{64,80},{80,96},{96,112},{1,17},{17... | collective-permute-start | bytes 3145736 | tf_op jit(solution)/shard_map/ppermute | solution.py:354
  14.8 1.9 %collective-permute-start.1 = (bf16[16,256,128]{2,1,0:T(8,128)(2,1)}, bf16[16,256,128]{2,1,0:T(8,128)(2,1)}, u32[]{:S(2)}, u32[]{:S(2)}) collective-permute-start(bf16[16,256,128]{2,1,0:T(8,128)(2,1)} %bitcast.9), channel_id=1, source_target_pairs={{16,0},{32,16},{48,32},{64,48},{80,64},{96,80},{112,96},{17,1},{33... | collective-permute-start | bytes 3145736 | tf_op jit(solution)/shard_map/ppermute | solution.py:354
  16.8 1.3 collective-permute-start.3
  18.0 3.8 %collective-permute-start.4 = (bf16[16,256,128]{2,1,0:T(8,128)(2,1)}, bf16[16,256,128]{2,1,0:T(8,128)(2,1)}, u32[]{:S(2)}, u32[]{:S(2)}) collective-permute-start(bf16[16,256,128]{2,1,0:T(8,128)(2,1)} %bitcast.11), channel_id=1, source_target_pairs={{0,15},{1,0},{2,1},{3,2},{4,3},{5,4},{6,5},{7,6},{8,7},{9,8},{10,9... | collective-permute-start | bytes 3145736 | tf_op jit(solution)/shard_map/ppermute | solution.py:354
  22.5 4.3 %weights.1.packed = bf16[16,64,1024]{2,1,0:T(8,128)(2,1)S(1)} custom-call(s32[16]{0:T(128)S(1)} %copy-done.13, f32[16,16,64,64]{3,2,1,0:T(8,128)} %coupling.1), custom_call_target="tpu_custom_call" | custom-call | flops 1000 | bytes 1000 | tf_op jit(solution)/shard_map/weights/pallas_call | solution.py:241
  26.8 8.4 %tables.1 = (f32[24,64,64]{2,1,0:T(8,128)S(1)}, f32[24,64,64]{2,1,0:T(8,128)S(1)}) custom-call(s32[24,1]{1,0:T(8,128)S(1)} %fusion.18.nodes, f32[64,64,256]{2,1,0:T(8,128)} %bitcast.5, f32[64,64,256]{2,1,0:T(8,128)} %bitcast.6), custom_call_target="tpu_custom_call" | custom-call | flops 1000 | bytes 1000 | tf_op jit(solution)/shard_map/tables/pallas_call | solution.py:147
  36.1 0.9 copy-done.3
  37.1 1.0 copy-done.8
  38.1 1.9 %upward.1.refs_0_ = f32[64,128]{1,0:T(8,128)S(1)} custom-call(s32[16]{0:T(128)S(1)} %broadcast_subtract_fusion.1.parent.refs_0_, f32[16,64,128]{2,1,0:T(8,128)S(1)} %copy-done.8, f32[16,64,64]{2,1,0:T(8,128)S(1)} %copy-done.1, f32[8,64,64]{2,1,0:T(8,128)S(1)} %copy-done.3), custom_call_target="tpu_custom_call" | custom-call | flops 1000 | bytes 1000 | tf_op jit(solution)/shard_map/upward/pallas_call | solution.py:107
  40.0 8.6 %collective-permute-done.3 = bf16[16,256,128]{2,1,0:T(8,128)(2,1)} collective-permute-done((bf16[16,256,128]{2,1,0:T(8,128)(2,1)}, bf16[16,256,128]{2,1,0:T(8,128)(2,1)}, u32[]{:S(2)}, u32[]{:S(2)}) %collective-permute-start.3) | collective-permute-done | bytes 1048608 | tf_op jit(solution)/shard_map/ppermute | solution.py:354
  48.6 2.3 %constant_dynamic-update-slice_fusion.1 = bf16[32,256,128]{2,1,0:T(8,128)(2,1)} fusion(bf16[16,256,128]{2,1,0:T(8,128)(2,1)} %collective-permute-done.3), kind=kLoop, calls=%fused_computation.46 | loop fusion | bytes 2097152
  50.9 2.3 %constant_dynamic-update-slice_fusion.refs_3_ = bf16[32,256,128]{2,1,0:T(8,128)(2,1)} fusion(bf16[32,256,128]{2,1,0:T(8,128)(2,1)} %constant_dynamic-update-slice_fusion.1, bf16[16,256,128]{2,1,0:T(8,128)(2,1)} %collective-permute-done.4), kind=kLoop, calls=%fused_computation.45 | loop fusion | bytes 2097152 | tf_op jit(solution)/shard_map/concatenate | solution.py:422
  53.2 5.2 %collective-permute-start.11 = (bf16[32,256,128]{2,1,0:T(8,128)(2,1)}, bf16[32,256,128]{2,1,0:T(8,128)(2,1)}, u32[]{:S(2)}, u32[]{:S(2)}) collective-permute-start(bf16[32,256,128]{2,1,0:T(8,128)(2,1)} %constant_dynamic-update-slice_fusion.refs_3_), channel_id=1, source_target_pairs={{0,16},{16,32},{32,48},{48,64},{64,80},{80,96},{96,112},{1,17},{17... | collective-permute-start | bytes 6291464 | tf_op jit(solution)/shard_map/ppermute | solution.py:354
  58.5 1.9 %collective-permute-start.12 = (bf16[32,256,128]{2,1,0:T(8,128)(2,1)}, bf16[32,256,128]{2,1,0:T(8,128)(2,1)}, u32[]{:S(2)}, u32[]{:S(2)}) collective-permute-start(bf16[32,256,128]{2,1,0:T(8,128)(2,1)} %constant_dynamic-update-slice_fusion.refs_3_), channel_id=1, source_target_pairs={{16,0},{32,16},{48,32},{64,48},{80,64},{96,80},{112,96},{17,1},{33... | collective-permute-start | bytes 6291464 | tf_op jit(solution)/shard_map/ppermute | solution.py:354
  60.5 3.6 %collective-permute-start.5 = (f32[64,128]{1,0:T(8,128)S(1)}, f32[64,128]{1,0:T(8,128)S(1)}, u32[]{:S(2)}, u32[]{:S(2)}) collective-permute-start(f32[64,128]{1,0:T(8,128)S(1)} %upward.1.refs_0_), channel_id=1, source_target_pairs={{0,2},{1,3},{2,0},{3,1},{4,6},{5,7},{6,4},{7,5},{8,10},{9,11},{10,... | collective-permute-start | bytes 98312 | tf_op jit(solution)/shard_map/ppermute | solution.py:366
  64.4 3.0 %collective-permute-done.5.refs_2_ = f32[64,128]{1,0:T(8,128)S(1)} collective-permute-done((f32[64,128]{1,0:T(8,128)S(1)}, f32[64,128]{1,0:T(8,128)S(1)}, u32[]{:S(2)}, u32[]{:S(2)}) %collective-permute-start.5) | collective-permute-done | bytes 32800 | tf_op jit(solution)/shard_map/ppermute | solution.py:366
  67.4 1.9 %collective-permute-done.6.refs_3_ = f32[64,128]{1,0:T(8,128)S(1)} collective-permute-done((f32[64,128]{1,0:T(8,128)S(1)}, f32[64,128]{1,0:T(8,128)S(1)}, u32[]{:S(2)}, u32[]{:S(2)}) %collective-permute-start.6) | collective-permute-done | bytes 32800 | tf_op jit(solution)/shard_map/ppermute | solution.py:366
  70.5 1.3 collective-permute-start.7
  71.8 2.6 %collective-permute-start.8 = (f32[64,128]{1,0:T(8,128)S(1)}, f32[64,128]{1,0:T(8,128)S(1)}, u32[]{:S(2)}, u32[]{:S(2)}) collective-permute-start(f32[64,128]{1,0:T(8,128)S(1)} %get-tuple-element.33.refs_0_), channel_id=1, source_target_pairs={{0,8},{1,9},{2,10},{3,11},{4,12},{5,13},{6,14},{7,15},{8,0},{9,1},... | collective-permute-start | bytes 98312 | tf_op jit(solution)/shard_map/ppermute | solution.py:366
  74.4 3.8 %collective-permute-done.8.refs_2_ = f32[64,128]{1,0:T(8,128)S(1)} collective-permute-done((f32[64,128]{1,0:T(8,128)S(1)}, f32[64,128]{1,0:T(8,128)S(1)}, u32[]{:S(2)}, u32[]{:S(2)}) %collective-permute-start.8) | collective-permute-done | bytes 32800 | tf_op jit(solution)/shard_map/ppermute | solution.py:366
  78.2 1.3 collective-permute-done.9.refs_3_
  79.5 1.3 combine_four.4
  81.4 1.1 collective-permute-start.10
  84.2 1.9 %collective-permute-done.12.refs_4_ = bf16[32,256,128]{2,1,0:T(8,128)(2,1)} collective-permute-done((bf16[32,256,128]{2,1,0:T(8,128)(2,1)}, bf16[32,256,128]{2,1,0:T(8,128)(2,1)}, u32[]{:S(2)}, u32[]{:S(2)}) %collective-permute-start.12) | collective-permute-done | bytes 2097184 | tf_op jit(solution)/shard_map/ppermute | solution.py:354
  86.2 1.4 %collective-permute-start.13 = (f32[64,128]{1,0:T(8,128)}, f32[64,128]{1,0:T(8,128)S(1)}, u32[]{:S(2)}, u32[]{:S(2)}) collective-permute-start(f32[64,128]{1,0:T(8,128)} %combine.1.refs_0_), channel_id=1, source_target_pairs={{0,32},{1,33},{2,34},{3,35},{4,36},{5,37},{6,38},{7,39},{8,40},{9,... | collective-permute-start | bytes 98312 | tf_op jit(solution)/shard_map/ppermute | solution.py:366
  87.5 1.9 %collective-permute-start.14 = (f32[64,128]{1,0:T(8,128)}, f32[64,128]{1,0:T(8,128)}, u32[]{:S(2)}, u32[]{:S(2)}) collective-permute-start(f32[64,128]{1,0:T(8,128)} %combine.1.refs_0_), channel_id=1, source_target_pairs={{0,64},{1,65},{2,66},{3,67},{4,68},{5,69},{6,70},{7,71},{8,72},{9,... | collective-permute-start | bytes 98312 | tf_op jit(solution)/shard_map/ppermute | solution.py:366
  92.3 15.9 %near.1.near_part = f32[16,256,128]{2,1,0:T(8,128)S(1)} custom-call(s32[128]{0:T(128)S(1)} %reshape.204.position, bf16[16,8,256,256]{3,2,1,0:T(8,128)(2,1)} %blocks.1, bf16[16,256,128]{2,1,0:T(8,128)(2,1)} %bitcast.12, bf16[16,256,128]{2,1,0:T(8,128)(2,1)} %collective-permute-done.1.refs_1_, bf16[16,256,128]{2,1,0:T(8,128)(2,1)} %collective-permute-done.refs_2_, ...), custom_call_target="tpu_custom_call" | custom-call | flops 1000 | bytes 1000 | tf_op jit(solution)/shard_map/near/pallas_call | solution.py:282
  108.2 1.4 %copy-done = f32[16,256,128]{2,1,0:T(8,128)} copy-done((f32[16,256,128]{2,1,0:T(8,128)}, f32[16,256,128]{2,1,0:T(8,128)S(1)}, u32[]{:S(2)}) %copy-start) | copy-done | bytes 2097176
  109.6 1.9 %combine_four.5 = (f32[64,128]{1,0:T(8,128)S(1)}, f32[64,128]{1,0:T(8,128)}) custom-call(f32[64,128]{1,0:T(8,128)} %combine.1.refs_0_, f32[64,128]{1,0:T(8,128)S(1)} %collective-permute-done.13.refs_1_.refs_6_, f32[64,128]{1,0:T(8,128)} %collective-permute-done.14.refs_2_, f32[64,128]{1,0:T(8,128)} %collective-permute-done.15.refs_3_, ...), custom_call_target="tpu_custom_call" | custom-call | flops 1000 | bytes 1000 | tf_op jit(solution)/shard_map/combine_four/pallas_call | solution.py:185
  111.5 2.9 %downward.1.on_leaf = f32[16,64,128]{2,1,0:T(8,128)S(1)} custom-call(s32[16]{0:T(128)S(1)} %broadcast_subtract_fusion.1.parent.refs_0_, f32[64,128]{1,0:T(8,128)S(1)} %collective-permute-done.2.refs_1_, f32[64,128]{1,0:T(8,128)S(1)} %copy-done.10, f32[64,128]{1,0:T(8,128)S(1)} %collective-permute-done.7.refs_1_.refs_3_, f32[64,128]{1,0:T(8,128)S(1)} %copy-done.12, ...), custom_call_target="tpu_custom_call" | custom-call | flops 1000 | bytes 1000 | tf_op jit(solution)/shard_map/downward/pallas_call | solution.py:212
  115.3 8.6 %final.1 = bf16[16,256,128]{2,1,0:T(8,128)(2,1)} custom-call(s32[256]{0:T(256)S(1)} %reshape.202.rows, bf16[16,64,1024]{2,1,0:T(8,128)(2,1)S(1)} %weights.1.packed, bf16[256,64,128]{2,1,0:T(8,128)(2,1)} %all-gather.2.cloned.1.call-done.coefs, f32[16,64,128]{2,1,0:T(8,128)} %copy-done.2, bf16[16,64,256]{2,1,0:T(8,128)(2,1)} %bitcast.14, f32[16,256,128]{2,1,0:T(8,128)} %copy-done), custom_call_target="tpu_custom_call" | custom-call | flops 1000 | bytes 1000 | tf_op jit(solution)/shard_map/final/pallas_call | solution.py:329
  (57 shorter events, 10.0 us)
Async XLA Ops:
  6.5 108.7 %all-gather.2.cloned.1.call-start = ((), (), s32[]{:S(2)}) async-start(), calls=%async_computation | async-start | bytes 4456448 | tf_op jit(solution)/shard_map/all_gather | solution.py:400
  9.1 0.8 copy-start.7
  9.9 30.1 %collective-permute-start = (bf16[16,256,128]{2,1,0:T(8,128)(2,1)}, bf16[16,256,128]{2,1,0:T(8,128)(2,1)}, u32[]{:S(2)}, u32[]{:S(2)}) collective-permute-start(bf16[16,256,128]{2,1,0:T(8,128)(2,1)} %bitcast.8), channel_id=1, source_target_pairs={{0,16},{16,32},{32,48},{48,64},{64,80},{80,96},{96,112},{1,17},{17... | collective-permute-start | bytes 3145736 | tf_op jit(solution)/shard_map/ppermute | solution.py:354
  14.8 25.2 %collective-permute-start.1 = (bf16[16,256,128]{2,1,0:T(8,128)(2,1)}, bf16[16,256,128]{2,1,0:T(8,128)(2,1)}, u32[]{:S(2)}, u32[]{:S(2)}) collective-permute-start(bf16[16,256,128]{2,1,0:T(8,128)(2,1)} %bitcast.9), channel_id=1, source_target_pairs={{16,0},{32,16},{48,32},{64,48},{80,64},{96,80},{112,96},{17,1},{33... | collective-permute-start | bytes 3145736 | tf_op jit(solution)/shard_map/ppermute | solution.py:354
  16.8 31.8 %collective-permute-start.3 = (bf16[16,256,128]{2,1,0:T(8,128)(2,1)}, bf16[16,256,128]{2,1,0:T(8,128)(2,1)}, u32[]{:S(2)}, u32[]{:S(2)}) collective-permute-start(bf16[16,256,128]{2,1,0:T(8,128)(2,1)} %bitcast.10), channel_id=1, source_target_pairs={{0,1},{1,2},{2,3},{3,4},{4,5},{5,6},{6,7},{7,8},{8,9},{9,10},{10,1... | collective-permute-start | bytes 3145736 | tf_op jit(solution)/shard_map/ppermute | solution.py:354
  18.0 30.5 %collective-permute-start.4 = (bf16[16,256,128]{2,1,0:T(8,128)(2,1)}, bf16[16,256,128]{2,1,0:T(8,128)(2,1)}, u32[]{:S(2)}, u32[]{:S(2)}) collective-permute-start(bf16[16,256,128]{2,1,0:T(8,128)(2,1)} %bitcast.11), channel_id=1, source_target_pairs={{0,15},{1,0},{2,1},{3,2},{4,3},{5,4},{6,5},{7,6},{8,7},{9,8},{10,9... | collective-permute-start | bytes 3145736 | tf_op jit(solution)/shard_map/ppermute | solution.py:354
  21.8 0.7 copy-start.13
  26.8 9.3 %copy-start.16 = (s32[16]{0:T(128)S(1)}, s32[16]{0:T(128)}, u32[]{:S(2)}) copy-start(s32[16]{0:T(128)} %param.14) | copy-start | bytes 196
  26.8 9.3 %copy-start.1 = (f32[16,64,64]{2,1,0:T(8,128)S(1)}, f32[16,64,64]{2,1,0:T(8,128)}, u32[]{:S(2)}) copy-start(f32[16,64,64]{2,1,0:T(8,128)} %refs_11_.1) | copy-start | bytes 786436
  35.2 0.9 copy-start.5
  36.1 1.0 copy-start.3
  37.1 1.0 copy-start.8
  50.9 31.6 %copy-start.14 = (s32[16,16]{1,0:T(8,128)S(1)}, s32[16,16]{1,0:T(8,128)}, u32[]{:S(2)}) copy-start(s32[16,16]{1,0:T(8,128)} %param.21) | copy-start | bytes 3076
  50.9 39.1 %copy-start.15 = (s32[16,8]{0,1:T(8,128)S(1)}, s32[16,8]{0,1:T(8,128)}, u32[]{:S(2)}) copy-start(s32[16,8]{0,1:T(8,128)} %param.19) | copy-start | bytes 1540
  53.2 31.0 %collective-permute-start.11 = (bf16[32,256,128]{2,1,0:T(8,128)(2,1)}, bf16[32,256,128]{2,1,0:T(8,128)(2,1)}, u32[]{:S(2)}, u32[]{:S(2)}) collective-permute-start(bf16[32,256,128]{2,1,0:T(8,128)(2,1)} %constant_dynamic-update-slice_fusion.refs_3_), channel_id=1, source_target_pairs={{0,16},{16,32},{32,48},{48,64},{64,80},{80,96},{96,112},{1,17},{17... | collective-permute-start | bytes 6291464 | tf_op jit(solution)/shard_map/ppermute | solution.py:354
  58.5 27.7 %collective-permute-start.12 = (bf16[32,256,128]{2,1,0:T(8,128)(2,1)}, bf16[32,256,128]{2,1,0:T(8,128)(2,1)}, u32[]{:S(2)}, u32[]{:S(2)}) collective-permute-start(bf16[32,256,128]{2,1,0:T(8,128)(2,1)} %constant_dynamic-update-slice_fusion.refs_3_), channel_id=1, source_target_pairs={{16,0},{32,16},{48,32},{64,48},{80,64},{96,80},{112,96},{17,1},{33... | collective-permute-start | bytes 6291464 | tf_op jit(solution)/shard_map/ppermute | solution.py:354
  60.4 3.9 %collective-permute-start.2 = (f32[64,128]{1,0:T(8,128)S(1)}, f32[64,128]{1,0:T(8,128)S(1)}, u32[]{:S(2)}, u32[]{:S(2)}) collective-permute-start(f32[64,128]{1,0:T(8,128)S(1)} %upward.1.refs_0_), channel_id=1, source_target_pairs={{0,1},{1,0},{2,3},{3,2},{4,5},{5,4},{6,7},{7,6},{8,9},{9,8},{10,11... | collective-permute-start | bytes 98312 | tf_op jit(solution)/shard_map/ppermute | solution.py:366
  60.5 6.8 %collective-permute-start.5 = (f32[64,128]{1,0:T(8,128)S(1)}, f32[64,128]{1,0:T(8,128)S(1)}, u32[]{:S(2)}, u32[]{:S(2)}) collective-permute-start(f32[64,128]{1,0:T(8,128)S(1)} %upward.1.refs_0_), channel_id=1, source_target_pairs={{0,2},{1,3},{2,0},{3,1},{4,6},{5,7},{6,4},{7,5},{8,10},{9,11},{10,... | collective-permute-start | bytes 98312 | tf_op jit(solution)/shard_map/ppermute | solution.py:366
  64.1 5.2 %collective-permute-start.6 = (f32[64,128]{1,0:T(8,128)S(1)}, f32[64,128]{1,0:T(8,128)S(1)}, u32[]{:S(2)}, u32[]{:S(2)}) collective-permute-start(f32[64,128]{1,0:T(8,128)S(1)} %upward.1.refs_0_), channel_id=1, source_target_pairs={{0,3},{1,2},{2,1},{3,0},{4,7},{5,6},{6,5},{7,4},{8,11},{9,10},{10,... | collective-permute-start | bytes 98312 | tf_op jit(solution)/shard_map/ppermute | solution.py:366
  70.5 4.0 %collective-permute-start.7 = (f32[64,128]{1,0:T(8,128)S(1)}, f32[64,128]{1,0:T(8,128)S(1)}, u32[]{:S(2)}, u32[]{:S(2)}) collective-permute-start(f32[64,128]{1,0:T(8,128)S(1)} %get-tuple-element.33.refs_0_), channel_id=1, source_target_pairs={{0,4},{1,5},{2,6},{3,7},{4,0},{5,1},{6,2},{7,3},{8,12},{9,13},{10,... | collective-permute-start | bytes 98312 | tf_op jit(solution)/shard_map/ppermute | solution.py:366
  71.8 6.5 %collective-permute-start.8 = (f32[64,128]{1,0:T(8,128)S(1)}, f32[64,128]{1,0:T(8,128)S(1)}, u32[]{:S(2)}, u32[]{:S(2)}) collective-permute-start(f32[64,128]{1,0:T(8,128)S(1)} %get-tuple-element.33.refs_0_), channel_id=1, source_target_pairs={{0,8},{1,9},{2,10},{3,11},{4,12},{5,13},{6,14},{7,15},{8,0},{9,1},... | collective-permute-start | bytes 98312 | tf_op jit(solution)/shard_map/ppermute | solution.py:366
  74.4 5.2 %collective-permute-start.9 = (f32[64,128]{1,0:T(8,128)S(1)}, f32[64,128]{1,0:T(8,128)}, u32[]{:S(2)}, u32[]{:S(2)}) collective-permute-start(f32[64,128]{1,0:T(8,128)S(1)} %get-tuple-element.33.refs_0_), channel_id=1, source_target_pairs={{0,12},{1,13},{2,14},{3,15},{4,8},{5,9},{6,10},{7,11},{8,4},{9,5},... | collective-permute-start | bytes 98312 | tf_op jit(solution)/shard_map/ppermute | solution.py:366
  81.4 1.9 %collective-permute-start.10 = (f32[64,128]{1,0:T(8,128)S(1)}, f32[64,128]{1,0:T(8,128)S(1)}, u32[]{:S(2)}, u32[]{:S(2)}) collective-permute-start(f32[64,128]{1,0:T(8,128)S(1)} %get-tuple-element.35.refs_0_), channel_id=1, source_target_pairs={{0,16},{1,17},{2,18},{3,19},{4,20},{5,21},{6,22},{7,23},{8,24},{9,... | collective-permute-start | bytes 98312 | tf_op jit(solution)/shard_map/ppermute | solution.py:366
  86.2 23.4 %collective-permute-start.13 = (f32[64,128]{1,0:T(8,128)}, f32[64,128]{1,0:T(8,128)S(1)}, u32[]{:S(2)}, u32[]{:S(2)}) collective-permute-start(f32[64,128]{1,0:T(8,128)} %combine.1.refs_0_), channel_id=1, source_target_pairs={{0,32},{1,33},{2,34},{3,35},{4,36},{5,37},{6,38},{7,39},{8,40},{9,... | collective-permute-start | bytes 98312 | tf_op jit(solution)/shard_map/ppermute | solution.py:366
  87.5 22.1 %collective-permute-start.14 = (f32[64,128]{1,0:T(8,128)}, f32[64,128]{1,0:T(8,128)}, u32[]{:S(2)}, u32[]{:S(2)}) collective-permute-start(f32[64,128]{1,0:T(8,128)} %combine.1.refs_0_), channel_id=1, source_target_pairs={{0,64},{1,65},{2,66},{3,67},{4,68},{5,69},{6,70},{7,71},{8,72},{9,... | collective-permute-start | bytes 98312 | tf_op jit(solution)/shard_map/ppermute | solution.py:366
  89.5 20.1 %collective-permute-start.15 = (f32[64,128]{1,0:T(8,128)}, f32[64,128]{1,0:T(8,128)}, u32[]{:S(2)}, u32[]{:S(2)}) collective-permute-start(f32[64,128]{1,0:T(8,128)} %combine.1.refs_0_), channel_id=1, source_target_pairs={{0,96},{1,97},{2,98},{3,99},{4,100},{5,101},{6,102},{7,103},{8,104... | collective-permute-start | bytes 98312 | tf_op jit(solution)/shard_map/ppermute | solution.py:366
  92.3 19.2 %copy-start.4 = (f32[8,64,64]{2,1,0:T(8,128)S(1)}, f32[8,64,64]{2,1,0:T(8,128)}, u32[]{:S(2)}) copy-start(f32[8,64,64]{2,1,0:T(8,128)} %refs_10_.1) | copy-start | bytes 393220
  92.3 19.2 %copy-start.6 = (f32[24,64,64]{2,1,0:T(8,128)S(1)}, f32[24,64,64]{2,1,0:T(8,128)}, u32[]{:S(2)}) copy-start(f32[24,64,64]{2,1,0:T(8,128)} %copy-done.5) | copy-start | bytes 1179652
  92.3 19.2 %copy-start.10 = (f32[64,128]{1,0:T(8,128)S(1)}, f32[64,128]{1,0:T(8,128)}, u32[]{:S(2)}) copy-start(f32[64,128]{1,0:T(8,128)} %copy-done.9) | copy-start | bytes 98308
  92.3 19.2 %copy-start.12 = (f32[64,128]{1,0:T(8,128)S(1)}, f32[64,128]{1,0:T(8,128)}, u32[]{:S(2)}) copy-start(f32[64,128]{1,0:T(8,128)} %copy-done.11) | copy-start | bytes 98308
  108.2 1.4 %copy-start = (f32[16,256,128]{2,1,0:T(8,128)}, f32[16,256,128]{2,1,0:T(8,128)S(1)}, u32[]{:S(2)}) copy-start(f32[16,256,128]{2,1,0:T(8,128)S(1)} %near.1.near_part) | copy-start | bytes 6291460
  114.5 0.8 copy-start.2
  (2 other events, 1.3 us)
Sparse Core Ops, SparseCore 0:
  10.0 71.4 all-gather.1

commit v4 on v3

--- a/solution.py
+++ b/solution.py
@@ -46,74 +46,62 @@
     return pl.CostEstimate(flops=flops, bytes_accessed=nbytes, transcendentals=0)
 
 
-def coefs_kernel(sources, bases, leaf_out, exact_out, held, basis, sems):
+def coefs_kernel(parent, sources, bases, up, root, leaf_out, root_out, held, basis, up_held, root_held, clusters, sems, tail_sems):
     group = sems.shape[0]
     step = held.shape[0] // group
     copies = []
     for part in range(group):
         rows = pl.ds(part * step, step)
-        copies.append(
-            (
-                pltpu.make_async_copy(sources.at[rows], held.at[rows], sems.at[part, 0]),
-                pltpu.make_async_copy(bases.at[rows], basis.at[rows], sems.at[part, 1]),
-            )
-        )
-    for pair in copies:
-        for copy in pair:
-            copy.start()
-    for part, pair in enumerate(copies):
-        for copy in pair:
-            copy.wait()
+        copies.append(pltpu.make_async_copy(sources.at[rows], held.at[rows], sems.at[part, 0]))
+        copies.append(pltpu.make_async_copy(bases.at[rows], basis.at[rows], sems.at[part, 1]))
+    tails = [
+        pltpu.make_async_copy(up, up_held, tail_sems.at[0]),
+        pltpu.make_async_copy(root, root_held, tail_sems.at[1]),
+    ]
+    for copy in copies + tails:
+        copy.start()
+    clusters[...] = jnp.zeros_like(clusters)
+    exact = []
+    for part in range(group):
+        copies[2 * part].wait()
+        copies[2 * part + 1].wait()
         for leaf in range(part * step, (part + 1) * step):
-            coefs = dot(basis[leaf], held[leaf])
-            leaf_out[leaf] = coefs.astype(bf16)
-            exact_out[leaf] = coefs
-
-
-def leaf_coefficients(panels, bases):
+            exact.append(dot(basis[leaf], held[leaf]))
+            leaf_out[leaf] = exact[leaf].astype(bf16)
+    for tail in tails:
+        tail.wait()
+    for leaf, coefs in enumerate(exact):
+        clusters[parent[leaf]] += dot_t(up_held[leaf], coefs, highest)
+    total = dot_t(root_held[0], clusters[0], highest)
+    for cluster in range(1, root_held.shape[0]):
+        total = total + dot_t(root_held[cluster], clusters[cluster], highest)
+    root_out[...] = total
+
+
+def leaf_coefficients(local_parent, panels, bases, up_transfer, root_transfer):
     leaves, size, rhs = panels.shape
     rank = bases.shape[1]
     return pl.pallas_call(
         coefs_kernel,
         out_shape=(
             jax.ShapeDtypeStruct((leaves, rank, rhs), bf16),
-            jax.ShapeDtypeStruct((leaves, rank, rhs), f32),
+            jax.ShapeDtypeStruct((rank, rhs), f32),
         ),
-        in_specs=[anywhere(), anywhere()],
+        in_specs=[scalars()] + [anywhere()] * 4,
         out_specs=(whole(), whole()),
         scratch_shapes=[
             pltpu.VMEM((leaves, size, rhs), bf16),
             pltpu.VMEM((leaves, rank, size), bf16),
+            pltpu.VMEM(up_transfer.shape, f32),
+            pltpu.VMEM(root_transfer.shape, f32),
+            pltpu.VMEM((root_transfer.shape[0], rank, rhs), f32),
             pltpu.SemaphoreType.DMA((4, 2)),
+            pltpu.SemaphoreType.DMA((2,)),
         ],
-        compiler_params=params(8),
+        compiler_params=params(12),
         cost_estimate=cost(1000, 1000),
         name="coefs",
-    )(in_hbm(panels), in_hbm(bases))
-
-
-def upward_kernel(parent, coefs, up, root, root_out, clusters):
-    clusters[...] = jnp.zeros_like(clusters)
-    for leaf in range(coefs.shape[0]):
-        clusters[parent[leaf]] += dot_t(up[leaf], coefs[leaf], highest)
-    total = dot_t(root[0], clusters[0], highest)
-    for cluster in range(1, root.shape[0]):
-        total = total + dot_t(root[cluster], clusters[cluster], highest)
-    root_out[...] = total
-
-
-def upward(local_parent, leaf_coefs, up_transfer, root_transfer):
-    leaves, rank, rhs = leaf_coefs.shape
-    return pl.pallas_call(
-        upward_kernel,
-        out_shape=jax.ShapeDtypeStruct((rank, rhs), f32),
-        in_specs=[scalars(), whole(), whole(), whole()],
-        out_specs=whole(),
-        scratch_shapes=[pltpu.VMEM((root_transfer.shape[0], rank, rhs), f32)],
-        compiler_params=params(8),
-        cost_estimate=cost(1000, 1000),
-        name="upward",
-    )(local_parent, leaf_coefs, up_transfer, root_transfer)
+    )(local_parent, *[in_hbm(array) for array in (panels, bases, up_transfer, root_transfer)])
 
 
 def tables_kernel(nodes, transfer, coupling, transfer_out, coupling_out, held, sems):
@@ -263,12 +251,12 @@
     fetches = [
         pltpu.make_async_copy(blocks.at[leaf], matrices.at[leaf], block_sems.at[leaf]) for leaf in range(leaves)
     ]
-    for copy in copies:
+    for copy in copies + fetches[:1]:
         copy.start()
-    for fetch in fetches:
-        fetch.start()
     for copy in copies:
         copy.wait()
+    for fetch in fetches[1:]:
+        fetch.start()
     for leaf in range(leaves):
         fetches[leaf].wait()
         wide = jnp.concatenate([matrices[leaf, slot] for slot in range(slots)], axis=1)
@@ -293,7 +281,7 @@
         compiler_params=params(36),
         cost_estimate=cost(1000, 1000),
         name="near",
-    )(position, in_hbm(near_blocks), *[in_hbm(piece) for piece in pieces])
+    )(position, in_hbm(near_blocks), *pieces)
 
 
 def final_kernel(rows, packed, coefs, on_leaf, bases, near_part, out, *scratch):
@@ -305,10 +293,12 @@
         for index, (source, target) in enumerate(((coefs, held), (on_leaf, term), (bases, basis)))
     ]
     nears = [pltpu.make_async_copy(near_part.at[leaf], close.at[leaf], near_sems.at[leaf]) for leaf in range(leaves)]
-    for load in loads + nears:
+    for load in loads:
         load.start()
     for load in loads:
         load.wait()
+    for load in nears:
+        load.start()
     stores = []
     for leaf in range(leaves):
         for slot in range(slots):
@@ -393,56 +383,47 @@
     device = slab_pos * sector_count + sector_pos
     panels = sources.reshape(leaf_total, leaf_size, rhs_count)
 
-    sides = both(panels, "sector", True)
-    below, above = both(panels, "slab", False)
     local_parent = leaf_parent - device * cluster_total
-    leaf_coefs, exact_coefs = leaf_coefficients(panels, bases)
+    leaf_coefs, root = leaf_coefficients(local_parent, panels, bases, up_transfer, root_transfer)
     slab_coefs = lax.all_gather(leaf_coefs, "sector", axis=0, tiled=True)
-    root = upward(local_parent, exact_coefs, up_transfer, root_transfer)
-    slots = jnp.arange(24, dtype=jnp.int32)
-    starts = [0, 2, 5]
-    level_of = jnp.where(slots < 2 * depth, slots % depth, (slots - 2 * depth) // 2 * 5 // 2)
-    flips = jnp.where(slots < 2 * depth, slots // depth, 2 + slots % 2)
-    nodes = ((devices + device) >> jnp.minimum(level_of, depth - 1)) ^ flips
-    transfer, coupling = tables(nodes[:, None], top_transfer, top_coupling)
-    both_axes = ("slab", "sector")
-
-    def exchange(level, root):
-        return [root] + [partner(root, both_axes, flip << level) for flip in (1, 2, 3)]
-
-    def climb(level, quad):
-        extra = 2 * depth + 2 * starts.index(level)
-        picks = (level, depth + level, extra, extra + 1, level + 1, depth + level + 1)
-        return combine_four(picks, quad, transfer)
-
-    packed = weights(far_count, far_coupling)
-    root, below, above, transfer, packed = after(root, below, above, transfer, packed)
-    quad = exchange(0, root)
-    quad[0], *sides = after(quad[0], *sides)
-    pair = jnp.concatenate(sides)
-    far = both(pair, "slab", False)
-    across, current = climb(0, quad)
-    siblings = [quad[1], across]
-    quad = exchange(2, current)
-    across, current = climb(2, quad)
-    siblings += [quad[1], across]
-    siblings.append(partner(current, both_axes, 1 << 4))
-    current = combine(4, depth + 4, current, siblings[-1], transfer)
-    current, *far = after(current, *far)
-    quad = exchange(5, current)
-    across, _ = climb(5, quad)
-    siblings += [quad[1], across]
-    on_leaf = downward(local_parent, siblings, transfer, coupling, root_transfer, up_transfer)
 
     owner_device = near_list // leaf_total
     slab_offset = (owner_device // sector_count - slab_pos) % 3
     sector_offset = (owner_device % sector_count - sector_pos) % sector_count
-    side = (3 + 2 * slab_offset + jnp.where(sector_offset == 1, 1, 0)) * leaf_total
-    position = jnp.where(sector_offset == 0, slab_offset * leaf_total, side) + near_list % leaf_total
-    pieces = [panels, above, below, pair, far[1], far[0]]
-    near_part = near(position.reshape(-1), near_blocks, pieces)
-
+    row = jnp.where(sector_offset == 0, 0, jnp.where(sector_offset == 1, 6, 3)) + slab_offset
+    position = (row * leaf_total + near_list % leaf_total).reshape(-1)
     far_rows = (far_list - slab_pos * (sector_count * leaf_total)).reshape(-1)
+
+    both_axes = ("slab", "sector")
+    quad = [root] + [partner(root, both_axes, flip) for flip in (1, 2, 3)]
+    shared, *quad = after(panels, *quad)
+    sides = both(shared, "sector", True)
+    below, above = both(shared, "slab", False)
+    slots = jnp.arange(2 * depth + 2, dtype=jnp.int32)
+    level_of = jnp.where(slots < 2 * depth, slots % depth, 0)
+    flips = jnp.where(slots < 2 * depth, slots // depth, 2 + slots % 2)
+    nodes = ((devices + device) >> level_of) ^ flips
+    nodes, position, far_rows, *quad = after(nodes, position, far_rows, *quad)
+    transfer, coupling = tables(nodes[:, None], top_transfer, top_coupling)
+
+    picks = (0, depth, 2 * depth, 2 * depth + 1, 1, depth + 1)
+    across, current = combine_four(picks, quad, transfer)
+    siblings = [quad[1], across]
+    for level in range(2, depth):
+        if level == depth - 2:
+            current, below, above, *sides = after(current, below, above, *sides)
+        siblings.append(partner(current, both_axes, 1 << level))
+        if level < depth - 1:
+            current = combine(level, depth + level, current, siblings[-1], transfer)
+    corners = [both(side, "slab", False) for side in sides]
+    on_leaf = downward(local_parent, siblings, transfer, coupling, root_transfer, up_transfer)
+
+    packed = weights(far_count, far_coupling)
+    pieces = [panels, above, below]
+    for side, corner in zip(sides, corners):
+        pieces += [side, corner[1], corner[0]]
+    near_part = near(position, near_blocks, pieces)
+
     field = final(far_rows, packed, slab_coefs, on_leaf, bases, near_part)
     return field.reshape(leaf_total * leaf_size, rhs_count)
 

time: 131 us -> 134 us (1.023)
  waiting for transfers between devices: 20.9 us -> 37 us
  local copies, waits for them, and re-layouts: 14.7 us -> 3.49 us
  Pallas kernels: 48.9 us -> 38.7 us
  starting transfers between devices: 31.9 us -> 38.6 us
  other arithmetic: 0.67 us -> 2.09 us
    ppermute x10 -> x8, waiting for transfers between devices: 10.4 us -> 37 us  [partner(): lax.ppermute(array, axis, [(i, i ^ flip) for i in range(lax.axis_size(axi...]
    ppermute x6 -> x8, waiting for transfers between devices: 10.5 us -> 0.02 us  [shifted(): return lax.ppermute(array, axis, pairs)]
    unnamed x35 -> x16, local copies, waits for them, and re-layouts: 10.1 us -> 3.16 us
    ppermute x6 -> x8, starting transfers between devices: 19.1 us -> 25 us  [shifted(): return lax.ppermute(array, axis, pairs)]
    pallas_call x1, Pallas kernels: 15.9 us -> 10.3 us  [near(): pl.pallas_call(near_kernel, out_shape=jax.ShapeDtypeStruct((leaves, size,...]
    pallas_call x3 -> x1, Pallas kernels: 3.72 us -> 0.52 us  [combine_four(): pl.pallas_call(lambda *refs: combine_four_kernel(picks, *refs), out_shape...]
    concatenate x1 -> x0, local copies, waits for them, and re-layouts: 2.34 us -> none  [local(): pair = jnp.concatenate(sides)]
    pallas_call x1 -> x0, Pallas kernels: 1.86 us -> none  [upward(): pl.pallas_call(upward_kernel, out_shape=jax.ShapeDtypeStruct((rank, rhs),...]
  transfers between devices with their start and end apart: 17 -> 17, of which waited for: 7 -> 6; matrix products, arithmetic and copies ran while one was open for 6% -> 1% of each run, Pallas kernels for 29% -> 20%
where the time goes in v4:
time: 134 us
  Pallas kernels  38.7 us (29%)
  starting transfers between devices  38.6 us (29%)
  waiting for transfers between devices  37 us (28%)
  between operations  13.7 us (10%)
  local copies, waits for them, and re-layouts  3.49 us (3%)
  other arithmetic  2.09 us (2%)
    ppermute x8, waiting for transfers between devices, partner(): lax.ppermute(array, axis, [(i, i ^ flip) for i in range(lax.axis_size(axi...  37 us
    ppermute x8, starting transfers between devices, shifted(): return lax.ppermute(array, axis, pairs)  25 us
    ppermute x8, starting transfers between devices, partner(): lax.ppermute(array, axis, [(i, i ^ flip) for i in range(lax.axis_size(axi...  13.7 us
    pallas_call x1, Pallas kernels, near(): pl.pallas_call(near_kernel, out_shape=jax.ShapeDtypeStruct((leaves, size,...  10.3 us
    pallas_call x1, Pallas kernels, final(): pl.pallas_call(final_kernel, out_shape=jax.ShapeDtypeStruct((leaves, size...  8.61 us
    pallas_call x1, Pallas kernels, tables(): pl.pallas_call(tables_kernel, out_shape=(jax.ShapeDtypeStruct((count, ran...  7.59 us
    pallas_call x1, Pallas kernels, weights(): pl.pallas_call(weights_kernel, out_shape=jax.ShapeDtypeStruct((leaves, ra...  4.16 us
    pallas_call x1, Pallas kernels, leaf_coefficients(): pl.pallas_call(coefs_kernel, out_shape=(jax.ShapeDtypeStruct((leaves, ran...  3.63 us
  transfers between devices with their start and end apart: 17, of which 6 were waited for; matrix products, arithmetic and copies ran while one was open for 1% of the time, Pallas kernels for 20%

profile of v4, /device:TPU:1, one launch (start us, length us, event | category | flops | bytes accessed | tf_op | source)
XLA Modules:
  0.0 133.6 jit_solution(2877893813867142486)
XLA Ops:
  6.5 0.7 broadcast_subtract_fusion.1.parent.refs_0_
  7.2 3.6 %coefs.1 = (bf16[16,64,128]{2,1,0:T(8,128)(2,1)}, f32[64,128]{1,0:T(8,128)S(1)}) custom-call(s32[16]{0:T(128)S(1)} %broadcast_subtract_fusion.1.parent.refs_0_, bf16[16,256,128]{2,1,0:T(8,128)(2,1)} %bitcast.6, bf16[16,64,256]{2,1,0:T(8,128)(2,1)} %bitcast.14, f32[16,64,64]{2,1,0:T(8,128)} %refs_11_.1, f32[8,64,64]{2,1,0:T(8,128)} %refs_10_.1), custom_call_target="tpu_custom_call" | custom-call | flops 1000 | bytes 1000 | tf_op jit(solution)/shard_map/coefs/pallas_call | solution.py:84
  10.9 2.1 %collective-permute-start = (f32[64,128]{1,0:T(8,128)S(1)}, f32[64,128]{1,0:T(8,128)S(1)}, u32[]{:S(2)}, u32[]{:S(2)}) collective-permute-start(f32[64,128]{1,0:T(8,128)S(1)} %get-tuple-element.36.refs_0_), channel_id=1, source_target_pairs={{0,1},{1,0},{2,3},{3,2},{4,5},{5,4},{6,7},{7,6},{8,9},{9,8},{10,11... | collective-permute-start | bytes 98312 | tf_op jit(solution)/shard_map/ppermute | solution.py:356
  13.0 2.5 %collective-permute-start.1 = (f32[64,128]{1,0:T(8,128)S(1)}, f32[64,128]{1,0:T(8,128)S(1)}, u32[]{:S(2)}, u32[]{:S(2)}) collective-permute-start(f32[64,128]{1,0:T(8,128)S(1)} %get-tuple-element.36.refs_0_), channel_id=1, source_target_pairs={{0,2},{1,3},{2,0},{3,1},{4,6},{5,7},{6,4},{7,5},{8,10},{9,11},{10,... | collective-permute-start | bytes 98312 | tf_op jit(solution)/shard_map/ppermute | solution.py:356
  15.5 1.8 %collective-permute-done.1.refs_2_ = f32[64,128]{1,0:T(8,128)S(1)} collective-permute-done((f32[64,128]{1,0:T(8,128)S(1)}, f32[64,128]{1,0:T(8,128)S(1)}, u32[]{:S(2)}, u32[]{:S(2)}) %collective-permute-start.1) | collective-permute-done | bytes 32800 | tf_op jit(solution)/shard_map/ppermute | solution.py:356
  17.2 2.2 %collective-permute-done.2.refs_3_ = f32[64,128]{1,0:T(8,128)S(1)} collective-permute-done((f32[64,128]{1,0:T(8,128)S(1)}, f32[64,128]{1,0:T(8,128)S(1)}, u32[]{:S(2)}, u32[]{:S(2)}) %collective-permute-start.2) | collective-permute-done | bytes 32800 | tf_op jit(solution)/shard_map/ppermute | solution.py:356
  19.4 5.8 %collective-permute-start.6 = (bf16[16,256,128]{2,1,0:T(8,128)(2,1)}, bf16[16,256,128]{2,1,0:T(8,128)(2,1)S(1)}, u32[]{:S(2)}, u32[]{:S(2)}) collective-permute-start(bf16[16,256,128]{2,1,0:T(8,128)(2,1)} %bitcast.7), channel_id=1, source_target_pairs={{0,16},{16,32},{32,48},{48,64},{64,80},{80,96},{96,112},{1,17},{17... | collective-permute-start | bytes 3145736 | tf_op jit(solution)/shard_map/ppermute | solution.py:344
  25.2 1.9 %collective-permute-start.7 = (bf16[16,256,128]{2,1,0:T(8,128)(2,1)}, bf16[16,256,128]{2,1,0:T(8,128)(2,1)S(1)}, u32[]{:S(2)}, u32[]{:S(2)}) collective-permute-start(bf16[16,256,128]{2,1,0:T(8,128)(2,1)} %bitcast.8), channel_id=1, source_target_pairs={{16,0},{32,16},{48,32},{64,48},{80,64},{96,80},{112,96},{17,1},{33... | collective-permute-start | bytes 3145736 | tf_op jit(solution)/shard_map/ppermute | solution.py:344
  27.2 4.8 %collective-permute-start.9 = (bf16[16,256,128]{2,1,0:T(8,128)(2,1)}, bf16[16,256,128]{2,1,0:T(8,128)(2,1)}, u32[]{:S(2)}, u32[]{:S(2)}) collective-permute-start(bf16[16,256,128]{2,1,0:T(8,128)(2,1)} %bitcast.10), channel_id=1, source_target_pairs={{0,15},{1,0},{2,1},{3,2},{4,3},{5,4},{6,5},{7,6},{8,7},{9,8},{10,9... | collective-permute-start | bytes 3145736 | tf_op jit(solution)/shard_map/ppermute | solution.py:344
  32.0 0.7 fusion.6
  32.9 0.7 broadcast_subtract_fusion
  33.8 7.6 %tables.1 = (f32[16,64,64]{2,1,0:T(8,128)S(1)}, f32[16,64,64]{2,1,0:T(8,128)S(1)}) custom-call(s32[16,1]{1,0:T(8,128)S(1)} %copy.18.nodes, f32[64,64,256]{2,1,0:T(8,128)} %bitcast.12, f32[64,64,256]{2,1,0:T(8,128)} %bitcast.13), custom_call_target="tpu_custom_call" | custom-call | flops 1000 | bytes 1000 | tf_op jit(solution)/shard_map/tables/pallas_call | solution.py:135
  41.4 0.5 combine_four.1
  42.0 13.5 %collective-permute-done.3.refs_1_.refs_3_ = f32[64,128]{1,0:T(8,128)S(1)} collective-permute-done((f32[64,128]{1,0:T(8,128)S(1)}, f32[64,128]{1,0:T(8,128)S(1)}, u32[]{:S(2)}, u32[]{:S(2)}) %collective-permute-start.3) | collective-permute-done | bytes 32800 | tf_op jit(solution)/shard_map/ppermute | solution.py:356
  55.7 2.4 %collective-permute-start.4 = (f32[64,128]{1,0:T(8,128)S(1)}, f32[64,128]{1,0:T(8,128)S(1)}, u32[]{:S(2)}, u32[]{:S(2)}) collective-permute-start(f32[64,128]{1,0:T(8,128)S(1)} %combine.4.refs_0_), channel_id=1, source_target_pairs={{0,8},{1,9},{2,10},{3,11},{4,12},{5,13},{6,14},{7,15},{8,0},{9,1},... | collective-permute-start | bytes 98312 | tf_op jit(solution)/shard_map/ppermute | solution.py:356
  58.1 2.0 %collective-permute-done.4.refs_1_.refs_4_ = f32[64,128]{1,0:T(8,128)S(1)} collective-permute-done((f32[64,128]{1,0:T(8,128)S(1)}, f32[64,128]{1,0:T(8,128)S(1)}, u32[]{:S(2)}, u32[]{:S(2)}) %collective-permute-start.4) | collective-permute-done | bytes 32800 | tf_op jit(solution)/shard_map/ppermute | solution.py:356
  60.3 1.6 %collective-permute-start.5 = (f32[64,128]{1,0:T(8,128)S(1)}, f32[64,128]{1,0:T(8,128)S(1)}, u32[]{:S(2)}, u32[]{:S(2)}) collective-permute-start(f32[64,128]{1,0:T(8,128)S(1)} %combine.5.refs_0_), channel_id=1, source_target_pairs={{0,16},{1,17},{2,18},{3,19},{4,20},{5,21},{6,22},{7,23},{8,24},{9,... | collective-permute-start | bytes 98312 | tf_op jit(solution)/shard_map/ppermute | solution.py:356
  61.9 0.9 collective-permute-done.5.refs_1_.refs_5_
  63.1 1.0 copy-done.5
  64.0 2.2 %collective-permute-start.12 = (bf16[16,256,128]{2,1,0:T(8,128)(2,1)}, bf16[16,256,128]{2,1,0:T(8,128)(2,1)S(1)}, u32[]{:S(2)}, u32[]{:S(2)}) collective-permute-start(bf16[16,256,128]{2,1,0:T(8,128)(2,1)} %collective-permute-done.8.refs_3_), channel_id=1, source_target_pairs={{16,0},{32,16},{48,32},{64,48},{80,64},{96,80},{112,96},{17,1},{33... | collective-permute-start | bytes 3145736 | tf_op jit(solution)/shard_map/ppermute | solution.py:344
  66.3 4.6 %collective-permute-start.13 = (bf16[16,256,128]{2,1,0:T(8,128)(2,1)}, bf16[16,256,128]{2,1,0:T(8,128)(2,1)S(1)}, u32[]{:S(2)}, u32[]{:S(2)}) collective-permute-start(bf16[16,256,128]{2,1,0:T(8,128)(2,1)} %collective-permute-done.8.refs_3_), channel_id=1, source_target_pairs={{0,16},{16,32},{32,48},{48,64},{64,80},{80,96},{96,112},{1,17},{17... | collective-permute-start | bytes 3145736 | tf_op jit(solution)/shard_map/ppermute | solution.py:344
  70.9 1.9 %collective-permute-start.14 = (bf16[16,256,128]{2,1,0:T(8,128)(2,1)}, bf16[16,256,128]{2,1,0:T(8,128)(2,1)S(1)}, u32[]{:S(2)}, u32[]{:S(2)}) collective-permute-start(bf16[16,256,128]{2,1,0:T(8,128)(2,1)} %collective-permute-done.9.refs_6_), channel_id=1, source_target_pairs={{16,0},{32,16},{48,32},{64,48},{80,64},{96,80},{112,96},{17,1},{33... | collective-permute-start | bytes 3145736 | tf_op jit(solution)/shard_map/ppermute | solution.py:344
  72.8 3.6 %collective-permute-start.15 = (bf16[16,256,128]{2,1,0:T(8,128)(2,1)}, bf16[16,256,128]{2,1,0:T(8,128)(2,1)S(1)}, u32[]{:S(2)}, u32[]{:S(2)}) collective-permute-start(bf16[16,256,128]{2,1,0:T(8,128)(2,1)} %collective-permute-done.9.refs_6_), channel_id=1, source_target_pairs={{0,16},{16,32},{32,48},{48,64},{64,80},{80,96},{96,112},{1,17},{17... | collective-permute-start | bytes 3145736 | tf_op jit(solution)/shard_map/ppermute | solution.py:344
  76.5 1.6 %collective-permute-start.10 = (f32[64,128]{1,0:T(8,128)S(1)}, f32[64,128]{1,0:T(8,128)S(1)}, u32[]{:S(2)}, u32[]{:S(2)}) collective-permute-start(f32[64,128]{1,0:T(8,128)S(1)} %combine.6.refs_0_), channel_id=1, source_target_pairs={{0,32},{1,33},{2,34},{3,35},{4,36},{5,37},{6,38},{7,39},{8,40},{9,... | collective-permute-start | bytes 98312 | tf_op jit(solution)/shard_map/ppermute | solution.py:356
  78.0 16.7 %collective-permute-done.10.refs_1_.refs_6_ = f32[64,128]{1,0:T(8,128)S(1)} collective-permute-done((f32[64,128]{1,0:T(8,128)S(1)}, f32[64,128]{1,0:T(8,128)S(1)}, u32[]{:S(2)}, u32[]{:S(2)}) %collective-permute-start.10) | collective-permute-done | bytes 32800 | tf_op jit(solution)/shard_map/ppermute | solution.py:356
  95.1 3.4 %collective-permute-start.11 = (f32[64,128]{1,0:T(8,128)S(1)}, f32[64,128]{1,0:T(8,128)S(1)}, u32[]{:S(2)}, u32[]{:S(2)}) collective-permute-start(f32[64,128]{1,0:T(8,128)S(1)} %combine.7), channel_id=1, source_target_pairs={{0,64},{1,65},{2,66},{3,67},{4,68},{5,69},{6,70},{7,71},{8,72},{9,... | collective-permute-start | bytes 98312 | tf_op jit(solution)/shard_map/ppermute | solution.py:356
  98.5 4.2 %weights.1.packed = bf16[16,64,1024]{2,1,0:T(8,128)(2,1)S(1)} custom-call(s32[16]{0:T(128)S(1)} %copy-done.7, f32[16,16,64,64]{3,2,1,0:T(8,128)} %coupling.1), custom_call_target="tpu_custom_call" | custom-call | flops 1000 | bytes 1000 | tf_op jit(solution)/shard_map/weights/pallas_call | solution.py:229
  102.7 2.9 %downward.1.on_leaf = f32[16,64,128]{2,1,0:T(8,128)S(1)} custom-call(s32[16]{0:T(128)S(1)} %broadcast_subtract_fusion.1.parent.refs_0_, f32[64,128]{1,0:T(8,128)S(1)} %collective-permute-done.refs_1_, f32[64,128]{1,0:T(8,128)S(1)} %get-tuple-element.41.refs_2_, f32[64,128]{1,0:T(8,128)S(1)} %collective-permute-done.3.refs_1_.refs_3_, ...), custom_call_target="tpu_custom_call" | custom-call | flops 1000 | bytes 1000 | tf_op jit(solution)/shard_map/downward/pallas_call | solution.py:200
  105.6 0.8 copy-done.3
  106.5 10.3 %near.1.near_part = f32[16,256,128]{2,1,0:T(8,128)S(1)} custom-call(s32[128]{0:T(128)S(1)} %reshape.12.position, bf16[16,8,256,256]{3,2,1,0:T(8,128)(2,1)} %blocks.1, bf16[16,256,128]{2,1,0:T(8,128)(2,1)S(1)} %bitcast.11, bf16[16,256,128]{2,1,0:T(8,128)(2,1)S(1)} %copy-done.6, bf16[16,256,128]{2,1,0:T(8,128)(2,1)S(1)} %collective-permute-done.6.refs_2_, ...), custom_call_target="tpu_custom_call" | custom-call | flops 1000 | bytes 1000 | tf_op jit(solution)/shard_map/near/pallas_call | solution.py:270
  116.8 1.4 %copy-done = f32[16,256,128]{2,1,0:T(8,128)} copy-done((f32[16,256,128]{2,1,0:T(8,128)}, f32[16,256,128]{2,1,0:T(8,128)S(1)}, u32[]{:S(2)}) %copy-start) | copy-done | bytes 2097176
  118.1 8.6 %final.1 = bf16[16,256,128]{2,1,0:T(8,128)(2,1)} custom-call(s32[256]{0:T(256)S(1)} %reshape.13.rows, bf16[16,64,1024]{2,1,0:T(8,128)(2,1)S(1)} %weights.1.packed, bf16[256,64,128]{2,1,0:T(8,128)(2,1)} %all-gather.2.cloned.1.call-done.coefs, f32[16,64,128]{2,1,0:T(8,128)} %copy-done.3, bf16[16,64,256]{2,1,0:T(8,128)(2,1)} %bitcast.15, f32[16,256,128]{2,1,0:T(8,128)} %copy-done), custom_call_target="tpu_custom_call" | custom-call | flops 1000 | bytes 1000 | tf_op jit(solution)/shard_map/final/pallas_call | solution.py:319
  (38 shorter events, 1.6 us)
Async XLA Ops:
  6.5 111.6 %all-gather.2.cloned.1.call-start = ((), (), s32[]{:S(2)}) async-start(), calls=%async_computation | async-start | bytes 4456448 | tf_op jit(solution)/shard_map/all_gather | solution.py:388
  10.9 4.6 %collective-permute-start = (f32[64,128]{1,0:T(8,128)S(1)}, f32[64,128]{1,0:T(8,128)S(1)}, u32[]{:S(2)}, u32[]{:S(2)}) collective-permute-start(f32[64,128]{1,0:T(8,128)S(1)} %get-tuple-element.36.refs_0_), channel_id=1, source_target_pairs={{0,1},{1,0},{2,3},{3,2},{4,5},{5,4},{6,7},{7,6},{8,9},{9,8},{10,11... | collective-permute-start | bytes 98312 | tf_op jit(solution)/shard_map/ppermute | solution.py:356
  13.0 4.3 %collective-permute-start.1 = (f32[64,128]{1,0:T(8,128)S(1)}, f32[64,128]{1,0:T(8,128)S(1)}, u32[]{:S(2)}, u32[]{:S(2)}) collective-permute-start(f32[64,128]{1,0:T(8,128)S(1)} %get-tuple-element.36.refs_0_), channel_id=1, source_target_pairs={{0,2},{1,3},{2,0},{3,1},{4,6},{5,7},{6,4},{7,5},{8,10},{9,11},{10,... | collective-permute-start | bytes 98312 | tf_op jit(solution)/shard_map/ppermute | solution.py:356
  15.4 4.0 %collective-permute-start.2 = (f32[64,128]{1,0:T(8,128)S(1)}, f32[64,128]{1,0:T(8,128)S(1)}, u32[]{:S(2)}, u32[]{:S(2)}) collective-permute-start(f32[64,128]{1,0:T(8,128)S(1)} %get-tuple-element.36.refs_0_), channel_id=1, source_target_pairs={{0,3},{1,2},{2,1},{3,0},{4,7},{5,6},{6,5},{7,4},{8,11},{9,10},{10,... | collective-permute-start | bytes 98312 | tf_op jit(solution)/shard_map/ppermute | solution.py:356
  19.4 43.6 %collective-permute-start.6 = (bf16[16,256,128]{2,1,0:T(8,128)(2,1)}, bf16[16,256,128]{2,1,0:T(8,128)(2,1)S(1)}, u32[]{:S(2)}, u32[]{:S(2)}) collective-permute-start(bf16[16,256,128]{2,1,0:T(8,128)(2,1)} %bitcast.7), channel_id=1, source_target_pairs={{0,16},{16,32},{32,48},{48,64},{64,80},{80,96},{96,112},{1,17},{17... | collective-permute-start | bytes 3145736 | tf_op jit(solution)/shard_map/ppermute | solution.py:344
  25.2 37.8 %collective-permute-start.7 = (bf16[16,256,128]{2,1,0:T(8,128)(2,1)}, bf16[16,256,128]{2,1,0:T(8,128)(2,1)S(1)}, u32[]{:S(2)}, u32[]{:S(2)}) collective-permute-start(bf16[16,256,128]{2,1,0:T(8,128)(2,1)} %bitcast.8), channel_id=1, source_target_pairs={{16,0},{32,16},{48,32},{64,48},{80,64},{96,80},{112,96},{17,1},{33... | collective-permute-start | bytes 3145736 | tf_op jit(solution)/shard_map/ppermute | solution.py:344
  27.1 36.9 %collective-permute-start.8 = (bf16[16,256,128]{2,1,0:T(8,128)(2,1)}, bf16[16,256,128]{2,1,0:T(8,128)(2,1)}, u32[]{:S(2)}, u32[]{:S(2)}) collective-permute-start(bf16[16,256,128]{2,1,0:T(8,128)(2,1)} %bitcast.9), channel_id=1, source_target_pairs={{0,1},{1,2},{2,3},{3,4},{4,5},{5,6},{6,7},{7,8},{8,9},{9,10},{10,1... | collective-permute-start | bytes 3145736 | tf_op jit(solution)/shard_map/ppermute | solution.py:344
  27.2 36.8 %collective-permute-start.9 = (bf16[16,256,128]{2,1,0:T(8,128)(2,1)}, bf16[16,256,128]{2,1,0:T(8,128)(2,1)}, u32[]{:S(2)}, u32[]{:S(2)}) collective-permute-start(bf16[16,256,128]{2,1,0:T(8,128)(2,1)} %bitcast.10), channel_id=1, source_target_pairs={{0,15},{1,0},{2,1},{3,2},{4,3},{5,4},{6,5},{7,6},{8,7},{9,8},{10,9... | collective-permute-start | bytes 3145736 | tf_op jit(solution)/shard_map/ppermute | solution.py:344
  33.8 64.7 %copy-start.7 = (s32[16]{0:T(128)S(1)}, s32[16]{0:T(128)}, u32[]{:S(2)}) copy-start(s32[16]{0:T(128)} %count.1) | copy-start | bytes 196
  41.9 13.6 %collective-permute-start.3 = (f32[64,128]{1,0:T(8,128)S(1)}, f32[64,128]{1,0:T(8,128)S(1)}, u32[]{:S(2)}, u32[]{:S(2)}) collective-permute-start(f32[64,128]{1,0:T(8,128)S(1)} %get-tuple-element.42.refs_0_), channel_id=1, source_target_pairs={{0,4},{1,5},{2,6},{3,7},{4,0},{5,1},{6,2},{7,3},{8,12},{9,13},{10,... | collective-permute-start | bytes 98312 | tf_op jit(solution)/shard_map/ppermute | solution.py:356
  55.7 4.3 %collective-permute-start.4 = (f32[64,128]{1,0:T(8,128)S(1)}, f32[64,128]{1,0:T(8,128)S(1)}, u32[]{:S(2)}, u32[]{:S(2)}) collective-permute-start(f32[64,128]{1,0:T(8,128)S(1)} %combine.4.refs_0_), channel_id=1, source_target_pairs={{0,8},{1,9},{2,10},{3,11},{4,12},{5,13},{6,14},{7,15},{8,0},{9,1},... | collective-permute-start | bytes 98312 | tf_op jit(solution)/shard_map/ppermute | solution.py:356
  60.3 2.4 %collective-permute-start.5 = (f32[64,128]{1,0:T(8,128)S(1)}, f32[64,128]{1,0:T(8,128)S(1)}, u32[]{:S(2)}, u32[]{:S(2)}) collective-permute-start(f32[64,128]{1,0:T(8,128)S(1)} %combine.5.refs_0_), channel_id=1, source_target_pairs={{0,16},{1,17},{2,18},{3,19},{4,20},{5,21},{6,22},{7,23},{8,24},{9,... | collective-permute-start | bytes 98312 | tf_op jit(solution)/shard_map/ppermute | solution.py:356
  63.0 1.0 copy-start.5
  64.0 42.4 %collective-permute-start.12 = (bf16[16,256,128]{2,1,0:T(8,128)(2,1)}, bf16[16,256,128]{2,1,0:T(8,128)(2,1)S(1)}, u32[]{:S(2)}, u32[]{:S(2)}) collective-permute-start(bf16[16,256,128]{2,1,0:T(8,128)(2,1)} %collective-permute-done.8.refs_3_), channel_id=1, source_target_pairs={{16,0},{32,16},{48,32},{64,48},{80,64},{96,80},{112,96},{17,1},{33... | collective-permute-start | bytes 3145736 | tf_op jit(solution)/shard_map/ppermute | solution.py:344
  66.3 40.1 %collective-permute-start.13 = (bf16[16,256,128]{2,1,0:T(8,128)(2,1)}, bf16[16,256,128]{2,1,0:T(8,128)(2,1)S(1)}, u32[]{:S(2)}, u32[]{:S(2)}) collective-permute-start(bf16[16,256,128]{2,1,0:T(8,128)(2,1)} %collective-permute-done.8.refs_3_), channel_id=1, source_target_pairs={{0,16},{16,32},{32,48},{48,64},{64,80},{80,96},{96,112},{1,17},{17... | collective-permute-start | bytes 3145736 | tf_op jit(solution)/shard_map/ppermute | solution.py:344
  70.9 35.5 %collective-permute-start.14 = (bf16[16,256,128]{2,1,0:T(8,128)(2,1)}, bf16[16,256,128]{2,1,0:T(8,128)(2,1)S(1)}, u32[]{:S(2)}, u32[]{:S(2)}) collective-permute-start(bf16[16,256,128]{2,1,0:T(8,128)(2,1)} %collective-permute-done.9.refs_6_), channel_id=1, source_target_pairs={{16,0},{32,16},{48,32},{64,48},{80,64},{96,80},{112,96},{17,1},{33... | collective-permute-start | bytes 3145736 | tf_op jit(solution)/shard_map/ppermute | solution.py:344
  72.8 33.6 %collective-permute-start.15 = (bf16[16,256,128]{2,1,0:T(8,128)(2,1)}, bf16[16,256,128]{2,1,0:T(8,128)(2,1)S(1)}, u32[]{:S(2)}, u32[]{:S(2)}) collective-permute-start(bf16[16,256,128]{2,1,0:T(8,128)(2,1)} %collective-permute-done.9.refs_6_), channel_id=1, source_target_pairs={{0,16},{16,32},{32,48},{48,64},{64,80},{80,96},{96,112},{1,17},{17... | collective-permute-start | bytes 3145736 | tf_op jit(solution)/shard_map/ppermute | solution.py:344
  76.5 18.3 %collective-permute-start.10 = (f32[64,128]{1,0:T(8,128)S(1)}, f32[64,128]{1,0:T(8,128)S(1)}, u32[]{:S(2)}, u32[]{:S(2)}) collective-permute-start(f32[64,128]{1,0:T(8,128)S(1)} %combine.6.refs_0_), channel_id=1, source_target_pairs={{0,32},{1,33},{2,34},{3,35},{4,36},{5,37},{6,38},{7,39},{8,40},{9,... | collective-permute-start | bytes 98312 | tf_op jit(solution)/shard_map/ppermute | solution.py:356
  95.0 7.6 %copy-start.2 = (f32[16,64,64]{2,1,0:T(8,128)S(1)}, f32[16,64,64]{2,1,0:T(8,128)}, u32[]{:S(2)}) copy-start(f32[16,64,64]{2,1,0:T(8,128)} %refs_11_.1) | copy-start | bytes 786436
  95.0 7.6 %copy-start.4 = (f32[8,64,64]{2,1,0:T(8,128)S(1)}, f32[8,64,64]{2,1,0:T(8,128)}, u32[]{:S(2)}) copy-start(f32[8,64,64]{2,1,0:T(8,128)} %refs_10_.1) | copy-start | bytes 393220
  95.0 11.4 %copy-start.1 = (bf16[4096,128]{1,0:T(8,128)(2,1)S(1)}, bf16[4096,128]{1,0:T(8,128)(2,1)}, u32[]{:S(2)}) copy-start(bf16[4096,128]{1,0:T(8,128)(2,1)} %param.12) | copy-start | bytes 3145732
  95.0 11.4 %copy-start.6 = (bf16[16,256,128]{2,1,0:T(8,128)(2,1)S(1)}, bf16[16,256,128]{2,1,0:T(8,128)(2,1)}, u32[]{:S(2)}) copy-start(bf16[16,256,128]{2,1,0:T(8,128)(2,1)} %copy-done.5) | copy-start | bytes 3145732
  95.1 7.6 %collective-permute-start.11 = (f32[64,128]{1,0:T(8,128)S(1)}, f32[64,128]{1,0:T(8,128)S(1)}, u32[]{:S(2)}, u32[]{:S(2)}) collective-permute-start(f32[64,128]{1,0:T(8,128)S(1)} %combine.7), channel_id=1, source_target_pairs={{0,64},{1,65},{2,66},{3,67},{4,68},{5,69},{6,70},{7,71},{8,72},{9,... | collective-permute-start | bytes 98312 | tf_op jit(solution)/shard_map/ppermute | solution.py:356
  105.6 0.8 copy-start.3
  116.8 1.4 %copy-start = (f32[16,256,128]{2,1,0:T(8,128)}, f32[16,256,128]{2,1,0:T(8,128)S(1)}, u32[]{:S(2)}) copy-start(f32[16,256,128]{2,1,0:T(8,128)S(1)} %near.1.near_part) | copy-start | bytes 6291460
Sparse Core Ops, SparseCore 0:
  11.0 72.9 all-gather.1

commit v5 on v4

--- a/solution.py
+++ b/solution.py
@@ -239,8 +239,8 @@
 
 
 def near_kernel(position, blocks, *refs):
-    pieces = refs[:-5]
-    out, held, matrices, piece_sems, block_sems = refs[-5:]
+    pieces = refs[:-7]
+    out, held, matrices, piece_sems, block_sems, sums, out_sems = refs[-7:]
     leaves, slots = blocks.shape[:2]
     copies = []
     first = 0
@@ -257,11 +257,16 @@
         copy.wait()
     for fetch in fetches[1:]:
         fetch.start()
+    stores = []
     for leaf in range(leaves):
         fetches[leaf].wait()
         wide = jnp.concatenate([matrices[leaf, slot] for slot in range(slots)], axis=1)
         tall = jnp.concatenate([held[position[leaf * slots + slot]] for slot in range(slots)], axis=0)
-        out[leaf] = dot(wide, tall)
+        sums[leaf] = dot(wide, tall)
+        stores.append(pltpu.make_async_copy(sums.at[leaf], out.at[leaf], out_sems.at[leaf]))
+        stores[leaf].start()
+    for store in stores:
+        store.wait()
 
 
 def near(position, near_blocks, pieces):
@@ -269,13 +274,15 @@
     rhs = pieces[0].shape[2]
     return pl.pallas_call(
         near_kernel,
-        out_shape=jax.ShapeDtypeStruct((leaves, size, rhs), f32),
+        out_shape=pltpu.HBM((leaves, size, rhs), f32),
         in_specs=[scalars()] + [anywhere()] * (1 + len(pieces)),
-        out_specs=whole(),
+        out_specs=pl.BlockSpec(memory_space=pltpu.HBM),
         scratch_shapes=[
             pltpu.VMEM((sum(piece.shape[0] for piece in pieces), size, rhs), bf16),
             pltpu.VMEM(near_blocks.shape, bf16),
             pltpu.SemaphoreType.DMA((len(pieces),)),
+            pltpu.SemaphoreType.DMA((leaves,)),
+            pltpu.VMEM((leaves, size, rhs), f32),
             pltpu.SemaphoreType.DMA((leaves,)),
         ],
         compiler_params=params(36),
@@ -335,7 +342,7 @@
         compiler_params=params(24),
         cost_estimate=cost(1000, 1000),
         name="final",
-    )(far_rows, packed, *[in_hbm(array) for array in (slab_coefs, on_leaf, bases, near_part)])
+    )(far_rows, packed, in_hbm(slab_coefs), on_leaf, in_hbm(bases), in_hbm(near_part))
 
 
 def shifted(array, axis, step, closed):
@@ -398,7 +405,8 @@
     quad = [root] + [partner(root, both_axes, flip) for flip in (1, 2, 3)]
     shared, *quad = after(panels, *quad)
     sides = both(shared, "sector", True)
-    below, above = both(shared, "slab", False)
+    later, position, far_rows = after(panels, position, far_rows)
+    below, above = both(later, "slab", False)
     slots = jnp.arange(2 * depth + 2, dtype=jnp.int32)
     level_of = jnp.where(slots < 2 * depth, slots % depth, 0)
     flips = jnp.where(slots < 2 * depth, slots // depth, 2 + slots % 2)
@@ -409,21 +417,22 @@
     picks = (0, depth, 2 * depth, 2 * depth + 1, 1, depth + 1)
     across, current = combine_four(picks, quad, transfer)
     siblings = [quad[1], across]
+    packed = weights(far_count, far_coupling)
     for level in range(2, depth):
+        sibling = partner(current, both_axes, 1 << level)
+        if level == 2:
+            current, sibling, packed, below, above, *sides = after(current, sibling, packed, below, above, *sides)
+            corners = [both(side, "slab", False) for side in sides]
+            pieces = [panels, above, below]
+            for side, corner in zip(sides, corners):
+                pieces += [side, corner[1], corner[0]]
         if level == depth - 2:
-            current, below, above, *sides = after(current, below, above, *sides)
-        siblings.append(partner(current, both_axes, 1 << level))
+            near_part = near(position, near_blocks, pieces)
+            current, sibling, near_part = after(current, sibling, near_part)
+        siblings.append(sibling)
         if level < depth - 1:
-            current = combine(level, depth + level, current, siblings[-1], transfer)
-    corners = [both(side, "slab", False) for side in sides]
+            current = combine(level, depth + level, current, sibling, transfer)
     on_leaf = downward(local_parent, siblings, transfer, coupling, root_transfer, up_transfer)
-
-    packed = weights(far_count, far_coupling)
-    pieces = [panels, above, below]
-    for side, corner in zip(sides, corners):
-        pieces += [side, corner[1], corner[0]]
-    near_part = near(position, near_blocks, pieces)
-
     field = final(far_rows, packed, slab_coefs, on_leaf, bases, near_part)
     return field.reshape(leaf_total * leaf_size, rhs_count)
 

time: 134 us -> 121 us (0.903)
  waiting for transfers between devices: 37 us -> 29.7 us
  starting transfers between devices: 38.6 us -> 35.3 us
  local copies, waits for them, and re-layouts: 3.49 us -> 0.35 us
    ppermute x8, waiting for transfers between devices: 37 us -> 19.3 us  [partner(): lax.ppermute(array, axis, [(i, i ^ flip) for i in range(lax.axis_size(axi...]
    ppermute x8, waiting for transfers between devices: 0.02 us -> 10.3 us  [shifted(): return lax.ppermute(array, axis, pairs)]
    ppermute x8, starting transfers between devices: 13.7 us -> 9.93 us  [partner(): lax.ppermute(array, axis, [(i, i ^ flip) for i in range(lax.axis_size(axi...]
    unnamed x16 -> x8, local copies, waits for them, and re-layouts: 3.16 us -> 0.02 us
  transfers between devices with their start and end apart: 17 -> 17, of which waited for: 6 -> 7; matrix products, arithmetic and copies ran while one was open for 1% -> 1% of each run, Pallas kernels for 20% -> 23%
where the time goes in v5:
time: 121 us
  Pallas kernels  39.5 us (33%)
  starting transfers between devices  35.3 us (29%)
  waiting for transfers between devices  29.7 us (25%)
  between operations  13.6 us (11%)
  other arithmetic  2.09 us (2%)
    ppermute x8, starting transfers between devices, shifted(): return lax.ppermute(array, axis, pairs)  25.3 us
    ppermute x8, waiting for transfers between devices, partner(): lax.ppermute(array, axis, [(i, i ^ flip) for i in range(lax.axis_size(axi...  19.3 us
    pallas_call x1, Pallas kernels, near(): pl.pallas_call(near_kernel, out_shape=pltpu.HBM((leaves, size, rhs), f32)...  11.3 us
    ppermute x8, waiting for transfers between devices, shifted(): return lax.ppermute(array, axis, pairs)  10.3 us
    ppermute x8, starting transfers between devices, partner(): lax.ppermute(array, axis, [(i, i ^ flip) for i in range(lax.axis_size(axi...  9.93 us
    pallas_call x1, Pallas kernels, final(): pl.pallas_call(final_kernel, out_shape=jax.ShapeDtypeStruct((leaves, size...  8.46 us
    pallas_call x1, Pallas kernels, tables(): pl.pallas_call(tables_kernel, out_shape=(jax.ShapeDtypeStruct((count, ran...  7.59 us
    pallas_call x1, Pallas kernels, weights(): pl.pallas_call(weights_kernel, out_shape=jax.ShapeDtypeStruct((leaves, ra...  4.16 us
  transfers between devices with their start and end apart: 17, of which 7 were waited for; matrix products, arithmetic and copies ran while one was open for 1% of the time, Pallas kernels for 23%

profile of v5, /device:TPU:1, one launch (start us, length us, event | category | flops | bytes accessed | tf_op | source)
XLA Modules:
  0.0 120.5 jit_solution(14561724972768537198)
XLA Ops:
  6.5 0.7 broadcast_subtract_fusion.1.parent.refs_0_
  7.2 3.6 %coefs.1 = (bf16[16,64,128]{2,1,0:T(8,128)(2,1)}, f32[64,128]{1,0:T(8,128)S(1)}) custom-call(s32[16]{0:T(128)S(1)} %broadcast_subtract_fusion.1.parent.refs_0_, bf16[16,256,128]{2,1,0:T(8,128)(2,1)} %bitcast.6, bf16[16,64,256]{2,1,0:T(8,128)(2,1)} %bitcast.14, f32[16,64,64]{2,1,0:T(8,128)} %refs_11_.1, f32[8,64,64]{2,1,0:T(8,128)} %refs_10_.1), custom_call_target="tpu_custom_call" | custom-call | flops 1000 | bytes 1000 | tf_op jit(solution)/shard_map/coefs/pallas_call | solution.py:84
  10.9 2.1 %collective-permute-start = (f32[64,128]{1,0:T(8,128)S(1)}, f32[64,128]{1,0:T(8,128)S(1)}, u32[]{:S(2)}, u32[]{:S(2)}) collective-permute-start(f32[64,128]{1,0:T(8,128)S(1)} %get-tuple-element.44.refs_0_), channel_id=1, source_target_pairs={{0,1},{1,0},{2,3},{3,2},{4,5},{5,4},{6,7},{7,6},{8,9},{9,8},{10,11... | collective-permute-start | bytes 98312 | tf_op jit(solution)/shard_map/ppermute | solution.py:363
  13.0 2.5 %collective-permute-start.1 = (f32[64,128]{1,0:T(8,128)S(1)}, f32[64,128]{1,0:T(8,128)S(1)}, u32[]{:S(2)}, u32[]{:S(2)}) collective-permute-start(f32[64,128]{1,0:T(8,128)S(1)} %get-tuple-element.44.refs_0_), channel_id=1, source_target_pairs={{0,2},{1,3},{2,0},{3,1},{4,6},{5,7},{6,4},{7,5},{8,10},{9,11},{10,... | collective-permute-start | bytes 98312 | tf_op jit(solution)/shard_map/ppermute | solution.py:363
  15.5 0.7 broadcast_subtract_fusion
  16.2 0.7 fusion.6
  17.1 5.1 %collective-permute-start.4 = (bf16[16,256,128]{2,1,0:T(8,128)(2,1)}, bf16[16,256,128]{2,1,0:T(8,128)(2,1)S(1)}, u32[]{:S(2)}, u32[]{:S(2)}) collective-permute-start(bf16[16,256,128]{2,1,0:T(8,128)(2,1)} %bitcast.7), channel_id=1, source_target_pairs={{0,16},{16,32},{32,48},{48,64},{64,80},{80,96},{96,112},{1,17},{17... | collective-permute-start | bytes 3145736 | tf_op jit(solution)/shard_map/ppermute | solution.py:351
  22.2 1.9 %collective-permute-start.5 = (bf16[16,256,128]{2,1,0:T(8,128)(2,1)}, bf16[16,256,128]{2,1,0:T(8,128)(2,1)}, u32[]{:S(2)}, u32[]{:S(2)}) collective-permute-start(bf16[16,256,128]{2,1,0:T(8,128)(2,1)} %bitcast.8), channel_id=1, source_target_pairs={{16,0},{32,16},{48,32},{64,48},{80,64},{96,80},{112,96},{17,1},{33... | collective-permute-start | bytes 3145736 | tf_op jit(solution)/shard_map/ppermute | solution.py:351
  24.3 5.0 %collective-permute-start.7 = (bf16[16,256,128]{2,1,0:T(8,128)(2,1)}, bf16[16,256,128]{2,1,0:T(8,128)(2,1)}, u32[]{:S(2)}, u32[]{:S(2)}) collective-permute-start(bf16[16,256,128]{2,1,0:T(8,128)(2,1)} %bitcast.10), channel_id=1, source_target_pairs={{0,15},{1,0},{2,1},{3,2},{4,3},{5,4},{6,5},{7,6},{8,7},{9,8},{10,9... | collective-permute-start | bytes 3145736 | tf_op jit(solution)/shard_map/ppermute | solution.py:351
  29.4 7.6 %tables.1 = (f32[16,64,64]{2,1,0:T(8,128)S(1)}, f32[16,64,64]{2,1,0:T(8,128)S(1)}) custom-call(s32[16,1]{1,0:T(8,128)S(1)} %copy.18.nodes, f32[64,64,256]{2,1,0:T(8,128)} %bitcast.12, f32[64,64,256]{2,1,0:T(8,128)} %bitcast.13), custom_call_target="tpu_custom_call" | custom-call | flops 1000 | bytes 1000 | tf_op jit(solution)/shard_map/tables/pallas_call | solution.py:135
  37.0 0.5 combine_four.1
  37.6 4.2 %weights.1.packed = bf16[16,64,1024]{2,1,0:T(8,128)(2,1)S(1)} custom-call(s32[16]{0:T(128)S(1)} %copy-done.3, f32[16,16,64,64]{3,2,1,0:T(8,128)} %coupling.1), custom_call_target="tpu_custom_call" | custom-call | flops 1000 | bytes 1000 | tf_op jit(solution)/shard_map/weights/pallas_call | solution.py:229
  41.7 12.3 %collective-permute-done.3.refs_1_.refs_3_ = f32[64,128]{1,0:T(8,128)S(1)} collective-permute-done((f32[64,128]{1,0:T(8,128)S(1)}, f32[64,128]{1,0:T(8,128)S(1)}, u32[]{:S(2)}, u32[]{:S(2)}) %collective-permute-start.3) | collective-permute-done | bytes 32800 | tf_op jit(solution)/shard_map/ppermute | solution.py:363
  54.0 1.0 collective-permute-done.6.refs_3_
  55.0 1.9 %collective-permute-start.11 = (bf16[16,256,128]{2,1,0:T(8,128)(2,1)}, bf16[16,256,128]{2,1,0:T(8,128)(2,1)S(1)}, u32[]{:S(2)}, u32[]{:S(2)}) collective-permute-start(bf16[16,256,128]{2,1,0:T(8,128)(2,1)} %collective-permute-done.6.refs_3_), channel_id=1, source_target_pairs={{16,0},{32,16},{48,32},{64,48},{80,64},{96,80},{112,96},{17,1},{33... | collective-permute-start | bytes 3145736 | tf_op jit(solution)/shard_map/ppermute | solution.py:351
  57.0 5.8 %collective-permute-start.12 = (bf16[16,256,128]{2,1,0:T(8,128)(2,1)}, bf16[16,256,128]{2,1,0:T(8,128)(2,1)S(1)}, u32[]{:S(2)}, u32[]{:S(2)}) collective-permute-start(bf16[16,256,128]{2,1,0:T(8,128)(2,1)} %collective-permute-done.6.refs_3_), channel_id=1, source_target_pairs={{0,16},{16,32},{32,48},{48,64},{64,80},{80,96},{96,112},{1,17},{17... | collective-permute-start | bytes 3145736 | tf_op jit(solution)/shard_map/ppermute | solution.py:351
  62.7 1.9 %collective-permute-start.13 = (bf16[16,256,128]{2,1,0:T(8,128)(2,1)}, bf16[16,256,128]{2,1,0:T(8,128)(2,1)S(1)}, u32[]{:S(2)}, u32[]{:S(2)}) collective-permute-start(bf16[16,256,128]{2,1,0:T(8,128)(2,1)} %collective-permute-done.7.refs_6_), channel_id=1, source_target_pairs={{16,0},{32,16},{48,32},{64,48},{80,64},{96,80},{112,96},{17,1},{33... | collective-permute-start | bytes 3145736 | tf_op jit(solution)/shard_map/ppermute | solution.py:351
  64.7 3.6 %collective-permute-start.14 = (bf16[16,256,128]{2,1,0:T(8,128)(2,1)}, bf16[16,256,128]{2,1,0:T(8,128)(2,1)S(1)}, u32[]{:S(2)}, u32[]{:S(2)}) collective-permute-start(bf16[16,256,128]{2,1,0:T(8,128)(2,1)} %collective-permute-done.7.refs_6_), channel_id=1, source_target_pairs={{0,16},{16,32},{32,48},{48,64},{64,80},{80,96},{96,112},{1,17},{17... | collective-permute-start | bytes 3145736 | tf_op jit(solution)/shard_map/ppermute | solution.py:351
  68.3 0.3 combine.4.refs_0_
  68.6 0.7 collective-permute-start.8
  69.3 4.4 %collective-permute-done.8.refs_1_.refs_4_ = f32[64,128]{1,0:T(8,128)S(1)} collective-permute-done((f32[64,128]{1,0:T(8,128)S(1)}, f32[64,128]{1,0:T(8,128)S(1)}, u32[]{:S(2)}, u32[]{:S(2)}) %collective-permute-start.8) | collective-permute-done | bytes 32800 | tf_op jit(solution)/shard_map/ppermute | solution.py:363
  73.7 0.2 combine.5.refs_0_
  74.1 1.2 collective-permute-done.9.refs_1_.refs_5_
  75.6 1.6 %collective-permute-start.10 = (f32[64,128]{1,0:T(8,128)S(1)}, f32[64,128]{1,0:T(8,128)S(1)}, u32[]{:S(2)}, u32[]{:S(2)}) collective-permute-start(f32[64,128]{1,0:T(8,128)S(1)} %combine.6.refs_0_), channel_id=1, source_target_pairs={{0,32},{1,33},{2,34},{3,35},{4,36},{5,37},{6,38},{7,39},{8,40},{9,... | collective-permute-start | bytes 98312 | tf_op jit(solution)/shard_map/ppermute | solution.py:363
  77.1 8.3 %collective-permute-done.13.refs_7_ = bf16[16,256,128]{2,1,0:T(8,128)(2,1)S(1)} collective-permute-done((bf16[16,256,128]{2,1,0:T(8,128)(2,1)}, bf16[16,256,128]{2,1,0:T(8,128)(2,1)S(1)}, u32[]{:S(2)}, u32[]{:S(2)}) %collective-permute-start.13) | collective-permute-done | bytes 1048608 | tf_op jit(solution)/shard_map/ppermute | solution.py:351
  85.5 0.9 collective-permute-done.14.refs_8_
  86.4 11.3 %near.1.near_part = f32[16,256,128]{2,1,0:T(8,128)} custom-call(s32[128]{0:T(128)S(1)} %reshape.13.position, bf16[16,8,256,256]{3,2,1,0:T(8,128)(2,1)} %blocks.1, bf16[16,256,128]{2,1,0:T(8,128)(2,1)S(1)} %bitcast.11, bf16[16,256,128]{2,1,0:T(8,128)(2,1)} %collective-permute-done.5.refs_1_, bf16[16,256,128]{2,1,0:T(8,128)(2,1)S(1)} %collective-permute-done.4.refs_2_, ...), custom_call_target="tpu_custom_call" | custom-call | flops 1000 | bytes 1000 | tf_op jit(solution)/shard_map/near/pallas_call | solution.py:275
  97.7 0.3 combine.7
  97.9 2.9 %collective-permute-start.15 = (f32[64,128]{1,0:T(8,128)S(1)}, f32[64,128]{1,0:T(8,128)S(1)}, u32[]{:S(2)}, u32[]{:S(2)}) collective-permute-start(f32[64,128]{1,0:T(8,128)S(1)} %combine.7), channel_id=1, source_target_pairs={{0,64},{1,65},{2,66},{3,67},{4,68},{5,69},{6,70},{7,71},{8,72},{9,... | collective-permute-start | bytes 98312 | tf_op jit(solution)/shard_map/ppermute | solution.py:363
  100.8 1.5 %collective-permute-done.15.refs_7_ = f32[64,128]{1,0:T(8,128)S(1)} collective-permute-done((f32[64,128]{1,0:T(8,128)S(1)}, f32[64,128]{1,0:T(8,128)S(1)}, u32[]{:S(2)}, u32[]{:S(2)}) %collective-permute-start.15) | collective-permute-done | bytes 32800 | tf_op jit(solution)/shard_map/ppermute | solution.py:363
  102.3 2.9 %downward.1.on_leaf = f32[16,64,128]{2,1,0:T(8,128)S(1)} custom-call(s32[16]{0:T(128)S(1)} %broadcast_subtract_fusion.1.parent.refs_0_, f32[64,128]{1,0:T(8,128)S(1)} %collective-permute-done.refs_1_, f32[64,128]{1,0:T(8,128)S(1)} %get-tuple-element.55.refs_2_, f32[64,128]{1,0:T(8,128)S(1)} %collective-permute-done.3.refs_1_.refs_3_, ...), custom_call_target="tpu_custom_call" | custom-call | flops 1000 | bytes 1000 | tf_op jit(solution)/shard_map/downward/pallas_call | solution.py:200
  105.2 8.5 %final.1 = bf16[16,256,128]{2,1,0:T(8,128)(2,1)} custom-call(s32[256]{0:T(256)S(1)} %reshape.14.rows, bf16[16,64,1024]{2,1,0:T(8,128)(2,1)S(1)} %weights.1.packed, bf16[256,64,128]{2,1,0:T(8,128)(2,1)} %all-gather.2.cloned.1.call-done.coefs, f32[16,64,128]{2,1,0:T(8,128)S(1)} %downward.1.on_leaf, bf16[16,64,256]{2,1,0:T(8,128)(2,1)} %bitcast.15, ...), custom_call_target="tpu_custom_call" | custom-call | flops 1000 | bytes 1000 | tf_op jit(solution)/shard_map/final/pallas_call | solution.py:326
  (30 shorter events, 0.9 us)
Async XLA Ops:
  6.5 98.7 %all-gather.2.cloned.1.call-start = ((), (), s32[]{:S(2)}) async-start(), calls=%async_computation | async-start | bytes 4456448 | tf_op jit(solution)/shard_map/all_gather | solution.py:395
  10.9 13.3 %collective-permute-start = (f32[64,128]{1,0:T(8,128)S(1)}, f32[64,128]{1,0:T(8,128)S(1)}, u32[]{:S(2)}, u32[]{:S(2)}) collective-permute-start(f32[64,128]{1,0:T(8,128)S(1)} %get-tuple-element.44.refs_0_), channel_id=1, source_target_pairs={{0,1},{1,0},{2,3},{3,2},{4,5},{5,4},{6,7},{7,6},{8,9},{9,8},{10,11... | collective-permute-start | bytes 98312 | tf_op jit(solution)/shard_map/ppermute | solution.py:363
  13.0 11.2 %collective-permute-start.1 = (f32[64,128]{1,0:T(8,128)S(1)}, f32[64,128]{1,0:T(8,128)S(1)}, u32[]{:S(2)}, u32[]{:S(2)}) collective-permute-start(f32[64,128]{1,0:T(8,128)S(1)} %get-tuple-element.44.refs_0_), channel_id=1, source_target_pairs={{0,2},{1,3},{2,0},{3,1},{4,6},{5,7},{6,4},{7,5},{8,10},{9,11},{10,... | collective-permute-start | bytes 98312 | tf_op jit(solution)/shard_map/ppermute | solution.py:363
  15.4 8.8 %collective-permute-start.2 = (f32[64,128]{1,0:T(8,128)S(1)}, f32[64,128]{1,0:T(8,128)S(1)}, u32[]{:S(2)}, u32[]{:S(2)}) collective-permute-start(f32[64,128]{1,0:T(8,128)S(1)} %get-tuple-element.44.refs_0_), channel_id=1, source_target_pairs={{0,3},{1,2},{2,1},{3,0},{4,7},{5,6},{6,5},{7,4},{8,11},{9,10},{10,... | collective-permute-start | bytes 98312 | tf_op jit(solution)/shard_map/ppermute | solution.py:363
  17.1 36.9 %collective-permute-start.4 = (bf16[16,256,128]{2,1,0:T(8,128)(2,1)}, bf16[16,256,128]{2,1,0:T(8,128)(2,1)S(1)}, u32[]{:S(2)}, u32[]{:S(2)}) collective-permute-start(bf16[16,256,128]{2,1,0:T(8,128)(2,1)} %bitcast.7), channel_id=1, source_target_pairs={{0,16},{16,32},{32,48},{48,64},{64,80},{80,96},{96,112},{1,17},{17... | collective-permute-start | bytes 3145736 | tf_op jit(solution)/shard_map/ppermute | solution.py:351
  22.2 31.8 %collective-permute-start.5 = (bf16[16,256,128]{2,1,0:T(8,128)(2,1)}, bf16[16,256,128]{2,1,0:T(8,128)(2,1)}, u32[]{:S(2)}, u32[]{:S(2)}) collective-permute-start(bf16[16,256,128]{2,1,0:T(8,128)(2,1)} %bitcast.8), channel_id=1, source_target_pairs={{16,0},{32,16},{48,32},{64,48},{80,64},{96,80},{112,96},{17,1},{33... | collective-permute-start | bytes 3145736 | tf_op jit(solution)/shard_map/ppermute | solution.py:351
  24.2 30.8 %collective-permute-start.6 = (bf16[16,256,128]{2,1,0:T(8,128)(2,1)}, bf16[16,256,128]{2,1,0:T(8,128)(2,1)}, u32[]{:S(2)}, u32[]{:S(2)}) collective-permute-start(bf16[16,256,128]{2,1,0:T(8,128)(2,1)} %bitcast.9), channel_id=1, source_target_pairs={{0,1},{1,2},{2,3},{3,4},{4,5},{5,6},{6,7},{7,8},{8,9},{9,10},{10,1... | collective-permute-start | bytes 3145736 | tf_op jit(solution)/shard_map/ppermute | solution.py:351
  24.3 30.8 %collective-permute-start.7 = (bf16[16,256,128]{2,1,0:T(8,128)(2,1)}, bf16[16,256,128]{2,1,0:T(8,128)(2,1)}, u32[]{:S(2)}, u32[]{:S(2)}) collective-permute-start(bf16[16,256,128]{2,1,0:T(8,128)(2,1)} %bitcast.10), channel_id=1, source_target_pairs={{0,15},{1,0},{2,1},{3,2},{4,3},{5,4},{6,5},{7,6},{8,7},{9,8},{10,9... | collective-permute-start | bytes 3145736 | tf_op jit(solution)/shard_map/ppermute | solution.py:351
  29.4 8.2 %copy-start.3 = (s32[16]{0:T(128)S(1)}, s32[16]{0:T(128)}, u32[]{:S(2)}) copy-start(s32[16]{0:T(128)} %count.1) | copy-start | bytes 196
  37.5 48.9 %copy-start = (bf16[4096,128]{1,0:T(8,128)(2,1)S(1)}, bf16[4096,128]{1,0:T(8,128)(2,1)}, u32[]{:S(2)}) copy-start(bf16[4096,128]{1,0:T(8,128)(2,1)} %param.12) | copy-start | bytes 3145732
  37.5 16.5 %collective-permute-start.3 = (f32[64,128]{1,0:T(8,128)S(1)}, f32[64,128]{1,0:T(8,128)S(1)}, u32[]{:S(2)}, u32[]{:S(2)}) collective-permute-start(f32[64,128]{1,0:T(8,128)S(1)} %get-tuple-element.57.refs_0_), channel_id=1, source_target_pairs={{0,4},{1,5},{2,6},{3,7},{4,0},{5,1},{6,2},{7,3},{8,12},{9,13},{10,... | collective-permute-start | bytes 98312 | tf_op jit(solution)/shard_map/ppermute | solution.py:363
  55.0 22.1 %collective-permute-start.11 = (bf16[16,256,128]{2,1,0:T(8,128)(2,1)}, bf16[16,256,128]{2,1,0:T(8,128)(2,1)S(1)}, u32[]{:S(2)}, u32[]{:S(2)}) collective-permute-start(bf16[16,256,128]{2,1,0:T(8,128)(2,1)} %collective-permute-done.6.refs_3_), channel_id=1, source_target_pairs={{16,0},{32,16},{48,32},{64,48},{80,64},{96,80},{112,96},{17,1},{33... | collective-permute-start | bytes 3145736 | tf_op jit(solution)/shard_map/ppermute | solution.py:351
  57.0 20.2 %collective-permute-start.12 = (bf16[16,256,128]{2,1,0:T(8,128)(2,1)}, bf16[16,256,128]{2,1,0:T(8,128)(2,1)S(1)}, u32[]{:S(2)}, u32[]{:S(2)}) collective-permute-start(bf16[16,256,128]{2,1,0:T(8,128)(2,1)} %collective-permute-done.6.refs_3_), channel_id=1, source_target_pairs={{0,16},{16,32},{32,48},{48,64},{64,80},{80,96},{96,112},{1,17},{17... | collective-permute-start | bytes 3145736 | tf_op jit(solution)/shard_map/ppermute | solution.py:351
  62.7 22.7 %collective-permute-start.13 = (bf16[16,256,128]{2,1,0:T(8,128)(2,1)}, bf16[16,256,128]{2,1,0:T(8,128)(2,1)S(1)}, u32[]{:S(2)}, u32[]{:S(2)}) collective-permute-start(bf16[16,256,128]{2,1,0:T(8,128)(2,1)} %collective-permute-done.7.refs_6_), channel_id=1, source_target_pairs={{16,0},{32,16},{48,32},{64,48},{80,64},{96,80},{112,96},{17,1},{33... | collective-permute-start | bytes 3145736 | tf_op jit(solution)/shard_map/ppermute | solution.py:351
  64.7 21.7 %collective-permute-start.14 = (bf16[16,256,128]{2,1,0:T(8,128)(2,1)}, bf16[16,256,128]{2,1,0:T(8,128)(2,1)S(1)}, u32[]{:S(2)}, u32[]{:S(2)}) collective-permute-start(bf16[16,256,128]{2,1,0:T(8,128)(2,1)} %collective-permute-done.7.refs_6_), channel_id=1, source_target_pairs={{0,16},{16,32},{32,48},{48,64},{64,80},{80,96},{96,112},{1,17},{17... | collective-permute-start | bytes 3145736 | tf_op jit(solution)/shard_map/ppermute | solution.py:351
  68.6 5.2 %collective-permute-start.8 = (f32[64,128]{1,0:T(8,128)S(1)}, f32[64,128]{1,0:T(8,128)S(1)}, u32[]{:S(2)}, u32[]{:S(2)}) collective-permute-start(f32[64,128]{1,0:T(8,128)S(1)} %combine.4.refs_0_), channel_id=1, source_target_pairs={{0,8},{1,9},{2,10},{3,11},{4,12},{5,13},{6,14},{7,15},{8,0},{9,1},... | collective-permute-start | bytes 98312 | tf_op jit(solution)/shard_map/ppermute | solution.py:363
  74.0 1.3 %collective-permute-start.9 = (f32[64,128]{1,0:T(8,128)S(1)}, f32[64,128]{1,0:T(8,128)S(1)}, u32[]{:S(2)}, u32[]{:S(2)}) collective-permute-start(f32[64,128]{1,0:T(8,128)S(1)} %combine.5.refs_0_), channel_id=1, source_target_pairs={{0,16},{1,17},{2,18},{3,19},{4,20},{5,21},{6,22},{7,23},{8,24},{9,... | collective-permute-start | bytes 98312 | tf_op jit(solution)/shard_map/ppermute | solution.py:363
  75.5 26.7 %copy-start.1 = (f32[16,64,64]{2,1,0:T(8,128)S(1)}, f32[16,64,64]{2,1,0:T(8,128)}, u32[]{:S(2)}) copy-start(f32[16,64,64]{2,1,0:T(8,128)} %refs_11_.1) | copy-start | bytes 786436
  75.6 26.7 %copy-start.2 = (f32[8,64,64]{2,1,0:T(8,128)S(1)}, f32[8,64,64]{2,1,0:T(8,128)}, u32[]{:S(2)}) copy-start(f32[8,64,64]{2,1,0:T(8,128)} %refs_10_.1) | copy-start | bytes 393220
  75.6 22.1 %collective-permute-start.10 = (f32[64,128]{1,0:T(8,128)S(1)}, f32[64,128]{1,0:T(8,128)S(1)}, u32[]{:S(2)}, u32[]{:S(2)}) collective-permute-start(f32[64,128]{1,0:T(8,128)S(1)} %combine.6.refs_0_), channel_id=1, source_target_pairs={{0,32},{1,33},{2,34},{3,35},{4,36},{5,37},{6,38},{7,39},{8,40},{9,... | collective-permute-start | bytes 98312 | tf_op jit(solution)/shard_map/ppermute | solution.py:363
  97.9 4.3 %collective-permute-start.15 = (f32[64,128]{1,0:T(8,128)S(1)}, f32[64,128]{1,0:T(8,128)S(1)}, u32[]{:S(2)}, u32[]{:S(2)}) collective-permute-start(f32[64,128]{1,0:T(8,128)S(1)} %combine.7), channel_id=1, source_target_pairs={{0,64},{1,65},{2,66},{3,67},{4,68},{5,69},{6,70},{7,71},{8,72},{9,... | collective-permute-start | bytes 98312 | tf_op jit(solution)/shard_map/ppermute | solution.py:363
Sparse Core Ops, SparseCore 0:
  11.0 75.8 all-gather.1

commit v6 on v5

--- a/solution.py
+++ b/solution.py
@@ -300,16 +300,17 @@
         for index, (source, target) in enumerate(((coefs, held), (on_leaf, term), (bases, basis)))
     ]
     nears = [pltpu.make_async_copy(near_part.at[leaf], close.at[leaf], near_sems.at[leaf]) for leaf in range(leaves)]
-    for load in loads:
-        load.start()
-    for load in loads:
-        load.wait()
-    for load in nears:
+    loads[0].start()
+    loads[0].wait()
+    for load in loads[1:] + nears:
         load.start()
     stores = []
     for leaf in range(leaves):
         for slot in range(slots):
             picked[leaf, slot * rank : (slot + 1) * rank] = held[rows[leaf * slots + slot]]
+        if leaf == 0:
+            loads[1].wait()
+            loads[2].wait()
         expansion = (term[leaf] + dot(packed[leaf], picked[leaf])).astype(bf16)
         nears[leaf].wait()
         results[leaf] = (dot_t(basis[leaf], expansion) + close[leaf]).astype(bf16)
@@ -402,30 +403,30 @@
     far_rows = (far_list - slab_pos * (sector_count * leaf_total)).reshape(-1)
 
     both_axes = ("slab", "sector")
-    quad = [root] + [partner(root, both_axes, flip) for flip in (1, 2, 3)]
-    shared, *quad = after(panels, *quad)
-    sides = both(shared, "sector", True)
-    later, position, far_rows = after(panels, position, far_rows)
-    below, above = both(later, "slab", False)
+    sides = both(panels, "sector", True)
     slots = jnp.arange(2 * depth + 2, dtype=jnp.int32)
     level_of = jnp.where(slots < 2 * depth, slots % depth, 0)
     flips = jnp.where(slots < 2 * depth, slots // depth, 2 + slots % 2)
     nodes = ((devices + device) >> level_of) ^ flips
-    nodes, position, far_rows, *quad = after(nodes, position, far_rows, *quad)
     transfer, coupling = tables(nodes[:, None], top_transfer, top_coupling)
-
+    below, above = both(panels, "slab", False)
+    packed = weights(far_count, far_coupling)
+
+    root, below, above, packed, transfer, position, far_rows = after(
+        root, below, above, packed, transfer, position, far_rows
+    )
+    quad = [root] + [partner(root, both_axes, flip) for flip in (1, 2, 3)]
+    flat = after(*quad, *sides)
+    quad, sides = flat[:4], flat[4:]
+    corners = [both(side, "slab", False) for side in sides]
+    pieces = [panels, above, below]
+    for side, corner in zip(sides, corners):
+        pieces += [side, corner[1], corner[0]]
     picks = (0, depth, 2 * depth, 2 * depth + 1, 1, depth + 1)
     across, current = combine_four(picks, quad, transfer)
     siblings = [quad[1], across]
-    packed = weights(far_count, far_coupling)
     for level in range(2, depth):
         sibling = partner(current, both_axes, 1 << level)
-        if level == 2:
-            current, sibling, packed, below, above, *sides = after(current, sibling, packed, below, above, *sides)
-            corners = [both(side, "slab", False) for side in sides]
-            pieces = [panels, above, below]
-            for side, corner in zip(sides, corners):
-                pieces += [side, corner[1], corner[0]]
         if level == depth - 2:
             near_part = near(position, near_blocks, pieces)
             current, sibling, near_part = after(current, sibling, near_part)

time: 121 us -> 119 us (0.983)
  waiting for transfers between devices: 29.7 us -> 23.7 us
  local copies, waits for them, and re-layouts: 0.35 us -> 2.93 us
  Pallas kernels: 39.5 us -> 40.9 us
  other arithmetic: 2.09 us -> 0.71 us
    ppermute x8, waiting for transfers between devices: 19.3 us -> 9.3 us  [partner(): lax.ppermute(array, axis, [(i, i ^ flip) for i in range(lax.axis_size(axi...]
    ppermute x8, waiting for transfers between devices: 10.3 us -> 14.4 us  [shifted(): return lax.ppermute(array, axis, pairs)]
    unnamed x8 -> x16, local copies, waits for them, and re-layouts: 0.02 us -> 2.69 us
    ppermute x8, starting transfers between devices: 9.93 us -> 11.8 us  [partner(): lax.ppermute(array, axis, [(i, i ^ flip) for i in range(lax.axis_size(axi...]
    ppermute x8, starting transfers between devices: 25.3 us -> 24 us  [shifted(): return lax.ppermute(array, axis, pairs)]
  transfers between devices with their start and end apart: 17 -> 17, of which waited for: 7 -> 9; matrix products, arithmetic and copies ran while one was open for 1% -> 0% of each run, Pallas kernels for 23% -> 24%
where the time goes in v6:
time: 119 us; the launch traced here: 118 us
  Pallas kernels  40.9 us (34%)
  starting transfers between devices  35.8 us (30%)
  waiting for transfers between devices  23.7 us (20%)
  between operations  13.6 us (11%)
  local copies, waits for them, and re-layouts  2.93 us (2%)
    ppermute x8, starting transfers between devices, shifted(): return lax.ppermute(array, axis, pairs)  24 us
    ppermute x8, waiting for transfers between devices, shifted(): return lax.ppermute(array, axis, pairs)  14.4 us
    ppermute x8, starting transfers between devices, partner(): lax.ppermute(array, axis, [(i, i ^ flip) for i in range(lax.axis_size(axi...  11.8 us
    pallas_call x1, Pallas kernels, near(): pl.pallas_call(near_kernel, out_shape=pltpu.HBM((leaves, size, rhs), f32)...  11.6 us
    pallas_call x1, Pallas kernels, final(): pl.pallas_call(final_kernel, out_shape=jax.ShapeDtypeStruct((leaves, size...  9.38 us
    ppermute x8, waiting for transfers between devices, partner(): lax.ppermute(array, axis, [(i, i ^ flip) for i in range(lax.axis_size(axi...  9.3 us
    pallas_call x1, Pallas kernels, tables(): pl.pallas_call(tables_kernel, out_shape=(jax.ShapeDtypeStruct((count, ran...  7.59 us
    pallas_call x1, Pallas kernels, weights(): pl.pallas_call(weights_kernel, out_shape=jax.ShapeDtypeStruct((leaves, ra...  4.27 us
  transfers between devices with their start and end apart: 17, of which 9 were waited for; matrix products, arithmetic and copies ran while one was open for 0% of the time, Pallas kernels for 24%

profile of v6, /device:TPU:1, one launch (start us, length us, event | category | flops | bytes accessed | tf_op | source)
XLA Modules:
  0.0 117.6 jit_solution(18153258680279824855)
XLA Ops:
  6.5 0.7 broadcast_subtract_fusion.1.parent.refs_0_
  7.2 3.6 %coefs.1 = (bf16[16,64,128]{2,1,0:T(8,128)(2,1)}, f32[64,128]{1,0:T(8,128)S(1)}) custom-call(s32[16]{0:T(128)S(1)} %broadcast_subtract_fusion.1.parent.refs_0_, bf16[16,256,128]{2,1,0:T(8,128)(2,1)} %bitcast.5, bf16[16,64,256]{2,1,0:T(8,128)(2,1)} %bitcast.13, f32[16,64,64]{2,1,0:T(8,128)} %refs_11_.1, f32[8,64,64]{2,1,0:T(8,128)} %refs_10_.1), custom_call_target="tpu_custom_call" | custom-call | flops 1000 | bytes 1000 | tf_op jit(solution)/shard_map/coefs/pallas_call | solution.py:84
  10.9 4.9 %collective-permute-start = (bf16[16,256,128]{2,1,0:T(8,128)(2,1)}, bf16[16,256,128]{2,1,0:T(8,128)(2,1)}, u32[]{:S(2)}, u32[]{:S(2)}) collective-permute-start(bf16[16,256,128]{2,1,0:T(8,128)(2,1)} %bitcast.6), channel_id=1, source_target_pairs={{0,16},{16,32},{32,48},{48,64},{64,80},{80,96},{96,112},{1,17},{17... | collective-permute-start | bytes 3145736 | tf_op jit(solution)/shard_map/ppermute | solution.py:352
  15.8 1.9 %collective-permute-start.1 = (bf16[16,256,128]{2,1,0:T(8,128)(2,1)}, bf16[16,256,128]{2,1,0:T(8,128)(2,1)}, u32[]{:S(2)}, u32[]{:S(2)}) collective-permute-start(bf16[16,256,128]{2,1,0:T(8,128)(2,1)} %bitcast.7), channel_id=1, source_target_pairs={{16,0},{32,16},{48,32},{64,48},{80,64},{96,80},{112,96},{17,1},{33... | collective-permute-start | bytes 3145736 | tf_op jit(solution)/shard_map/ppermute | solution.py:352
  17.7 1.3 %collective-permute-start.5 = (bf16[16,256,128]{2,1,0:T(8,128)(2,1)}, bf16[16,256,128]{2,1,0:T(8,128)(2,1)}, u32[]{:S(2)}, u32[]{:S(2)}) collective-permute-start(bf16[16,256,128]{2,1,0:T(8,128)(2,1)} %bitcast.8), channel_id=1, source_target_pairs={{0,1},{1,2},{2,3},{3,4},{4,5},{5,6},{6,7},{7,8},{8,9},{9,10},{10,1... | collective-permute-start | bytes 3145736 | tf_op jit(solution)/shard_map/ppermute | solution.py:352
  19.0 3.8 %collective-permute-start.6 = (bf16[16,256,128]{2,1,0:T(8,128)(2,1)}, bf16[16,256,128]{2,1,0:T(8,128)(2,1)}, u32[]{:S(2)}, u32[]{:S(2)}) collective-permute-start(bf16[16,256,128]{2,1,0:T(8,128)(2,1)} %bitcast.9), channel_id=1, source_target_pairs={{0,15},{1,0},{2,1},{3,2},{4,3},{5,4},{6,5},{7,6},{8,7},{9,8},{10,9... | collective-permute-start | bytes 3145736 | tf_op jit(solution)/shard_map/ppermute | solution.py:352
  22.8 0.7 copy-done.5
  23.5 4.3 %weights.1.packed = bf16[16,64,1024]{2,1,0:T(8,128)(2,1)S(1)} custom-call(s32[16]{0:T(128)S(1)} %copy-done.5, f32[16,16,64,64]{3,2,1,0:T(8,128)} %coupling.1), custom_call_target="tpu_custom_call" | custom-call | flops 1000 | bytes 1000 | tf_op jit(solution)/shard_map/weights/pallas_call | solution.py:229
  27.8 7.6 %tables.1 = (f32[16,64,64]{2,1,0:T(8,128)S(1)}, f32[16,64,64]{2,1,0:T(8,128)S(1)}) custom-call(s32[16,1]{1,0:T(8,128)S(1)} %fusion.11.nodes, f32[64,64,256]{2,1,0:T(8,128)} %bitcast.11, f32[64,64,256]{2,1,0:T(8,128)} %bitcast.12), custom_call_target="tpu_custom_call" | custom-call | flops 1000 | bytes 1000 | tf_op jit(solution)/shard_map/tables/pallas_call | solution.py:135
  35.4 0.8 copy-done.3
  36.7 3.8 %collective-permute-start.4 = (f32[64,128]{1,0:T(8,128)S(1)}, f32[64,128]{1,0:T(8,128)S(1)}, u32[]{:S(2)}, u32[]{:S(2)}) collective-permute-start(f32[64,128]{1,0:T(8,128)S(1)} %get-tuple-element.34.refs_0_), channel_id=1, source_target_pairs={{0,3},{1,2},{2,1},{3,0},{4,7},{5,6},{6,5},{7,4},{8,11},{9,10},{10,... | collective-permute-start | bytes 98312 | tf_op jit(solution)/shard_map/ppermute | solution.py:364
  40.5 9.5 %collective-permute-done.5.refs_3_ = bf16[16,256,128]{2,1,0:T(8,128)(2,1)} collective-permute-done((bf16[16,256,128]{2,1,0:T(8,128)(2,1)}, bf16[16,256,128]{2,1,0:T(8,128)(2,1)}, u32[]{:S(2)}, u32[]{:S(2)}) %collective-permute-start.5) | collective-permute-done | bytes 1048608 | tf_op jit(solution)/shard_map/ppermute | solution.py:352
  50.0 0.6 collective-permute-done.6.refs_6_
  50.8 1.9 %collective-permute-start.11 = (bf16[16,256,128]{2,1,0:T(8,128)(2,1)}, bf16[16,256,128]{2,1,0:T(8,128)(2,1)S(1)}, u32[]{:S(2)}, u32[]{:S(2)}) collective-permute-start(bf16[16,256,128]{2,1,0:T(8,128)(2,1)} %collective-permute-done.5.refs_3_), channel_id=1, source_target_pairs={{16,0},{32,16},{48,32},{64,48},{80,64},{96,80},{112,96},{17,1},{33... | collective-permute-start | bytes 3145736 | tf_op jit(solution)/shard_map/ppermute | solution.py:352
  52.7 4.6 %collective-permute-start.12 = (bf16[16,256,128]{2,1,0:T(8,128)(2,1)}, bf16[16,256,128]{2,1,0:T(8,128)(2,1)S(1)}, u32[]{:S(2)}, u32[]{:S(2)}) collective-permute-start(bf16[16,256,128]{2,1,0:T(8,128)(2,1)} %collective-permute-done.5.refs_3_), channel_id=1, source_target_pairs={{0,16},{16,32},{32,48},{48,64},{64,80},{80,96},{96,112},{1,17},{17... | collective-permute-start | bytes 3145736 | tf_op jit(solution)/shard_map/ppermute | solution.py:352
  57.4 1.9 %collective-permute-start.13 = (bf16[16,256,128]{2,1,0:T(8,128)(2,1)}, bf16[16,256,128]{2,1,0:T(8,128)(2,1)S(1)}, u32[]{:S(2)}, u32[]{:S(2)}) collective-permute-start(bf16[16,256,128]{2,1,0:T(8,128)(2,1)} %collective-permute-done.6.refs_6_), channel_id=1, source_target_pairs={{16,0},{32,16},{48,32},{64,48},{80,64},{96,80},{112,96},{17,1},{33... | collective-permute-start | bytes 3145736 | tf_op jit(solution)/shard_map/ppermute | solution.py:352
  59.3 3.6 %collective-permute-start.14 = (bf16[16,256,128]{2,1,0:T(8,128)(2,1)}, bf16[16,256,128]{2,1,0:T(8,128)(2,1)S(1)}, u32[]{:S(2)}, u32[]{:S(2)}) collective-permute-start(bf16[16,256,128]{2,1,0:T(8,128)(2,1)} %collective-permute-done.6.refs_6_), channel_id=1, source_target_pairs={{0,16},{16,32},{32,48},{48,64},{64,80},{80,96},{96,112},{1,17},{17... | collective-permute-start | bytes 3145736 | tf_op jit(solution)/shard_map/ppermute | solution.py:352
  63.5 0.7 collective-permute-start.7
  64.2 3.2 %collective-permute-done.7.refs_1_.refs_3_ = f32[64,128]{1,0:T(8,128)S(1)} collective-permute-done((f32[64,128]{1,0:T(8,128)S(1)}, f32[64,128]{1,0:T(8,128)S(1)}, u32[]{:S(2)}, u32[]{:S(2)}) %collective-permute-start.7) | collective-permute-done | bytes 32800 | tf_op jit(solution)/shard_map/ppermute | solution.py:364
  67.7 2.4 %collective-permute-start.8 = (f32[64,128]{1,0:T(8,128)S(1)}, f32[64,128]{1,0:T(8,128)S(1)}, u32[]{:S(2)}, u32[]{:S(2)}) collective-permute-start(f32[64,128]{1,0:T(8,128)S(1)} %combine.4.refs_0_), channel_id=1, source_target_pairs={{0,8},{1,9},{2,10},{3,11},{4,12},{5,13},{6,14},{7,15},{8,0},{9,1},... | collective-permute-start | bytes 98312 | tf_op jit(solution)/shard_map/ppermute | solution.py:364
  70.1 3.3 %collective-permute-done.8.refs_1_.refs_4_ = f32[64,128]{1,0:T(8,128)S(1)} collective-permute-done((f32[64,128]{1,0:T(8,128)S(1)}, f32[64,128]{1,0:T(8,128)S(1)}, u32[]{:S(2)}, u32[]{:S(2)}) %collective-permute-start.8) | collective-permute-done | bytes 32800 | tf_op jit(solution)/shard_map/ppermute | solution.py:364
  73.6 0.5 collective-permute-start.9
  74.1 0.9 collective-permute-done.9.refs_1_.refs_5_
  75.2 1.6 %collective-permute-start.10 = (f32[64,128]{1,0:T(8,128)S(1)}, f32[64,128]{1,0:T(8,128)S(1)}, u32[]{:S(2)}, u32[]{:S(2)}) collective-permute-start(f32[64,128]{1,0:T(8,128)S(1)} %combine.6.refs_0_), channel_id=1, source_target_pairs={{0,32},{1,33},{2,34},{3,35},{4,36},{5,37},{6,38},{7,39},{8,40},{9,... | collective-permute-start | bytes 98312 | tf_op jit(solution)/shard_map/ppermute | solution.py:364
  76.8 3.3 %collective-permute-done.13.refs_7_ = bf16[16,256,128]{2,1,0:T(8,128)(2,1)S(1)} collective-permute-done((bf16[16,256,128]{2,1,0:T(8,128)(2,1)}, bf16[16,256,128]{2,1,0:T(8,128)(2,1)S(1)}, u32[]{:S(2)}, u32[]{:S(2)}) %collective-permute-start.13) | collective-permute-done | bytes 1048608 | tf_op jit(solution)/shard_map/ppermute | solution.py:352
  80.1 0.9 collective-permute-done.14.refs_8_
  81.0 1.2 %copy-done = bf16[4096,128]{1,0:T(8,128)(2,1)S(1)} copy-done((bf16[4096,128]{1,0:T(8,128)(2,1)S(1)}, bf16[4096,128]{1,0:T(8,128)(2,1)}, u32[]{:S(2)}) %copy-start) | copy-done | bytes 1048600
  82.2 11.6 %near.1.near_part = f32[16,256,128]{2,1,0:T(8,128)} custom-call(s32[128]{0:T(128)S(1)} %reshape.101.position, bf16[16,8,256,256]{3,2,1,0:T(8,128)(2,1)} %blocks.1, bf16[16,256,128]{2,1,0:T(8,128)(2,1)S(1)} %bitcast.10, bf16[16,256,128]{2,1,0:T(8,128)(2,1)} %collective-permute-done.1.refs_1_, bf16[16,256,128]{2,1,0:T(8,128)(2,1)} %collective-permute-done.refs_2_, ...), custom_call_target="tpu_custom_call" | custom-call | flops 1000 | bytes 1000 | tf_op jit(solution)/shard_map/near/pallas_call | solution.py:275
  94.1 2.7 %collective-permute-start.15 = (f32[64,128]{1,0:T(8,128)S(1)}, f32[64,128]{1,0:T(8,128)S(1)}, u32[]{:S(2)}, u32[]{:S(2)}) collective-permute-start(f32[64,128]{1,0:T(8,128)S(1)} %combine.7), channel_id=1, source_target_pairs={{0,64},{1,65},{2,66},{3,67},{4,68},{5,69},{6,70},{7,71},{8,72},{9,... | collective-permute-start | bytes 98312 | tf_op jit(solution)/shard_map/ppermute | solution.py:364
  96.7 1.7 %collective-permute-done.15.refs_7_ = f32[64,128]{1,0:T(8,128)S(1)} collective-permute-done((f32[64,128]{1,0:T(8,128)S(1)}, f32[64,128]{1,0:T(8,128)S(1)}, u32[]{:S(2)}, u32[]{:S(2)}) %collective-permute-start.15) | collective-permute-done | bytes 32800 | tf_op jit(solution)/shard_map/ppermute | solution.py:364
  98.4 2.9 %downward.1.on_leaf = f32[16,64,128]{2,1,0:T(8,128)S(1)} custom-call(s32[16]{0:T(128)S(1)} %broadcast_subtract_fusion.1.parent.refs_0_, f32[64,128]{1,0:T(8,128)S(1)} %collective-permute-done.2.refs_1_, f32[64,128]{1,0:T(8,128)S(1)} %get-tuple-element.38.refs_2_, f32[64,128]{1,0:T(8,128)S(1)} %collective-permute-done.7.refs_1_.refs_3_, ...), custom_call_target="tpu_custom_call" | custom-call | flops 1000 | bytes 1000 | tf_op jit(solution)/shard_map/downward/pallas_call | solution.py:200
  101.4 9.4 %final.1 = bf16[16,256,128]{2,1,0:T(8,128)(2,1)} custom-call(s32[256]{0:T(256)S(1)} %reshape.102.rows, bf16[16,64,1024]{2,1,0:T(8,128)(2,1)S(1)} %weights.1.packed, bf16[256,64,128]{2,1,0:T(8,128)(2,1)} %all-gather.2.cloned.1.call-done.coefs, f32[16,64,128]{2,1,0:T(8,128)S(1)} %downward.1.on_leaf, bf16[16,64,256]{2,1,0:T(8,128)(2,1)} %bitcast.14, ...), custom_call_target="tpu_custom_call" | custom-call | flops 1000 | bytes 1000 | tf_op jit(solution)/shard_map/final/pallas_call | solution.py:327
  (37 shorter events, 2.3 us)
Async XLA Ops:
  6.5 94.8 %all-gather.2.cloned.1.call-start = ((), (), s32[]{:S(2)}) async-start(), calls=%async_computation | async-start | bytes 4456448 | tf_op jit(solution)/shard_map/all_gather | solution.py:396
  10.9 25.6 %collective-permute-start = (bf16[16,256,128]{2,1,0:T(8,128)(2,1)}, bf16[16,256,128]{2,1,0:T(8,128)(2,1)}, u32[]{:S(2)}, u32[]{:S(2)}) collective-permute-start(bf16[16,256,128]{2,1,0:T(8,128)(2,1)} %bitcast.6), channel_id=1, source_target_pairs={{0,16},{16,32},{32,48},{48,64},{64,80},{80,96},{96,112},{1,17},{17... | collective-permute-start | bytes 3145736 | tf_op jit(solution)/shard_map/ppermute | solution.py:352
  15.8 20.7 %collective-permute-start.1 = (bf16[16,256,128]{2,1,0:T(8,128)(2,1)}, bf16[16,256,128]{2,1,0:T(8,128)(2,1)}, u32[]{:S(2)}, u32[]{:S(2)}) collective-permute-start(bf16[16,256,128]{2,1,0:T(8,128)(2,1)} %bitcast.7), channel_id=1, source_target_pairs={{16,0},{32,16},{48,32},{64,48},{80,64},{96,80},{112,96},{17,1},{33... | collective-permute-start | bytes 3145736 | tf_op jit(solution)/shard_map/ppermute | solution.py:352
  17.7 32.2 %collective-permute-start.5 = (bf16[16,256,128]{2,1,0:T(8,128)(2,1)}, bf16[16,256,128]{2,1,0:T(8,128)(2,1)}, u32[]{:S(2)}, u32[]{:S(2)}) collective-permute-start(bf16[16,256,128]{2,1,0:T(8,128)(2,1)} %bitcast.8), channel_id=1, source_target_pairs={{0,1},{1,2},{2,3},{3,4},{4,5},{5,6},{6,7},{7,8},{8,9},{9,10},{10,1... | collective-permute-start | bytes 3145736 | tf_op jit(solution)/shard_map/ppermute | solution.py:352
  19.0 31.6 %collective-permute-start.6 = (bf16[16,256,128]{2,1,0:T(8,128)(2,1)}, bf16[16,256,128]{2,1,0:T(8,128)(2,1)}, u32[]{:S(2)}, u32[]{:S(2)}) collective-permute-start(bf16[16,256,128]{2,1,0:T(8,128)(2,1)} %bitcast.9), channel_id=1, source_target_pairs={{0,15},{1,0},{2,1},{3,2},{4,3},{5,4},{6,5},{7,6},{8,7},{9,8},{10,9... | collective-permute-start | bytes 3145736 | tf_op jit(solution)/shard_map/ppermute | solution.py:352
  22.8 0.7 copy-start.5
  27.8 8.4 %copy-start.7 = (s32[16,8]{0,1:T(8,128)S(1)}, s32[16,8]{0,1:T(8,128)}, u32[]{:S(2)}) copy-start(s32[16,8]{0,1:T(8,128)} %param.19) | copy-start | bytes 1540
  27.8 8.6 %copy-start.6 = (s32[16,16]{1,0:T(8,128)S(1)}, s32[16,16]{1,0:T(8,128)}, u32[]{:S(2)}) copy-start(s32[16,16]{1,0:T(8,128)} %param.21) | copy-start | bytes 3076
  35.4 0.8 copy-start.3
  36.5 14.1 %collective-permute-start.2 = (f32[64,128]{1,0:T(8,128)S(1)}, f32[64,128]{1,0:T(8,128)S(1)}, u32[]{:S(2)}, u32[]{:S(2)}) collective-permute-start(f32[64,128]{1,0:T(8,128)S(1)} %get-tuple-element.34.refs_0_), channel_id=1, source_target_pairs={{0,1},{1,0},{2,3},{3,2},{4,5},{5,4},{6,7},{7,6},{8,9},{9,8},{10,11... | collective-permute-start | bytes 98312 | tf_op jit(solution)/shard_map/ppermute | solution.py:364
  36.6 14.0 %collective-permute-start.3 = (f32[64,128]{1,0:T(8,128)S(1)}, f32[64,128]{1,0:T(8,128)S(1)}, u32[]{:S(2)}, u32[]{:S(2)}) collective-permute-start(f32[64,128]{1,0:T(8,128)S(1)} %get-tuple-element.34.refs_0_), channel_id=1, source_target_pairs={{0,2},{1,3},{2,0},{3,1},{4,6},{5,7},{6,4},{7,5},{8,10},{9,11},{10,... | collective-permute-start | bytes 98312 | tf_op jit(solution)/shard_map/ppermute | solution.py:364
  36.7 14.1 %collective-permute-start.4 = (f32[64,128]{1,0:T(8,128)S(1)}, f32[64,128]{1,0:T(8,128)S(1)}, u32[]{:S(2)}, u32[]{:S(2)}) collective-permute-start(f32[64,128]{1,0:T(8,128)S(1)} %get-tuple-element.34.refs_0_), channel_id=1, source_target_pairs={{0,3},{1,2},{2,1},{3,0},{4,7},{5,6},{6,5},{7,4},{8,11},{9,10},{10,... | collective-permute-start | bytes 98312 | tf_op jit(solution)/shard_map/ppermute | solution.py:364
  50.8 25.9 %collective-permute-start.11 = (bf16[16,256,128]{2,1,0:T(8,128)(2,1)}, bf16[16,256,128]{2,1,0:T(8,128)(2,1)S(1)}, u32[]{:S(2)}, u32[]{:S(2)}) collective-permute-start(bf16[16,256,128]{2,1,0:T(8,128)(2,1)} %collective-permute-done.5.refs_3_), channel_id=1, source_target_pairs={{16,0},{32,16},{48,32},{64,48},{80,64},{96,80},{112,96},{17,1},{33... | collective-permute-start | bytes 3145736 | tf_op jit(solution)/shard_map/ppermute | solution.py:352
  52.7 24.0 %collective-permute-start.12 = (bf16[16,256,128]{2,1,0:T(8,128)(2,1)}, bf16[16,256,128]{2,1,0:T(8,128)(2,1)S(1)}, u32[]{:S(2)}, u32[]{:S(2)}) collective-permute-start(bf16[16,256,128]{2,1,0:T(8,128)(2,1)} %collective-permute-done.5.refs_3_), channel_id=1, source_target_pairs={{0,16},{16,32},{32,48},{48,64},{64,80},{80,96},{96,112},{1,17},{17... | collective-permute-start | bytes 3145736 | tf_op jit(solution)/shard_map/ppermute | solution.py:352
  57.4 22.7 %collective-permute-start.13 = (bf16[16,256,128]{2,1,0:T(8,128)(2,1)}, bf16[16,256,128]{2,1,0:T(8,128)(2,1)S(1)}, u32[]{:S(2)}, u32[]{:S(2)}) collective-permute-start(bf16[16,256,128]{2,1,0:T(8,128)(2,1)} %collective-permute-done.6.refs_6_), channel_id=1, source_target_pairs={{16,0},{32,16},{48,32},{64,48},{80,64},{96,80},{112,96},{17,1},{33... | collective-permute-start | bytes 3145736 | tf_op jit(solution)/shard_map/ppermute | solution.py:352
  59.3 21.7 %collective-permute-start.14 = (bf16[16,256,128]{2,1,0:T(8,128)(2,1)}, bf16[16,256,128]{2,1,0:T(8,128)(2,1)S(1)}, u32[]{:S(2)}, u32[]{:S(2)}) collective-permute-start(bf16[16,256,128]{2,1,0:T(8,128)(2,1)} %collective-permute-done.6.refs_6_), channel_id=1, source_target_pairs={{0,16},{16,32},{32,48},{48,64},{64,80},{80,96},{96,112},{1,17},{17... | collective-permute-start | bytes 3145736 | tf_op jit(solution)/shard_map/ppermute | solution.py:352
  63.5 3.9 %collective-permute-start.7 = (f32[64,128]{1,0:T(8,128)S(1)}, f32[64,128]{1,0:T(8,128)S(1)}, u32[]{:S(2)}, u32[]{:S(2)}) collective-permute-start(f32[64,128]{1,0:T(8,128)S(1)} %get-tuple-element.39.refs_0_), channel_id=1, source_target_pairs={{0,4},{1,5},{2,6},{3,7},{4,0},{5,1},{6,2},{7,3},{8,12},{9,13},{10,... | collective-permute-start | bytes 98312 | tf_op jit(solution)/shard_map/ppermute | solution.py:364
  67.7 5.7 %collective-permute-start.8 = (f32[64,128]{1,0:T(8,128)S(1)}, f32[64,128]{1,0:T(8,128)S(1)}, u32[]{:S(2)}, u32[]{:S(2)}) collective-permute-start(f32[64,128]{1,0:T(8,128)S(1)} %combine.4.refs_0_), channel_id=1, source_target_pairs={{0,8},{1,9},{2,10},{3,11},{4,12},{5,13},{6,14},{7,15},{8,0},{9,1},... | collective-permute-start | bytes 98312 | tf_op jit(solution)/shard_map/ppermute | solution.py:364
  73.3 25.1 %copy-start.2 = (f32[8,64,64]{2,1,0:T(8,128)S(1)}, f32[8,64,64]{2,1,0:T(8,128)}, u32[]{:S(2)}) copy-start(f32[8,64,64]{2,1,0:T(8,128)} %refs_10_.1) | copy-start | bytes 393220
  73.6 1.4 %collective-permute-start.9 = (f32[64,128]{1,0:T(8,128)S(1)}, f32[64,128]{1,0:T(8,128)S(1)}, u32[]{:S(2)}, u32[]{:S(2)}) collective-permute-start(f32[64,128]{1,0:T(8,128)S(1)} %combine.5.refs_0_), channel_id=1, source_target_pairs={{0,16},{1,17},{2,18},{3,19},{4,20},{5,21},{6,22},{7,23},{8,24},{9,... | collective-permute-start | bytes 98312 | tf_op jit(solution)/shard_map/ppermute | solution.py:364
  75.0 23.5 %copy-start.1 = (f32[16,64,64]{2,1,0:T(8,128)S(1)}, f32[16,64,64]{2,1,0:T(8,128)}, u32[]{:S(2)}) copy-start(f32[16,64,64]{2,1,0:T(8,128)} %refs_11_.1) | copy-start | bytes 786436
  75.2 18.6 %collective-permute-start.10 = (f32[64,128]{1,0:T(8,128)S(1)}, f32[64,128]{1,0:T(8,128)S(1)}, u32[]{:S(2)}, u32[]{:S(2)}) collective-permute-start(f32[64,128]{1,0:T(8,128)S(1)} %combine.6.refs_0_), channel_id=1, source_target_pairs={{0,32},{1,33},{2,34},{3,35},{4,36},{5,37},{6,38},{7,39},{8,40},{9,... | collective-permute-start | bytes 98312 | tf_op jit(solution)/shard_map/ppermute | solution.py:364
  81.0 1.2 %copy-start = (bf16[4096,128]{1,0:T(8,128)(2,1)S(1)}, bf16[4096,128]{1,0:T(8,128)(2,1)}, u32[]{:S(2)}) copy-start(bf16[4096,128]{1,0:T(8,128)(2,1)} %param.12) | copy-start | bytes 3145732
  82.2 16.2 %copy-start.4 = (f32[16,64,64]{2,1,0:T(8,128)S(1)}, f32[16,64,64]{2,1,0:T(8,128)}, u32[]{:S(2)}) copy-start(f32[16,64,64]{2,1,0:T(8,128)} %copy-done.3) | copy-start | bytes 786436
  94.1 4.3 %collective-permute-start.15 = (f32[64,128]{1,0:T(8,128)S(1)}, f32[64,128]{1,0:T(8,128)S(1)}, u32[]{:S(2)}, u32[]{:S(2)}) collective-permute-start(f32[64,128]{1,0:T(8,128)S(1)} %combine.7), channel_id=1, source_target_pairs={{0,64},{1,65},{2,66},{3,67},{4,68},{5,69},{6,70},{7,71},{8,72},{9,... | collective-permute-start | bytes 98312 | tf_op jit(solution)/shard_map/ppermute | solution.py:364
Sparse Core Ops, SparseCore 0:
  11.0 69.3 all-gather.1

commit v7 on v6

--- a/solution.py
+++ b/solution.py
@@ -5,17 +5,34 @@
 from jax.experimental.pallas import tpu as pltpu
 from jax.sharding import PartitionSpec as P
 
-highest = lax.Precision.HIGHEST
 f32 = jnp.float32
 bf16 = jnp.bfloat16
 
 
-def dot_t(a, b, precision=None):
-    return lax.dot_general(a, b, (((0,), (0,)), ((), ())), precision=precision, preferred_element_type=f32)
-
-
-def dot(a, b, precision=None):
-    return lax.dot_general(a, b, (((1,), (0,)), ((), ())), precision=precision, preferred_element_type=f32)
+def dot_t(a, b):
+    return lax.dot_general(a, b, (((0,), (0,)), ((), ())), preferred_element_type=f32)
+
+
+def dot(a, b):
+    return lax.dot_general(a, b, (((1,), (0,)), ((), ())), preferred_element_type=f32)
+
+
+def halves(a):
+    high = a.astype(bf16)
+    return high, (a - high.astype(f32)).astype(bf16)
+
+
+def fine(product, a, b):
+    (a_high, a_low), (b_high, b_low) = halves(a), halves(b)
+    return product(a_high, b_high) + (product(a_high, b_low) + product(a_low, b_high))
+
+
+def fine_t(a, b):
+    return fine(dot_t, a, b)
+
+
+def fine_dot(a, b):
+    return fine(dot, a, b)
 
 
 def dot_r(a, b):
@@ -71,10 +88,10 @@
     for tail in tails:
         tail.wait()
     for leaf, coefs in enumerate(exact):
-        clusters[parent[leaf]] += dot_t(up_held[leaf], coefs, highest)
-    total = dot_t(root_held[0], clusters[0], highest)
+        clusters[parent[leaf]] += fine_t(up_held[leaf], coefs)
+    total = fine_t(root_held[0], clusters[0])
     for cluster in range(1, root_held.shape[0]):
-        total = total + dot_t(root_held[cluster], clusters[cluster], highest)
+        total = total + fine_t(root_held[cluster], clusters[cluster])
     root_out[...] = total
 
 
@@ -145,8 +162,8 @@
 
 
 def combine_kernel(own, other, current, sibling, mats, out):
-    total = dot_t(mats[own], current[...], highest)
-    out[...] = total + dot_t(mats[other], sibling[...], highest)
+    total = fine_t(mats[own], current[...])
+    out[...] = total + fine_t(mats[other], sibling[...])
 
 
 def combine(own, other, current, sibling, mats):
@@ -163,10 +180,10 @@
 
 def combine_four_kernel(picks, root, one, two, three, mats, sibling_out, out):
     own, other, second, third, own_up, other_up = picks
-    sibling = dot_t(mats[second], two[...], highest) + dot_t(mats[third], three[...], highest)
+    sibling = fine_t(mats[second], two[...]) + fine_t(mats[third], three[...])
     sibling_out[...] = sibling
-    lower = dot_t(mats[own], root[...], highest) + dot_t(mats[other], one[...], highest)
-    out[...] = dot_t(mats[own_up], lower, highest) + dot_t(mats[other_up], sibling, highest)
+    lower = fine_t(mats[own], root[...]) + fine_t(mats[other], one[...])
+    out[...] = fine_t(mats[own_up], lower) + fine_t(mats[other_up], sibling)
 
 
 def combine_four(picks, roots, mats):
@@ -184,14 +201,14 @@
 def downward_kernel(depth, parent, *refs):
     siblings = refs[:depth]
     transfer, coupling, root, up, out, clusters = refs[depth:]
-    down = dot(coupling[depth - 1], siblings[depth - 1][...], highest)
+    down = fine_dot(coupling[depth - 1], siblings[depth - 1][...])
     for level in reversed(range(depth - 1)):
-        across = dot(coupling[level], siblings[level][...], highest)
-        down = across + dot(transfer[level], down, highest)
+        across = fine_dot(coupling[level], siblings[level][...])
+        down = across + fine_dot(transfer[level], down)
     for cluster in range(root.shape[0]):
-        clusters[cluster] = dot(root[cluster], down, highest)
+        clusters[cluster] = fine_dot(root[cluster], down)
     for leaf in range(up.shape[0]):
-        out[leaf] = dot(up[leaf], clusters[parent[leaf]], highest)
+        out[leaf] = fine_dot(up[leaf], clusters[parent[leaf]])
 
 
 def downward(local_parent, siblings, transfer, coupling, root_transfer, up_transfer):
@@ -300,17 +317,16 @@
         for index, (source, target) in enumerate(((coefs, held), (on_leaf, term), (bases, basis)))
     ]
     nears = [pltpu.make_async_copy(near_part.at[leaf], close.at[leaf], near_sems.at[leaf]) for leaf in range(leaves)]
-    loads[0].start()
-    loads[0].wait()
-    for load in loads[1:] + nears:
+    for load in loads:
+        load.start()
+    for load in loads:
+        load.wait()
+    for load in nears:
         load.start()
     stores = []
     for leaf in range(leaves):
         for slot in range(slots):
             picked[leaf, slot * rank : (slot + 1) * rank] = held[rows[leaf * slots + slot]]
-        if leaf == 0:
-            loads[1].wait()
-            loads[2].wait()
         expansion = (term[leaf] + dot(packed[leaf], picked[leaf])).astype(bf16)
         nears[leaf].wait()
         results[leaf] = (dot_t(basis[leaf], expansion) + close[leaf]).astype(bf16)
@@ -419,7 +435,7 @@
     flat = after(*quad, *sides)
     quad, sides = flat[:4], flat[4:]
     corners = [both(side, "slab", False) for side in sides]
-    pieces = [panels, above, below]
+    pieces = [in_hbm(panels), above, below]
     for side, corner in zip(sides, corners):
         pieces += [side, corner[1], corner[0]]
     picks = (0, depth, 2 * depth, 2 * depth + 1, 1, depth + 1)
@@ -427,7 +443,7 @@
     siblings = [quad[1], across]
     for level in range(2, depth):
         sibling = partner(current, both_axes, 1 << level)
-        if level == depth - 2:
+        if level == depth - 1:
             near_part = near(position, near_blocks, pieces)
             current, sibling, near_part = after(current, sibling, near_part)
         siblings.append(sibling)

time: 119 us -> 114 us (0.958)
  Pallas kernels: 40.9 us -> 38.9 us
  local copies, waits for them, and re-layouts: 2.93 us -> 1.73 us
    ppermute x8, waiting for transfers between devices: 14.4 us -> 10.1 us  [shifted(): return lax.ppermute(array, axis, pairs)]
    ppermute x8, waiting for transfers between devices: 9.3 us -> 12.7 us  [partner(): lax.ppermute(array, axis, [(i, i ^ flip) for i in range(lax.axis_size(axi...]
    unnamed x16 -> x14, local copies, waits for them, and re-layouts: 2.69 us -> 1.49 us
  transfers between devices with their start and end apart: 17 -> 17, of which waited for: 9 -> 7; matrix products, arithmetic and copies ran while one was open for 0% -> 0% of each run, Pallas kernels for 24% -> 24%
where the time goes in v7:
time: 114 us
  Pallas kernels  38.9 us (34%)
  starting transfers between devices  35.7 us (31%)
  waiting for transfers between devices  22.8 us (20%)
  between operations  13.7 us (12%)
  local copies, waits for them, and re-layouts  1.73 us (2%)
    ppermute x8, starting transfers between devices, shifted(): return lax.ppermute(array, axis, pairs)  24 us
    ppermute x8, waiting for transfers between devices, partner(): lax.ppermute(array, axis, [(i, i ^ flip) for i in range(lax.axis_size(axi...  12.7 us
    pallas_call x1, Pallas kernels, near(): pl.pallas_call(near_kernel, out_shape=pltpu.HBM((leaves, size, rhs), f32)...  11.8 us
    ppermute x8, starting transfers between devices, partner(): lax.ppermute(array, axis, [(i, i ^ flip) for i in range(lax.axis_size(axi...  11.6 us
    ppermute x8, waiting for transfers between devices, shifted(): return lax.ppermute(array, axis, pairs)  10.1 us
    pallas_call x1, Pallas kernels, final(): pl.pallas_call(final_kernel, out_shape=jax.ShapeDtypeStruct((leaves, size...  8.46 us
    pallas_call x1, Pallas kernels, tables(): pl.pallas_call(tables_kernel, out_shape=(jax.ShapeDtypeStruct((count, ran...  7.59 us
    pallas_call x1, Pallas kernels, weights(): pl.pallas_call(weights_kernel, out_shape=jax.ShapeDtypeStruct((leaves, ra...  4.27 us
  transfers between devices with their start and end apart: 17, of which 7 were waited for; matrix products, arithmetic and copies ran while one was open for 0% of the time, Pallas kernels for 24%

profile of v7, /device:TPU:1, one launch (start us, length us, event | category | flops | bytes accessed | tf_op | source)
XLA Modules:
  0.0 113.6 jit_solution(14405960884939997239)
XLA Ops:
  6.5 0.7 broadcast_subtract_fusion.1.parent.refs_0_
  7.2 3.4 %coefs.1 = (bf16[16,64,128]{2,1,0:T(8,128)(2,1)}, f32[64,128]{1,0:T(8,128)S(1)}) custom-call(s32[16]{0:T(128)S(1)} %broadcast_subtract_fusion.1.parent.refs_0_, bf16[16,256,128]{2,1,0:T(8,128)(2,1)} %bitcast.7, bf16[16,64,256]{2,1,0:T(8,128)(2,1)} %bitcast.13, f32[16,64,64]{2,1,0:T(8,128)} %refs_11_.1, f32[8,64,64]{2,1,0:T(8,128)} %refs_10_.1), custom_call_target="tpu_custom_call" | custom-call | flops 1000 | bytes 1000 | tf_op jit(solution)/shard_map/coefs/pallas_call | solution.py:101
  10.6 4.9 %collective-permute-start = (bf16[16,256,128]{2,1,0:T(8,128)(2,1)}, bf16[16,256,128]{2,1,0:T(8,128)(2,1)}, u32[]{:S(2)}, u32[]{:S(2)}) collective-permute-start(bf16[16,256,128]{2,1,0:T(8,128)(2,1)} %bitcast.8), channel_id=1, source_target_pairs={{0,16},{16,32},{32,48},{48,64},{64,80},{80,96},{96,112},{1,17},{17... | collective-permute-start | bytes 3145736 | tf_op jit(solution)/shard_map/ppermute | solution.py:368
  15.6 1.9 %collective-permute-start.1 = (bf16[16,256,128]{2,1,0:T(8,128)(2,1)}, bf16[16,256,128]{2,1,0:T(8,128)(2,1)}, u32[]{:S(2)}, u32[]{:S(2)}) collective-permute-start(bf16[16,256,128]{2,1,0:T(8,128)(2,1)} %bitcast.9), channel_id=1, source_target_pairs={{16,0},{32,16},{48,32},{64,48},{80,64},{96,80},{112,96},{17,1},{33... | collective-permute-start | bytes 3145736 | tf_op jit(solution)/shard_map/ppermute | solution.py:368
  17.5 1.3 %collective-permute-start.5 = (bf16[16,256,128]{2,1,0:T(8,128)(2,1)}, bf16[16,256,128]{2,1,0:T(8,128)(2,1)}, u32[]{:S(2)}, u32[]{:S(2)}) collective-permute-start(bf16[16,256,128]{2,1,0:T(8,128)(2,1)} %bitcast.10), channel_id=1, source_target_pairs={{0,1},{1,2},{2,3},{3,4},{4,5},{5,6},{6,7},{7,8},{8,9},{9,10},{10,1... | collective-permute-start | bytes 3145736 | tf_op jit(solution)/shard_map/ppermute | solution.py:368
  18.8 3.8 %collective-permute-start.6 = (bf16[16,256,128]{2,1,0:T(8,128)(2,1)}, bf16[16,256,128]{2,1,0:T(8,128)(2,1)}, u32[]{:S(2)}, u32[]{:S(2)}) collective-permute-start(bf16[16,256,128]{2,1,0:T(8,128)(2,1)} %bitcast.11), channel_id=1, source_target_pairs={{0,15},{1,0},{2,1},{3,2},{4,3},{5,4},{6,5},{7,6},{8,7},{9,8},{10,9... | collective-permute-start | bytes 3145736 | tf_op jit(solution)/shard_map/ppermute | solution.py:368
  22.6 0.7 copy-done.4
  23.3 4.3 %weights.1.packed = bf16[16,64,1024]{2,1,0:T(8,128)(2,1)S(1)} custom-call(s32[16]{0:T(128)S(1)} %copy-done.4, f32[16,16,64,64]{3,2,1,0:T(8,128)} %coupling.1), custom_call_target="tpu_custom_call" | custom-call | flops 1000 | bytes 1000 | tf_op jit(solution)/shard_map/weights/pallas_call | solution.py:246
  27.6 7.6 %tables.1 = (f32[16,64,64]{2,1,0:T(8,128)S(1)}, f32[16,64,64]{2,1,0:T(8,128)S(1)}) custom-call(s32[16,1]{1,0:T(8,128)S(1)} %fusion.11.nodes, f32[64,64,256]{2,1,0:T(8,128)} %bitcast.5, f32[64,64,256]{2,1,0:T(8,128)} %bitcast.6), custom_call_target="tpu_custom_call" | custom-call | flops 1000 | bytes 1000 | tf_op jit(solution)/shard_map/tables/pallas_call | solution.py:152
  35.2 0.8 copy-done.2
  36.5 3.8 %collective-permute-start.4 = (f32[64,128]{1,0:T(8,128)S(1)}, f32[64,128]{1,0:T(8,128)S(1)}, u32[]{:S(2)}, u32[]{:S(2)}) collective-permute-start(f32[64,128]{1,0:T(8,128)S(1)} %get-tuple-element.33.refs_0_), channel_id=1, source_target_pairs={{0,3},{1,2},{2,1},{3,0},{4,7},{5,6},{6,5},{7,4},{8,11},{9,10},{10,... | collective-permute-start | bytes 98312 | tf_op jit(solution)/shard_map/ppermute | solution.py:380
  40.2 9.5 %collective-permute-done.5.refs_3_ = bf16[16,256,128]{2,1,0:T(8,128)(2,1)} collective-permute-done((bf16[16,256,128]{2,1,0:T(8,128)(2,1)}, bf16[16,256,128]{2,1,0:T(8,128)(2,1)}, u32[]{:S(2)}, u32[]{:S(2)}) %collective-permute-start.5) | collective-permute-done | bytes 1048608 | tf_op jit(solution)/shard_map/ppermute | solution.py:368
  49.8 0.6 collective-permute-done.6.refs_6_
  50.4 0.2 collective-permute-done.4.refs_3_
  50.6 1.9 %collective-permute-start.12 = (bf16[16,256,128]{2,1,0:T(8,128)(2,1)}, bf16[16,256,128]{2,1,0:T(8,128)(2,1)S(1)}, u32[]{:S(2)}, u32[]{:S(2)}) collective-permute-start(bf16[16,256,128]{2,1,0:T(8,128)(2,1)} %collective-permute-done.5.refs_3_), channel_id=1, source_target_pairs={{16,0},{32,16},{48,32},{64,48},{80,64},{96,80},{112,96},{17,1},{33... | collective-permute-start | bytes 3145736 | tf_op jit(solution)/shard_map/ppermute | solution.py:368
  52.5 4.6 %collective-permute-start.13 = (bf16[16,256,128]{2,1,0:T(8,128)(2,1)}, bf16[16,256,128]{2,1,0:T(8,128)(2,1)S(1)}, u32[]{:S(2)}, u32[]{:S(2)}) collective-permute-start(bf16[16,256,128]{2,1,0:T(8,128)(2,1)} %collective-permute-done.5.refs_3_), channel_id=1, source_target_pairs={{0,16},{16,32},{32,48},{48,64},{64,80},{80,96},{96,112},{1,17},{17... | collective-permute-start | bytes 3145736 | tf_op jit(solution)/shard_map/ppermute | solution.py:368
  57.2 1.9 %collective-permute-start.14 = (bf16[16,256,128]{2,1,0:T(8,128)(2,1)}, bf16[16,256,128]{2,1,0:T(8,128)(2,1)S(1)}, u32[]{:S(2)}, u32[]{:S(2)}) collective-permute-start(bf16[16,256,128]{2,1,0:T(8,128)(2,1)} %collective-permute-done.6.refs_6_), channel_id=1, source_target_pairs={{16,0},{32,16},{48,32},{64,48},{80,64},{96,80},{112,96},{17,1},{33... | collective-permute-start | bytes 3145736 | tf_op jit(solution)/shard_map/ppermute | solution.py:368
  59.1 3.6 %collective-permute-start.15 = (bf16[16,256,128]{2,1,0:T(8,128)(2,1)}, bf16[16,256,128]{2,1,0:T(8,128)(2,1)S(1)}, u32[]{:S(2)}, u32[]{:S(2)}) collective-permute-start(bf16[16,256,128]{2,1,0:T(8,128)(2,1)} %collective-permute-done.6.refs_6_), channel_id=1, source_target_pairs={{0,16},{16,32},{32,48},{48,64},{64,80},{80,96},{96,112},{1,17},{17... | collective-permute-start | bytes 3145736 | tf_op jit(solution)/shard_map/ppermute | solution.py:368
  62.7 0.4 combine_four.1
  63.2 0.7 collective-permute-start.7
  63.9 3.2 %collective-permute-done.7.refs_1_.refs_3_ = f32[64,128]{1,0:T(8,128)S(1)} collective-permute-done((f32[64,128]{1,0:T(8,128)S(1)}, f32[64,128]{1,0:T(8,128)S(1)}, u32[]{:S(2)}, u32[]{:S(2)}) %collective-permute-start.7) | collective-permute-done | bytes 32800 | tf_op jit(solution)/shard_map/ppermute | solution.py:380
  67.3 2.3 %collective-permute-start.8 = (f32[64,128]{1,0:T(8,128)S(1)}, f32[64,128]{1,0:T(8,128)S(1)}, u32[]{:S(2)}, u32[]{:S(2)}) collective-permute-start(f32[64,128]{1,0:T(8,128)S(1)} %combine.4.refs_0_), channel_id=1, source_target_pairs={{0,8},{1,9},{2,10},{3,11},{4,12},{5,13},{6,14},{7,15},{8,0},{9,1},... | collective-permute-start | bytes 98312 | tf_op jit(solution)/shard_map/ppermute | solution.py:380
  69.6 3.3 %collective-permute-done.8.refs_1_.refs_4_ = f32[64,128]{1,0:T(8,128)S(1)} collective-permute-done((f32[64,128]{1,0:T(8,128)S(1)}, f32[64,128]{1,0:T(8,128)S(1)}, u32[]{:S(2)}, u32[]{:S(2)}) %collective-permute-start.8) | collective-permute-done | bytes 32800 | tf_op jit(solution)/shard_map/ppermute | solution.py:380
  72.9 0.2 combine.5.refs_0_
  73.1 0.5 collective-permute-start.9
  73.6 0.9 collective-permute-done.9.refs_1_.refs_5_
  74.6 1.3 %collective-permute-start.10 = (f32[64,128]{1,0:T(8,128)S(1)}, f32[64,128]{1,0:T(8,128)S(1)}, u32[]{:S(2)}, u32[]{:S(2)}) collective-permute-start(f32[64,128]{1,0:T(8,128)S(1)} %combine.6.refs_0_), channel_id=1, source_target_pairs={{0,32},{1,33},{2,34},{3,35},{4,36},{5,37},{6,38},{7,39},{8,40},{9,... | collective-permute-start | bytes 98312 | tf_op jit(solution)/shard_map/ppermute | solution.py:380
  76.0 5.1 %collective-permute-done.10.refs_1_.refs_6_ = f32[64,128]{1,0:T(8,128)S(1)} collective-permute-done((f32[64,128]{1,0:T(8,128)S(1)}, f32[64,128]{1,0:T(8,128)S(1)}, u32[]{:S(2)}, u32[]{:S(2)}) %collective-permute-start.10) | collective-permute-done | bytes 32800 | tf_op jit(solution)/shard_map/ppermute | solution.py:380
  81.3 2.9 %collective-permute-start.11 = (f32[64,128]{1,0:T(8,128)S(1)}, f32[64,128]{1,0:T(8,128)S(1)}, u32[]{:S(2)}, u32[]{:S(2)}) collective-permute-start(f32[64,128]{1,0:T(8,128)S(1)} %combine.7), channel_id=1, source_target_pairs={{0,64},{1,65},{2,66},{3,67},{4,68},{5,69},{6,70},{7,71},{8,72},{9,... | collective-permute-start | bytes 98312 | tf_op jit(solution)/shard_map/ppermute | solution.py:380
  84.1 11.8 %near.1.near_part = f32[16,256,128]{2,1,0:T(8,128)} custom-call(s32[128]{0:T(128)S(1)} %reshape.101.position, bf16[16,8,256,256]{3,2,1,0:T(8,128)(2,1)} %blocks.1, bf16[16,256,128]{2,1,0:T(8,128)(2,1)} %bitcast.12, bf16[16,256,128]{2,1,0:T(8,128)(2,1)} %collective-permute-done.1.refs_1_, bf16[16,256,128]{2,1,0:T(8,128)(2,1)} %collective-permute-done.refs_2_, ...), custom_call_target="tpu_custom_call" | custom-call | flops 1000 | bytes 1000 | tf_op jit(solution)/shard_map/near/pallas_call | solution.py:292
  96.0 2.2 %downward.1.on_leaf = f32[16,64,128]{2,1,0:T(8,128)S(1)} custom-call(s32[16]{0:T(128)S(1)} %broadcast_subtract_fusion.1.parent.refs_0_, f32[64,128]{1,0:T(8,128)S(1)} %collective-permute-done.2.refs_1_, f32[64,128]{1,0:T(8,128)S(1)} %get-tuple-element.37.refs_2_, f32[64,128]{1,0:T(8,128)S(1)} %collective-permute-done.7.refs_1_.refs_3_, ...), custom_call_target="tpu_custom_call" | custom-call | flops 1000 | bytes 1000 | tf_op jit(solution)/shard_map/downward/pallas_call | solution.py:217
  98.2 8.5 %final.1 = bf16[16,256,128]{2,1,0:T(8,128)(2,1)} custom-call(s32[256]{0:T(256)S(1)} %reshape.102.rows, bf16[16,64,1024]{2,1,0:T(8,128)(2,1)S(1)} %weights.1.packed, bf16[256,64,128]{2,1,0:T(8,128)(2,1)} %all-gather.2.cloned.1.call-done.coefs, f32[16,64,128]{2,1,0:T(8,128)S(1)} %downward.1.on_leaf, bf16[16,64,256]{2,1,0:T(8,128)(2,1)} %bitcast.14, ...), custom_call_target="tpu_custom_call" | custom-call | flops 1000 | bytes 1000 | tf_op jit(solution)/shard_map/final/pallas_call | solution.py:343
  (35 shorter events, 1.2 us)
Async XLA Ops:
  6.5 91.7 %all-gather.2.cloned.1.call-start = ((), (), s32[]{:S(2)}) async-start(), calls=%async_computation | async-start | bytes 4456448 | tf_op jit(solution)/shard_map/all_gather | solution.py:412
  10.6 25.7 %collective-permute-start = (bf16[16,256,128]{2,1,0:T(8,128)(2,1)}, bf16[16,256,128]{2,1,0:T(8,128)(2,1)}, u32[]{:S(2)}, u32[]{:S(2)}) collective-permute-start(bf16[16,256,128]{2,1,0:T(8,128)(2,1)} %bitcast.8), channel_id=1, source_target_pairs={{0,16},{16,32},{32,48},{48,64},{64,80},{80,96},{96,112},{1,17},{17... | collective-permute-start | bytes 3145736 | tf_op jit(solution)/shard_map/ppermute | solution.py:368
  15.6 20.7 %collective-permute-start.1 = (bf16[16,256,128]{2,1,0:T(8,128)(2,1)}, bf16[16,256,128]{2,1,0:T(8,128)(2,1)}, u32[]{:S(2)}, u32[]{:S(2)}) collective-permute-start(bf16[16,256,128]{2,1,0:T(8,128)(2,1)} %bitcast.9), channel_id=1, source_target_pairs={{16,0},{32,16},{48,32},{64,48},{80,64},{96,80},{112,96},{17,1},{33... | collective-permute-start | bytes 3145736 | tf_op jit(solution)/shard_map/ppermute | solution.py:368
  17.5 32.2 %collective-permute-start.5 = (bf16[16,256,128]{2,1,0:T(8,128)(2,1)}, bf16[16,256,128]{2,1,0:T(8,128)(2,1)}, u32[]{:S(2)}, u32[]{:S(2)}) collective-permute-start(bf16[16,256,128]{2,1,0:T(8,128)(2,1)} %bitcast.10), channel_id=1, source_target_pairs={{0,1},{1,2},{2,3},{3,4},{4,5},{5,6},{6,7},{7,8},{8,9},{9,10},{10,1... | collective-permute-start | bytes 3145736 | tf_op jit(solution)/shard_map/ppermute | solution.py:368
  18.8 31.6 %collective-permute-start.6 = (bf16[16,256,128]{2,1,0:T(8,128)(2,1)}, bf16[16,256,128]{2,1,0:T(8,128)(2,1)}, u32[]{:S(2)}, u32[]{:S(2)}) collective-permute-start(bf16[16,256,128]{2,1,0:T(8,128)(2,1)} %bitcast.11), channel_id=1, source_target_pairs={{0,15},{1,0},{2,1},{3,2},{4,3},{5,4},{6,5},{7,6},{8,7},{9,8},{10,9... | collective-permute-start | bytes 3145736 | tf_op jit(solution)/shard_map/ppermute | solution.py:368
  22.6 0.7 copy-start.4
  27.6 8.4 %copy-start.6 = (s32[16,8]{0,1:T(8,128)S(1)}, s32[16,8]{0,1:T(8,128)}, u32[]{:S(2)}) copy-start(s32[16,8]{0,1:T(8,128)} %param.19) | copy-start | bytes 1540
  27.6 8.6 %copy-start.5 = (s32[16,16]{1,0:T(8,128)S(1)}, s32[16,16]{1,0:T(8,128)}, u32[]{:S(2)}) copy-start(s32[16,16]{1,0:T(8,128)} %param.21) | copy-start | bytes 3076
  35.2 0.8 copy-start.2
  36.3 14.1 %collective-permute-start.2 = (f32[64,128]{1,0:T(8,128)S(1)}, f32[64,128]{1,0:T(8,128)S(1)}, u32[]{:S(2)}, u32[]{:S(2)}) collective-permute-start(f32[64,128]{1,0:T(8,128)S(1)} %get-tuple-element.33.refs_0_), channel_id=1, source_target_pairs={{0,1},{1,0},{2,3},{3,2},{4,5},{5,4},{6,7},{7,6},{8,9},{9,8},{10,11... | collective-permute-start | bytes 98312 | tf_op jit(solution)/shard_map/ppermute | solution.py:380
  36.4 14.0 %collective-permute-start.3 = (f32[64,128]{1,0:T(8,128)S(1)}, f32[64,128]{1,0:T(8,128)S(1)}, u32[]{:S(2)}, u32[]{:S(2)}) collective-permute-start(f32[64,128]{1,0:T(8,128)S(1)} %get-tuple-element.33.refs_0_), channel_id=1, source_target_pairs={{0,2},{1,3},{2,0},{3,1},{4,6},{5,7},{6,4},{7,5},{8,10},{9,11},{10,... | collective-permute-start | bytes 98312 | tf_op jit(solution)/shard_map/ppermute | solution.py:380
  36.5 14.1 %collective-permute-start.4 = (f32[64,128]{1,0:T(8,128)S(1)}, f32[64,128]{1,0:T(8,128)S(1)}, u32[]{:S(2)}, u32[]{:S(2)}) collective-permute-start(f32[64,128]{1,0:T(8,128)S(1)} %get-tuple-element.33.refs_0_), channel_id=1, source_target_pairs={{0,3},{1,2},{2,1},{3,0},{4,7},{5,6},{6,5},{7,4},{8,11},{9,10},{10,... | collective-permute-start | bytes 98312 | tf_op jit(solution)/shard_map/ppermute | solution.py:380
  50.6 33.5 %collective-permute-start.12 = (bf16[16,256,128]{2,1,0:T(8,128)(2,1)}, bf16[16,256,128]{2,1,0:T(8,128)(2,1)S(1)}, u32[]{:S(2)}, u32[]{:S(2)}) collective-permute-start(bf16[16,256,128]{2,1,0:T(8,128)(2,1)} %collective-permute-done.5.refs_3_), channel_id=1, source_target_pairs={{16,0},{32,16},{48,32},{64,48},{80,64},{96,80},{112,96},{17,1},{33... | collective-permute-start | bytes 3145736 | tf_op jit(solution)/shard_map/ppermute | solution.py:368
  52.5 31.6 %collective-permute-start.13 = (bf16[16,256,128]{2,1,0:T(8,128)(2,1)}, bf16[16,256,128]{2,1,0:T(8,128)(2,1)S(1)}, u32[]{:S(2)}, u32[]{:S(2)}) collective-permute-start(bf16[16,256,128]{2,1,0:T(8,128)(2,1)} %collective-permute-done.5.refs_3_), channel_id=1, source_target_pairs={{0,16},{16,32},{32,48},{48,64},{64,80},{80,96},{96,112},{1,17},{17... | collective-permute-start | bytes 3145736 | tf_op jit(solution)/shard_map/ppermute | solution.py:368
  57.2 27.0 %collective-permute-start.14 = (bf16[16,256,128]{2,1,0:T(8,128)(2,1)}, bf16[16,256,128]{2,1,0:T(8,128)(2,1)S(1)}, u32[]{:S(2)}, u32[]{:S(2)}) collective-permute-start(bf16[16,256,128]{2,1,0:T(8,128)(2,1)} %collective-permute-done.6.refs_6_), channel_id=1, source_target_pairs={{16,0},{32,16},{48,32},{64,48},{80,64},{96,80},{112,96},{17,1},{33... | collective-permute-start | bytes 3145736 | tf_op jit(solution)/shard_map/ppermute | solution.py:368
  59.1 25.1 %collective-permute-start.15 = (bf16[16,256,128]{2,1,0:T(8,128)(2,1)}, bf16[16,256,128]{2,1,0:T(8,128)(2,1)S(1)}, u32[]{:S(2)}, u32[]{:S(2)}) collective-permute-start(bf16[16,256,128]{2,1,0:T(8,128)(2,1)} %collective-permute-done.6.refs_6_), channel_id=1, source_target_pairs={{0,16},{16,32},{32,48},{48,64},{64,80},{80,96},{96,112},{1,17},{17... | collective-permute-start | bytes 3145736 | tf_op jit(solution)/shard_map/ppermute | solution.py:368
  63.2 3.9 %collective-permute-start.7 = (f32[64,128]{1,0:T(8,128)S(1)}, f32[64,128]{1,0:T(8,128)S(1)}, u32[]{:S(2)}, u32[]{:S(2)}) collective-permute-start(f32[64,128]{1,0:T(8,128)S(1)} %get-tuple-element.38.refs_0_), channel_id=1, source_target_pairs={{0,4},{1,5},{2,6},{3,7},{4,0},{5,1},{6,2},{7,3},{8,12},{9,13},{10,... | collective-permute-start | bytes 98312 | tf_op jit(solution)/shard_map/ppermute | solution.py:380
  67.3 5.6 %collective-permute-start.8 = (f32[64,128]{1,0:T(8,128)S(1)}, f32[64,128]{1,0:T(8,128)S(1)}, u32[]{:S(2)}, u32[]{:S(2)}) collective-permute-start(f32[64,128]{1,0:T(8,128)S(1)} %combine.4.refs_0_), channel_id=1, source_target_pairs={{0,8},{1,9},{2,10},{3,11},{4,12},{5,13},{6,14},{7,15},{8,0},{9,1},... | collective-permute-start | bytes 98312 | tf_op jit(solution)/shard_map/ppermute | solution.py:380
  73.1 1.3 %collective-permute-start.9 = (f32[64,128]{1,0:T(8,128)S(1)}, f32[64,128]{1,0:T(8,128)S(1)}, u32[]{:S(2)}, u32[]{:S(2)}) collective-permute-start(f32[64,128]{1,0:T(8,128)S(1)} %combine.5.refs_0_), channel_id=1, source_target_pairs={{0,16},{1,17},{2,18},{3,19},{4,20},{5,21},{6,22},{7,23},{8,24},{9,... | collective-permute-start | bytes 98312 | tf_op jit(solution)/shard_map/ppermute | solution.py:380
  74.6 6.4 %collective-permute-start.10 = (f32[64,128]{1,0:T(8,128)S(1)}, f32[64,128]{1,0:T(8,128)S(1)}, u32[]{:S(2)}, u32[]{:S(2)}) collective-permute-start(f32[64,128]{1,0:T(8,128)S(1)} %combine.6.refs_0_), channel_id=1, source_target_pairs={{0,32},{1,33},{2,34},{3,35},{4,36},{5,37},{6,38},{7,39},{8,40},{9,... | collective-permute-start | bytes 98312 | tf_op jit(solution)/shard_map/ppermute | solution.py:380
  81.2 14.8 %copy-start = (f32[16,64,64]{2,1,0:T(8,128)S(1)}, f32[16,64,64]{2,1,0:T(8,128)}, u32[]{:S(2)}) copy-start(f32[16,64,64]{2,1,0:T(8,128)} %refs_11_.1) | copy-start | bytes 786436
  81.2 14.8 %copy-start.1 = (f32[8,64,64]{2,1,0:T(8,128)S(1)}, f32[8,64,64]{2,1,0:T(8,128)}, u32[]{:S(2)}) copy-start(f32[8,64,64]{2,1,0:T(8,128)} %refs_10_.1) | copy-start | bytes 393220
  81.3 14.8 %copy-start.3 = (f32[16,64,64]{2,1,0:T(8,128)S(1)}, f32[16,64,64]{2,1,0:T(8,128)}, u32[]{:S(2)}) copy-start(f32[16,64,64]{2,1,0:T(8,128)} %copy-done.2) | copy-start | bytes 786436
  81.3 14.7 %collective-permute-start.11 = (f32[64,128]{1,0:T(8,128)S(1)}, f32[64,128]{1,0:T(8,128)S(1)}, u32[]{:S(2)}, u32[]{:S(2)}) collective-permute-start(f32[64,128]{1,0:T(8,128)S(1)} %combine.7), channel_id=1, source_target_pairs={{0,64},{1,65},{2,66},{3,67},{4,68},{5,69},{6,70},{7,71},{8,72},{9,... | collective-permute-start | bytes 98312 | tf_op jit(solution)/shard_map/ppermute | solution.py:380
Sparse Core Ops, SparseCore 0:
  10.8 69.3 all-gather.1

commit v8 on v7

--- a/solution.py
+++ b/solution.py
@@ -88,14 +88,14 @@
     for tail in tails:
         tail.wait()
     for leaf, coefs in enumerate(exact):
-        clusters[parent[leaf]] += fine_t(up_held[leaf], coefs)
+        clusters[lax.rem(parent[leaf], clusters.shape[0])] += fine_t(up_held[leaf], coefs)
     total = fine_t(root_held[0], clusters[0])
     for cluster in range(1, root_held.shape[0]):
         total = total + fine_t(root_held[cluster], clusters[cluster])
     root_out[...] = total
 
 
-def leaf_coefficients(local_parent, panels, bases, up_transfer, root_transfer):
+def leaf_coefficients(leaf_parent, panels, bases, up_transfer, root_transfer):
     leaves, size, rhs = panels.shape
     rank = bases.shape[1]
     return pl.pallas_call(
@@ -118,7 +118,7 @@
         compiler_params=params(12),
         cost_estimate=cost(1000, 1000),
         name="coefs",
-    )(local_parent, *[in_hbm(array) for array in (panels, bases, up_transfer, root_transfer)])
+    )(leaf_parent, *[in_hbm(array) for array in (panels, bases, up_transfer, root_transfer)])
 
 
 def tables_kernel(nodes, transfer, coupling, transfer_out, coupling_out, held, sems):
@@ -198,34 +198,6 @@
     )(*roots, mats)
 
 
-def downward_kernel(depth, parent, *refs):
-    siblings = refs[:depth]
-    transfer, coupling, root, up, out, clusters = refs[depth:]
-    down = fine_dot(coupling[depth - 1], siblings[depth - 1][...])
-    for level in reversed(range(depth - 1)):
-        across = fine_dot(coupling[level], siblings[level][...])
-        down = across + fine_dot(transfer[level], down)
-    for cluster in range(root.shape[0]):
-        clusters[cluster] = fine_dot(root[cluster], down)
-    for leaf in range(up.shape[0]):
-        out[leaf] = fine_dot(up[leaf], clusters[parent[leaf]])
-
-
-def downward(local_parent, siblings, transfer, coupling, root_transfer, up_transfer):
-    depth = len(siblings)
-    rank, rhs = siblings[0].shape
-    return pl.pallas_call(
-        lambda *refs: downward_kernel(depth, *refs),
-        out_shape=jax.ShapeDtypeStruct((up_transfer.shape[0], rank, rhs), f32),
-        in_specs=[scalars()] + [whole()] * (depth + 4),
-        out_specs=whole(),
-        scratch_shapes=[pltpu.VMEM((root_transfer.shape[0], rank, rhs), f32)],
-        compiler_params=params(16),
-        cost_estimate=cost(1000, 1000),
-        name="downward",
-    )(local_parent, *siblings, transfer, coupling, root_transfer, up_transfer)
-
-
 def weights_kernel(count, coupling, out, held, sems):
     leaves, slots, _, rank = coupling.shape
     copies = [pltpu.make_async_copy(coupling.at[leaf], held.at[leaf], sems.at[leaf]) for leaf in range(leaves)]
@@ -255,21 +227,28 @@
     )(far_count, in_hbm(far_coupling))
 
 
-def near_kernel(position, blocks, *refs):
-    pieces = refs[:-7]
-    out, held, matrices, piece_sems, block_sems, sums, out_sems = refs[-7:]
+def near_kernel(position, rows, packed, blocks, coefs, *refs):
+    pieces = refs[:-10]
+    out, far_out, held, matrices, table, piece_sems, block_sems, sums, out_sems, table_sem = refs[-10:]
     leaves, slots = blocks.shape[:2]
+    far_slots = rows.shape[0] // leaves
     copies = []
     first = 0
     for index, piece in enumerate(pieces):
-        rows = pl.ds(first, piece.shape[0])
-        copies.append(pltpu.make_async_copy(piece, held.at[rows], piece_sems.at[index]))
+        span = pl.ds(first, piece.shape[0])
+        copies.append(pltpu.make_async_copy(piece, held.at[span], piece_sems.at[index]))
         first += piece.shape[0]
     fetches = [
         pltpu.make_async_copy(blocks.at[leaf], matrices.at[leaf], block_sems.at[leaf]) for leaf in range(leaves)
     ]
+    load = pltpu.make_async_copy(coefs, table, table_sem)
+    load.start()
     for copy in copies + fetches[:1]:
         copy.start()
+    load.wait()
+    for leaf in range(leaves):
+        tall = jnp.concatenate([table[rows[leaf * far_slots + slot]] for slot in range(far_slots)], axis=0)
+        far_out[leaf] = dot(packed[leaf], tall)
     for copy in copies:
         copy.wait()
     for fetch in fetches[1:]:
@@ -286,48 +265,50 @@
         store.wait()
 
 
-def near(position, near_blocks, pieces):
+def near(position, far_rows, packed, near_blocks, slab_coefs, pieces):
     leaves, slots, size, _ = near_blocks.shape
-    rhs = pieces[0].shape[2]
+    rank, rhs = slab_coefs.shape[1:]
     return pl.pallas_call(
         near_kernel,
-        out_shape=pltpu.HBM((leaves, size, rhs), f32),
-        in_specs=[scalars()] + [anywhere()] * (1 + len(pieces)),
-        out_specs=pl.BlockSpec(memory_space=pltpu.HBM),
+        out_shape=(pltpu.HBM((leaves, size, rhs), f32), jax.ShapeDtypeStruct((leaves, rank, rhs), f32)),
+        in_specs=[scalars(), scalars(), whole()] + [anywhere()] * (2 + len(pieces)),
+        out_specs=(pl.BlockSpec(memory_space=pltpu.HBM), whole()),
         scratch_shapes=[
             pltpu.VMEM((sum(piece.shape[0] for piece in pieces), size, rhs), bf16),
             pltpu.VMEM(near_blocks.shape, bf16),
+            pltpu.VMEM(slab_coefs.shape, bf16),
             pltpu.SemaphoreType.DMA((len(pieces),)),
             pltpu.SemaphoreType.DMA((leaves,)),
             pltpu.VMEM((leaves, size, rhs), f32),
             pltpu.SemaphoreType.DMA((leaves,)),
+            pltpu.SemaphoreType.DMA,
         ],
-        compiler_params=params(36),
+        compiler_params=params(42),
         cost_estimate=cost(1000, 1000),
         name="near",
-    )(position, in_hbm(near_blocks), *pieces)
-
-
-def final_kernel(rows, packed, coefs, on_leaf, bases, near_part, out, *scratch):
-    held, picked, results, term, basis, close, load_sems, near_sems, out_sems = scratch
-    leaves, rank, wide = packed.shape
-    slots = wide // rank
-    loads = [
-        pltpu.make_async_copy(source, target, load_sems.at[index])
-        for index, (source, target) in enumerate(((coefs, held), (on_leaf, term), (bases, basis)))
-    ]
+    )(position, far_rows, packed, in_hbm(near_blocks), in_hbm(slab_coefs), *pieces)
+
+
+def final_kernel(depth, parent, *refs):
+    siblings = refs[:depth]
+    transfer, coupling, root, up, far_part, bases, near_part, out = refs[depth : depth + 8]
+    clusters, results, basis, close, basis_sem, near_sems, out_sems = refs[depth + 8 :]
+    leaves = up.shape[0]
+    load = pltpu.make_async_copy(bases, basis, basis_sem)
     nears = [pltpu.make_async_copy(near_part.at[leaf], close.at[leaf], near_sems.at[leaf]) for leaf in range(leaves)]
-    for load in loads:
-        load.start()
-    for load in loads:
-        load.wait()
-    for load in nears:
-        load.start()
+    for copy in [load] + nears:
+        copy.start()
+    down = fine_dot(coupling[depth - 1], siblings[depth - 1][...])
+    for level in reversed(range(depth - 1)):
+        across = fine_dot(coupling[level], siblings[level][...])
+        down = across + fine_dot(transfer[level], down)
+    for cluster in range(root.shape[0]):
+        clusters[cluster] = fine_dot(root[cluster], down)
+    load.wait()
     stores = []
     for leaf in range(leaves):
-        for slot in range(slots):
-            picked[leaf, slot * rank : (slot + 1) * rank] = held[rows[leaf * slots + slot]]
-        expansion = (term[leaf] + dot(packed[leaf], picked[leaf])).astype(bf16)
+        on_leaf = fine_dot(up[leaf], clusters[lax.rem(parent[leaf], root.shape[0])])
+        expansion = (on_leaf + far_part[leaf]).astype(bf16)
         nears[leaf].wait()
         results[leaf] = (dot_t(basis[leaf], expansion) + close[leaf]).astype(bf16)
         stores.append(pltpu.make_async_copy(results.at[leaf], out.at[leaf], out_sems.at[leaf]))
@@ -336,30 +317,38 @@
         store.wait()
 
 
-def final(far_rows, packed, slab_coefs, on_leaf, bases, near_part):
+def final(leaf_parent, siblings, transfer, coupling, root_transfer, up_transfer, far_part, bases, near_part):
     leaves, rank, size = bases.shape
     rhs = near_part.shape[2]
-    wide = packed.shape[2]
-    return pl.pallas_call(
-        final_kernel,
+    depth = len(siblings)
+    return pl.pallas_call(
+        lambda *refs: final_kernel(depth, *refs),
         out_shape=jax.ShapeDtypeStruct((leaves, size, rhs), bf16),
-        in_specs=[scalars(), whole()] + [anywhere()] * 4,
+        in_specs=[scalars()] + [whole()] * (depth + 5) + [anywhere()] * 2,
         out_specs=anywhere(),
         scratch_shapes=[
-            pltpu.VMEM(slab_coefs.shape, bf16),
-            pltpu.VMEM((leaves, wide, rhs), bf16),
+            pltpu.VMEM((root_transfer.shape[0], rank, rhs), f32),
             pltpu.VMEM((leaves, size, rhs), bf16),
-            pltpu.VMEM(on_leaf.shape, f32),
             pltpu.VMEM(bases.shape, bf16),
             pltpu.VMEM(near_part.shape, f32),
-            pltpu.SemaphoreType.DMA((3,)),
+            pltpu.SemaphoreType.DMA,
             pltpu.SemaphoreType.DMA((leaves,)),
             pltpu.SemaphoreType.DMA((leaves,)),
         ],
-        compiler_params=params(24),
+        compiler_params=params(12),
         cost_estimate=cost(1000, 1000),
         name="final",
-    )(far_rows, packed, in_hbm(slab_coefs), on_leaf, in_hbm(bases), in_hbm(near_part))
+    )(
+        leaf_parent,
+        *siblings,
+        transfer,
+        coupling,
+        root_transfer,
+        up_transfer,
+        far_part,
+        in_hbm(bases),
+        in_hbm(near_part),
+    )
 
 
 def shifted(array, axis, step, closed):
@@ -397,7 +386,6 @@
     leaf_total, leaf_size, _ = bases.shape
     bases = bases.transpose(0, 2, 1)
     rhs_count = sources.shape[1]
-    cluster_total = leaf_total // 2
     slab_count = lax.axis_size("slab")
     sector_count = lax.axis_size("sector")
     devices = slab_count * sector_count
@@ -407,8 +395,7 @@
     device = slab_pos * sector_count + sector_pos
     panels = sources.reshape(leaf_total, leaf_size, rhs_count)
 
-    local_parent = leaf_parent - device * cluster_total
-    leaf_coefs, root = leaf_coefficients(local_parent, panels, bases, up_transfer, root_transfer)
+    leaf_coefs, root = leaf_coefficients(leaf_parent, panels, bases, up_transfer, root_transfer)
     slab_coefs = lax.all_gather(leaf_coefs, "sector", axis=0, tiled=True)
 
     owner_device = near_list // leaf_total
@@ -442,15 +429,18 @@
     across, current = combine_four(picks, quad, transfer)
     siblings = [quad[1], across]
     for level in range(2, depth):
+        if level == depth - 1:
+            current, slab_coefs = after(current, slab_coefs)
         sibling = partner(current, both_axes, 1 << level)
         if level == depth - 1:
-            near_part = near(position, near_blocks, pieces)
-            current, sibling, near_part = after(current, sibling, near_part)
+            near_part, far_part = near(position, far_rows, packed, near_blocks, slab_coefs, pieces)
+            sibling, near_part, far_part = after(sibling, near_part, far_part)
         siblings.append(sibling)
         if level < depth - 1:
             current = combine(level, depth + level, current, sibling, transfer)
-    on_leaf = downward(local_parent, siblings, transfer, coupling, root_transfer, up_transfer)
-    field = final(far_rows, packed, slab_coefs, on_leaf, bases, near_part)
+    field = final(
+        leaf_parent, siblings, transfer, coupling, root_transfer, up_transfer, far_part, bases, near_part
+    )
     return field.reshape(leaf_total * leaf_size, rhs_count)
 
 

time: 114 us -> 122 us (1.070)
  the two profiles are of different devices: /device:TPU:1 before, /device:TPU:0 now
where the time goes in v8:
time: 122 us; the launch traced here: 121 us
  Pallas kernels  38.8 us (32%)
  waiting for transfers between devices  33.7 us (28%)
  starting transfers between devices  30.9 us (25%)
  between operations  13.7 us (11%)
  local copies, waits for them, and re-layouts  4.23 us (3%)
    ppermute x8, starting transfers between devices, shifted(): return lax.ppermute(array, axis, pairs)  19.8 us
    ppermute x8, waiting for transfers between devices, partner(): lax.ppermute(array, axis, [(i, i ^ flip) for i in range(lax.axis_size(axi...  17.4 us
    ppermute x8, waiting for transfers between devices, shifted(): return lax.ppermute(array, axis, pairs)  16.3 us
    pallas_call x1, Pallas kernels, near(): pl.pallas_call(near_kernel, out_shape=(pltpu.HBM((leaves, size, rhs), f32...  14.7 us
    ppermute x8, starting transfers between devices, partner(): lax.ppermute(array, axis, [(i, i ^ flip) for i in range(lax.axis_size(axi...  11 us
    pallas_call x1, Pallas kernels, tables(): pl.pallas_call(tables_kernel, out_shape=(jax.ShapeDtypeStruct((count, ran...  7.59 us
    pallas_call x1, Pallas kernels, final(): pl.pallas_call(lambda *refs: final_kernel(depth, *refs), out_shape=jax.Sh...  7.53 us
    pallas_call x1, Pallas kernels, weights(): pl.pallas_call(weights_kernel, out_shape=jax.ShapeDtypeStruct((leaves, ra...  4.31 us
  transfers between devices with their start and end apart: 17, of which 6 were waited for; matrix products, arithmetic and copies ran while one was open for 0% of the time, Pallas kernels for 23%

profile of v8, /device:TPU:0, one launch (start us, length us, event | category | flops | bytes accessed | tf_op | source)
XLA Modules:
  0.0 121.4 jit_solution(8556675527754974764)
XLA Ops:
  6.5 0.7 copy-done.9
  7.2 3.5 %coefs.1 = (bf16[16,64,128]{2,1,0:T(8,128)(2,1)}, f32[64,128]{1,0:T(8,128)S(1)}) custom-call(s32[16]{0:T(128)S(1)} %copy-done.9, bf16[16,256,128]{2,1,0:T(8,128)(2,1)} %bitcast.7, bf16[16,64,256]{2,1,0:T(8,128)(2,1)} %bitcast.13, f32[16,64,64]{2,1,0:T(8,128)} %refs_11_.1, f32[8,64,64]{2,1,0:T(8,128)} %refs_10_.1), custom_call_target="tpu_custom_call" | custom-call | flops 1000 | bytes 1000 | tf_op jit(solution)/shard_map/coefs/pallas_call | solution.py:101
  10.7 1.3 %collective-permute-start.1 = (bf16[16,256,128]{2,1,0:T(8,128)(2,1)}, bf16[16,256,128]{2,1,0:T(8,128)(2,1)}, u32[]{:S(2)}, u32[]{:S(2)}) collective-permute-start(bf16[16,256,128]{2,1,0:T(8,128)(2,1)} %bitcast.8), channel_id=1, source_target_pairs={{16,0},{32,16},{48,32},{64,48},{80,64},{96,80},{112,96},{17,1},{33... | collective-permute-start | bytes 3145736 | tf_op jit(solution)/shard_map/ppermute | solution.py:357
  12.0 4.1 %collective-permute-start = (bf16[16,256,128]{2,1,0:T(8,128)(2,1)}, bf16[16,256,128]{2,1,0:T(8,128)(2,1)}, u32[]{:S(2)}, u32[]{:S(2)}) collective-permute-start(bf16[16,256,128]{2,1,0:T(8,128)(2,1)} %bitcast.9), channel_id=1, source_target_pairs={{0,16},{16,32},{32,48},{48,64},{64,80},{80,96},{96,112},{1,17},{17... | collective-permute-start | bytes 3145736 | tf_op jit(solution)/shard_map/ppermute | solution.py:357
  16.1 5.3 %collective-permute-start.6 = (bf16[16,256,128]{2,1,0:T(8,128)(2,1)}, bf16[16,256,128]{2,1,0:T(8,128)(2,1)}, u32[]{:S(2)}, u32[]{:S(2)}) collective-permute-start(bf16[16,256,128]{2,1,0:T(8,128)(2,1)} %bitcast.10), channel_id=1, source_target_pairs={{0,15},{1,0},{2,1},{3,2},{4,3},{5,4},{6,5},{7,6},{8,7},{9,8},{10,9... | collective-permute-start | bytes 3145736 | tf_op jit(solution)/shard_map/ppermute | solution.py:357
  21.4 0.7 copy-done.11
  22.1 4.3 %weights.1.packed = bf16[16,64,1024]{2,1,0:T(8,128)(2,1)S(1)} custom-call(s32[16]{0:T(128)S(1)} %copy-done.11, f32[16,16,64,64]{3,2,1,0:T(8,128)} %coupling.1), custom_call_target="tpu_custom_call" | custom-call | flops 1000 | bytes 1000 | tf_op jit(solution)/shard_map/weights/pallas_call | solution.py:218
  26.5 7.6 %tables.1 = (f32[16,64,64]{2,1,0:T(8,128)S(1)}, f32[16,64,64]{2,1,0:T(8,128)S(1)}) custom-call(s32[16,1]{1,0:T(8,128)S(1)} %fusion.11.nodes, f32[64,64,256]{2,1,0:T(8,128)} %bitcast.5, f32[64,64,256]{2,1,0:T(8,128)} %bitcast.6), custom_call_target="tpu_custom_call" | custom-call | flops 1000 | bytes 1000 | tf_op jit(solution)/shard_map/tables/pallas_call | solution.py:152
  34.1 0.8 copy-done.2
  35.2 1.9 %collective-permute-start.4 = (f32[64,128]{1,0:T(8,128)S(1)}, f32[64,128]{1,0:T(8,128)S(1)}, u32[]{:S(2)}, u32[]{:S(2)}) collective-permute-start(f32[64,128]{1,0:T(8,128)S(1)} %get-tuple-element.35.refs_0_), channel_id=1, source_target_pairs={{0,3},{1,2},{2,1},{3,0},{4,7},{5,6},{6,5},{7,4},{8,11},{9,10},{10,... | collective-permute-start | bytes 98312 | tf_op jit(solution)/shard_map/ppermute | solution.py:369
  37.1 2.3 %collective-permute-start.2 = (f32[64,128]{1,0:T(8,128)S(1)}, f32[64,128]{1,0:T(8,128)S(1)}, u32[]{:S(2)}, u32[]{:S(2)}) collective-permute-start(f32[64,128]{1,0:T(8,128)S(1)} %get-tuple-element.35.refs_0_), channel_id=1, source_target_pairs={{0,1},{1,0},{2,3},{3,2},{4,5},{5,4},{6,7},{7,6},{8,9},{9,8},{10,11... | collective-permute-start | bytes 98312 | tf_op jit(solution)/shard_map/ppermute | solution.py:369
  39.3 10.8 %collective-permute-done.6.refs_6_ = bf16[16,256,128]{2,1,0:T(8,128)(2,1)} collective-permute-done((bf16[16,256,128]{2,1,0:T(8,128)(2,1)}, bf16[16,256,128]{2,1,0:T(8,128)(2,1)}, u32[]{:S(2)}, u32[]{:S(2)}) %collective-permute-start.6) | collective-permute-done | bytes 1048608 | tf_op jit(solution)/shard_map/ppermute | solution.py:357
  50.1 5.5 %collective-permute-done.5.refs_3_ = bf16[16,256,128]{2,1,0:T(8,128)(2,1)} collective-permute-done((bf16[16,256,128]{2,1,0:T(8,128)(2,1)}, bf16[16,256,128]{2,1,0:T(8,128)(2,1)}, u32[]{:S(2)}, u32[]{:S(2)}) %collective-permute-start.5) | collective-permute-done | bytes 1048608 | tf_op jit(solution)/shard_map/ppermute | solution.py:357
  55.7 2.3 %collective-permute-start.13 = (bf16[16,256,128]{2,1,0:T(8,128)(2,1)}, bf16[16,256,128]{2,1,0:T(8,128)(2,1)}, u32[]{:S(2)}, u32[]{:S(2)}) collective-permute-start(bf16[16,256,128]{2,1,0:T(8,128)(2,1)} %collective-permute-done.5.refs_3_), channel_id=1, source_target_pairs={{0,16},{16,32},{32,48},{48,64},{64,80},{80,96},{96,112},{1,17},{17... | collective-permute-start | bytes 3145736 | tf_op jit(solution)/shard_map/ppermute | solution.py:357
  57.9 1.3 %collective-permute-start.12 = (bf16[16,256,128]{2,1,0:T(8,128)(2,1)}, bf16[16,256,128]{2,1,0:T(8,128)(2,1)}, u32[]{:S(2)}, u32[]{:S(2)}) collective-permute-start(bf16[16,256,128]{2,1,0:T(8,128)(2,1)} %collective-permute-done.5.refs_3_), channel_id=1, source_target_pairs={{16,0},{32,16},{48,32},{64,48},{80,64},{96,80},{112,96},{17,1},{33... | collective-permute-start | bytes 3145736 | tf_op jit(solution)/shard_map/ppermute | solution.py:357
  59.2 4.3 %collective-permute-start.15 = (bf16[16,256,128]{2,1,0:T(8,128)(2,1)}, bf16[16,256,128]{2,1,0:T(8,128)(2,1)}, u32[]{:S(2)}, u32[]{:S(2)}) collective-permute-start(bf16[16,256,128]{2,1,0:T(8,128)(2,1)} %collective-permute-done.6.refs_6_), channel_id=1, source_target_pairs={{0,16},{16,32},{32,48},{48,64},{64,80},{80,96},{96,112},{1,17},{17... | collective-permute-start | bytes 3145736 | tf_op jit(solution)/shard_map/ppermute | solution.py:357
  63.5 1.3 %collective-permute-start.14 = (bf16[16,256,128]{2,1,0:T(8,128)(2,1)}, bf16[16,256,128]{2,1,0:T(8,128)(2,1)}, u32[]{:S(2)}, u32[]{:S(2)}) collective-permute-start(bf16[16,256,128]{2,1,0:T(8,128)(2,1)} %collective-permute-done.6.refs_6_), channel_id=1, source_target_pairs={{16,0},{32,16},{48,32},{64,48},{80,64},{96,80},{112,96},{17,1},{33... | collective-permute-start | bytes 3145736 | tf_op jit(solution)/shard_map/ppermute | solution.py:357
  64.8 0.4 combine_four.1
  65.2 0.6 copy-done.6
  65.8 4.8 %collective-permute-done.7.refs_1_.refs_3_ = f32[64,128]{1,0:T(8,128)S(1)} collective-permute-done((f32[64,128]{1,0:T(8,128)S(1)}, f32[64,128]{1,0:T(8,128)S(1)}, u32[]{:S(2)}, u32[]{:S(2)}) %collective-permute-start.7) | collective-permute-done | bytes 32800 | tf_op jit(solution)/shard_map/ppermute | solution.py:369
  70.6 0.2 combine.4.refs_0_
  70.8 0.5 collective-permute-start.8
  71.3 5.8 %collective-permute-done.8.refs_1_.refs_4_ = f32[64,128]{1,0:T(8,128)S(1)} collective-permute-done((f32[64,128]{1,0:T(8,128)S(1)}, f32[64,128]{1,0:T(8,128)S(1)}, u32[]{:S(2)}, u32[]{:S(2)}) %collective-permute-start.8) | collective-permute-done | bytes 32800 | tf_op jit(solution)/shard_map/ppermute | solution.py:369
  77.2 0.2 combine.5.refs_0_
  77.4 1.2 collective-permute-done.9.refs_1_.refs_5_
  78.8 2.7 %collective-permute-start.10 = (f32[64,128]{1,0:T(8,128)S(1)}, f32[64,128]{1,0:T(8,128)S(1)}, u32[]{:S(2)}, u32[]{:S(2)}) collective-permute-start(f32[64,128]{1,0:T(8,128)S(1)} %combine.6.refs_0_), channel_id=1, source_target_pairs={{0,32},{1,33},{2,34},{3,35},{4,36},{5,37},{6,38},{7,39},{8,40},{9,... | collective-permute-start | bytes 98312 | tf_op jit(solution)/shard_map/ppermute | solution.py:369
  81.5 5.6 %collective-permute-done.10.refs_1_.refs_6_ = f32[64,128]{1,0:T(8,128)S(1)} collective-permute-done((f32[64,128]{1,0:T(8,128)S(1)}, f32[64,128]{1,0:T(8,128)S(1)}, u32[]{:S(2)}, u32[]{:S(2)}) %collective-permute-start.10) | collective-permute-done | bytes 32800 | tf_op jit(solution)/shard_map/ppermute | solution.py:369
  87.4 0.6 copy-done.4
  88.0 0.6 copy-done.8
  88.6 3.5 %collective-permute-start.11 = (f32[64,128]{1,0:T(8,128)}, f32[64,128]{1,0:T(8,128)S(1)}, u32[]{:S(2)}, u32[]{:S(2)}) collective-permute-start(f32[64,128]{1,0:T(8,128)} %copy-done.8), channel_id=1, source_target_pairs={{0,64},{1,65},{2,66},{3,67},{4,68},{5,69},{6,70},{7,71},{8,72},{9,... | collective-permute-start | bytes 98312 | tf_op jit(solution)/shard_map/ppermute | solution.py:369
  92.2 14.7 %near.1 = (f32[16,256,128]{2,1,0:T(8,128)}, f32[16,64,128]{2,1,0:T(8,128)S(1)}) custom-call(s32[128]{0:T(128)S(1)} %reshape.101.position, s32[256]{0:T(256)S(1)} %reshape.102.rows, bf16[16,64,1024]{2,1,0:T(8,128)(2,1)S(1)} %weights.1.packed, bf16[16,8,256,256]{3,2,1,0:T(8,128)(2,1)} %blocks.1, bf16[256,64,128]{2,1,0:T(8,128)(2,1)} %all-gather.2.cloned.1.call-done.coefs, ...), custom_call_target="tpu_custom_call" | custom-call | flops 1000 | bytes 1000 | tf_op jit(solution)/shard_map/near/pallas_call | solution.py:271
  107.0 7.5 %final.1 = bf16[16,256,128]{2,1,0:T(8,128)(2,1)} custom-call(s32[16]{0:T(128)S(1)} %copy-done.10, f32[64,128]{1,0:T(8,128)S(1)} %collective-permute-done.2.refs_1_, f32[64,128]{1,0:T(8,128)S(1)} %copy-done.7, f32[64,128]{1,0:T(8,128)S(1)} %collective-permute-done.7.refs_1_.refs_3_, f32[64,128]{1,0:T(8,128)S(1)} %collective-permute-done.8.refs_1_.refs_4_, ...), custom_call_target="tpu_custom_call" | custom-call | flops 1000 | bytes 1000 | tf_op jit(solution)/shard_map/final/pallas_call | solution.py:324
  (47 shorter events, 0.8 us)
Async XLA Ops:
  6.5 82.0 %all-gather.2.cloned.1.call-start = ((), (), s32[]{:S(2)}) async-start(), calls=%async_computation | async-start | bytes 4456448 | tf_op jit(solution)/shard_map/all_gather | solution.py:399
  6.5 0.7 copy-start.9
  10.7 24.5 %collective-permute-start.1 = (bf16[16,256,128]{2,1,0:T(8,128)(2,1)}, bf16[16,256,128]{2,1,0:T(8,128)(2,1)}, u32[]{:S(2)}, u32[]{:S(2)}) collective-permute-start(bf16[16,256,128]{2,1,0:T(8,128)(2,1)} %bitcast.8), channel_id=1, source_target_pairs={{16,0},{32,16},{48,32},{64,48},{80,64},{96,80},{112,96},{17,1},{33... | collective-permute-start | bytes 3145736 | tf_op jit(solution)/shard_map/ppermute | solution.py:357
  12.0 23.2 %collective-permute-start = (bf16[16,256,128]{2,1,0:T(8,128)(2,1)}, bf16[16,256,128]{2,1,0:T(8,128)(2,1)}, u32[]{:S(2)}, u32[]{:S(2)}) collective-permute-start(bf16[16,256,128]{2,1,0:T(8,128)(2,1)} %bitcast.9), channel_id=1, source_target_pairs={{0,16},{16,32},{32,48},{48,64},{64,80},{80,96},{96,112},{1,17},{17... | collective-permute-start | bytes 3145736 | tf_op jit(solution)/shard_map/ppermute | solution.py:357
  16.1 34.0 %collective-permute-start.6 = (bf16[16,256,128]{2,1,0:T(8,128)(2,1)}, bf16[16,256,128]{2,1,0:T(8,128)(2,1)}, u32[]{:S(2)}, u32[]{:S(2)}) collective-permute-start(bf16[16,256,128]{2,1,0:T(8,128)(2,1)} %bitcast.10), channel_id=1, source_target_pairs={{0,15},{1,0},{2,1},{3,2},{4,3},{5,4},{6,5},{7,6},{8,7},{9,8},{10,9... | collective-permute-start | bytes 3145736 | tf_op jit(solution)/shard_map/ppermute | solution.py:357
  21.4 34.2 %collective-permute-start.5 = (bf16[16,256,128]{2,1,0:T(8,128)(2,1)}, bf16[16,256,128]{2,1,0:T(8,128)(2,1)}, u32[]{:S(2)}, u32[]{:S(2)}) collective-permute-start(bf16[16,256,128]{2,1,0:T(8,128)(2,1)} %bitcast.11), channel_id=1, source_target_pairs={{0,1},{1,2},{2,3},{3,4},{4,5},{5,6},{6,7},{7,8},{8,9},{9,10},{10,1... | collective-permute-start | bytes 3145736 | tf_op jit(solution)/shard_map/ppermute | solution.py:357
  21.4 0.7 copy-start.11
  26.4 8.4 %copy-start.13 = (s32[16,8]{0,1:T(8,128)S(1)}, s32[16,8]{0,1:T(8,128)}, u32[]{:S(2)}) copy-start(s32[16,8]{0,1:T(8,128)} %param.19) | copy-start | bytes 1540
  26.4 8.6 %copy-start.12 = (s32[16,16]{1,0:T(8,128)S(1)}, s32[16,16]{1,0:T(8,128)}, u32[]{:S(2)}) copy-start(s32[16,16]{1,0:T(8,128)} %param.21) | copy-start | bytes 3076
  34.1 0.8 copy-start.2
  35.2 20.5 %collective-permute-start.4 = (f32[64,128]{1,0:T(8,128)S(1)}, f32[64,128]{1,0:T(8,128)S(1)}, u32[]{:S(2)}, u32[]{:S(2)}) collective-permute-start(f32[64,128]{1,0:T(8,128)S(1)} %get-tuple-element.35.refs_0_), channel_id=1, source_target_pairs={{0,3},{1,2},{2,1},{3,0},{4,7},{5,6},{6,5},{7,4},{8,11},{9,10},{10,... | collective-permute-start | bytes 98312 | tf_op jit(solution)/shard_map/ppermute | solution.py:369
  37.1 18.6 %collective-permute-start.3 = (f32[64,128]{1,0:T(8,128)S(1)}, f32[64,128]{1,0:T(8,128)S(1)}, u32[]{:S(2)}, u32[]{:S(2)}) collective-permute-start(f32[64,128]{1,0:T(8,128)S(1)} %get-tuple-element.35.refs_0_), channel_id=1, source_target_pairs={{0,2},{1,3},{2,0},{3,1},{4,6},{5,7},{6,4},{7,5},{8,10},{9,11},{10,... | collective-permute-start | bytes 98312 | tf_op jit(solution)/shard_map/ppermute | solution.py:369
  37.1 18.6 %collective-permute-start.2 = (f32[64,128]{1,0:T(8,128)S(1)}, f32[64,128]{1,0:T(8,128)S(1)}, u32[]{:S(2)}, u32[]{:S(2)}) collective-permute-start(f32[64,128]{1,0:T(8,128)S(1)} %get-tuple-element.35.refs_0_), channel_id=1, source_target_pairs={{0,1},{1,0},{2,3},{3,2},{4,5},{5,4},{6,7},{7,6},{8,9},{9,8},{10,11... | collective-permute-start | bytes 98312 | tf_op jit(solution)/shard_map/ppermute | solution.py:369
  55.7 36.5 %collective-permute-start.13 = (bf16[16,256,128]{2,1,0:T(8,128)(2,1)}, bf16[16,256,128]{2,1,0:T(8,128)(2,1)}, u32[]{:S(2)}, u32[]{:S(2)}) collective-permute-start(bf16[16,256,128]{2,1,0:T(8,128)(2,1)} %collective-permute-done.5.refs_3_), channel_id=1, source_target_pairs={{0,16},{16,32},{32,48},{48,64},{64,80},{80,96},{96,112},{1,17},{17... | collective-permute-start | bytes 3145736 | tf_op jit(solution)/shard_map/ppermute | solution.py:357
  57.9 34.2 %collective-permute-start.12 = (bf16[16,256,128]{2,1,0:T(8,128)(2,1)}, bf16[16,256,128]{2,1,0:T(8,128)(2,1)}, u32[]{:S(2)}, u32[]{:S(2)}) collective-permute-start(bf16[16,256,128]{2,1,0:T(8,128)(2,1)} %collective-permute-done.5.refs_3_), channel_id=1, source_target_pairs={{16,0},{32,16},{48,32},{64,48},{80,64},{96,80},{112,96},{17,1},{33... | collective-permute-start | bytes 3145736 | tf_op jit(solution)/shard_map/ppermute | solution.py:357
  59.2 33.0 %collective-permute-start.15 = (bf16[16,256,128]{2,1,0:T(8,128)(2,1)}, bf16[16,256,128]{2,1,0:T(8,128)(2,1)}, u32[]{:S(2)}, u32[]{:S(2)}) collective-permute-start(bf16[16,256,128]{2,1,0:T(8,128)(2,1)} %collective-permute-done.6.refs_6_), channel_id=1, source_target_pairs={{0,16},{16,32},{32,48},{48,64},{64,80},{80,96},{96,112},{1,17},{17... | collective-permute-start | bytes 3145736 | tf_op jit(solution)/shard_map/ppermute | solution.py:357
  63.5 28.7 %collective-permute-start.14 = (bf16[16,256,128]{2,1,0:T(8,128)(2,1)}, bf16[16,256,128]{2,1,0:T(8,128)(2,1)}, u32[]{:S(2)}, u32[]{:S(2)}) collective-permute-start(bf16[16,256,128]{2,1,0:T(8,128)(2,1)} %collective-permute-done.6.refs_6_), channel_id=1, source_target_pairs={{16,0},{32,16},{48,32},{64,48},{80,64},{96,80},{112,96},{17,1},{33... | collective-permute-start | bytes 3145736 | tf_op jit(solution)/shard_map/ppermute | solution.py:357
  65.2 0.6 copy-start.6
  65.8 4.8 %collective-permute-start.7 = (f32[64,128]{1,0:T(8,128)S(1)}, f32[64,128]{1,0:T(8,128)S(1)}, u32[]{:S(2)}, u32[]{:S(2)}) collective-permute-start(f32[64,128]{1,0:T(8,128)S(1)} %get-tuple-element.40.refs_0_), channel_id=1, source_target_pairs={{0,4},{1,5},{2,6},{3,7},{4,0},{5,1},{6,2},{7,3},{8,12},{9,13},{10,... | collective-permute-start | bytes 98312 | tf_op jit(solution)/shard_map/ppermute | solution.py:369
  70.8 6.4 %collective-permute-start.8 = (f32[64,128]{1,0:T(8,128)S(1)}, f32[64,128]{1,0:T(8,128)S(1)}, u32[]{:S(2)}, u32[]{:S(2)}) collective-permute-start(f32[64,128]{1,0:T(8,128)S(1)} %combine.4.refs_0_), channel_id=1, source_target_pairs={{0,8},{1,9},{2,10},{3,11},{4,12},{5,13},{6,14},{7,15},{8,0},{9,1},... | collective-permute-start | bytes 98312 | tf_op jit(solution)/shard_map/ppermute | solution.py:369
  77.4 1.2 %collective-permute-start.9 = (f32[64,128]{1,0:T(8,128)S(1)}, f32[64,128]{1,0:T(8,128)S(1)}, u32[]{:S(2)}, u32[]{:S(2)}) collective-permute-start(f32[64,128]{1,0:T(8,128)S(1)} %combine.5.refs_0_), channel_id=1, source_target_pairs={{0,16},{1,17},{2,18},{3,19},{4,20},{5,21},{6,22},{7,23},{8,24},{9,... | collective-permute-start | bytes 98312 | tf_op jit(solution)/shard_map/ppermute | solution.py:369
  78.8 8.3 %collective-permute-start.10 = (f32[64,128]{1,0:T(8,128)S(1)}, f32[64,128]{1,0:T(8,128)S(1)}, u32[]{:S(2)}, u32[]{:S(2)}) collective-permute-start(f32[64,128]{1,0:T(8,128)S(1)} %combine.6.refs_0_), channel_id=1, source_target_pairs={{0,32},{1,33},{2,34},{3,35},{4,36},{5,37},{6,38},{7,39},{8,40},{9,... | collective-permute-start | bytes 98312 | tf_op jit(solution)/shard_map/ppermute | solution.py:369
  87.3 0.6 copy-start.4
  88.0 0.6 copy-start.8
  88.6 18.3 %copy-start = (f32[16,64,64]{2,1,0:T(8,128)S(1)}, f32[16,64,64]{2,1,0:T(8,128)}, u32[]{:S(2)}) copy-start(f32[16,64,64]{2,1,0:T(8,128)} %refs_11_.1) | copy-start | bytes 786436
  88.6 18.4 %copy-start.1 = (f32[8,64,64]{2,1,0:T(8,128)S(1)}, f32[8,64,64]{2,1,0:T(8,128)}, u32[]{:S(2)}) copy-start(f32[8,64,64]{2,1,0:T(8,128)} %refs_10_.1) | copy-start | bytes 393220
  88.6 18.4 %copy-start.10 = (s32[16]{0:T(128)S(1)}, s32[16]{0:T(128)}, u32[]{:S(2)}) copy-start(s32[16]{0:T(128)} %refs_0_.1) | copy-start | bytes 196
  88.6 18.4 %copy-start.3 = (f32[16,64,64]{2,1,0:T(8,128)S(1)}, f32[16,64,64]{2,1,0:T(8,128)}, u32[]{:S(2)}) copy-start(f32[16,64,64]{2,1,0:T(8,128)} %copy-done.2) | copy-start | bytes 786436
  88.6 18.4 %copy-start.5 = (f32[64,128]{1,0:T(8,128)S(1)}, f32[64,128]{1,0:T(8,128)}, u32[]{:S(2)}) copy-start(f32[64,128]{1,0:T(8,128)} %copy-done.4) | copy-start | bytes 98308
  88.6 18.4 %copy-start.7 = (f32[64,128]{1,0:T(8,128)S(1)}, f32[64,128]{1,0:T(8,128)}, u32[]{:S(2)}) copy-start(f32[64,128]{1,0:T(8,128)} %copy-done.6) | copy-start | bytes 98308
  88.6 18.3 %collective-permute-start.11 = (f32[64,128]{1,0:T(8,128)}, f32[64,128]{1,0:T(8,128)S(1)}, u32[]{:S(2)}, u32[]{:S(2)}) collective-permute-start(f32[64,128]{1,0:T(8,128)} %copy-done.8), channel_id=1, source_target_pairs={{0,64},{1,65},{2,66},{3,67},{4,68},{5,69},{6,70},{7,71},{8,72},{9,... | collective-permute-start | bytes 98312 | tf_op jit(solution)/shard_map/ppermute | solution.py:369
Sparse Core Ops, SparseCore 0:
  10.8 67.1 all-gather.1

commit v9 on v7

--- a/solution.py
+++ b/solution.py
@@ -88,14 +88,14 @@
     for tail in tails:
         tail.wait()
     for leaf, coefs in enumerate(exact):
-        clusters[parent[leaf]] += fine_t(up_held[leaf], coefs)
+        clusters[lax.rem(parent[leaf], clusters.shape[0])] += fine_t(up_held[leaf], coefs)
     total = fine_t(root_held[0], clusters[0])
     for cluster in range(1, root_held.shape[0]):
         total = total + fine_t(root_held[cluster], clusters[cluster])
     root_out[...] = total
 
 
-def leaf_coefficients(local_parent, panels, bases, up_transfer, root_transfer):
+def leaf_coefficients(leaf_parent, panels, bases, up_transfer, root_transfer):
     leaves, size, rhs = panels.shape
     rank = bases.shape[1]
     return pl.pallas_call(
@@ -118,7 +118,7 @@
         compiler_params=params(12),
         cost_estimate=cost(1000, 1000),
         name="coefs",
-    )(local_parent, *[in_hbm(array) for array in (panels, bases, up_transfer, root_transfer)])
+    )(leaf_parent, *[in_hbm(array) for array in (panels, bases, up_transfer, root_transfer)])
 
 
 def tables_kernel(nodes, transfer, coupling, transfer_out, coupling_out, held, sems):
@@ -208,10 +208,10 @@
     for cluster in range(root.shape[0]):
         clusters[cluster] = fine_dot(root[cluster], down)
     for leaf in range(up.shape[0]):
-        out[leaf] = fine_dot(up[leaf], clusters[parent[leaf]])
-
-
-def downward(local_parent, siblings, transfer, coupling, root_transfer, up_transfer):
+        out[leaf] = fine_dot(up[leaf], clusters[lax.rem(parent[leaf], root.shape[0])])
+
+
+def downward(leaf_parent, siblings, transfer, coupling, root_transfer, up_transfer):
     depth = len(siblings)
     rank, rhs = siblings[0].shape
     return pl.pallas_call(
@@ -223,14 +223,20 @@
         compiler_params=params(16),
         cost_estimate=cost(1000, 1000),
         name="downward",
-    )(local_parent, *siblings, transfer, coupling, root_transfer, up_transfer)
-
-
-def weights_kernel(count, coupling, out, held, sems):
+    )(leaf_parent, *siblings, transfer, coupling, root_transfer, up_transfer)
+
+
+def weights_kernel(count, coupling, bases, out, upright, held, basis, sems, basis_sem):
     leaves, slots, _, rank = coupling.shape
+    load = pltpu.make_async_copy(bases, basis, basis_sem)
     copies = [pltpu.make_async_copy(coupling.at[leaf], held.at[leaf], sems.at[leaf]) for leaf in range(leaves)]
-    for copy in copies:
+    for copy in [load] + copies:
         copy.start()
+    rows = lax.broadcasted_iota(jnp.int32, (rank, rank), 0)
+    unit = (rows == lax.broadcasted_iota(jnp.int32, (rank, rank), 1)).astype(bf16)
+    load.wait()
+    for leaf in range(leaves):
+        upright[leaf] = dot_t(basis[leaf], unit).astype(bf16)
     for leaf in range(leaves):
         used = count[leaf]
         copies[leaf].wait()
@@ -241,18 +247,27 @@
             out[leaf, :, 2 * pair * rank : 2 * (pair + 1) * rank] = joined
 
 
-def weights(far_count, far_coupling):
+def weights(far_count, far_coupling, bases):
     leaves, slots, rank, _ = far_coupling.shape
+    size = bases.shape[2]
     return pl.pallas_call(
         weights_kernel,
-        out_shape=jax.ShapeDtypeStruct((leaves, rank, slots * rank), bf16),
-        in_specs=[scalars(), anywhere()],
-        out_specs=whole(),
-        scratch_shapes=[pltpu.VMEM(far_coupling.shape, f32), pltpu.SemaphoreType.DMA((leaves,))],
+        out_shape=(
+            jax.ShapeDtypeStruct((leaves, rank, slots * rank), bf16),
+            jax.ShapeDtypeStruct((leaves, size, rank), bf16),
+        ),
+        in_specs=[scalars(), anywhere(), anywhere()],
+        out_specs=(whole(), whole()),
+        scratch_shapes=[
+            pltpu.VMEM(far_coupling.shape, f32),
+            pltpu.VMEM(bases.shape, bf16),
+            pltpu.SemaphoreType.DMA((leaves,)),
+            pltpu.SemaphoreType.DMA,
+        ],
         compiler_params=params(20),
         cost_estimate=cost(1000, 1000),
         name="weights",
-    )(far_count, in_hbm(far_coupling))
+    )(far_count, in_hbm(far_coupling), in_hbm(bases))
 
 
 def near_kernel(position, blocks, *refs):
@@ -309,7 +324,7 @@
 
 
 def final_kernel(rows, packed, coefs, on_leaf, bases, near_part, out, *scratch):
-    held, picked, results, term, basis, close, load_sems, near_sems, out_sems = scratch
+    held, results, term, basis, close, load_sems, near_sems, out_sems = scratch
     leaves, rank, wide = packed.shape
     slots = wide // rank
     loads = [
@@ -325,11 +340,10 @@
         load.start()
     stores = []
     for leaf in range(leaves):
-        for slot in range(slots):
-            picked[leaf, slot * rank : (slot + 1) * rank] = held[rows[leaf * slots + slot]]
-        expansion = (term[leaf] + dot(packed[leaf], picked[leaf])).astype(bf16)
+        tall = jnp.concatenate([held[rows[leaf * slots + slot]] for slot in range(slots)], axis=0)
+        expansion = (term[leaf] + dot(packed[leaf], tall)).astype(bf16)
         nears[leaf].wait()
-        results[leaf] = (dot_t(basis[leaf], expansion) + close[leaf]).astype(bf16)
+        results[leaf] = (dot(basis[leaf], expansion) + close[leaf]).astype(bf16)
         stores.append(pltpu.make_async_copy(results.at[leaf], out.at[leaf], out_sems.at[leaf]))
         stores[leaf].start()
     for store in stores:
@@ -337,9 +351,8 @@
 
 
 def final(far_rows, packed, slab_coefs, on_leaf, bases, near_part):
-    leaves, rank, size = bases.shape
+    leaves, size, rank = bases.shape
     rhs = near_part.shape[2]
-    wide = packed.shape[2]
     return pl.pallas_call(
         final_kernel,
         out_shape=jax.ShapeDtypeStruct((leaves, size, rhs), bf16),
@@ -347,7 +360,6 @@
         out_specs=anywhere(),
         scratch_shapes=[
             pltpu.VMEM(slab_coefs.shape, bf16),
-            pltpu.VMEM((leaves, wide, rhs), bf16),
             pltpu.VMEM((leaves, size, rhs), bf16),
             pltpu.VMEM(on_leaf.shape, f32),
             pltpu.VMEM(bases.shape, bf16),
@@ -397,7 +409,6 @@
     leaf_total, leaf_size, _ = bases.shape
     bases = bases.transpose(0, 2, 1)
     rhs_count = sources.shape[1]
-    cluster_total = leaf_total // 2
     slab_count = lax.axis_size("slab")
     sector_count = lax.axis_size("sector")
     devices = slab_count * sector_count
@@ -407,8 +418,7 @@
     device = slab_pos * sector_count + sector_pos
     panels = sources.reshape(leaf_total, leaf_size, rhs_count)
 
-    local_parent = leaf_parent - device * cluster_total
-    leaf_coefs, root = leaf_coefficients(local_parent, panels, bases, up_transfer, root_transfer)
+    leaf_coefs, root = leaf_coefficients(leaf_parent, panels, bases, up_transfer, root_transfer)
     slab_coefs = lax.all_gather(leaf_coefs, "sector", axis=0, tiled=True)
 
     owner_device = near_list // leaf_total
@@ -426,10 +436,10 @@
     nodes = ((devices + device) >> level_of) ^ flips
     transfer, coupling = tables(nodes[:, None], top_transfer, top_coupling)
     below, above = both(panels, "slab", False)
-    packed = weights(far_count, far_coupling)
-
-    root, below, above, packed, transfer, position, far_rows = after(
-        root, below, above, packed, transfer, position, far_rows
+    packed, upright = weights(far_count, far_coupling, bases)
+
+    root, below, above, packed, upright, transfer, position, far_rows = after(
+        root, below, above, packed, upright, transfer, position, far_rows
     )
     quad = [root] + [partner(root, both_axes, flip) for flip in (1, 2, 3)]
     flat = after(*quad, *sides)
@@ -449,8 +459,8 @@
         siblings.append(sibling)
         if level < depth - 1:
             current = combine(level, depth + level, current, sibling, transfer)
-    on_leaf = downward(local_parent, siblings, transfer, coupling, root_transfer, up_transfer)
-    field = final(far_rows, packed, slab_coefs, on_leaf, bases, near_part)
+    on_leaf = downward(leaf_parent, siblings, transfer, coupling, root_transfer, up_transfer)
+    field = final(far_rows, packed, slab_coefs, on_leaf, upright, near_part)
     return field.reshape(leaf_total * leaf_size, rhs_count)
 
 

time: 114 us -> 115 us (level)
  waiting for transfers between devices: 22.8 us -> 20.5 us
  local copies, waits for them, and re-layouts: 1.73 us -> 3.59 us
  Pallas kernels: 38.9 us -> 40.7 us
    ppermute x8, waiting for transfers between devices: 10.1 us -> 7.83 us  [shifted(): return lax.ppermute(array, axis, pairs)]
    pallas_call x1, Pallas kernels: 4.27 us -> 6.35 us  [weights(): pl.pallas_call(weights_kernel, out_shape=(jax.ShapeDtypeStruct((leaves, r...]
    unnamed x14 -> x20, local copies, waits for them, and re-layouts: 1.49 us -> 3.35 us
  transfers between devices with their start and end apart: 17 -> 17, of which waited for: 7 -> 7; matrix products, arithmetic and copies ran while one was open for 0% -> 0% of each run, Pallas kernels for 24% -> 25%
where the time goes in v9:
time: 115 us; the launch traced here: 114 us
  Pallas kernels  40.7 us (35%)
  starting transfers between devices  35.8 us (31%)
  waiting for transfers between devices  20.5 us (18%)
  between operations  13.7 us (12%)
  local copies, waits for them, and re-layouts  3.59 us (3%)
    ppermute x8, starting transfers between devices, shifted(): return lax.ppermute(array, axis, pairs)  24.1 us
    ppermute x8, waiting for transfers between devices, partner(): lax.ppermute(array, axis, [(i, i ^ flip) for i in range(lax.axis_size(axi...  12.7 us
    pallas_call x1, Pallas kernels, near(): pl.pallas_call(near_kernel, out_shape=pltpu.HBM((leaves, size, rhs), f32)...  11.8 us
    ppermute x8, starting transfers between devices, partner(): lax.ppermute(array, axis, [(i, i ^ flip) for i in range(lax.axis_size(axi...  11.8 us
    pallas_call x1, Pallas kernels, final(): pl.pallas_call(final_kernel, out_shape=jax.ShapeDtypeStruct((leaves, size...  8.08 us
    ppermute x8, waiting for transfers between devices, shifted(): return lax.ppermute(array, axis, pairs)  7.83 us
    pallas_call x1, Pallas kernels, tables(): pl.pallas_call(tables_kernel, out_shape=(jax.ShapeDtypeStruct((count, ran...  7.59 us
    pallas_call x1, Pallas kernels, weights(): pl.pallas_call(weights_kernel, out_shape=(jax.ShapeDtypeStruct((leaves, r...  6.35 us
  transfers between devices with their start and end apart: 17, of which 7 were waited for; matrix products, arithmetic and copies ran while one was open for 0% of the time, Pallas kernels for 25%

profile of v9, /device:TPU:1, one launch (start us, length us, event | category | flops | bytes accessed | tf_op | source)
XLA Modules:
  0.0 114.4 jit_solution(15788711752320644439)
XLA Ops:
  6.5 0.7 copy-done.5
  7.2 3.5 %coefs.1 = (bf16[16,64,128]{2,1,0:T(8,128)(2,1)}, f32[64,128]{1,0:T(8,128)S(1)}) custom-call(s32[16]{0:T(128)S(1)} %copy-done.5, bf16[16,256,128]{2,1,0:T(8,128)(2,1)} %bitcast.7, bf16[16,64,256]{2,1,0:T(8,128)(2,1)} %bitcast.13, f32[16,64,64]{2,1,0:T(8,128)} %refs_11_.1, f32[8,64,64]{2,1,0:T(8,128)} %refs_10_.1), custom_call_target="tpu_custom_call" | custom-call | flops 1000 | bytes 1000 | tf_op jit(solution)/shard_map/coefs/pallas_call | solution.py:101
  10.7 4.9 %collective-permute-start = (bf16[16,256,128]{2,1,0:T(8,128)(2,1)}, bf16[16,256,128]{2,1,0:T(8,128)(2,1)}, u32[]{:S(2)}, u32[]{:S(2)}) collective-permute-start(bf16[16,256,128]{2,1,0:T(8,128)(2,1)} %bitcast.8), channel_id=1, source_target_pairs={{0,16},{16,32},{32,48},{48,64},{64,80},{80,96},{96,112},{1,17},{17... | collective-permute-start | bytes 3145736 | tf_op jit(solution)/shard_map/ppermute | solution.py:380
  15.6 1.9 %collective-permute-start.1 = (bf16[16,256,128]{2,1,0:T(8,128)(2,1)}, bf16[16,256,128]{2,1,0:T(8,128)(2,1)}, u32[]{:S(2)}, u32[]{:S(2)}) collective-permute-start(bf16[16,256,128]{2,1,0:T(8,128)(2,1)} %bitcast.9), channel_id=1, source_target_pairs={{16,0},{32,16},{48,32},{64,48},{80,64},{96,80},{112,96},{17,1},{33... | collective-permute-start | bytes 3145736 | tf_op jit(solution)/shard_map/ppermute | solution.py:380
  17.6 1.3 %collective-permute-start.5 = (bf16[16,256,128]{2,1,0:T(8,128)(2,1)}, bf16[16,256,128]{2,1,0:T(8,128)(2,1)}, u32[]{:S(2)}, u32[]{:S(2)}) collective-permute-start(bf16[16,256,128]{2,1,0:T(8,128)(2,1)} %bitcast.10), channel_id=1, source_target_pairs={{0,1},{1,2},{2,3},{3,4},{4,5},{5,6},{6,7},{7,8},{8,9},{9,10},{10,1... | collective-permute-start | bytes 3145736 | tf_op jit(solution)/shard_map/ppermute | solution.py:380
  18.8 3.8 %collective-permute-start.6 = (bf16[16,256,128]{2,1,0:T(8,128)(2,1)}, bf16[16,256,128]{2,1,0:T(8,128)(2,1)}, u32[]{:S(2)}, u32[]{:S(2)}) collective-permute-start(bf16[16,256,128]{2,1,0:T(8,128)(2,1)} %bitcast.11), channel_id=1, source_target_pairs={{0,15},{1,0},{2,1},{3,2},{4,3},{5,4},{6,5},{7,6},{8,7},{9,8},{10,9... | collective-permute-start | bytes 3145736 | tf_op jit(solution)/shard_map/ppermute | solution.py:380
  22.6 0.7 copy-done.7
  23.3 6.3 %weights.1 = (bf16[16,64,1024]{2,1,0:T(8,128)(2,1)S(1)}, bf16[16,256,64]{2,1,0:T(8,128)(2,1)S(1)}) custom-call(s32[16]{0:T(128)S(1)} %copy-done.7, f32[16,16,64,64]{3,2,1,0:T(8,128)} %coupling.1, bf16[16,64,256]{2,1,0:T(8,128)(2,1)} %bitcast.14), custom_call_target="tpu_custom_call" | custom-call | flops 1000 | bytes 1000 | tf_op jit(solution)/shard_map/weights/pallas_call | solution.py:253
  29.7 1.0 copy-done.2
  30.7 7.6 %tables.1 = (f32[16,64,64]{2,1,0:T(8,128)S(1)}, f32[16,64,64]{2,1,0:T(8,128)S(1)}) custom-call(s32[16,1]{1,0:T(8,128)S(1)} %fusion.11.nodes, f32[64,64,256]{2,1,0:T(8,128)} %bitcast.5, f32[64,64,256]{2,1,0:T(8,128)} %bitcast.6), custom_call_target="tpu_custom_call" | custom-call | flops 1000 | bytes 1000 | tf_op jit(solution)/shard_map/tables/pallas_call | solution.py:152
  38.8 3.8 %collective-permute-start.4 = (f32[64,128]{1,0:T(8,128)S(1)}, f32[64,128]{1,0:T(8,128)S(1)}, u32[]{:S(2)}, u32[]{:S(2)}) collective-permute-start(f32[64,128]{1,0:T(8,128)S(1)} %get-tuple-element.38.refs_0_), channel_id=1, source_target_pairs={{0,3},{1,2},{2,1},{3,0},{4,7},{5,6},{6,5},{7,4},{8,11},{9,10},{10,... | collective-permute-start | bytes 98312 | tf_op jit(solution)/shard_map/ppermute | solution.py:392
  42.5 7.2 %collective-permute-done.5.refs_3_ = bf16[16,256,128]{2,1,0:T(8,128)(2,1)} collective-permute-done((bf16[16,256,128]{2,1,0:T(8,128)(2,1)}, bf16[16,256,128]{2,1,0:T(8,128)(2,1)}, u32[]{:S(2)}, u32[]{:S(2)}) %collective-permute-start.5) | collective-permute-done | bytes 1048608 | tf_op jit(solution)/shard_map/ppermute | solution.py:380
  49.7 0.6 collective-permute-done.6.refs_6_
  50.4 0.2 collective-permute-done.4.refs_3_
  50.6 1.9 %collective-permute-start.12 = (bf16[16,256,128]{2,1,0:T(8,128)(2,1)}, bf16[16,256,128]{2,1,0:T(8,128)(2,1)S(1)}, u32[]{:S(2)}, u32[]{:S(2)}) collective-permute-start(bf16[16,256,128]{2,1,0:T(8,128)(2,1)} %collective-permute-done.5.refs_3_), channel_id=1, source_target_pairs={{16,0},{32,16},{48,32},{64,48},{80,64},{96,80},{112,96},{17,1},{33... | collective-permute-start | bytes 3145736 | tf_op jit(solution)/shard_map/ppermute | solution.py:380
  52.5 4.7 %collective-permute-start.13 = (bf16[16,256,128]{2,1,0:T(8,128)(2,1)}, bf16[16,256,128]{2,1,0:T(8,128)(2,1)S(1)}, u32[]{:S(2)}, u32[]{:S(2)}) collective-permute-start(bf16[16,256,128]{2,1,0:T(8,128)(2,1)} %collective-permute-done.5.refs_3_), channel_id=1, source_target_pairs={{0,16},{16,32},{32,48},{48,64},{64,80},{80,96},{96,112},{1,17},{17... | collective-permute-start | bytes 3145736 | tf_op jit(solution)/shard_map/ppermute | solution.py:380
  57.2 1.9 %collective-permute-start.14 = (bf16[16,256,128]{2,1,0:T(8,128)(2,1)}, bf16[16,256,128]{2,1,0:T(8,128)(2,1)S(1)}, u32[]{:S(2)}, u32[]{:S(2)}) collective-permute-start(bf16[16,256,128]{2,1,0:T(8,128)(2,1)} %collective-permute-done.6.refs_6_), channel_id=1, source_target_pairs={{16,0},{32,16},{48,32},{64,48},{80,64},{96,80},{112,96},{17,1},{33... | collective-permute-start | bytes 3145736 | tf_op jit(solution)/shard_map/ppermute | solution.py:380
  59.1 3.6 %collective-permute-start.15 = (bf16[16,256,128]{2,1,0:T(8,128)(2,1)}, bf16[16,256,128]{2,1,0:T(8,128)(2,1)S(1)}, u32[]{:S(2)}, u32[]{:S(2)}) collective-permute-start(bf16[16,256,128]{2,1,0:T(8,128)(2,1)} %collective-permute-done.6.refs_6_), channel_id=1, source_target_pairs={{0,16},{16,32},{32,48},{48,64},{64,80},{80,96},{96,112},{1,17},{17... | collective-permute-start | bytes 3145736 | tf_op jit(solution)/shard_map/ppermute | solution.py:380
  62.8 0.4 combine_four.1
  63.2 0.7 collective-permute-start.7
  63.9 3.2 %collective-permute-done.7.refs_1_.refs_3_ = f32[64,128]{1,0:T(8,128)S(1)} collective-permute-done((f32[64,128]{1,0:T(8,128)S(1)}, f32[64,128]{1,0:T(8,128)S(1)}, u32[]{:S(2)}, u32[]{:S(2)}) %collective-permute-start.7) | collective-permute-done | bytes 32800 | tf_op jit(solution)/shard_map/ppermute | solution.py:392
  67.3 2.3 %collective-permute-start.8 = (f32[64,128]{1,0:T(8,128)S(1)}, f32[64,128]{1,0:T(8,128)S(1)}, u32[]{:S(2)}, u32[]{:S(2)}) collective-permute-start(f32[64,128]{1,0:T(8,128)S(1)} %combine.4.refs_0_), channel_id=1, source_target_pairs={{0,8},{1,9},{2,10},{3,11},{4,12},{5,13},{6,14},{7,15},{8,0},{9,1},... | collective-permute-start | bytes 98312 | tf_op jit(solution)/shard_map/ppermute | solution.py:392
  69.7 3.3 %collective-permute-done.8.refs_1_.refs_4_ = f32[64,128]{1,0:T(8,128)S(1)} collective-permute-done((f32[64,128]{1,0:T(8,128)S(1)}, f32[64,128]{1,0:T(8,128)S(1)}, u32[]{:S(2)}, u32[]{:S(2)}) %collective-permute-start.8) | collective-permute-done | bytes 32800 | tf_op jit(solution)/shard_map/ppermute | solution.py:392
  73.1 0.5 collective-permute-start.9
  73.6 0.9 collective-permute-done.9.refs_1_.refs_5_
  74.7 1.3 %collective-permute-start.10 = (f32[64,128]{1,0:T(8,128)S(1)}, f32[64,128]{1,0:T(8,128)S(1)}, u32[]{:S(2)}, u32[]{:S(2)}) collective-permute-start(f32[64,128]{1,0:T(8,128)S(1)} %combine.6.refs_0_), channel_id=1, source_target_pairs={{0,32},{1,33},{2,34},{3,35},{4,36},{5,37},{6,38},{7,39},{8,40},{9,... | collective-permute-start | bytes 98312 | tf_op jit(solution)/shard_map/ppermute | solution.py:392
  76.0 5.1 %collective-permute-done.10.refs_1_.refs_6_ = f32[64,128]{1,0:T(8,128)S(1)} collective-permute-done((f32[64,128]{1,0:T(8,128)S(1)}, f32[64,128]{1,0:T(8,128)S(1)}, u32[]{:S(2)}, u32[]{:S(2)}) %collective-permute-start.10) | collective-permute-done | bytes 32800 | tf_op jit(solution)/shard_map/ppermute | solution.py:392
  81.3 3.0 %collective-permute-start.11 = (f32[64,128]{1,0:T(8,128)S(1)}, f32[64,128]{1,0:T(8,128)S(1)}, u32[]{:S(2)}, u32[]{:S(2)}) collective-permute-start(f32[64,128]{1,0:T(8,128)S(1)} %combine.7), channel_id=1, source_target_pairs={{0,64},{1,65},{2,66},{3,67},{4,68},{5,69},{6,70},{7,71},{8,72},{9,... | collective-permute-start | bytes 98312 | tf_op jit(solution)/shard_map/ppermute | solution.py:392
  84.3 11.8 %near.1.near_part = f32[16,256,128]{2,1,0:T(8,128)} custom-call(s32[128]{0:T(128)S(1)} %reshape.101.position, bf16[16,8,256,256]{3,2,1,0:T(8,128)(2,1)} %blocks.1, bf16[16,256,128]{2,1,0:T(8,128)(2,1)} %bitcast.12, bf16[16,256,128]{2,1,0:T(8,128)(2,1)} %collective-permute-done.1.refs_1_, bf16[16,256,128]{2,1,0:T(8,128)(2,1)} %collective-permute-done.refs_2_, ...), custom_call_target="tpu_custom_call" | custom-call | flops 1000 | bytes 1000 | tf_op jit(solution)/shard_map/near/pallas_call | solution.py:307
  96.2 1.0 copy-done.4
  97.2 2.2 %downward.1.on_leaf = f32[16,64,128]{2,1,0:T(8,128)S(1)} custom-call(s32[16]{0:T(128)S(1)} %copy-done.6, f32[64,128]{1,0:T(8,128)S(1)} %collective-permute-done.2.refs_1_, f32[64,128]{1,0:T(8,128)S(1)} %get-tuple-element.42.refs_2_, f32[64,128]{1,0:T(8,128)S(1)} %collective-permute-done.7.refs_1_.refs_3_, ...), custom_call_target="tpu_custom_call" | custom-call | flops 1000 | bytes 1000 | tf_op jit(solution)/shard_map/downward/pallas_call | solution.py:217
  99.4 8.1 %final.1 = bf16[16,256,128]{2,1,0:T(8,128)(2,1)} custom-call(s32[256]{0:T(256)S(1)} %reshape.102.rows, bf16[16,64,1024]{2,1,0:T(8,128)(2,1)S(1)} %get-tuple-element.34.packed, bf16[256,64,128]{2,1,0:T(8,128)(2,1)} %all-gather.2.cloned.1.call-done.coefs, f32[16,64,128]{2,1,0:T(8,128)S(1)} %downward.1.on_leaf, bf16[16,256,64]{2,1,0:T(8,128)(2,1)} %copy-done.2, ...), custom_call_target="tpu_custom_call" | custom-call | flops 1000 | bytes 1000 | tf_op jit(solution)/shard_map/final/pallas_call | solution.py:356
  (40 shorter events, 1.4 us)
Async XLA Ops:
  6.5 92.9 %all-gather.2.cloned.1.call-start = ((), (), s32[]{:S(2)}) async-start(), calls=%async_computation | async-start | bytes 4456448 | tf_op jit(solution)/shard_map/all_gather | solution.py:422
  6.5 0.7 copy-start.5
  10.7 27.9 %collective-permute-start = (bf16[16,256,128]{2,1,0:T(8,128)(2,1)}, bf16[16,256,128]{2,1,0:T(8,128)(2,1)}, u32[]{:S(2)}, u32[]{:S(2)}) collective-permute-start(bf16[16,256,128]{2,1,0:T(8,128)(2,1)} %bitcast.8), channel_id=1, source_target_pairs={{0,16},{16,32},{32,48},{48,64},{64,80},{80,96},{96,112},{1,17},{17... | collective-permute-start | bytes 3145736 | tf_op jit(solution)/shard_map/ppermute | solution.py:380
  15.6 23.0 %collective-permute-start.1 = (bf16[16,256,128]{2,1,0:T(8,128)(2,1)}, bf16[16,256,128]{2,1,0:T(8,128)(2,1)}, u32[]{:S(2)}, u32[]{:S(2)}) collective-permute-start(bf16[16,256,128]{2,1,0:T(8,128)(2,1)} %bitcast.9), channel_id=1, source_target_pairs={{16,0},{32,16},{48,32},{64,48},{80,64},{96,80},{112,96},{17,1},{33... | collective-permute-start | bytes 3145736 | tf_op jit(solution)/shard_map/ppermute | solution.py:380
  17.6 32.2 %collective-permute-start.5 = (bf16[16,256,128]{2,1,0:T(8,128)(2,1)}, bf16[16,256,128]{2,1,0:T(8,128)(2,1)}, u32[]{:S(2)}, u32[]{:S(2)}) collective-permute-start(bf16[16,256,128]{2,1,0:T(8,128)(2,1)} %bitcast.10), channel_id=1, source_target_pairs={{0,1},{1,2},{2,3},{3,4},{4,5},{5,6},{6,7},{7,8},{8,9},{9,10},{10,1... | collective-permute-start | bytes 3145736 | tf_op jit(solution)/shard_map/ppermute | solution.py:380
  18.8 31.5 %collective-permute-start.6 = (bf16[16,256,128]{2,1,0:T(8,128)(2,1)}, bf16[16,256,128]{2,1,0:T(8,128)(2,1)}, u32[]{:S(2)}, u32[]{:S(2)}) collective-permute-start(bf16[16,256,128]{2,1,0:T(8,128)(2,1)} %bitcast.11), channel_id=1, source_target_pairs={{0,15},{1,0},{2,1},{3,2},{4,3},{5,4},{6,5},{7,6},{8,7},{9,8},{10,9... | collective-permute-start | bytes 3145736 | tf_op jit(solution)/shard_map/ppermute | solution.py:380
  22.6 0.7 copy-start.7
  29.7 1.0 copy-start.2
  30.6 7.6 %copy-start.9 = (s32[16,8]{0,1:T(8,128)S(1)}, s32[16,8]{0,1:T(8,128)}, u32[]{:S(2)}) copy-start(s32[16,8]{0,1:T(8,128)} %param.19) | copy-start | bytes 1540
  30.7 7.8 %copy-start.8 = (s32[16,16]{1,0:T(8,128)S(1)}, s32[16,16]{1,0:T(8,128)}, u32[]{:S(2)}) copy-start(s32[16,16]{1,0:T(8,128)} %param.21) | copy-start | bytes 3076
  38.3 57.9 %copy-start.3 = (f32[16,64,64]{2,1,0:T(8,128)}, f32[16,64,64]{2,1,0:T(8,128)S(1)}, u32[]{:S(2)}) copy-start(f32[16,64,64]{2,1,0:T(8,128)S(1)} %get-tuple-element.50.refs_9_) | copy-start | bytes 786436
  38.6 11.8 %collective-permute-start.2 = (f32[64,128]{1,0:T(8,128)S(1)}, f32[64,128]{1,0:T(8,128)S(1)}, u32[]{:S(2)}, u32[]{:S(2)}) collective-permute-start(f32[64,128]{1,0:T(8,128)S(1)} %get-tuple-element.38.refs_0_), channel_id=1, source_target_pairs={{0,1},{1,0},{2,3},{3,2},{4,5},{5,4},{6,7},{7,6},{8,9},{9,8},{10,11... | collective-permute-start | bytes 98312 | tf_op jit(solution)/shard_map/ppermute | solution.py:392
  38.7 11.7 %collective-permute-start.3 = (f32[64,128]{1,0:T(8,128)S(1)}, f32[64,128]{1,0:T(8,128)S(1)}, u32[]{:S(2)}, u32[]{:S(2)}) collective-permute-start(f32[64,128]{1,0:T(8,128)S(1)} %get-tuple-element.38.refs_0_), channel_id=1, source_target_pairs={{0,2},{1,3},{2,0},{3,1},{4,6},{5,7},{6,4},{7,5},{8,10},{9,11},{10,... | collective-permute-start | bytes 98312 | tf_op jit(solution)/shard_map/ppermute | solution.py:392
  38.8 11.8 %collective-permute-start.4 = (f32[64,128]{1,0:T(8,128)S(1)}, f32[64,128]{1,0:T(8,128)S(1)}, u32[]{:S(2)}, u32[]{:S(2)}) collective-permute-start(f32[64,128]{1,0:T(8,128)S(1)} %get-tuple-element.38.refs_0_), channel_id=1, source_target_pairs={{0,3},{1,2},{2,1},{3,0},{4,7},{5,6},{6,5},{7,4},{8,11},{9,10},{10,... | collective-permute-start | bytes 98312 | tf_op jit(solution)/shard_map/ppermute | solution.py:392
  50.6 33.7 %collective-permute-start.12 = (bf16[16,256,128]{2,1,0:T(8,128)(2,1)}, bf16[16,256,128]{2,1,0:T(8,128)(2,1)S(1)}, u32[]{:S(2)}, u32[]{:S(2)}) collective-permute-start(bf16[16,256,128]{2,1,0:T(8,128)(2,1)} %collective-permute-done.5.refs_3_), channel_id=1, source_target_pairs={{16,0},{32,16},{48,32},{64,48},{80,64},{96,80},{112,96},{17,1},{33... | collective-permute-start | bytes 3145736 | tf_op jit(solution)/shard_map/ppermute | solution.py:380
  52.5 31.8 %collective-permute-start.13 = (bf16[16,256,128]{2,1,0:T(8,128)(2,1)}, bf16[16,256,128]{2,1,0:T(8,128)(2,1)S(1)}, u32[]{:S(2)}, u32[]{:S(2)}) collective-permute-start(bf16[16,256,128]{2,1,0:T(8,128)(2,1)} %collective-permute-done.5.refs_3_), channel_id=1, source_target_pairs={{0,16},{16,32},{32,48},{48,64},{64,80},{80,96},{96,112},{1,17},{17... | collective-permute-start | bytes 3145736 | tf_op jit(solution)/shard_map/ppermute | solution.py:380
  57.2 27.1 %collective-permute-start.14 = (bf16[16,256,128]{2,1,0:T(8,128)(2,1)}, bf16[16,256,128]{2,1,0:T(8,128)(2,1)S(1)}, u32[]{:S(2)}, u32[]{:S(2)}) collective-permute-start(bf16[16,256,128]{2,1,0:T(8,128)(2,1)} %collective-permute-done.6.refs_6_), channel_id=1, source_target_pairs={{16,0},{32,16},{48,32},{64,48},{80,64},{96,80},{112,96},{17,1},{33... | collective-permute-start | bytes 3145736 | tf_op jit(solution)/shard_map/ppermute | solution.py:380
  59.1 25.2 %collective-permute-start.15 = (bf16[16,256,128]{2,1,0:T(8,128)(2,1)}, bf16[16,256,128]{2,1,0:T(8,128)(2,1)S(1)}, u32[]{:S(2)}, u32[]{:S(2)}) collective-permute-start(bf16[16,256,128]{2,1,0:T(8,128)(2,1)} %collective-permute-done.6.refs_6_), channel_id=1, source_target_pairs={{0,16},{16,32},{32,48},{48,64},{64,80},{80,96},{96,112},{1,17},{17... | collective-permute-start | bytes 3145736 | tf_op jit(solution)/shard_map/ppermute | solution.py:380
  63.2 3.9 %collective-permute-start.7 = (f32[64,128]{1,0:T(8,128)S(1)}, f32[64,128]{1,0:T(8,128)S(1)}, u32[]{:S(2)}, u32[]{:S(2)}) collective-permute-start(f32[64,128]{1,0:T(8,128)S(1)} %get-tuple-element.43.refs_0_), channel_id=1, source_target_pairs={{0,4},{1,5},{2,6},{3,7},{4,0},{5,1},{6,2},{7,3},{8,12},{9,13},{10,... | collective-permute-start | bytes 98312 | tf_op jit(solution)/shard_map/ppermute | solution.py:392
  67.3 5.6 %collective-permute-start.8 = (f32[64,128]{1,0:T(8,128)S(1)}, f32[64,128]{1,0:T(8,128)S(1)}, u32[]{:S(2)}, u32[]{:S(2)}) collective-permute-start(f32[64,128]{1,0:T(8,128)S(1)} %combine.4.refs_0_), channel_id=1, source_target_pairs={{0,8},{1,9},{2,10},{3,11},{4,12},{5,13},{6,14},{7,15},{8,0},{9,1},... | collective-permute-start | bytes 98312 | tf_op jit(solution)/shard_map/ppermute | solution.py:392
  73.1 1.3 %collective-permute-start.9 = (f32[64,128]{1,0:T(8,128)S(1)}, f32[64,128]{1,0:T(8,128)S(1)}, u32[]{:S(2)}, u32[]{:S(2)}) collective-permute-start(f32[64,128]{1,0:T(8,128)S(1)} %combine.5.refs_0_), channel_id=1, source_target_pairs={{0,16},{1,17},{2,18},{3,19},{4,20},{5,21},{6,22},{7,23},{8,24},{9,... | collective-permute-start | bytes 98312 | tf_op jit(solution)/shard_map/ppermute | solution.py:392
  74.7 6.4 %collective-permute-start.10 = (f32[64,128]{1,0:T(8,128)S(1)}, f32[64,128]{1,0:T(8,128)S(1)}, u32[]{:S(2)}, u32[]{:S(2)}) collective-permute-start(f32[64,128]{1,0:T(8,128)S(1)} %combine.6.refs_0_), channel_id=1, source_target_pairs={{0,32},{1,33},{2,34},{3,35},{4,36},{5,37},{6,38},{7,39},{8,40},{9,... | collective-permute-start | bytes 98312 | tf_op jit(solution)/shard_map/ppermute | solution.py:392
  81.3 14.9 %copy-start = (f32[16,64,64]{2,1,0:T(8,128)S(1)}, f32[16,64,64]{2,1,0:T(8,128)}, u32[]{:S(2)}) copy-start(f32[16,64,64]{2,1,0:T(8,128)} %refs_11_.1) | copy-start | bytes 786436
  81.3 14.9 %copy-start.1 = (f32[8,64,64]{2,1,0:T(8,128)S(1)}, f32[8,64,64]{2,1,0:T(8,128)}, u32[]{:S(2)}) copy-start(f32[8,64,64]{2,1,0:T(8,128)} %refs_10_.1) | copy-start | bytes 393220
  81.3 14.9 %copy-start.6 = (s32[16]{0:T(128)S(1)}, s32[16]{0:T(128)}, u32[]{:S(2)}) copy-start(s32[16]{0:T(128)} %refs_0_.1) | copy-start | bytes 196
  81.3 14.8 %collective-permute-start.11 = (f32[64,128]{1,0:T(8,128)S(1)}, f32[64,128]{1,0:T(8,128)S(1)}, u32[]{:S(2)}, u32[]{:S(2)}) collective-permute-start(f32[64,128]{1,0:T(8,128)S(1)} %combine.7), channel_id=1, source_target_pairs={{0,64},{1,65},{2,66},{3,67},{4,68},{5,69},{6,70},{7,71},{8,72},{9,... | collective-permute-start | bytes 98312 | tf_op jit(solution)/shard_map/ppermute | solution.py:392
  96.2 1.0 copy-start.4
Sparse Core Ops, SparseCore 0:
  10.8 69.1 all-gather.1

commit v10 on v7

--- a/solution.py
+++ b/solution.py
@@ -309,7 +309,7 @@
 
 
 def final_kernel(rows, packed, coefs, on_leaf, bases, near_part, out, *scratch):
-    held, picked, results, term, basis, close, load_sems, near_sems, out_sems = scratch
+    held, results, term, basis, close, load_sems, near_sems, out_sems = scratch
     leaves, rank, wide = packed.shape
     slots = wide // rank
     loads = [
@@ -325,9 +325,8 @@
         load.start()
     stores = []
     for leaf in range(leaves):
-        for slot in range(slots):
-            picked[leaf, slot * rank : (slot + 1) * rank] = held[rows[leaf * slots + slot]]
-        expansion = (term[leaf] + dot(packed[leaf], picked[leaf])).astype(bf16)
+        tall = jnp.concatenate([held[rows[leaf * slots + slot]] for slot in range(slots)], axis=0)
+        expansion = (term[leaf] + dot(packed[leaf], tall)).astype(bf16)
         nears[leaf].wait()
         results[leaf] = (dot_t(basis[leaf], expansion) + close[leaf]).astype(bf16)
         stores.append(pltpu.make_async_copy(results.at[leaf], out.at[leaf], out_sems.at[leaf]))
@@ -339,7 +338,6 @@
 def final(far_rows, packed, slab_coefs, on_leaf, bases, near_part):
     leaves, rank, size = bases.shape
     rhs = near_part.shape[2]
-    wide = packed.shape[2]
     return pl.pallas_call(
         final_kernel,
         out_shape=jax.ShapeDtypeStruct((leaves, size, rhs), bf16),
@@ -347,7 +345,6 @@
         out_specs=anywhere(),
         scratch_shapes=[
             pltpu.VMEM(slab_coefs.shape, bf16),
-            pltpu.VMEM((leaves, wide, rhs), bf16),
             pltpu.VMEM((leaves, size, rhs), bf16),
             pltpu.VMEM(on_leaf.shape, f32),
             pltpu.VMEM(bases.shape, bf16),

time: 114 us -> 114 us (level)
  no operation moved by 1% of the time
where the time goes in v10:
time: 114 us; the launch traced here: 113 us
  Pallas kernels  38.8 us (34%)
  starting transfers between devices  35.7 us (31%)
  waiting for transfers between devices  22.9 us (20%)
  between operations  13.7 us (12%)
  local copies, waits for them, and re-layouts  1.73 us (2%)
    ppermute x8, starting transfers between devices, shifted(): return lax.ppermute(array, axis, pairs)  24 us
    ppermute x8, waiting for transfers between devices, partner(): lax.ppermute(array, axis, [(i, i ^ flip) for i in range(lax.axis_size(axi...  12.7 us
    pallas_call x1, Pallas kernels, near(): pl.pallas_call(near_kernel, out_shape=pltpu.HBM((leaves, size, rhs), f32)...  11.8 us
    ppermute x8, starting transfers between devices, partner(): lax.ppermute(array, axis, [(i, i ^ flip) for i in range(lax.axis_size(axi...  11.6 us
    ppermute x8, waiting for transfers between devices, shifted(): return lax.ppermute(array, axis, pairs)  10.1 us
    pallas_call x1, Pallas kernels, final(): pl.pallas_call(final_kernel, out_shape=jax.ShapeDtypeStruct((leaves, size...  8.35 us
    pallas_call x1, Pallas kernels, tables(): pl.pallas_call(tables_kernel, out_shape=(jax.ShapeDtypeStruct((count, ran...  7.59 us
    pallas_call x1, Pallas kernels, weights(): pl.pallas_call(weights_kernel, out_shape=jax.ShapeDtypeStruct((leaves, ra...  4.27 us
  transfers between devices with their start and end apart: 17, of which 7 were waited for; matrix products, arithmetic and copies ran while one was open for 0% of the time, Pallas kernels for 24%

profile of v10, /device:TPU:1, one launch (start us, length us, event | category | flops | bytes accessed | tf_op | source)
XLA Modules:
  0.0 113.4 jit_solution(18346484638612818571)
XLA Ops:
  6.5 0.7 broadcast_subtract_fusion.1.parent.refs_0_
  7.2 3.4 %coefs.1 = (bf16[16,64,128]{2,1,0:T(8,128)(2,1)}, f32[64,128]{1,0:T(8,128)S(1)}) custom-call(s32[16]{0:T(128)S(1)} %broadcast_subtract_fusion.1.parent.refs_0_, bf16[16,256,128]{2,1,0:T(8,128)(2,1)} %bitcast.7, bf16[16,64,256]{2,1,0:T(8,128)(2,1)} %bitcast.13, f32[16,64,64]{2,1,0:T(8,128)} %refs_11_.1, f32[8,64,64]{2,1,0:T(8,128)} %refs_10_.1), custom_call_target="tpu_custom_call" | custom-call | flops 1000 | bytes 1000 | tf_op jit(solution)/shard_map/coefs/pallas_call | solution.py:101
  10.6 4.9 %collective-permute-start = (bf16[16,256,128]{2,1,0:T(8,128)(2,1)}, bf16[16,256,128]{2,1,0:T(8,128)(2,1)}, u32[]{:S(2)}, u32[]{:S(2)}) collective-permute-start(bf16[16,256,128]{2,1,0:T(8,128)(2,1)} %bitcast.8), channel_id=1, source_target_pairs={{0,16},{16,32},{32,48},{48,64},{64,80},{80,96},{96,112},{1,17},{17... | collective-permute-start | bytes 3145736 | tf_op jit(solution)/shard_map/ppermute | solution.py:365
  15.6 1.9 %collective-permute-start.1 = (bf16[16,256,128]{2,1,0:T(8,128)(2,1)}, bf16[16,256,128]{2,1,0:T(8,128)(2,1)}, u32[]{:S(2)}, u32[]{:S(2)}) collective-permute-start(bf16[16,256,128]{2,1,0:T(8,128)(2,1)} %bitcast.9), channel_id=1, source_target_pairs={{16,0},{32,16},{48,32},{64,48},{80,64},{96,80},{112,96},{17,1},{33... | collective-permute-start | bytes 3145736 | tf_op jit(solution)/shard_map/ppermute | solution.py:365
  17.5 1.3 %collective-permute-start.5 = (bf16[16,256,128]{2,1,0:T(8,128)(2,1)}, bf16[16,256,128]{2,1,0:T(8,128)(2,1)}, u32[]{:S(2)}, u32[]{:S(2)}) collective-permute-start(bf16[16,256,128]{2,1,0:T(8,128)(2,1)} %bitcast.10), channel_id=1, source_target_pairs={{0,1},{1,2},{2,3},{3,4},{4,5},{5,6},{6,7},{7,8},{8,9},{9,10},{10,1... | collective-permute-start | bytes 3145736 | tf_op jit(solution)/shard_map/ppermute | solution.py:365
  18.8 3.8 %collective-permute-start.6 = (bf16[16,256,128]{2,1,0:T(8,128)(2,1)}, bf16[16,256,128]{2,1,0:T(8,128)(2,1)}, u32[]{:S(2)}, u32[]{:S(2)}) collective-permute-start(bf16[16,256,128]{2,1,0:T(8,128)(2,1)} %bitcast.11), channel_id=1, source_target_pairs={{0,15},{1,0},{2,1},{3,2},{4,3},{5,4},{6,5},{7,6},{8,7},{9,8},{10,9... | collective-permute-start | bytes 3145736 | tf_op jit(solution)/shard_map/ppermute | solution.py:365
  22.6 0.7 copy-done.4
  23.3 4.3 %weights.1.packed = bf16[16,64,1024]{2,1,0:T(8,128)(2,1)S(1)} custom-call(s32[16]{0:T(128)S(1)} %copy-done.4, f32[16,16,64,64]{3,2,1,0:T(8,128)} %coupling.1), custom_call_target="tpu_custom_call" | custom-call | flops 1000 | bytes 1000 | tf_op jit(solution)/shard_map/weights/pallas_call | solution.py:246
  27.6 7.6 %tables.1 = (f32[16,64,64]{2,1,0:T(8,128)S(1)}, f32[16,64,64]{2,1,0:T(8,128)S(1)}) custom-call(s32[16,1]{1,0:T(8,128)S(1)} %fusion.11.nodes, f32[64,64,256]{2,1,0:T(8,128)} %bitcast.5, f32[64,64,256]{2,1,0:T(8,128)} %bitcast.6), custom_call_target="tpu_custom_call" | custom-call | flops 1000 | bytes 1000 | tf_op jit(solution)/shard_map/tables/pallas_call | solution.py:152
  35.2 0.8 copy-done.2
  36.5 3.8 %collective-permute-start.4 = (f32[64,128]{1,0:T(8,128)S(1)}, f32[64,128]{1,0:T(8,128)S(1)}, u32[]{:S(2)}, u32[]{:S(2)}) collective-permute-start(f32[64,128]{1,0:T(8,128)S(1)} %get-tuple-element.33.refs_0_), channel_id=1, source_target_pairs={{0,3},{1,2},{2,1},{3,0},{4,7},{5,6},{6,5},{7,4},{8,11},{9,10},{10,... | collective-permute-start | bytes 98312 | tf_op jit(solution)/shard_map/ppermute | solution.py:377
  40.2 9.5 %collective-permute-done.5.refs_3_ = bf16[16,256,128]{2,1,0:T(8,128)(2,1)} collective-permute-done((bf16[16,256,128]{2,1,0:T(8,128)(2,1)}, bf16[16,256,128]{2,1,0:T(8,128)(2,1)}, u32[]{:S(2)}, u32[]{:S(2)}) %collective-permute-start.5) | collective-permute-done | bytes 1048608 | tf_op jit(solution)/shard_map/ppermute | solution.py:365
  49.8 0.6 collective-permute-done.6.refs_6_
  50.4 0.2 collective-permute-done.4.refs_3_
  50.6 1.9 %collective-permute-start.12 = (bf16[16,256,128]{2,1,0:T(8,128)(2,1)}, bf16[16,256,128]{2,1,0:T(8,128)(2,1)S(1)}, u32[]{:S(2)}, u32[]{:S(2)}) collective-permute-start(bf16[16,256,128]{2,1,0:T(8,128)(2,1)} %collective-permute-done.5.refs_3_), channel_id=1, source_target_pairs={{16,0},{32,16},{48,32},{64,48},{80,64},{96,80},{112,96},{17,1},{33... | collective-permute-start | bytes 3145736 | tf_op jit(solution)/shard_map/ppermute | solution.py:365
  52.5 4.6 %collective-permute-start.13 = (bf16[16,256,128]{2,1,0:T(8,128)(2,1)}, bf16[16,256,128]{2,1,0:T(8,128)(2,1)S(1)}, u32[]{:S(2)}, u32[]{:S(2)}) collective-permute-start(bf16[16,256,128]{2,1,0:T(8,128)(2,1)} %collective-permute-done.5.refs_3_), channel_id=1, source_target_pairs={{0,16},{16,32},{32,48},{48,64},{64,80},{80,96},{96,112},{1,17},{17... | collective-permute-start | bytes 3145736 | tf_op jit(solution)/shard_map/ppermute | solution.py:365
  57.2 1.9 %collective-permute-start.14 = (bf16[16,256,128]{2,1,0:T(8,128)(2,1)}, bf16[16,256,128]{2,1,0:T(8,128)(2,1)S(1)}, u32[]{:S(2)}, u32[]{:S(2)}) collective-permute-start(bf16[16,256,128]{2,1,0:T(8,128)(2,1)} %collective-permute-done.6.refs_6_), channel_id=1, source_target_pairs={{16,0},{32,16},{48,32},{64,48},{80,64},{96,80},{112,96},{17,1},{33... | collective-permute-start | bytes 3145736 | tf_op jit(solution)/shard_map/ppermute | solution.py:365
  59.1 3.6 %collective-permute-start.15 = (bf16[16,256,128]{2,1,0:T(8,128)(2,1)}, bf16[16,256,128]{2,1,0:T(8,128)(2,1)S(1)}, u32[]{:S(2)}, u32[]{:S(2)}) collective-permute-start(bf16[16,256,128]{2,1,0:T(8,128)(2,1)} %collective-permute-done.6.refs_6_), channel_id=1, source_target_pairs={{0,16},{16,32},{32,48},{48,64},{64,80},{80,96},{96,112},{1,17},{17... | collective-permute-start | bytes 3145736 | tf_op jit(solution)/shard_map/ppermute | solution.py:365
  62.7 0.4 combine_four.1
  63.2 0.7 collective-permute-start.7
  63.9 3.2 %collective-permute-done.7.refs_1_.refs_3_ = f32[64,128]{1,0:T(8,128)S(1)} collective-permute-done((f32[64,128]{1,0:T(8,128)S(1)}, f32[64,128]{1,0:T(8,128)S(1)}, u32[]{:S(2)}, u32[]{:S(2)}) %collective-permute-start.7) | collective-permute-done | bytes 32800 | tf_op jit(solution)/shard_map/ppermute | solution.py:377
  67.3 2.3 %collective-permute-start.8 = (f32[64,128]{1,0:T(8,128)S(1)}, f32[64,128]{1,0:T(8,128)S(1)}, u32[]{:S(2)}, u32[]{:S(2)}) collective-permute-start(f32[64,128]{1,0:T(8,128)S(1)} %combine.4.refs_0_), channel_id=1, source_target_pairs={{0,8},{1,9},{2,10},{3,11},{4,12},{5,13},{6,14},{7,15},{8,0},{9,1},... | collective-permute-start | bytes 98312 | tf_op jit(solution)/shard_map/ppermute | solution.py:377
  69.6 3.3 %collective-permute-done.8.refs_1_.refs_4_ = f32[64,128]{1,0:T(8,128)S(1)} collective-permute-done((f32[64,128]{1,0:T(8,128)S(1)}, f32[64,128]{1,0:T(8,128)S(1)}, u32[]{:S(2)}, u32[]{:S(2)}) %collective-permute-start.8) | collective-permute-done | bytes 32800 | tf_op jit(solution)/shard_map/ppermute | solution.py:377
  73.1 0.5 collective-permute-start.9
  73.6 0.9 collective-permute-done.9.refs_1_.refs_5_
  74.4 0.2 combine.6.refs_0_
  74.6 1.3 %collective-permute-start.10 = (f32[64,128]{1,0:T(8,128)S(1)}, f32[64,128]{1,0:T(8,128)S(1)}, u32[]{:S(2)}, u32[]{:S(2)}) collective-permute-start(f32[64,128]{1,0:T(8,128)S(1)} %combine.6.refs_0_), channel_id=1, source_target_pairs={{0,32},{1,33},{2,34},{3,35},{4,36},{5,37},{6,38},{7,39},{8,40},{9,... | collective-permute-start | bytes 98312 | tf_op jit(solution)/shard_map/ppermute | solution.py:377
  76.0 5.1 %collective-permute-done.10.refs_1_.refs_6_ = f32[64,128]{1,0:T(8,128)S(1)} collective-permute-done((f32[64,128]{1,0:T(8,128)S(1)}, f32[64,128]{1,0:T(8,128)S(1)}, u32[]{:S(2)}, u32[]{:S(2)}) %collective-permute-start.10) | collective-permute-done | bytes 32800 | tf_op jit(solution)/shard_map/ppermute | solution.py:377
  81.3 2.9 %collective-permute-start.11 = (f32[64,128]{1,0:T(8,128)S(1)}, f32[64,128]{1,0:T(8,128)S(1)}, u32[]{:S(2)}, u32[]{:S(2)}) collective-permute-start(f32[64,128]{1,0:T(8,128)S(1)} %combine.7), channel_id=1, source_target_pairs={{0,64},{1,65},{2,66},{3,67},{4,68},{5,69},{6,70},{7,71},{8,72},{9,... | collective-permute-start | bytes 98312 | tf_op jit(solution)/shard_map/ppermute | solution.py:377
  84.1 11.8 %near.1.near_part = f32[16,256,128]{2,1,0:T(8,128)} custom-call(s32[128]{0:T(128)S(1)} %reshape.101.position, bf16[16,8,256,256]{3,2,1,0:T(8,128)(2,1)} %blocks.1, bf16[16,256,128]{2,1,0:T(8,128)(2,1)} %bitcast.12, bf16[16,256,128]{2,1,0:T(8,128)(2,1)} %collective-permute-done.1.refs_1_, bf16[16,256,128]{2,1,0:T(8,128)(2,1)} %collective-permute-done.refs_2_, ...), custom_call_target="tpu_custom_call" | custom-call | flops 1000 | bytes 1000 | tf_op jit(solution)/shard_map/near/pallas_call | solution.py:292
  96.0 2.2 %downward.1.on_leaf = f32[16,64,128]{2,1,0:T(8,128)S(1)} custom-call(s32[16]{0:T(128)S(1)} %broadcast_subtract_fusion.1.parent.refs_0_, f32[64,128]{1,0:T(8,128)S(1)} %collective-permute-done.2.refs_1_, f32[64,128]{1,0:T(8,128)S(1)} %get-tuple-element.37.refs_2_, f32[64,128]{1,0:T(8,128)S(1)} %collective-permute-done.7.refs_1_.refs_3_, ...), custom_call_target="tpu_custom_call" | custom-call | flops 1000 | bytes 1000 | tf_op jit(solution)/shard_map/downward/pallas_call | solution.py:217
  98.2 8.3 %final.1 = bf16[16,256,128]{2,1,0:T(8,128)(2,1)} custom-call(s32[256]{0:T(256)S(1)} %reshape.102.rows, bf16[16,64,1024]{2,1,0:T(8,128)(2,1)S(1)} %weights.1.packed, bf16[256,64,128]{2,1,0:T(8,128)(2,1)} %all-gather.2.cloned.1.call-done.coefs, f32[16,64,128]{2,1,0:T(8,128)S(1)} %downward.1.on_leaf, bf16[16,64,256]{2,1,0:T(8,128)(2,1)} %bitcast.14, ...), custom_call_target="tpu_custom_call" | custom-call | flops 1000 | bytes 1000 | tf_op jit(solution)/shard_map/final/pallas_call | solution.py:341
  (35 shorter events, 1.2 us)
Async XLA Ops:
  6.5 91.7 %all-gather.2.cloned.1.call-start = ((), (), s32[]{:S(2)}) async-start(), calls=%async_computation | async-start | bytes 4456448 | tf_op jit(solution)/shard_map/all_gather | solution.py:409
  10.6 25.7 %collective-permute-start = (bf16[16,256,128]{2,1,0:T(8,128)(2,1)}, bf16[16,256,128]{2,1,0:T(8,128)(2,1)}, u32[]{:S(2)}, u32[]{:S(2)}) collective-permute-start(bf16[16,256,128]{2,1,0:T(8,128)(2,1)} %bitcast.8), channel_id=1, source_target_pairs={{0,16},{16,32},{32,48},{48,64},{64,80},{80,96},{96,112},{1,17},{17... | collective-permute-start | bytes 3145736 | tf_op jit(solution)/shard_map/ppermute | solution.py:365
  15.6 20.7 %collective-permute-start.1 = (bf16[16,256,128]{2,1,0:T(8,128)(2,1)}, bf16[16,256,128]{2,1,0:T(8,128)(2,1)}, u32[]{:S(2)}, u32[]{:S(2)}) collective-permute-start(bf16[16,256,128]{2,1,0:T(8,128)(2,1)} %bitcast.9), channel_id=1, source_target_pairs={{16,0},{32,16},{48,32},{64,48},{80,64},{96,80},{112,96},{17,1},{33... | collective-permute-start | bytes 3145736 | tf_op jit(solution)/shard_map/ppermute | solution.py:365
  17.5 32.2 %collective-permute-start.5 = (bf16[16,256,128]{2,1,0:T(8,128)(2,1)}, bf16[16,256,128]{2,1,0:T(8,128)(2,1)}, u32[]{:S(2)}, u32[]{:S(2)}) collective-permute-start(bf16[16,256,128]{2,1,0:T(8,128)(2,1)} %bitcast.10), channel_id=1, source_target_pairs={{0,1},{1,2},{2,3},{3,4},{4,5},{5,6},{6,7},{7,8},{8,9},{9,10},{10,1... | collective-permute-start | bytes 3145736 | tf_op jit(solution)/shard_map/ppermute | solution.py:365
  18.8 31.6 %collective-permute-start.6 = (bf16[16,256,128]{2,1,0:T(8,128)(2,1)}, bf16[16,256,128]{2,1,0:T(8,128)(2,1)}, u32[]{:S(2)}, u32[]{:S(2)}) collective-permute-start(bf16[16,256,128]{2,1,0:T(8,128)(2,1)} %bitcast.11), channel_id=1, source_target_pairs={{0,15},{1,0},{2,1},{3,2},{4,3},{5,4},{6,5},{7,6},{8,7},{9,8},{10,9... | collective-permute-start | bytes 3145736 | tf_op jit(solution)/shard_map/ppermute | solution.py:365
  22.6 0.7 copy-start.4
  27.6 8.4 %copy-start.6 = (s32[16,8]{0,1:T(8,128)S(1)}, s32[16,8]{0,1:T(8,128)}, u32[]{:S(2)}) copy-start(s32[16,8]{0,1:T(8,128)} %param.19) | copy-start | bytes 1540
  27.6 8.6 %copy-start.5 = (s32[16,16]{1,0:T(8,128)S(1)}, s32[16,16]{1,0:T(8,128)}, u32[]{:S(2)}) copy-start(s32[16,16]{1,0:T(8,128)} %param.21) | copy-start | bytes 3076
  35.2 0.8 copy-start.2
  36.3 14.1 %collective-permute-start.2 = (f32[64,128]{1,0:T(8,128)S(1)}, f32[64,128]{1,0:T(8,128)S(1)}, u32[]{:S(2)}, u32[]{:S(2)}) collective-permute-start(f32[64,128]{1,0:T(8,128)S(1)} %get-tuple-element.33.refs_0_), channel_id=1, source_target_pairs={{0,1},{1,0},{2,3},{3,2},{4,5},{5,4},{6,7},{7,6},{8,9},{9,8},{10,11... | collective-permute-start | bytes 98312 | tf_op jit(solution)/shard_map/ppermute | solution.py:377
  36.4 14.0 %collective-permute-start.3 = (f32[64,128]{1,0:T(8,128)S(1)}, f32[64,128]{1,0:T(8,128)S(1)}, u32[]{:S(2)}, u32[]{:S(2)}) collective-permute-start(f32[64,128]{1,0:T(8,128)S(1)} %get-tuple-element.33.refs_0_), channel_id=1, source_target_pairs={{0,2},{1,3},{2,0},{3,1},{4,6},{5,7},{6,4},{7,5},{8,10},{9,11},{10,... | collective-permute-start | bytes 98312 | tf_op jit(solution)/shard_map/ppermute | solution.py:377
  36.5 14.1 %collective-permute-start.4 = (f32[64,128]{1,0:T(8,128)S(1)}, f32[64,128]{1,0:T(8,128)S(1)}, u32[]{:S(2)}, u32[]{:S(2)}) collective-permute-start(f32[64,128]{1,0:T(8,128)S(1)} %get-tuple-element.33.refs_0_), channel_id=1, source_target_pairs={{0,3},{1,2},{2,1},{3,0},{4,7},{5,6},{6,5},{7,4},{8,11},{9,10},{10,... | collective-permute-start | bytes 98312 | tf_op jit(solution)/shard_map/ppermute | solution.py:377
  50.6 33.5 %collective-permute-start.12 = (bf16[16,256,128]{2,1,0:T(8,128)(2,1)}, bf16[16,256,128]{2,1,0:T(8,128)(2,1)S(1)}, u32[]{:S(2)}, u32[]{:S(2)}) collective-permute-start(bf16[16,256,128]{2,1,0:T(8,128)(2,1)} %collective-permute-done.5.refs_3_), channel_id=1, source_target_pairs={{16,0},{32,16},{48,32},{64,48},{80,64},{96,80},{112,96},{17,1},{33... | collective-permute-start | bytes 3145736 | tf_op jit(solution)/shard_map/ppermute | solution.py:365
  52.5 31.6 %collective-permute-start.13 = (bf16[16,256,128]{2,1,0:T(8,128)(2,1)}, bf16[16,256,128]{2,1,0:T(8,128)(2,1)S(1)}, u32[]{:S(2)}, u32[]{:S(2)}) collective-permute-start(bf16[16,256,128]{2,1,0:T(8,128)(2,1)} %collective-permute-done.5.refs_3_), channel_id=1, source_target_pairs={{0,16},{16,32},{32,48},{48,64},{64,80},{80,96},{96,112},{1,17},{17... | collective-permute-start | bytes 3145736 | tf_op jit(solution)/shard_map/ppermute | solution.py:365
  57.2 27.0 %collective-permute-start.14 = (bf16[16,256,128]{2,1,0:T(8,128)(2,1)}, bf16[16,256,128]{2,1,0:T(8,128)(2,1)S(1)}, u32[]{:S(2)}, u32[]{:S(2)}) collective-permute-start(bf16[16,256,128]{2,1,0:T(8,128)(2,1)} %collective-permute-done.6.refs_6_), channel_id=1, source_target_pairs={{16,0},{32,16},{48,32},{64,48},{80,64},{96,80},{112,96},{17,1},{33... | collective-permute-start | bytes 3145736 | tf_op jit(solution)/shard_map/ppermute | solution.py:365
  59.1 25.1 %collective-permute-start.15 = (bf16[16,256,128]{2,1,0:T(8,128)(2,1)}, bf16[16,256,128]{2,1,0:T(8,128)(2,1)S(1)}, u32[]{:S(2)}, u32[]{:S(2)}) collective-permute-start(bf16[16,256,128]{2,1,0:T(8,128)(2,1)} %collective-permute-done.6.refs_6_), channel_id=1, source_target_pairs={{0,16},{16,32},{32,48},{48,64},{64,80},{80,96},{96,112},{1,17},{17... | collective-permute-start | bytes 3145736 | tf_op jit(solution)/shard_map/ppermute | solution.py:365
  63.2 3.9 %collective-permute-start.7 = (f32[64,128]{1,0:T(8,128)S(1)}, f32[64,128]{1,0:T(8,128)S(1)}, u32[]{:S(2)}, u32[]{:S(2)}) collective-permute-start(f32[64,128]{1,0:T(8,128)S(1)} %get-tuple-element.38.refs_0_), channel_id=1, source_target_pairs={{0,4},{1,5},{2,6},{3,7},{4,0},{5,1},{6,2},{7,3},{8,12},{9,13},{10,... | collective-permute-start | bytes 98312 | tf_op jit(solution)/shard_map/ppermute | solution.py:377
  67.3 5.6 %collective-permute-start.8 = (f32[64,128]{1,0:T(8,128)S(1)}, f32[64,128]{1,0:T(8,128)S(1)}, u32[]{:S(2)}, u32[]{:S(2)}) collective-permute-start(f32[64,128]{1,0:T(8,128)S(1)} %combine.4.refs_0_), channel_id=1, source_target_pairs={{0,8},{1,9},{2,10},{3,11},{4,12},{5,13},{6,14},{7,15},{8,0},{9,1},... | collective-permute-start | bytes 98312 | tf_op jit(solution)/shard_map/ppermute | solution.py:377
  73.1 1.3 %collective-permute-start.9 = (f32[64,128]{1,0:T(8,128)S(1)}, f32[64,128]{1,0:T(8,128)S(1)}, u32[]{:S(2)}, u32[]{:S(2)}) collective-permute-start(f32[64,128]{1,0:T(8,128)S(1)} %combine.5.refs_0_), channel_id=1, source_target_pairs={{0,16},{1,17},{2,18},{3,19},{4,20},{5,21},{6,22},{7,23},{8,24},{9,... | collective-permute-start | bytes 98312 | tf_op jit(solution)/shard_map/ppermute | solution.py:377
  74.6 6.4 %collective-permute-start.10 = (f32[64,128]{1,0:T(8,128)S(1)}, f32[64,128]{1,0:T(8,128)S(1)}, u32[]{:S(2)}, u32[]{:S(2)}) collective-permute-start(f32[64,128]{1,0:T(8,128)S(1)} %combine.6.refs_0_), channel_id=1, source_target_pairs={{0,32},{1,33},{2,34},{3,35},{4,36},{5,37},{6,38},{7,39},{8,40},{9,... | collective-permute-start | bytes 98312 | tf_op jit(solution)/shard_map/ppermute | solution.py:377
  81.2 14.8 %copy-start = (f32[16,64,64]{2,1,0:T(8,128)S(1)}, f32[16,64,64]{2,1,0:T(8,128)}, u32[]{:S(2)}) copy-start(f32[16,64,64]{2,1,0:T(8,128)} %refs_11_.1) | copy-start | bytes 786436
  81.2 14.8 %copy-start.1 = (f32[8,64,64]{2,1,0:T(8,128)S(1)}, f32[8,64,64]{2,1,0:T(8,128)}, u32[]{:S(2)}) copy-start(f32[8,64,64]{2,1,0:T(8,128)} %refs_10_.1) | copy-start | bytes 393220
  81.3 14.8 %copy-start.3 = (f32[16,64,64]{2,1,0:T(8,128)S(1)}, f32[16,64,64]{2,1,0:T(8,128)}, u32[]{:S(2)}) copy-start(f32[16,64,64]{2,1,0:T(8,128)} %copy-done.2) | copy-start | bytes 786436
  81.3 14.7 %collective-permute-start.11 = (f32[64,128]{1,0:T(8,128)S(1)}, f32[64,128]{1,0:T(8,128)S(1)}, u32[]{:S(2)}, u32[]{:S(2)}) collective-permute-start(f32[64,128]{1,0:T(8,128)S(1)} %combine.7), channel_id=1, source_target_pairs={{0,64},{1,65},{2,66},{3,67},{4,68},{5,69},{6,70},{7,71},{8,72},{9,... | collective-permute-start | bytes 98312 | tf_op jit(solution)/shard_map/ppermute | solution.py:377
Sparse Core Ops, SparseCore 0:
  10.8 69.3 all-gather.1
